TPU v7x, 128 devices: a whole 4x4x4 slice. The times are simulated.
128 devices in a mesh: gx: 8 (over x_hi, y), gy: 4 (over x_lo, core), gz: 4 (over z).
Axes of the slice: x: 4 (x_hi: 2, x_lo: 2; x = x_hi * 2 + x_lo), y: 4, z: 4, core: 2. Of those that a mesh axis runs over, the one named last changes fastest.
Arguments:
- preact: bfloat16 [16384, 12288], P('gx', 'gy'), may hold values from -6 to 6
- grad_output: bfloat16 [16384, 4608], P(('gx', 'gy'), 'gz'), may hold values from -1.5 to 1.5
- down_weight: bfloat16 [12288, 4608], P('gy', 'gz'), may hold values from -0.09375 to 0.09375
Outputs:
- grad_pre: bfloat16 [16384, 12288], P(('gx', 'gz'), 'gy')
- grad_down: bfloat16 [12288, 4608], P(('gy', 'gx'), 'gz')
All inputs are finite; a program needn't handle non-finite values.
Results may differ from a plain program's by a relative error of at most 0.013.
Values may be sent and summed in bfloat16 or wider, within the bound.
No kernel may reach another device: no remote copies, remote signals or barrier semaphores. Data moves between devices by JAX's collectives and lax.ppermute only.
A program may use at most 256 MiB of HBM per device.

v0:
```python
import math

import jax
import jax.numpy as jnp
from jax import lax
from jax.sharding import PartitionSpec as P

root_half = 1.0 / math.sqrt(2.0)
slope_scale = 1.0 / math.sqrt(2.0 * math.pi)


def unit_slope(values):
    return (
        0.5 * (1.0 + lax.erf(values * root_half))
        + values * jnp.exp(-0.5 * values * values) * slope_scale
    )


def shards(preact, grad_output, down_weight):
    pre_wide = preact.astype(jnp.float32)
    activation = (0.5 * pre_wide * (1.0 + lax.erf(pre_wide * root_half))).astype(jnp.bfloat16)
    output_rows = lax.all_gather(grad_output, "gy", axis=0, tiled=True)
    contract_cols = (((1,), (1,)), ((), ()))
    part = lax.dot_general(
        output_rows, down_weight, contract_cols, preferred_element_type=jnp.float32
    )
    share_rows = preact.shape[0] // lax.axis_size("gz")
    share_start = lax.axis_index("gz") * share_rows
    grad_act = lax.psum(part.astype(jnp.bfloat16), "gz").astype(jnp.float32)
    grad_full = (grad_act * unit_slope(pre_wide)).astype(jnp.bfloat16)
    grad_pre = lax.dynamic_slice_in_dim(grad_full, share_start, share_rows, 0)
    contract_rows = (((0,), (0,)), ((), ()))
    summed = lax.psum_scatter(
        lax.dot_general(
            activation, output_rows, contract_rows, preferred_element_type=jnp.float32
        ).astype(jnp.bfloat16),
        "gx",
        scatter_dimension=0,
        tiled=True,
    )
    return (grad_pre, summed)


def solution(mesh):
    return jax.shard_map(
        shards,
        mesh=mesh,
        in_specs=(P("gx", "gy"), P(("gx", "gy"), "gz"), P("gy", "gz")),
        out_specs=(P(("gx", "gz"), "gy"), P(("gy", "gx"), "gz")),
        check_vma=False,
    )
```

profile of v0, /device:TPU:0, one launch (start us, length us, event | category | flops | bytes accessed | tf_op | source)
XLA Modules:
  0.0 430.3 jit_solution(13618585214397267806)
XLA Ops:
  7.2 0.0 all-gather.2.cloned.1.call-start
  7.2 0.7 all-gather.2.cloned.1.call-update
  7.9 0.0 all-reduce.2.cloned.1.call-start
  7.9 54.5 %all-gather.2.cloned.1.call-done = bf16[2048,1152]{1,0:T(8,128)(2,1)} async-done(((bf16[512,1152]{1,0:T(8,128)(2,1)}), bf16[2048,1152]{1,0:T(8,128)(2,1)}) %all-gather.2.cloned.1.call-update) | async-done | bytes 4718608 | tf_op jit(solution)/shard_map/all_gather | solution.py:22
  62.4 22.1 %convolution_convert_fusion = bf16[2048,3072]{1,0:T(8,128)(2,1)} fusion(bf16[2048,1152]{1,0:T(8,128)(2,1)} %all-gather.2.cloned.1.call-done, bf16[3072,1152]{1,0:T(8,128)(2,1)} %param.5), kind=kOutput, calls=%fused_computation.6 | convolution fusion | flops 14501806080 | bytes 24379392 | tf_op jit(solution)/shard_map/dot_general | solution.py:24
  84.5 0.0 all-reduce.2.cloned.1.call-update
  84.5 0.2 reduce-scatter.2.cloned.1.call-start
  84.7 22.6 %multiply_multiply_fusion = (f32[2048,3072]{1,0:T(8,128)}, f32[2048,3072]{1,0:T(8,128)}) fusion(bf16[2048,3072]{1,0:T(8,128)(2,1)} %param.3), kind=kLoop, calls=%fused_computation | loop fusion | flops 31457280 | bytes 62914560 | tf_op jit(solution)/shard_map/mul | solution.py:15
  107.4 25.2 %fusion.2 = bf16[3072,1152]{1,0:T(8,128)(2,1)} fusion(bf16[2048,1152]{1,0:T(8,128)(2,1)} %all-gather.2.cloned.1.call-done, f32[2048,3072]{1,0:T(8,128)} %get-tuple-element.3, bf16[2048,3072]{1,0:T(8,128)(2,1)} %param.3), kind=kOutput, calls=%fused_computation.5 | convolution fusion | flops 14524219392 | bytes 49545216 | tf_op jit(solution)/shard_map/dot_general | solution.py:34
  132.6 0.0 reduce-scatter.2.cloned.1.call-update
  132.6 14.8 %convert_element_type.20 = f32[2048,3072]{1,0:T(8,128)} convert(bf16[2048,3072]{1,0:T(8,128)(2,1)} %param.3) | non-fusion elementwise | flops 6291456 | bytes 37748736 | tf_op jit(solution)/shard_map/convert_element_type | solution.py:20
  147.4 167.0 %all-reduce.2.cloned.1.call-done = bf16[2048,3072]{1,0:T(8,128)(2,1)} async-done(((bf16[2048,3072]{1,0:T(8,128)(2,1)}), bf16[2048,3072]{1,0:T(8,128)(2,1)}) %all-reduce.2.cloned.1.call-update) | async-done | bytes 12582928 | tf_op jit(solution)/shard_map/psum | solution.py:29
  314.4 10.2 %fusion.5 = bf16[512,3072]{1,0:T(8,128)(2,1)} fusion(f32[2048,3072]{1,0:T(8,128)} %get-tuple-element.3, s32[]{:T(128)S(6)} %select_n.3, f32[2048,3072]{1,0:T(8,128)} %convert_element_type.20, f32[2048,3072]{1,0:T(8,128)} %get-tuple-element.2, bf16[2048,3072]{1,0:T(8,128)(2,1)} %all-reduce.2.cloned.1.call-done), kind=kLoop, calls=%fused_computation.10 | loop fusion | flops 11010048 | bytes 25165828 | tf_op jit(solution)/shard_map/convert_element_type | solution.py:30
  324.6 99.2 %reduce-scatter.2.cloned.1.call-done = bf16[384,1152]{1,0:T(8,128)(2,1)} async-done(((bf16[3072,1152]{1,0:T(8,128)(2,1)}), bf16[384,1152]{1,0:T(8,128)(2,1)}) %reduce-scatter.2.cloned.1.call-update) | async-done | bytes 884752 | tf_op jit(solution)/shard_map/reduce_scatter | solution.py:33
Async XLA Ops:
  7.2 55.2 %all-gather.2.cloned.1.call-start = ((), (), s32[]{:S(2)}) async-start(), calls=%async_computation.1 | async-start | bytes 5898240 | tf_op jit(solution)/shard_map/all_gather | solution.py:22
  7.9 306.5 %all-reduce.2.cloned.1.call-start = ((), (), s32[]{:S(2)}) async-start(), calls=%async_computation.2 | async-start | bytes 25165824 | tf_op jit(solution)/shard_map/psum | solution.py:29
  84.5 339.3 %reduce-scatter.2.cloned.1.call-start = ((), (), s32[]{:S(2)}) async-start(), calls=%async_computation.3 | async-start | bytes 7962624 | tf_op jit(solution)/shard_map/reduce_scatter | solution.py:33
Sparse Core Ops, SparseCore 0:
  9.7 52.7 all-gather.1
  84.6 229.7 all-reduce.1
  318.9 104.7 reduce-scatter.1
where the time goes:
time: 431 us; the launch traced here: 430 us
  waiting for transfers between devices  321 us (74%)
  other arithmetic  47.6 us (11%)
  matrix products  47.3 us (11%)
  between operations  13.7 us (3%)
    psum x1, waiting for transfers between devices, shards(): grad_act = lax.psum(part.astype(jnp.bfloat16), 'gz').astype(jnp.float32)  167 us
    reduce_scatter x1, waiting for transfers between devices, shards(): lax.psum_scatter(lax.dot_general(activation, output_rows, contract_rows,...  99.2 us
    all_gather x1, waiting for transfers between devices, shards(): output_rows = lax.all_gather(grad_output, 'gy', axis=0, tiled=True)  54.5 us
    dot_general x1, matrix products, shards(): lax.dot_general(activation, output_rows, contract_rows, preferred_element...  25.2 us
    mul x1, other arithmetic, unit_slope(): -0.5 * values * values  22.6 us
    dot_general x1, matrix products, shards(): lax.dot_general(output_rows, down_weight, contract_cols, preferred_elemen...  22.1 us
    convert_element_type x1, other arithmetic, shards(): pre_wide = preact.astype(jnp.float32)  14.8 us
    convert_element_type x1, other arithmetic, shards(): grad_full = (grad_act * unit_slope(pre_wide)).astype(jnp.bfloat16)  10.2 us
  transfers between devices with their start and end apart: 3, of which 3 were waited for; matrix products, arithmetic and copies ran while one was open for 17% of the time, Pallas kernels for 0%

commit v1 on v0

v1 whole, which is shorter than its diff:
```python
import math

import jax
import jax.numpy as jnp
from jax import lax
from jax.sharding import PartitionSpec as P

root_half = 1.0 / math.sqrt(2.0)
slope_scale = 1.0 / math.sqrt(2.0 * math.pi)
STAGES = ((0, 128), (128, 256), (256, 384), (384, 512))
bf16 = jnp.bfloat16
f32 = jnp.float32


def unit_slope(values):
    return (
        0.5 * (1.0 + lax.erf(values * root_half))
        + values * jnp.exp(-0.5 * values * values) * slope_scale
    )


def gz_ring(step):
    return [(i, (i + step) % 4) for i in range(4)]


def gx_move(dh, dy):
    return [(h * 4 + y, (h + dh) % 2 * 4 + (y + dy) % 4) for h in range(2) for y in range(4)]


def gy_move(dl, dc):
    return [(l * 2 + c, (l + dl) % 2 * 2 + (c + dc) % 2) for l in range(2) for c in range(2)]


def after(value, *others):
    return lax.optimization_barrier((value,) + others)[0]


def shards(preact, grad_output, down_weight):
    gy = lax.axis_index("gy")
    gz = lax.axis_index("gz")
    gx = lax.axis_index("gx")
    core, lo = gy % 2, gy // 2
    y = gx % 4
    h = gx // 4

    contract_cols = (((1,), (1,)), ((), ()))
    contract_rows = (((0,), (0,)), ((), ()))

    gathered = []
    scattered = []
    previous = None
    for start, stop in STAGES:
        own = grad_output[start:stop]
        if previous is not None:
            own = after(own, previous)
        across = lax.ppermute(own, "gy", gy_move(1, 0))
        partner = lax.ppermute(own, "gy", gy_move(0, 1))
        corner = lax.ppermute(across, "gy", gy_move(0, 1))
        previous = across
        near = jnp.where(core == 0, jnp.stack((own, partner)), jnp.stack((partner, own)))
        far = jnp.where(core == 0, jnp.stack((across, corner)), jnp.stack((corner, across)))
        pieces = jnp.where(lo == 0, jnp.concatenate((near, far)), jnp.concatenate((far, near)))
        gathered.append(pieces)
    for pieces in gathered:
        rows = pieces.reshape(-1, pieces.shape[-1])
        part = lax.dot_general(rows, down_weight, contract_cols, preferred_element_type=f32)
        scattered.append(
            lax.psum_scatter(part.astype(bf16), "gz", scatter_dimension=0, tiled=True)
        )

    pre_wide = preact.astype(f32)
    activation = (0.5 * pre_wide * (1.0 + lax.erf(pre_wide * root_half))).astype(bf16)
    output_rows = jnp.concatenate(gathered, axis=1).reshape(-1, grad_output.shape[1])
    chunk = preact.shape[1] // 8

    def term(h_dest, y_dest):
        cols = lax.dynamic_slice_in_dim(activation, (h_dest * 4 + y_dest) * chunk, chunk, 1)
        return lax.dot_general(cols, output_rows, contract_rows, preferred_element_type=f32)

    up, down = gx_move(0, 1), gx_move(0, -1)
    y_up, y_down, y_far = (y + 1) % 4, (y + 3) % 4, (y + 2) % 4
    a_far = lax.ppermute(term(0, y_far).astype(bf16), "gx", down)
    b_far = lax.ppermute(term(1, y_far).astype(bf16), "gx", up)
    a_side = lax.ppermute(term(0, y_up).astype(bf16), "gx", up)
    b_side = lax.ppermute(term(1, y_down).astype(bf16), "gx", down)
    a_sum = lax.ppermute((term(0, y_down) + a_far.astype(f32)).astype(bf16), "gx", down)
    b_sum = lax.ppermute((term(1, y_up) + b_far.astype(f32)).astype(bf16), "gx", up)
    a_own = term(0, y) + a_side.astype(f32) + a_sum.astype(f32)
    b_own = term(1, y) + b_side.astype(f32) + b_sum.astype(f32)
    keep = jnp.where(h == 0, a_own, b_own)
    give = jnp.where(h == 0, b_own, a_own).astype(bf16)
    taken = lax.ppermute(give, "gx", gx_move(1, 0))
    grad_down = (keep + taken.astype(f32)).astype(bf16)

    outs = []
    for (start, stop), summed in zip(STAGES, scattered):
        rows = lax.dynamic_slice_in_dim(preact, gz * 512 + start, stop - start, 0).astype(f32)
        outs.append((summed.astype(f32) * unit_slope(rows)).astype(bf16))
    grad_pre = jnp.concatenate(outs)
    return (grad_pre, grad_down)


def solution(mesh):
    return jax.shard_map(
        shards,
        mesh=mesh,
        in_specs=(P("gx", "gy"), P(("gx", "gy"), "gz"), P("gy", "gz")),
        out_specs=(P(("gx", "gz"), "gy"), P(("gy", "gx"), "gz")),
        check_vma=False,
    )
```

time: 431 us -> 218 us (0.51)
  waiting for transfers between devices: 321 us -> 81.6 us
  matrix products: 47.3 us -> 71.1 us
  other arithmetic: 47.6 us -> 25.9 us
  starting transfers between devices: 0.3 us -> 21 us
    psum x1 -> x0, waiting for transfers between devices: 167 us -> none  [shards(): grad_act = lax.psum(part.astype(jnp.bfloat16), 'gz').astype(jnp.float32)]
    reduce_scatter x1 -> x4, waiting for transfers between devices: 99.2 us -> 0.02 us  [shards(): lax.psum_scatter(part.astype(bf16), 'gz', scatter_dimension=0, tiled=True)]
    ppermute x0 -> x19, waiting for transfers between devices: none -> 81.5 us  [the longest x4 26.3 us: shards(): across = lax.ppermute(own, 'gy', gy_move(1, 0))]
    all_gather x1 -> x0, waiting for transfers between devices: 54.5 us -> none  [shards(): output_rows = lax.all_gather(grad_output, 'gy', axis=0, tiled=True)]
    dot_general x2 -> x12, matrix products: 47.3 us -> 71.1 us  [the longest x8 38.9 us: term(): lax.dot_general(cols, output_rows, contract_rows, preferred_element_type=...]
    mul x1 -> x0, other arithmetic: 22.6 us -> none  [unit_slope(): -0.5 * values * values]
    ppermute x0 -> x19, starting transfers between devices: none -> 20.7 us  [the longest x4 6.95 us: shards(): across = lax.ppermute(own, 'gy', gy_move(1, 0))]
    convert_element_type x2 -> x3, other arithmetic: 25 us -> 20 us  [the longest x1 10.7 us: shards(): (0.5 * pre_wide * (1.0 + lax.erf(pre_wide * root_half))).astype(bf16)]
  transfers between devices with their start and end apart: 3 -> 23, of which waited for: 3 -> 11; matrix products, arithmetic and copies ran while one was open for 17% -> 39% of each run, Pallas kernels for 0% -> 0%
where the time goes in v1:
time: 218 us; the launch traced here: 217 us
  waiting for transfers between devices  81.6 us (37%)
  matrix products  71.1 us (33%)
  other arithmetic  25.9 us (12%)
  starting transfers between devices  21 us (10%)
  between operations  14 us (6%)
  local copies, waits for them, and re-layouts  3.39 us (2%)
    dot_general x8, matrix products, term(): lax.dot_general(cols, output_rows, contract_rows, preferred_element_type=...  38.9 us
    dot_general x4, matrix products, shards(): lax.dot_general(rows, down_weight, contract_cols, preferred_element_type=...  32.2 us
    ppermute x4, waiting for transfers between devices, shards(): across = lax.ppermute(own, 'gy', gy_move(1, 0))  26.3 us
    ppermute x1, waiting for transfers between devices, shards(): taken = lax.ppermute(give, 'gx', gx_move(1, 0))  19.1 us
    ppermute x1, waiting for transfers between devices, shards(): lax.ppermute((term(0, y_down) + a_far.astype(f32)).astype(bf16), 'gx', down)  12.4 us
    convert_element_type x1, other arithmetic, shards(): (0.5 * pre_wide * (1.0 + lax.erf(pre_wide * root_half))).astype(bf16)  10.7 us
    ppermute x1, waiting for transfers between devices, shards(): a_far = lax.ppermute(term(0, y_far).astype(bf16), 'gx', down)  9.52 us
    ppermute x4, starting transfers between devices, shards(): across = lax.ppermute(own, 'gy', gy_move(1, 0))  6.95 us
  transfers between devices with their start and end apart: 23, of which 11 were waited for; matrix products, arithmetic and copies ran while one was open for 39% of the time, Pallas kernels for 0%

profile of v1, /device:TPU:0, one launch (start us, length us, event | category | flops | bytes accessed | tf_op | source)
XLA Modules:
  0.0 217.0 jit_solution(10185969578115145140)
XLA Ops:
  7.2 0.0 reduce-scatter.7.cloned.1.call-start
  7.2 1.4 slice_bitcast_fusion
  8.6 1.7 collective-permute-start.1
  10.3 7.0 %collective-permute-done.1 = bf16[128,1152]{1,0:T(8,128)(2,1)S(1)} collective-permute-done((bf16[128,1152]{1,0:T(8,128)(2,1)S(1)}, bf16[128,1152]{1,0:T(8,128)(2,1)S(1)}, u32[]{:S(2)}, u32[]{:S(2)}) %collective-permute-start.1) | collective-permute-done | bytes 294944 | tf_op jit(solution)/shard_map/ppermute | solution.py:56
  17.3 1.7 collective-permute-start.4
  19.0 0.5 collective-permute-start.2
  19.5 0.1 maximum_select_fusion.4
  19.6 5.5 %collective-permute-done.4 = bf16[128,1152]{1,0:T(8,128)(2,1)S(1)} collective-permute-done((bf16[128,1152]{1,0:T(8,128)(2,1)S(1)}, bf16[128,1152]{1,0:T(8,128)(2,1)S(1)}, u32[]{:S(2)}, u32[]{:S(2)}) %collective-permute-start.4) | collective-permute-done | bytes 294944 | tf_op jit(solution)/shard_map/ppermute | solution.py:56
  25.1 0.1 maximum_select_fusion.6
  25.3 0.1 maximum_select_fusion.5
  25.4 1.3 collective-permute-done.5
  26.7 0.1 maximum_select_fusion.7
  26.8 0.5 maximum_select_fusion
  27.3 1.0 copy-done.2
  28.3 5.8 %convolution_convert_fusion.2 = bf16[512,3072]{1,0:T(8,128)(2,1)} fusion(bf16[512,1152]{1,0:T(8,128)(2,1)S(1)} %bitcast.51, bf16[3072,1152]{1,0:T(8,128)(2,1)S(1)} %copy-done.2), kind=kOutput, calls=%fused_computation.9 | convolution fusion | flops 3625451520 | bytes 11403264 | tf_op jit(solution)/shard_map/dot_general | solution.py:66
  34.1 0.0 reduce-scatter.7.cloned.1.call-update
  34.1 0.0 reduce-scatter.5.cloned.1.call-start
  34.1 8.6 %convolution_convert_fusion.3 = bf16[512,3072]{1,0:T(8,128)(2,1)} fusion(bf16[512,1152]{1,0:T(8,128)(2,1)S(1)} %bitcast.50, bf16[3072,1152]{1,0:T(8,128)(2,1)} %param.5), kind=kOutput, calls=%fused_computation.10 | convolution fusion | flops 3625451520 | bytes 11403264 | tf_op jit(solution)/shard_map/dot_general | solution.py:66
  42.8 0.0 reduce-scatter.5.cloned.1.call-update
  42.8 0.0 reduce-scatter.11.cloned.1.call-start
  42.8 1.8 collective-permute-start.7
  44.7 0.2 collective-permute-start.6
  44.9 7.5 %collective-permute-done.7 = bf16[128,1152]{1,0:T(8,128)(2,1)S(1)} collective-permute-done((bf16[128,1152]{1,0:T(8,128)(2,1)S(1)}, bf16[128,1152]{1,0:T(8,128)(2,1)S(1)}, u32[]{:S(2)}, u32[]{:S(2)}) %collective-permute-start.7) | collective-permute-done | bytes 294944 | tf_op jit(solution)/shard_map/ppermute | solution.py:56
  52.4 1.7 collective-permute-start.10
  54.1 0.5 collective-permute-start.8
  54.6 0.1 maximum_select_fusion.8
  54.7 6.4 %collective-permute-done.10 = bf16[128,1152]{1,0:T(8,128)(2,1)S(1)} collective-permute-done((bf16[128,1152]{1,0:T(8,128)(2,1)S(1)}, bf16[128,1152]{1,0:T(8,128)(2,1)S(1)}, u32[]{:S(2)}, u32[]{:S(2)}) %collective-permute-start.10) | collective-permute-done | bytes 294944 | tf_op jit(solution)/shard_map/ppermute | solution.py:56
  61.1 0.1 maximum_select_fusion.10
  61.2 0.1 maximum_select_fusion.9
  61.4 1.3 collective-permute-done.11
  62.7 0.1 maximum_select_fusion.11
  62.8 0.5 maximum_select_fusion.2
  63.3 1.0 copy-done
  64.3 8.8 %convolution_convert_fusion = bf16[512,3072]{1,0:T(8,128)(2,1)} fusion(bf16[512,1152]{1,0:T(8,128)(2,1)S(1)} %bitcast.53, bf16[3072,1152]{1,0:T(8,128)(2,1)} %param.5), kind=kOutput, calls=%fused_computation.7 | convolution fusion | flops 3625451520 | bytes 11403264 | tf_op jit(solution)/shard_map/dot_general | solution.py:66
  73.0 0.0 reduce-scatter.11.cloned.1.call-update
  73.1 0.2 reduce-scatter.9.cloned.1.call-start
  73.4 10.7 %fusion.1 = bf16[2048,3072]{1,0:T(8,128)(2,1)} fusion(bf16[2048,3072]{1,0:T(8,128)(2,1)} %param.3), kind=kLoop, calls=%fused_computation.3 | loop fusion | flops 37748736 | bytes 25165824 | tf_op jit(solution)/shard_map/convert_element_type | solution.py:72
  84.1 2.3 %pad_maximum_fusion = bf16[4,512,1152]{2,1,0:T(8,128)(2,1)} fusion(bf16[4,128,1152]{2,1,0:T(8,128)(2,1)S(1)} %copy-done.1, bf16[4,128,1152]{2,1,0:T(8,128)(2,1)S(1)} %get-tuple-element.21, bf16[4,128,1152]{2,1,0:T(8,128)(2,1)S(1)} %get-tuple-element.20, bf16[4,128,1152]{2,1,0:T(8,128)(2,1)S(1)} %get-tuple-element.19), kind=kLoop, calls=%fused_computation.6 | loop fusion | flops 18874368 | bytes 9437184 | tf_op jit(solution)/shard_map/concatenate | solution.py:73
  86.4 9.0 %convolution_convert_fusion.1 = bf16[512,3072]{1,0:T(8,128)(2,1)} fusion(bf16[512,1152]{1,0:T(8,128)(2,1)S(1)} %bitcast.52, bf16[3072,1152]{1,0:T(8,128)(2,1)} %param.5), kind=kOutput, calls=%fused_computation.8 | convolution fusion | flops 3625451520 | bytes 11403264 | tf_op jit(solution)/shard_map/dot_general | solution.py:66
  95.4 0.0 reduce-scatter.9.cloned.1.call-update
  95.4 6.2 %convolution_convert_fusion.7 = bf16[384,1152]{1,0:T(8,128)(2,1)} fusion(bf16[2048,1152]{1,0:T(8,128)(2,1)} %bitcast.38, bf16[2048,3072]{1,0:T(8,128)(2,1)} %fusion.1, s32[]{:T(128)S(6)} %select_n.179), kind=kOutput, calls=%fused_computation.15 | convolution fusion | flops 1812381696 | bytes 7176196 | tf_op jit(solution)/shard_map/dot_general | solution.py:78
  101.6 1.7 collective-permute-start.12
  103.4 3.7 %convolution_convert_fusion.6 = bf16[384,1152]{1,0:T(8,128)(2,1)S(1)} fusion(bf16[2048,1152]{1,0:T(8,128)(2,1)S(1)} %bitcast.42, bf16[2048,3072]{1,0:T(8,128)(2,1)} %fusion.1, s32[]{:T(128)S(6)} %select_n.183), kind=kOutput, calls=%fused_computation.14 | convolution fusion | flops 1812381696 | bytes 7176196 | tf_op jit(solution)/shard_map/dot_general | solution.py:78
  107.1 1.6 collective-permute-start.13
  108.6 3.7 %convolution_convert_fusion.4 = bf16[384,1152]{1,0:T(8,128)(2,1)S(1)} fusion(bf16[2048,1152]{1,0:T(8,128)(2,1)S(1)} %bitcast.43, bf16[2048,3072]{1,0:T(8,128)(2,1)} %fusion.1, s32[]{:T(128)S(6)} %select_n.187), kind=kOutput, calls=%fused_computation.12 | convolution fusion | flops 1812381696 | bytes 7176196 | tf_op jit(solution)/shard_map/dot_general | solution.py:78
  112.3 0.6 collective-permute-start.16
  112.9 4.6 %convolution_convert_fusion.5 = bf16[384,1152]{1,0:T(8,128)(2,1)} fusion(bf16[2048,1152]{1,0:T(8,128)(2,1)S(1)} %bitcast.44, bf16[2048,3072]{1,0:T(8,128)(2,1)} %fusion.1, s32[]{:T(128)S(6)} %select_n.185), kind=kOutput, calls=%fused_computation.13 | convolution fusion | flops 1812381696 | bytes 7176196 | tf_op jit(solution)/shard_map/dot_general | solution.py:78
  117.4 2.7 %collective-permute-start.15 = (bf16[384,1152]{1,0:T(8,128)(2,1)}, bf16[384,1152]{1,0:T(8,128)(2,1)}, u32[]{:S(2)}, u32[]{:S(2)}) collective-permute-start(bf16[384,1152]{1,0:T(8,128)(2,1)} %convolution_convert_fusion.5), channel_id=1, source_target_pairs={{0,48},{16,0},{32,16},{48,32},{64,112},{80,64},{96,80},{112,96},{1... | collective-permute-start | bytes 2654216 | tf_op jit(solution)/shard_map/ppermute | solution.py:85
  120.1 9.5 %collective-permute-done.13 = bf16[384,1152]{1,0:T(8,128)(2,1)S(1)} collective-permute-done((bf16[384,1152]{1,0:T(8,128)(2,1)S(1)}, bf16[384,1152]{1,0:T(8,128)(2,1)S(1)}, u32[]{:S(2)}, u32[]{:S(2)}) %collective-permute-start.13) | collective-permute-done | bytes 884768 | tf_op jit(solution)/shard_map/ppermute | solution.py:82
  129.7 4.6 %add_convert_fusion.2 = bf16[384,1152]{1,0:T(8,128)(2,1)} fusion(bf16[384,1152]{1,0:T(8,128)(2,1)S(1)} %collective-permute-done.13, bf16[2048,1152]{1,0:T(8,128)(2,1)S(1)} %bitcast.45, bf16[2048,3072]{1,0:T(8,128)(2,1)} %fusion.1, s32[]{:T(128)S(6)} %select_n.181), kind=kOutput, calls=%fused_computation.37 | convolution fusion | flops 1813266432 | bytes 8060932 | tf_op jit(solution)/shard_map/dot_general | solution.py:78
  134.3 2.6 %collective-permute-start.14 = (bf16[384,1152]{1,0:T(8,128)(2,1)}, bf16[384,1152]{1,0:T(8,128)(2,1)}, u32[]{:S(2)}, u32[]{:S(2)}) collective-permute-start(bf16[384,1152]{1,0:T(8,128)(2,1)} %add_convert_fusion.2), channel_id=1, source_target_pairs={{0,48},{16,0},{32,16},{48,32},{64,112},{80,64},{96,80},{112,96},{1... | collective-permute-start | bytes 2654216 | tf_op jit(solution)/shard_map/ppermute | solution.py:86
  136.9 6.9 %collective-permute-done.16 = bf16[384,1152]{1,0:T(8,128)(2,1)S(1)} collective-permute-done((bf16[384,1152]{1,0:T(8,128)(2,1)S(1)}, bf16[384,1152]{1,0:T(8,128)(2,1)S(1)}, u32[]{:S(2)}, u32[]{:S(2)}) %collective-permute-start.16) | collective-permute-done | bytes 884768 | tf_op jit(solution)/shard_map/ppermute | solution.py:83
  143.8 4.6 %add_convert_fusion.1 = bf16[384,1152]{1,0:T(8,128)(2,1)} fusion(bf16[384,1152]{1,0:T(8,128)(2,1)S(1)} %collective-permute-done.16, bf16[2048,1152]{1,0:T(8,128)(2,1)S(1)} %bitcast.46, bf16[2048,3072]{1,0:T(8,128)(2,1)} %fusion.1, s32[]{:T(128)S(6)} %select_n.186), kind=kOutput, calls=%fused_computation.35 | convolution fusion | flops 1813266432 | bytes 8060932 | tf_op jit(solution)/shard_map/dot_general | solution.py:78
  148.5 0.3 collective-permute-start.17
  148.8 5.3 %fusion.38 = f32[384,1152]{1,0:T(8,128)S(1)} fusion(bf16[2048,1152]{1,0:T(8,128)(2,1)} %bitcast.39, bf16[2048,3072]{1,0:T(8,128)(2,1)} %fusion.1, s32[]{:T(128)S(6)} %select_n.184), kind=kOutput, calls=%fused_computation.70 | convolution fusion | flops 1811939328 | bytes 8060932 | tf_op jit(solution)/shard_map/dot_general | solution.py:78
  154.1 12.4 %collective-permute-done.14 = bf16[384,1152]{1,0:T(8,128)(2,1)} collective-permute-done((bf16[384,1152]{1,0:T(8,128)(2,1)}, bf16[384,1152]{1,0:T(8,128)(2,1)}, u32[]{:S(2)}, u32[]{:S(2)}) %collective-permute-start.14) | collective-permute-done | bytes 884768 | tf_op jit(solution)/shard_map/ppermute | solution.py:86
  166.6 4.5 %collective-permute-done.17 = bf16[384,1152]{1,0:T(8,128)(2,1)} collective-permute-done((bf16[384,1152]{1,0:T(8,128)(2,1)}, bf16[384,1152]{1,0:T(8,128)(2,1)}, u32[]{:S(2)}, u32[]{:S(2)}) %collective-permute-start.17) | collective-permute-done | bytes 884768 | tf_op jit(solution)/shard_map/ppermute | solution.py:87
  171.1 6.2 %select_convert_fusion = (bf16[384,1152]{1,0:T(8,128)(2,1)}, f32[384,1152]{1,0:T(8,128)}) fusion(pred[]{:T(512)S(6)} %eq.14, bf16[384,1152]{1,0:T(8,128)(2,1)} %collective-permute-done.14, bf16[384,1152]{1,0:T(8,128)(2,1)S(1)} %collective-permute-done.12, bf16[384,1152]{1,0:T(8,128)(2,1)} %collective-permute-done.17, f32[384,1152]{1,0:T(8,128)S(1)} %fusion.38, ...), kind=kOutput, calls=%fused_computation.33 | convolution fusion | flops 1816363008 | bytes 14254085 | tf_op jit(solution)/shard_map/dot_general | solution.py:78
  177.3 2.9 %collective-permute-start.18 = (bf16[384,1152]{1,0:T(8,128)(2,1)}, bf16[384,1152]{1,0:T(8,128)(2,1)}, u32[]{:S(2)}, u32[]{:S(2)}) collective-permute-start(bf16[384,1152]{1,0:T(8,128)(2,1)} %get-tuple-element.17), channel_id=1, source_target_pairs={{0,64},{16,80},{32,96},{48,112},{64,0},{80,16},{96,32},{112,48},{1... | collective-permute-start | bytes 2654216 | tf_op jit(solution)/shard_map/ppermute | solution.py:92
  180.3 19.1 %collective-permute-done.18 = bf16[384,1152]{1,0:T(8,128)(2,1)} collective-permute-done((bf16[384,1152]{1,0:T(8,128)(2,1)}, bf16[384,1152]{1,0:T(8,128)(2,1)}, u32[]{:S(2)}, u32[]{:S(2)}) %collective-permute-start.18) | collective-permute-done | bytes 884768 | tf_op jit(solution)/shard_map/ppermute | solution.py:92
  199.4 4.1 %add_convert_fusion = bf16[384,1152]{1,0:T(8,128)(2,1)} fusion(bf16[384,1152]{1,0:T(8,128)(2,1)} %collective-permute-done.18, pred[]{:T(512)S(6)} %eq.14, bf16[384,1152]{1,0:T(8,128)(2,1)} %collective-permute-done.14, f32[384,1152]{1,0:T(8,128)} %get-tuple-element.18, bf16[384,1152]{1,0:T(8,128)(2,1)S(1)} %collective-permute-done.12, ...), kind=kLoop, calls=%fused_computation.32 | loop fusion | flops 5308416 | bytes 8847361 | tf_op jit(solution)/shard_map/convert_element_type | solution.py:93
  203.4 0.0 reduce-scatter.9.cloned.1.call-done
  203.5 5.2 %fusion.51 = (bf16[128,3072]{1,0:T(8,128)(2,1)S(1)}, bf16[128,3072]{1,0:T(8,128)(2,1)S(1)}, bf16[128,3072]{1,0:T(8,128)(2,1)S(1)}, bf16[128,3072]{1,0:T(8,128)(2,1)S(1)}) fusion(bf16[128,3072]{1,0:T(8,128)(2,1)} %reduce-scatter.5.cloned.1.call-done, bf16[2048,3072]{1,0:T(8,128)(2,1)} %param.3, s32[]{:T(128)S(6)} %select_n.158, s32[]{:T(128)S(6)} %select_n.168, ...), kind=kLoop, calls=%fused_computation.81 | loop fusion | flops 18874368 | bytes 9437200 | tf_op jit(solution)/shard_map/convert_element_type | solution.py:98
  208.7 1.8 pad_maximum_fusion.1
  (30 shorter events, 0.1 us)
Async XLA Ops:
  7.2 196.3 %reduce-scatter.7.cloned.1.call-start = ((), (), s32[]{:S(2)}) async-start(), calls=%async_computation.5 | async-start | bytes 3932160 | tf_op jit(solution)/shard_map/reduce_scatter | solution.py:68
  8.6 8.7 %collective-permute-start.1 = (bf16[128,1152]{1,0:T(8,128)(2,1)S(1)}, bf16[128,1152]{1,0:T(8,128)(2,1)S(1)}, u32[]{:S(2)}, u32[]{:S(2)}) collective-permute-start(bf16[128,1152]{1,0:T(8,128)(2,1)S(1)} %get-tuple-element.14), channel_id=1, source_target_pairs={{0,8},{4,12},{8,0},{12,4},{1,9},{5,13},{9,1},{13,5},{2,10},{6,14},... | collective-permute-start | bytes 884744 | tf_op jit(solution)/shard_map/ppermute | solution.py:56
  10.2 9.3 %collective-permute-start = (bf16[128,1152]{1,0:T(8,128)(2,1)S(1)}, bf16[128,1152]{1,0:T(8,128)(2,1)S(1)}, u32[]{:S(2)}, u32[]{:S(2)}) collective-permute-start(bf16[128,1152]{1,0:T(8,128)(2,1)S(1)} %get-tuple-element.14), channel_id=1, source_target_pairs={{0,4},{4,0},{8,12},{12,8},{1,5},{5,1},{9,13},{13,9},{2,6},{6,2},{1... | collective-permute-start | bytes 884744 | tf_op jit(solution)/shard_map/ppermute | solution.py:57
  17.3 7.9 %collective-permute-start.4 = (bf16[128,1152]{1,0:T(8,128)(2,1)S(1)}, bf16[128,1152]{1,0:T(8,128)(2,1)S(1)}, u32[]{:S(2)}, u32[]{:S(2)}) collective-permute-start(bf16[128,1152]{1,0:T(8,128)(2,1)S(1)} %get-tuple-element.5), channel_id=1, source_target_pairs={{0,8},{4,12},{8,0},{12,4},{1,9},{5,13},{9,1},{13,5},{2,10},{6,14},... | collective-permute-start | bytes 884744 | tf_op jit(solution)/shard_map/ppermute | solution.py:56
  19.0 6.1 %collective-permute-start.3 = (bf16[128,1152]{1,0:T(8,128)(2,1)S(1)}, bf16[128,1152]{1,0:T(8,128)(2,1)S(1)}, u32[]{:S(2)}, u32[]{:S(2)}) collective-permute-start(bf16[128,1152]{1,0:T(8,128)(2,1)S(1)} %get-tuple-element.5), channel_id=1, source_target_pairs={{0,4},{4,0},{8,12},{12,8},{1,5},{5,1},{9,13},{13,9},{2,6},{6,2},{1... | collective-permute-start | bytes 884744 | tf_op jit(solution)/shard_map/ppermute | solution.py:57
  19.0 6.2 %collective-permute-start.2 = (bf16[128,1152]{1,0:T(8,128)(2,1)S(1)}, bf16[128,1152]{1,0:T(8,128)(2,1)S(1)}, u32[]{:S(2)}, u32[]{:S(2)}) collective-permute-start(bf16[128,1152]{1,0:T(8,128)(2,1)S(1)} %collective-permute-done.1), channel_id=1, source_target_pairs={{0,4},{4,0},{8,12},{12,8},{1,5},{5,1},{9,13},{13,9},{2,6},{6,2},{1... | collective-permute-start | bytes 884744 | tf_op jit(solution)/shard_map/ppermute | solution.py:58
  25.1 1.6 collective-permute-start.5
  25.3 3.0 %copy-start.2 = (bf16[3072,1152]{1,0:T(8,128)(2,1)S(1)}, bf16[3072,1152]{1,0:T(8,128)(2,1)}, u32[]{:S(2)}) copy-start(bf16[3072,1152]{1,0:T(8,128)(2,1)} %param.5) | copy-start | bytes 21233668
  34.1 169.4 %reduce-scatter.5.cloned.1.call-start = ((), (), s32[]{:S(2)}) async-start(), calls=%async_computation.4 | async-start | bytes 3932160 | tf_op jit(solution)/shard_map/reduce_scatter | solution.py:68
  42.8 160.6 %reduce-scatter.11.cloned.1.call-start = ((), (), s32[]{:S(2)}) async-start(), calls=%async_computation.7 | async-start | bytes 3932160 | tf_op jit(solution)/shard_map/reduce_scatter | solution.py:68
  42.8 9.5 %collective-permute-start.7 = (bf16[128,1152]{1,0:T(8,128)(2,1)S(1)}, bf16[128,1152]{1,0:T(8,128)(2,1)S(1)}, u32[]{:S(2)}, u32[]{:S(2)}) collective-permute-start(bf16[128,1152]{1,0:T(8,128)(2,1)S(1)} %get-tuple-element.6), channel_id=1, source_target_pairs={{0,8},{4,12},{8,0},{12,4},{1,9},{5,13},{9,1},{13,5},{2,10},{6,14},... | collective-permute-start | bytes 884744 | tf_op jit(solution)/shard_map/ppermute | solution.py:56
  44.7 9.9 %collective-permute-start.6 = (bf16[128,1152]{1,0:T(8,128)(2,1)S(1)}, bf16[128,1152]{1,0:T(8,128)(2,1)S(1)}, u32[]{:S(2)}, u32[]{:S(2)}) collective-permute-start(bf16[128,1152]{1,0:T(8,128)(2,1)S(1)} %get-tuple-element.6), channel_id=1, source_target_pairs={{0,4},{4,0},{8,12},{12,8},{1,5},{5,1},{9,13},{13,9},{2,6},{6,2},{1... | collective-permute-start | bytes 884744 | tf_op jit(solution)/shard_map/ppermute | solution.py:57
  52.4 8.8 %collective-permute-start.10 = (bf16[128,1152]{1,0:T(8,128)(2,1)S(1)}, bf16[128,1152]{1,0:T(8,128)(2,1)S(1)}, u32[]{:S(2)}, u32[]{:S(2)}) collective-permute-start(bf16[128,1152]{1,0:T(8,128)(2,1)S(1)} %get-tuple-element.7), channel_id=1, source_target_pairs={{0,8},{4,12},{8,0},{12,4},{1,9},{5,13},{9,1},{13,5},{2,10},{6,14},... | collective-permute-start | bytes 884744 | tf_op jit(solution)/shard_map/ppermute | solution.py:56
  54.1 7.0 %collective-permute-start.9 = (bf16[128,1152]{1,0:T(8,128)(2,1)S(1)}, bf16[128,1152]{1,0:T(8,128)(2,1)S(1)}, u32[]{:S(2)}, u32[]{:S(2)}) collective-permute-start(bf16[128,1152]{1,0:T(8,128)(2,1)S(1)} %get-tuple-element.7), channel_id=1, source_target_pairs={{0,4},{4,0},{8,12},{12,8},{1,5},{5,1},{9,13},{13,9},{2,6},{6,2},{1... | collective-permute-start | bytes 884744 | tf_op jit(solution)/shard_map/ppermute | solution.py:57
  54.1 7.1 %collective-permute-start.8 = (bf16[128,1152]{1,0:T(8,128)(2,1)S(1)}, bf16[128,1152]{1,0:T(8,128)(2,1)S(1)}, u32[]{:S(2)}, u32[]{:S(2)}) collective-permute-start(bf16[128,1152]{1,0:T(8,128)(2,1)S(1)} %collective-permute-done.7), channel_id=1, source_target_pairs={{0,4},{4,0},{8,12},{12,8},{1,5},{5,1},{9,13},{13,9},{2,6},{6,2},{1... | collective-permute-start | bytes 884744 | tf_op jit(solution)/shard_map/ppermute | solution.py:58
  61.1 1.6 collective-permute-start.11
  63.3 1.0 copy-start
  73.1 130.4 %reduce-scatter.9.cloned.1.call-start = ((), (), s32[]{:S(2)}) async-start(), calls=%async_computation.6 | async-start | bytes 3932160 | tf_op jit(solution)/shard_map/reduce_scatter | solution.py:68
  73.4 10.7 %copy-start.1 = (bf16[4,128,1152]{2,1,0:T(8,128)(2,1)S(1)}, bf16[4,128,1152]{2,1,0:T(8,128)(2,1)}, u32[]{:S(2)}) copy-start(bf16[4,128,1152]{2,1,0:T(8,128)(2,1)} %copy-done) | copy-start | bytes 3538948
  95.4 8.0 %slice-start = ((s8[4718592]{0:T(1024)(128)(4,1)}), s8[524288]{0:T(1024)(128)(4,1)S(1)}, s32[]{:S(2)}) async-start(s8[4718592]{0:T(1024)(128)(4,1)} %bitcast.40), calls=%async_computation.8 | async-start | bytes 1048576
  95.4 8.0 %slice-start.1 = ((s8[4718592]{0:T(1024)(128)(4,1)}), s8[4194304]{0:T(1024)(128)(4,1)S(1)}, s32[]{:S(2)}) async-start(s8[4718592]{0:T(1024)(128)(4,1)} %bitcast.40), calls=%async_computation.9 | async-start | bytes 8388608
  101.6 52.5 %collective-permute-start.12 = (bf16[384,1152]{1,0:T(8,128)(2,1)}, bf16[384,1152]{1,0:T(8,128)(2,1)S(1)}, u32[]{:S(2)}, u32[]{:S(2)}) collective-permute-start(bf16[384,1152]{1,0:T(8,128)(2,1)} %convolution_convert_fusion.7), channel_id=1, source_target_pairs={{0,16},{16,32},{32,48},{48,0},{64,80},{80,96},{96,112},{112,64},{1... | collective-permute-start | bytes 2654216 | tf_op jit(solution)/shard_map/ppermute | solution.py:84
  107.1 22.6 %collective-permute-start.13 = (bf16[384,1152]{1,0:T(8,128)(2,1)S(1)}, bf16[384,1152]{1,0:T(8,128)(2,1)S(1)}, u32[]{:S(2)}, u32[]{:S(2)}) collective-permute-start(bf16[384,1152]{1,0:T(8,128)(2,1)S(1)} %convolution_convert_fusion.6), channel_id=1, source_target_pairs={{0,48},{16,0},{32,16},{48,32},{64,112},{80,64},{96,80},{112,96},{1... | collective-permute-start | bytes 2654216 | tf_op jit(solution)/shard_map/ppermute | solution.py:82
  112.3 31.6 %collective-permute-start.16 = (bf16[384,1152]{1,0:T(8,128)(2,1)S(1)}, bf16[384,1152]{1,0:T(8,128)(2,1)S(1)}, u32[]{:S(2)}, u32[]{:S(2)}) collective-permute-start(bf16[384,1152]{1,0:T(8,128)(2,1)S(1)} %convolution_convert_fusion.4), channel_id=1, source_target_pairs={{0,16},{16,32},{32,48},{48,0},{64,80},{80,96},{96,112},{112,64},{1... | collective-permute-start | bytes 2654216 | tf_op jit(solution)/shard_map/ppermute | solution.py:83
  117.4 36.7 %collective-permute-start.15 = (bf16[384,1152]{1,0:T(8,128)(2,1)}, bf16[384,1152]{1,0:T(8,128)(2,1)}, u32[]{:S(2)}, u32[]{:S(2)}) collective-permute-start(bf16[384,1152]{1,0:T(8,128)(2,1)} %convolution_convert_fusion.5), channel_id=1, source_target_pairs={{0,48},{16,0},{32,16},{48,32},{64,112},{80,64},{96,80},{112,96},{1... | collective-permute-start | bytes 2654216 | tf_op jit(solution)/shard_map/ppermute | solution.py:85
  134.3 32.3 %collective-permute-start.14 = (bf16[384,1152]{1,0:T(8,128)(2,1)}, bf16[384,1152]{1,0:T(8,128)(2,1)}, u32[]{:S(2)}, u32[]{:S(2)}) collective-permute-start(bf16[384,1152]{1,0:T(8,128)(2,1)} %add_convert_fusion.2), channel_id=1, source_target_pairs={{0,48},{16,0},{32,16},{48,32},{64,112},{80,64},{96,80},{112,96},{1... | collective-permute-start | bytes 2654216 | tf_op jit(solution)/shard_map/ppermute | solution.py:86
  148.5 22.6 %collective-permute-start.17 = (bf16[384,1152]{1,0:T(8,128)(2,1)}, bf16[384,1152]{1,0:T(8,128)(2,1)}, u32[]{:S(2)}, u32[]{:S(2)}) collective-permute-start(bf16[384,1152]{1,0:T(8,128)(2,1)} %add_convert_fusion.1), channel_id=1, source_target_pairs={{0,16},{16,32},{32,48},{48,0},{64,80},{80,96},{96,112},{112,64},{1... | collective-permute-start | bytes 2654216 | tf_op jit(solution)/shard_map/ppermute | solution.py:87
  148.8 22.3 %slice-start.2 = ((s8[4718592]{0:T(1024)(128)(4,1)}), s8[524288]{0:T(1024)(128)(4,1)S(1)}, s32[]{:S(2)}) async-start(s8[4718592]{0:T(1024)(128)(4,1)} %bitcast.47), calls=%async_computation.10 | async-start | bytes 1048576
  148.8 22.3 %slice-start.3 = ((s8[4718592]{0:T(1024)(128)(4,1)}), s8[4194304]{0:T(1024)(128)(4,1)S(1)}, s32[]{:S(2)}) async-start(s8[4718592]{0:T(1024)(128)(4,1)} %bitcast.47), calls=%async_computation.11 | async-start | bytes 8388608
  177.3 22.0 %collective-permute-start.18 = (bf16[384,1152]{1,0:T(8,128)(2,1)}, bf16[384,1152]{1,0:T(8,128)(2,1)}, u32[]{:S(2)}, u32[]{:S(2)}) collective-permute-start(bf16[384,1152]{1,0:T(8,128)(2,1)} %get-tuple-element.17), channel_id=1, source_target_pairs={{0,64},{16,80},{32,96},{48,112},{64,0},{80,16},{96,32},{112,48},{1... | collective-permute-start | bytes 2654216 | tf_op jit(solution)/shard_map/ppermute | solution.py:92
Sparse Core Ops, SparseCore 0:
  34.2 41.2 reduce-scatter.6
  78.5 38.0 reduce-scatter.4
  119.0 38.0 reduce-scatter.10
  159.3 38.0 reduce-scatter.8

commit v2 on v0

v2 whole, which is shorter than its diff:
```python
import functools
import math

import jax
import jax.numpy as jnp
from jax import lax
from jax.experimental import pallas as pl
from jax.experimental.pallas import tpu as pltpu
from jax.sharding import PartitionSpec as P

root_half = 1.0 / math.sqrt(2.0)
slope_scale = 1.0 / math.sqrt(2.0 * math.pi)
bf16 = jnp.bfloat16
f32 = jnp.float32
HEAD = 128
TILE = 512
COLS = 384
COST = 64
VMEM = 63 * 1024 * 1024


def gelu(values):
    return 0.5 * values * (1.0 + lax.erf(values * root_half))


def unit_slope(values):
    return (
        0.5 * (1.0 + lax.erf(values * root_half))
        + values * jnp.exp(-0.5 * values * values) * slope_scale
    )


def gz_ring(step):
    return [(i, (i + step) % 4) for i in range(4)]


def gx_move(dh, dy):
    return [(h * 4 + y, (h + dh) % 2 * 4 + (y + dy) % 4) for h in range(2) for y in range(4)]


def gy_move(dl, dc):
    return [(l * 2 + c, (l + dl) % 2 * 2 + (c + dc) % 2) for l in range(2) for c in range(2)]


def after(value, *others):
    return lax.optimization_barrier((value,) + others)[0]


def call(body, name, grid, prefetch, in_specs, out_specs, out_shape, flops, moved, **extra):
    return pl.pallas_call(
        body,
        name=name,
        out_shape=out_shape,
        grid_spec=pltpu.PrefetchScalarGridSpec(
            num_scalar_prefetch=prefetch, grid=grid, in_specs=in_specs, out_specs=out_specs
        ),
        compiler_params=pltpu.CompilerParams(
            dimension_semantics=("arbitrary",) * len(grid), vmem_limit_bytes=VMEM
        ),
        cost_estimate=pl.CostEstimate(
            flops=int(flops) // COST, bytes_accessed=int(moved) // COST, transcendentals=0
        ),
        **extra,
    )


def rows_dot(rows, weights):
    return lax.dot_general(rows, weights, (((1,), (1,)), ((), ())), preferred_element_type=f32)


def plain_dot(left, right):
    return lax.dot_general(left, right, (((1,), (0,)), ((), ())), preferred_element_type=f32)


ORDER, FAR, UP, DOWN, OWN, GZ, Y_FAR, Y_UP, Y_DOWN, Y, H = 0, 4, 5, 6, 7, 8, 9, 10, 11, 12, 13


def gelu_body(table, pre, head, tail):
    act = gelu(pre[...].astype(f32)).astype(bf16)
    head[...] = act[: head.shape[1]].T
    tail[...] = act[head.shape[1] :].T


def transposed_gelu(preact, table, half):
    rows, hidden = preact.shape
    piece = rows // 4
    tiles = hidden // 2 // TILE
    tail = piece - HEAD
    return call(
        gelu_body,
        "gelu_t",
        (tiles, 4),
        1,
        [pl.BlockSpec((piece, TILE), lambda t, j, o: (o[ORDER + j], half * tiles + t))],
        [
            pl.BlockSpec((TILE, HEAD), lambda t, j, o: (t, j)),
            pl.BlockSpec((TILE, tail), lambda t, j, o: (t, j)),
        ],
        [
            jax.ShapeDtypeStruct((hidden // 2, 4 * HEAD), bf16),
            jax.ShapeDtypeStruct((hidden // 2, 4 * tail), bf16),
        ],
        rows * hidden * 40,
        rows * hidden * 2,
    )(table, preact)


def tail_body(table, rows, weights, out):
    for r in range(4):
        out[r] = rows_dot(rows[table[ORDER + r]], weights[...]).astype(bf16)


def tail_parts(rows, weights, table):
    _, count, depth = rows.shape
    hidden = weights.shape[0]
    return call(
        tail_body,
        "tail_parts",
        (hidden // TILE,),
        1,
        [
            pl.BlockSpec((4, count, depth), lambda t, o: (0, 0, 0)),
            pl.BlockSpec((TILE, depth), lambda t, o: (t, 0)),
        ],
        pl.BlockSpec((4, count, TILE), lambda t, o: (0, 0, t)),
        jax.ShapeDtypeStruct((4, count, hidden), bf16),
        8 * count * depth * hidden,
        2 * (4 * count * depth + depth * hidden + 4 * count * hidden),
    )(table, rows, weights)


def head_body(adds, table, rows_a, rows_b, weights_a, weights_b, *refs):
    out_a, out_b = refs[-2:]
    sum_a = rows_dot(rows_a[0], weights_a[...])
    sum_b = rows_dot(rows_b[0], weights_b[...])
    if adds:
        sum_a += refs[0][...].astype(f32)
        sum_b += refs[1][...].astype(f32)
    out_a[...] = sum_a.astype(bf16)
    out_b[...] = sum_b.astype(bf16)


def head_parts(rows, weights, table, at_a, at_b, *arrived):
    _, count, depth = rows.shape
    hidden = weights.shape[0]
    tiles = hidden // 2 // TILE
    half = pl.BlockSpec((count, TILE), lambda t, p: (0, t))
    shape = jax.ShapeDtypeStruct((count, hidden // 2), bf16)
    return call(
        functools.partial(head_body, bool(arrived)),
        "head_parts",
        (tiles,),
        1,
        [
            pl.BlockSpec((1, count, depth), lambda t, p: (p[at_a], 0, 0)),
            pl.BlockSpec((1, count, depth), lambda t, p: (p[at_b], 0, 0)),
            pl.BlockSpec((TILE, depth), lambda t, p: (t, 0)),
            pl.BlockSpec((TILE, depth), lambda t, p: (tiles + t, 0)),
        ]
        + [half] * len(arrived),
        [half, half],
        [shape, shape],
        2 * count * depth * hidden,
        2 * (2 * count * depth + depth * hidden + count * hidden * (1 + len(arrived) // 2)),
    )(table, rows, rows, weights, weights, *arrived)


def head_last_body(table, rows, weights, pre, side_a, sum_a, side_b, sum_b, out):
    total = rows_dot(rows[0], weights[...])
    slope = unit_slope(pre[...].astype(f32))
    first = pl.program_id(0) < pl.num_programs(0) // 2

    @pl.when(first)
    def _():
        whole = total + side_a[...].astype(f32) + sum_a[...].astype(f32)
        out[...] = (whole * slope).astype(bf16)

    @pl.when(jnp.logical_not(first))
    def _():
        whole = total + side_b[...].astype(f32) + sum_b[...].astype(f32)
        out[...] = (whole * slope).astype(bf16)


def head_last(rows, weights, preact, table, side_a, sum_a, side_b, sum_b):
    share = preact.shape[0] // 4
    _, count, depth = rows.shape
    hidden = weights.shape[0]
    tiles = hidden // TILE
    half_a = pl.BlockSpec((count, TILE), lambda t, p: (0, jnp.minimum(t, tiles // 2 - 1)))
    half_b = pl.BlockSpec((count, TILE), lambda t, p: (0, jnp.maximum(t - tiles // 2, 0)))
    return call(
        head_last_body,
        "head_last",
        (tiles,),
        1,
        [
            pl.BlockSpec((1, count, depth), lambda t, p: (p[OWN], 0, 0)),
            pl.BlockSpec((TILE, depth), lambda t, p: (t, 0)),
            pl.BlockSpec((count, TILE), lambda t, p: (p[GZ] * (share // count), t)),
            half_a,
            half_a,
            half_b,
            half_b,
        ],
        pl.BlockSpec((count, TILE), lambda t, p: (0, t)),
        jax.ShapeDtypeStruct((share, hidden), bf16),
        2 * count * depth * hidden,
        2 * (count * depth + depth * hidden + 4 * count * hidden),
    )(table, rows, weights, preact, side_a, sum_a, side_b, sum_b)


def tail_last_body(table, summed, pre, held, out):
    out[...] = (summed[...].astype(f32) * unit_slope(pre[...].astype(f32))).astype(bf16)


def tail_last(summed, preact, table, held):
    count, hidden = summed.shape
    step = 128
    start = HEAD // step
    return call(
        tail_last_body,
        "tail_last",
        (count // step,),
        1,
        [
            pl.BlockSpec((step, hidden), lambda t, p: (t, 0)),
            pl.BlockSpec((step, hidden), lambda t, p: (p[GZ] * (held.shape[0] // step) + start + t, 0)),
            pl.BlockSpec(memory_space=pl.ANY),
        ],
        pl.BlockSpec((step, hidden), lambda t, p: (start + t, 0)),
        jax.ShapeDtypeStruct(held.shape, bf16),
        count * hidden * 40,
        6 * count * hidden,
        input_output_aliases={3: 0},
    )(table, summed, preact, held)


def term_of(left_head, left_tail, right_head, right_tail):
    return plain_dot(left_head[...], right_head[...]) + plain_dot(left_tail[...], right_tail[...])


def terms_body(adds, table, a_head, a_tail, b_head, b_tail, g_head, g_tail, *refs):
    out_a, out_b = refs[-2:]
    sum_a = term_of(a_head, a_tail, g_head, g_tail)
    sum_b = term_of(b_head, b_tail, g_head, g_tail)
    if adds:
        sum_a += refs[0][...].astype(f32)
        sum_b += refs[1][...].astype(f32)
    out_a[...] = sum_a.astype(bf16)
    out_b[...] = sum_b.astype(bf16)


def last_terms_body(table, a_head, a_tail, b_head, b_tail, g_head, g_tail, *refs):
    side_a, sum_a, side_b, sum_b, keep, give = refs
    whole_a = term_of(a_head, a_tail, g_head, g_tail)
    whole_a += side_a[...].astype(f32) + sum_a[...].astype(f32)
    whole_b = term_of(b_head, b_tail, g_head, g_tail)
    whole_b += side_b[...].astype(f32) + sum_b[...].astype(f32)
    first = table[H] == 0
    keep[...] = jnp.where(first, whole_a, whole_b)
    give[...] = jnp.where(first, whole_b, whole_a).astype(bf16)


def terms(acts, g_head, g_tail, table, at_a, at_b, arrived=(), last=False):
    head_depth, features = g_head.shape
    tail_depth = g_tail.shape[0]
    chunk = acts[0].shape[0] // 4
    left = [
        pl.BlockSpec((chunk, head_depth), lambda t, p: (p[at_a], 0)),
        pl.BlockSpec((chunk, tail_depth), lambda t, p: (p[at_a], 0)),
        pl.BlockSpec((chunk, head_depth), lambda t, p: (p[at_b], 0)),
        pl.BlockSpec((chunk, tail_depth), lambda t, p: (p[at_b], 0)),
    ]
    block = pl.BlockSpec((chunk, COLS), lambda t, p: (0, t))
    depth = head_depth + tail_depth
    return call(
        last_terms_body if last else functools.partial(terms_body, bool(arrived)),
        "last_terms" if last else "terms",
        (features // COLS,),
        1,
        left
        + [
            pl.BlockSpec((head_depth, COLS), lambda t, p: (0, t)),
            pl.BlockSpec((tail_depth, COLS), lambda t, p: (0, t)),
        ]
        + [block] * len(arrived),
        [block, block],
        [
            jax.ShapeDtypeStruct((chunk, features), f32 if last else bf16),
            jax.ShapeDtypeStruct((chunk, features), bf16),
        ],
        4 * chunk * depth * features,
        2 * (2 * chunk * depth + depth * features + 4 * chunk * features),
    )(table, *acts, g_head, g_tail, *arrived)


def shards(preact, grad_output, down_weight):
    gy = lax.axis_index("gy")
    gz = lax.axis_index("gz")
    gx = lax.axis_index("gx")
    y, h = gx % 4, gx // 4
    entries = [gy ^ j for j in range(4)]
    entries += [(gz + 2) % 4 ^ gy, (gz + 1) % 4 ^ gy, (gz + 3) % 4 ^ gy, gz ^ gy, gz]
    entries += [(y + 2) % 4, (y + 1) % 4, (y + 3) % 4, y, h, 0, 0]
    table = jnp.stack([jnp.asarray(entry, jnp.int32) for entry in entries])

    other_chip, other_core = gy_move(1, 0), gy_move(0, 1)
    z_up, z_down = gz_ring(1), gz_ring(-1)
    y_up, y_down = gx_move(0, 1), gx_move(0, -1)

    own, own_tail = grad_output[:HEAD], grad_output[HEAD:]
    across = lax.ppermute(own, "gy", other_chip)
    partner = lax.ppermute(own, "gy", other_core)
    partner_tail = lax.ppermute(own_tail, "gy", other_core)

    acts = transposed_gelu(preact, table, 0)
    table = after(table, *acts)

    corner = lax.ppermute(after(across, table), "gy", other_core)
    across_tail = lax.ppermute(after(own_tail, across, table), "gy", other_chip)
    head = jnp.stack((own, partner, across, corner))

    a_far, b_far = head_parts(head, down_weight, table, FAR, FAR)
    table = after(table, a_far)
    a_far = lax.ppermute(a_far, "gz", z_down)
    b_far = lax.ppermute(b_far, "gz", z_up)
    a_side, b_side = head_parts(head, down_weight, table, UP, DOWN)
    table = after(table, a_side)
    a_side = lax.ppermute(a_side, "gz", z_up)
    b_side = lax.ppermute(b_side, "gz", z_down)

    more = transposed_gelu(preact, table, 1)
    acts = [*acts, *more]
    table = after(table, *more)

    a_sum, b_sum = head_parts(head, down_weight, table, DOWN, UP, a_far, b_far)
    table = after(table, a_sum)
    a_sum = lax.ppermute(a_sum, "gz", z_down)
    b_sum = lax.ppermute(b_sum, "gz", z_up)

    table = after(table, a_side, b_side)
    corner_tail = lax.ppermute(after(across_tail, table), "gy", other_core)
    tail = jnp.stack((own_tail, partner_tail, across_tail, corner_tail))
    part = tail_parts(tail, down_weight, table)
    table = after(table, part)
    summed = lax.psum_scatter(
        part.reshape(-1, part.shape[2]), "gz", scatter_dimension=0, tiled=True
    )

    g_head = head.reshape(-1, head.shape[2])
    g_tail = tail.reshape(-1, tail.shape[2])
    c_far, d_far = terms(acts, g_head, g_tail, table, Y_FAR, Y_FAR)
    table = after(table, c_far)
    c_far = lax.ppermute(c_far, "gx", y_down)
    d_far = lax.ppermute(d_far, "gx", y_up)
    c_side, d_side = terms(acts, g_head, g_tail, table, Y_UP, Y_DOWN)
    table = after(table, c_side)
    c_side = lax.ppermute(c_side, "gx", y_up)
    d_side = lax.ppermute(d_side, "gx", y_down)

    held = head_last(head, down_weight, preact, table, a_side, a_sum, b_side, b_sum)
    table = after(table, held)

    c_sum, d_sum = terms(acts, g_head, g_tail, table, Y_DOWN, Y_UP, (c_far, d_far))
    table = after(table, c_sum)
    c_sum = lax.ppermute(c_sum, "gx", y_down)
    d_sum = lax.ppermute(d_sum, "gx", y_up)
    keep, give = terms(
        acts, g_head, g_tail, table, Y, Y, (c_side, c_sum, d_side, d_sum), last=True
    )
    taken = lax.ppermute(give, "gx", gx_move(1, 0))
    grad_down = (keep + taken.astype(f32)).astype(bf16)

    grad_pre = tail_last(summed, preact, table, held)
    return (grad_pre, grad_down)


def solution(mesh):
    return jax.shard_map(
        shards,
        mesh=mesh,
        in_specs=(P("gx", "gy"), P(("gx", "gy"), "gz"), P("gy", "gz")),
        out_specs=(P(("gx", "gz"), "gy"), P(("gy", "gx"), "gz")),
        check_vma=False,
    )
```

time: 431 us -> 215 us (0.50)
  waiting for transfers between devices: 321 us -> 48.1 us
  Pallas kernels: 0 us -> 115 us
  matrix products: 47.3 us -> 0 us
  other arithmetic: 47.6 us -> 8.08 us
  starting transfers between devices: 0.3 us -> 24.3 us
  local copies, waits for them, and re-layouts: 0 us -> 4.65 us
    psum x1 -> x0, waiting for transfers between devices: 167 us -> none  [shards(): grad_act = lax.psum(part.astype(jnp.bfloat16), 'gz').astype(jnp.float32)]
    pallas_call x0 -> x12, Pallas kernels: none -> 115 us  [the longest x4 39.2 us: terms(): call(last_terms_body if last else functools.partial(terms_body, bool(arri...]
    reduce_scatter x1, waiting for transfers between devices: 99.2 us -> 0.01 us  [shards(): lax.psum_scatter(part.reshape(-1, part.shape[2]), 'gz', scatter_dimension...]
    all_gather x1 -> x0, waiting for transfers between devices: 54.5 us -> none  [shards(): output_rows = lax.all_gather(grad_output, 'gy', axis=0, tiled=True)]
    ppermute x0 -> x19, waiting for transfers between devices: none -> 48.1 us  [the longest x1 18.8 us: shards(): d_sum = lax.ppermute(d_sum, 'gx', y_up)]
    dot_general x2 -> x0, matrix products: 47.3 us -> none  [the longest x1 25.2 us: shards(): lax.dot_general(activation, output_rows, contract_rows, preferred_element...]
    ppermute x0 -> x19, starting transfers between devices: none -> 24.3 us  [the longest x1 3.23 us: shards(): a_sum = lax.ppermute(a_sum, 'gz', z_down)]
    mul x1 -> x0, other arithmetic: 22.6 us -> none  [unit_slope(): -0.5 * values * values]
  transfers between devices with their start and end apart: 3 -> 20, of which waited for: 3 -> 4; matrix products, arithmetic and copies ran while one was open for 17% -> 4% of each run, Pallas kernels for 0% -> 43%
where the time goes in v2:
time: 215 us; the launch traced here: 214 us
  Pallas kernels  115 us (53%)
  waiting for transfers between devices  48.1 us (22%)
  starting transfers between devices  24.3 us (11%)
  between operations  14.1 us (7%)
  other arithmetic  8.08 us (4%)
  local copies, waits for them, and re-layouts  4.65 us (2%)
    pallas_call x4, Pallas kernels, terms(): call(last_terms_body if last else functools.partial(terms_body, bool(arri...  39.2 us
    pallas_call x2, Pallas kernels, transposed_gelu(): call(gelu_body, 'gelu_t', (tiles, 4), 1, [pl.BlockSpec((piece, TILE), lam...  22.4 us
    pallas_call x3, Pallas kernels, head_parts(): call(functools.partial(head_body, bool(arrived)), 'head_parts', (tiles,),...  20.9 us
    ppermute x1, waiting for transfers between devices, shards(): d_sum = lax.ppermute(d_sum, 'gx', y_up)  18.8 us
    ppermute x1, waiting for transfers between devices, shards(): taken = lax.ppermute(give, 'gx', gx_move(1, 0))  18.3 us
    pallas_call x1, Pallas kernels, tail_parts(): call(tail_body, 'tail_parts', (hidden // TILE,), 1, [pl.BlockSpec((4, cou...  17.7 us
    ppermute x1, waiting for transfers between devices, shards(): b_sum = lax.ppermute(b_sum, 'gz', z_up)  8.76 us
    pallas_call x1, Pallas kernels, head_last(): call(head_last_body, 'head_last', (tiles,), 1, [pl.BlockSpec((1, count, d...  8.64 us
  transfers between devices with their start and end apart: 20, of which 4 were waited for; matrix products, arithmetic and copies ran while one was open for 4% of the time, Pallas kernels for 43%

profile of v2, /device:TPU:0, one launch (start us, length us, event | category | flops | bytes accessed | tf_op | source)
XLA Modules:
  0.0 214.3 jit_solution(5450893343174171648)
XLA Ops:
  7.2 0.0 reduce-scatter.2.cloned.1.call-start
  7.2 1.8 slice_bitcast_fusion
  9.0 1.6 collective-permute-start.1
  10.6 0.0 collective-permute-start
  10.6 0.6 stack.89.table
  11.2 11.2 %gelu_t.2 = (bf16[1536,512]{1,0:T(8,128)(2,1)}, bf16[1536,1536]{1,0:T(8,128)(2,1)}) custom-call(s32[16]{0:T(128)} %stack.89.table, bf16[2048,3072]{1,0:T(8,128)(2,1)} %pre.7), custom_call_target="tpu_custom_call" | custom-call | flops 3932160 | bytes 196608 | tf_op jit(solution)/shard_map/gelu_t/pallas_call | solution.py:89
  22.4 0.0 copy-start
  22.4 0.0 collective-permute-done.1
  22.4 0.6 collective-permute-start.2
  23.0 2.2 %slice_bitcast_fusion.1 = (bf16[1,384,1152]{2,1,0:T(8,128)(2,1)S(1)}, bf16[384,1152]{1,0:T(8,128)(2,1)}) fusion(bf16[512,1152]{1,0:T(8,128)(2,1)} %param.4), kind=kLoop, calls=%fused_computation.4 | loop fusion | bytes 2654208 | tf_op jit(solution)/shard_map/stack | solution.py:343
  25.2 0.5 collective-permute-start.8
  25.7 0.0 collective-permute-done
  25.7 0.0 collective-permute-done.2
  25.7 0.0 copy-done
  25.7 2.2 %pad_maximum_fusion.1.rows_a.rows_b.rows = bf16[4,128,1152]{2,1,0:T(8,128)(2,1)} fusion(bf16[1,128,1152]{2,1,0:T(8,128)(2,1)S(1)} %bitcast.37, bf16[1,128,1152]{2,1,0:T(8,128)(2,1)} %bitcast.16, bf16[1,128,1152]{2,1,0:T(8,128)(2,1)} %bitcast.15, bf16[1,128,1152]{2,1,0:T(8,128)(2,1)S(1)} %copy-done), kind=kLoop, calls=%fused_computation.2 | loop fusion | flops 1769472 | bytes 2359296 | tf_op jit(solution)/shard_map/stack | solution.py:321
  27.9 7.2 %head_parts.3 = (bf16[128,1536]{1,0:T(8,128)(2,1)}, bf16[128,1536]{1,0:T(8,128)(2,1)}) custom-call(s32[16]{0:T(128)} %stack.89.table, bf16[4,128,1152]{2,1,0:T(8,128)(2,1)} %pad_maximum_fusion.1.rows_a.rows_b.rows, bf16[4,128,1152]{2,1,0:T(8,128)(2,1)} %pad_maximum_fusion.1.rows_a.rows_b.rows, bf16[3072,1152]{1,0:T(8,128)(2,1)} %weights.3, ...), custom_call_target="tpu_custom_call" | custom-call | flops 14155776 | bytes 132096 | tf_op jit(solution)/shard_map/head_parts/pallas_call | solution.py:149
  35.1 1.9 collective-permute-start.4
  37.0 2.2 %collective-permute-start.3 = (bf16[128,1536]{1,0:T(8,128)(2,1)}, bf16[128,1536]{1,0:T(8,128)(2,1)}, u32[]{:S(2)}, u32[]{:S(2)}) collective-permute-start(bf16[128,1536]{1,0:T(8,128)(2,1)} %get-tuple-element.38), channel_id=1, source_target_pairs={{0,3},{1,0},{2,1},{3,2},{4,7},{5,4},{6,5},{7,6},{8,11},{9,8},{10,9... | collective-permute-start | bytes 1179656 | tf_op jit(solution)/shard_map/ppermute | solution.py:325
  39.3 6.6 %head_parts.4 = (bf16[128,1536]{1,0:T(8,128)(2,1)}, bf16[128,1536]{1,0:T(8,128)(2,1)}) custom-call(s32[16]{0:T(128)} %stack.89.table, bf16[4,128,1152]{2,1,0:T(8,128)(2,1)} %pad_maximum_fusion.1.rows_a.rows_b.rows, bf16[4,128,1152]{2,1,0:T(8,128)(2,1)} %pad_maximum_fusion.1.rows_a.rows_b.rows, bf16[3072,1152]{1,0:T(8,128)(2,1)} %weights.3, ...), custom_call_target="tpu_custom_call" | custom-call | flops 14155776 | bytes 132096 | tf_op jit(solution)/shard_map/head_parts/pallas_call | solution.py:149
  45.9 2.0 collective-permute-start.6
  47.9 0.1 collective-permute-start.5
  47.9 11.2 %gelu_t.3 = (bf16[1536,512]{1,0:T(8,128)(2,1)}, bf16[1536,1536]{1,0:T(8,128)(2,1)}) custom-call(s32[16]{0:T(128)} %stack.89.table, bf16[2048,3072]{1,0:T(8,128)(2,1)} %pre.7), custom_call_target="tpu_custom_call" | custom-call | flops 3932160 | bytes 196608 | tf_op jit(solution)/shard_map/gelu_t/pallas_call | solution.py:89
  59.1 0.0 collective-permute-done.4.refs_1_
  59.1 0.0 collective-permute-start.7
  59.1 0.0 collective-permute-done.3.refs_0_
  59.2 7.1 %head_parts.5 = (bf16[128,1536]{1,0:T(8,128)(2,1)}, bf16[128,1536]{1,0:T(8,128)(2,1)}) custom-call(s32[16]{0:T(128)} %stack.89.table, bf16[4,128,1152]{2,1,0:T(8,128)(2,1)} %pad_maximum_fusion.1.rows_a.rows_b.rows, bf16[4,128,1152]{2,1,0:T(8,128)(2,1)} %pad_maximum_fusion.1.rows_a.rows_b.rows, bf16[3072,1152]{1,0:T(8,128)(2,1)} %weights.3, ...), custom_call_target="tpu_custom_call" | custom-call | flops 14155776 | bytes 144384 | tf_op jit(solution)/shard_map/head_parts/pallas_call | solution.py:149
  66.3 0.0 collective-permute-done.6.side_b
  66.3 0.0 collective-permute-done.5.side_a
  66.3 0.0 collective-permute-done.8
  66.3 0.6 collective-permute-start.9
  66.9 0.0 collective-permute-done.7
  66.9 2.3 %collective-permute-done.9 = bf16[384,1152]{1,0:T(8,128)(2,1)S(1)} collective-permute-done((bf16[384,1152]{1,0:T(8,128)(2,1)}, bf16[384,1152]{1,0:T(8,128)(2,1)S(1)}, u32[]{:S(2)}, u32[]{:S(2)}) %collective-permute-start.9) | collective-permute-done | bytes 884768 | tf_op jit(solution)/shard_map/ppermute | solution.py:342
  69.1 3.2 %pad_maximum_fusion.rows = bf16[4,384,1152]{2,1,0:T(8,128)(2,1)} fusion(bf16[1,384,1152]{2,1,0:T(8,128)(2,1)S(1)} %bitcast.36, bf16[1,384,1152]{2,1,0:T(8,128)(2,1)} %bitcast.20, bf16[1,384,1152]{2,1,0:T(8,128)(2,1)} %bitcast.19, bf16[1,384,1152]{2,1,0:T(8,128)(2,1)S(1)} %get-tuple-element.66), kind=kLoop, calls=%fused_computation | loop fusion | flops 5308416 | bytes 7077888 | tf_op jit(solution)/shard_map/stack | solution.py:343
  72.4 17.7 %tail_parts.1 = bf16[4,384,3072]{2,1,0:T(8,128)(2,1)} custom-call(s32[16]{0:T(128)} %stack.89.table, bf16[4,384,1152]{2,1,0:T(8,128)(2,1)} %pad_maximum_fusion.rows, bf16[3072,1152]{1,0:T(8,128)(2,1)} %weights.3), custom_call_target="tpu_custom_call" | custom-call | flops 169869312 | bytes 313344 | tf_op jit(solution)/shard_map/tail_parts/pallas_call | solution.py:116
  90.1 0.0 reduce-scatter.2.cloned.1.call-update
  90.1 9.3 %terms.3 = (bf16[384,1152]{1,0:T(8,128)(2,1)}, bf16[384,1152]{1,0:T(8,128)(2,1)}) custom-call(s32[16]{0:T(128)} %stack.89.table, bf16[1536,512]{1,0:T(8,128)(2,1)} %get-tuple-element.34.a_head, bf16[1536,1536]{1,0:T(8,128)(2,1)} %get-tuple-element.35.a_tail, bf16[1536,512]{1,0:T(8,128)(2,1)} %get-tuple-element.42.b_head, ...), custom_call_target="tpu_custom_call" | custom-call | flops 56623104 | bytes 178176 | tf_op jit(solution)/shard_map/terms/pallas_call | solution.py:276
  99.4 1.6 collective-permute-start.13
  101.0 1.7 collective-permute-start.12
  102.6 0.0 collective-permute-start.11
  102.6 3.2 %collective-permute-start.10 = (bf16[128,1536]{1,0:T(8,128)(2,1)}, bf16[128,1536]{1,0:T(8,128)(2,1)}, u32[]{:S(2)}, u32[]{:S(2)}) collective-permute-start(bf16[128,1536]{1,0:T(8,128)(2,1)} %get-tuple-element.46), channel_id=1, source_target_pairs={{0,3},{1,0},{2,1},{3,2},{4,7},{5,4},{6,5},{7,6},{8,11},{9,8},{10,9... | collective-permute-start | bytes 1179656 | tf_op jit(solution)/shard_map/ppermute | solution.py:338
  105.9 9.3 %terms.4 = (bf16[384,1152]{1,0:T(8,128)(2,1)}, bf16[384,1152]{1,0:T(8,128)(2,1)}) custom-call(s32[16]{0:T(128)} %stack.89.table, bf16[1536,512]{1,0:T(8,128)(2,1)} %get-tuple-element.34.a_head, bf16[1536,1536]{1,0:T(8,128)(2,1)} %get-tuple-element.35.a_tail, bf16[1536,512]{1,0:T(8,128)(2,1)} %get-tuple-element.42.b_head, ...), custom_call_target="tpu_custom_call" | custom-call | flops 56623104 | bytes 178176 | tf_op jit(solution)/shard_map/terms/pallas_call | solution.py:276
  115.2 0.4 collective-permute-start.14
  115.5 8.8 %collective-permute-done.11.sum_b = bf16[128,1536]{1,0:T(8,128)(2,1)} collective-permute-done((bf16[128,1536]{1,0:T(8,128)(2,1)}, bf16[128,1536]{1,0:T(8,128)(2,1)}, u32[]{:S(2)}, u32[]{:S(2)}) %collective-permute-start.11) | collective-permute-done | bytes 393248 | tf_op jit(solution)/shard_map/ppermute | solution.py:339
  124.3 1.8 collective-permute-start.16
  126.0 0.0 collective-permute-done.10.sum_a
  126.0 8.6 %head_last.1.held = bf16[512,3072]{1,0:T(8,128)(2,1)} custom-call(s32[16]{0:T(128)} %stack.89.table, bf16[4,128,1152]{2,1,0:T(8,128)(2,1)} %pad_maximum_fusion.1.rows_a.rows_b.rows, bf16[3072,1152]{1,0:T(8,128)(2,1)} %weights.3, bf16[2048,3072]{1,0:T(8,128)(2,1)} %pre.7, bf16[128,1536]{1,0:T(8,128)(2,1)} %collective-permute-done.5.side_a, ...), custom_call_target="tpu_custom_call" | custom-call | flops 14155776 | bytes 164352 | tf_op jit(solution)/shard_map/head_last/pallas_call | solution.py:191
  134.7 0.0 collective-permute-done.13.refs_1_
  134.7 0.0 collective-permute-done.12.refs_0_
  134.7 9.9 %terms.5 = (bf16[384,1152]{1,0:T(8,128)(2,1)}, bf16[384,1152]{1,0:T(8,128)(2,1)}) custom-call(s32[16]{0:T(128)} %stack.89.table, bf16[1536,512]{1,0:T(8,128)(2,1)} %get-tuple-element.34.a_head, bf16[1536,1536]{1,0:T(8,128)(2,1)} %get-tuple-element.35.a_tail, bf16[1536,512]{1,0:T(8,128)(2,1)} %get-tuple-element.42.b_head, ...), custom_call_target="tpu_custom_call" | custom-call | flops 56623104 | bytes 178176 | tf_op jit(solution)/shard_map/terms/pallas_call | solution.py:276
  144.6 0.4 collective-permute-start.17
  145.0 2.9 %collective-permute-start.15 = (bf16[384,1152]{1,0:T(8,128)(2,1)}, bf16[384,1152]{1,0:T(8,128)(2,1)}, u32[]{:S(2)}, u32[]{:S(2)}) collective-permute-start(bf16[384,1152]{1,0:T(8,128)(2,1)} %get-tuple-element.60), channel_id=1, source_target_pairs={{0,48},{16,0},{32,16},{48,32},{64,112},{80,64},{96,80},{112,96},{1... | collective-permute-start | bytes 2654216 | tf_op jit(solution)/shard_map/ppermute | solution.py:366
  147.9 0.0 collective-permute-done.16.refs_2_
  147.9 0.0 collective-permute-done.14.refs_0_
  147.9 0.0 copy-start.1
  147.9 18.8 %collective-permute-done.17.refs_3_ = bf16[384,1152]{1,0:T(8,128)(2,1)} collective-permute-done((bf16[384,1152]{1,0:T(8,128)(2,1)}, bf16[384,1152]{1,0:T(8,128)(2,1)}, u32[]{:S(2)}, u32[]{:S(2)}) %collective-permute-start.17) | collective-permute-done | bytes 884768 | tf_op jit(solution)/shard_map/ppermute | solution.py:367
  166.7 0.0 collective-permute-done.15.refs_1_
  166.7 0.0 copy-done.1
  166.7 10.7 %last_terms.1 = (f32[384,1152]{1,0:T(8,128)}, bf16[384,1152]{1,0:T(8,128)(2,1)}) custom-call(s32[16]{0:T(128)} %stack.89.table, bf16[1536,512]{1,0:T(8,128)(2,1)} %get-tuple-element.34.a_head, bf16[1536,1536]{1,0:T(8,128)(2,1)} %get-tuple-element.35.a_tail, bf16[1536,512]{1,0:T(8,128)(2,1)} %get-tuple-element.42.b_head, ...), custom_call_target="tpu_custom_call" | custom-call | flops 56623104 | bytes 178176 | tf_op jit(solution)/shard_map/last_terms/pallas_call | solution.py:276
  177.4 3.1 %collective-permute-start.18 = (bf16[384,1152]{1,0:T(8,128)(2,1)}, bf16[384,1152]{1,0:T(8,128)(2,1)S(1)}, u32[]{:S(2)}, u32[]{:S(2)}) collective-permute-start(bf16[384,1152]{1,0:T(8,128)(2,1)} %get-tuple-element.65), channel_id=1, source_target_pairs={{0,64},{16,80},{32,96},{48,112},{64,0},{80,16},{96,32},{112,48},{1... | collective-permute-start | bytes 2654216 | tf_op jit(solution)/shard_map/ppermute | solution.py:371
  180.5 18.3 %collective-permute-done.18 = bf16[384,1152]{1,0:T(8,128)(2,1)S(1)} collective-permute-done((bf16[384,1152]{1,0:T(8,128)(2,1)}, bf16[384,1152]{1,0:T(8,128)(2,1)S(1)}, u32[]{:S(2)}, u32[]{:S(2)}) %collective-permute-start.18) | collective-permute-done | bytes 884768 | tf_op jit(solution)/shard_map/ppermute | solution.py:371
  198.8 2.6 %add_convert_fusion = bf16[384,1152]{1,0:T(8,128)(2,1)} fusion(f32[384,1152]{1,0:T(8,128)} %get-tuple-element.64, bf16[384,1152]{1,0:T(8,128)(2,1)S(1)} %collective-permute-done.18), kind=kLoop, calls=%fused_computation.1 | loop fusion | flops 1327104 | bytes 3538944 | tf_op jit(solution)/shard_map/convert_element_type | solution.py:372
  201.4 0.0 reduce-scatter.2.cloned.1.call-done.summed
  201.4 6.1 %tail_last.1 = bf16[512,3072]{1,0:T(8,128)(2,1)} custom-call(s32[16]{0:T(128)} %stack.89.table, bf16[384,3072]{1,0:T(8,128)(2,1)} %reduce-scatter.2.cloned.1.call-done.summed, bf16[2048,3072]{1,0:T(8,128)(2,1)} %pre.7, bf16[512,3072]{1,0:T(8,128)(2,1)} %head_last.1.held), custom_call_target="tpu_custom_call", output_to_operand_aliasing={{}: (3, {})} | custom-call | flops 737280 | bytes 110592 | tf_op jit(solution)/shard_map/tail_last/pallas_call | solution.py:220
  (1 shorter events, 0.0 us)
Async XLA Ops:
  7.2 194.2 %reduce-scatter.2.cloned.1.call-start = ((), (), s32[]{:S(2)}) async-start(), calls=%async_computation.1 | async-start | bytes 11796480 | tf_op jit(solution)/shard_map/reduce_scatter | solution.py:346
  9.0 13.4 %collective-permute-start.1 = (bf16[128,1152]{1,0:T(8,128)(2,1)}, bf16[128,1152]{1,0:T(8,128)(2,1)}, u32[]{:S(2)}, u32[]{:S(2)}) collective-permute-start(bf16[128,1152]{1,0:T(8,128)(2,1)} %get-tuple-element.69), channel_id=1, source_target_pairs={{0,8},{4,12},{8,0},{12,4},{1,9},{5,13},{9,1},{13,5},{2,10},{6,14},... | collective-permute-start | bytes 884744 | tf_op jit(solution)/shard_map/ppermute | solution.py:312
  10.6 15.1 %collective-permute-start = (bf16[128,1152]{1,0:T(8,128)(2,1)}, bf16[128,1152]{1,0:T(8,128)(2,1)}, u32[]{:S(2)}, u32[]{:S(2)}) collective-permute-start(bf16[128,1152]{1,0:T(8,128)(2,1)} %get-tuple-element.69), channel_id=1, source_target_pairs={{0,4},{4,0},{8,12},{12,8},{1,5},{5,1},{9,13},{13,9},{2,6},{6,2},{1... | collective-permute-start | bytes 884744 | tf_op jit(solution)/shard_map/ppermute | solution.py:313
  22.4 3.3 %copy-start = (bf16[1,128,1152]{2,1,0:T(8,128)(2,1)S(1)}, bf16[1,128,1152]{2,1,0:T(8,128)(2,1)}, u32[]{:S(2)}) copy-start(bf16[1,128,1152]{2,1,0:T(8,128)(2,1)} %get-tuple-element.68) | copy-start | bytes 884740
  22.4 3.2 %collective-permute-start.2 = (bf16[128,1152]{1,0:T(8,128)(2,1)}, bf16[128,1152]{1,0:T(8,128)(2,1)S(1)}, u32[]{:S(2)}, u32[]{:S(2)}) collective-permute-start(bf16[128,1152]{1,0:T(8,128)(2,1)} %collective-permute-done.1), channel_id=1, source_target_pairs={{0,4},{4,0},{8,12},{12,8},{1,5},{5,1},{9,13},{13,9},{2,6},{6,2},{1... | collective-permute-start | bytes 884744 | tf_op jit(solution)/shard_map/ppermute | solution.py:319
  25.2 41.1 %collective-permute-start.8 = (bf16[384,1152]{1,0:T(8,128)(2,1)}, bf16[384,1152]{1,0:T(8,128)(2,1)}, u32[]{:S(2)}, u32[]{:S(2)}) collective-permute-start(bf16[384,1152]{1,0:T(8,128)(2,1)} %get-tuple-element.50), channel_id=1, source_target_pairs={{0,8},{4,12},{8,0},{12,4},{1,9},{5,13},{9,1},{13,5},{2,10},{6,14},... | collective-permute-start | bytes 2654216 | tf_op jit(solution)/shard_map/ppermute | solution.py:320
  35.1 24.0 %collective-permute-start.4 = (bf16[128,1536]{1,0:T(8,128)(2,1)}, bf16[128,1536]{1,0:T(8,128)(2,1)}, u32[]{:S(2)}, u32[]{:S(2)}) collective-permute-start(bf16[128,1536]{1,0:T(8,128)(2,1)} %get-tuple-element.45), channel_id=1, source_target_pairs={{0,1},{1,2},{2,3},{3,0},{4,5},{5,6},{6,7},{7,4},{8,9},{9,10},{10,1... | collective-permute-start | bytes 1179656 | tf_op jit(solution)/shard_map/ppermute | solution.py:326
  37.0 22.1 %collective-permute-start.3 = (bf16[128,1536]{1,0:T(8,128)(2,1)}, bf16[128,1536]{1,0:T(8,128)(2,1)}, u32[]{:S(2)}, u32[]{:S(2)}) collective-permute-start(bf16[128,1536]{1,0:T(8,128)(2,1)} %get-tuple-element.38), channel_id=1, source_target_pairs={{0,3},{1,0},{2,1},{3,2},{4,7},{5,4},{6,5},{7,6},{8,11},{9,8},{10,9... | collective-permute-start | bytes 1179656 | tf_op jit(solution)/shard_map/ppermute | solution.py:325
  45.9 20.4 %collective-permute-start.6 = (bf16[128,1536]{1,0:T(8,128)(2,1)}, bf16[128,1536]{1,0:T(8,128)(2,1)}, u32[]{:S(2)}, u32[]{:S(2)}) collective-permute-start(bf16[128,1536]{1,0:T(8,128)(2,1)} %get-tuple-element.48), channel_id=1, source_target_pairs={{0,3},{1,0},{2,1},{3,2},{4,7},{5,4},{6,5},{7,6},{8,11},{9,8},{10,9... | collective-permute-start | bytes 1179656 | tf_op jit(solution)/shard_map/ppermute | solution.py:330
  47.9 18.4 %collective-permute-start.5 = (bf16[128,1536]{1,0:T(8,128)(2,1)}, bf16[128,1536]{1,0:T(8,128)(2,1)}, u32[]{:S(2)}, u32[]{:S(2)}) collective-permute-start(bf16[128,1536]{1,0:T(8,128)(2,1)} %get-tuple-element.40), channel_id=1, source_target_pairs={{0,1},{1,2},{2,3},{3,0},{4,5},{5,6},{6,7},{7,4},{8,9},{9,10},{10,1... | collective-permute-start | bytes 1179656 | tf_op jit(solution)/shard_map/ppermute | solution.py:329
  59.1 7.7 %collective-permute-start.7 = (bf16[384,1152]{1,0:T(8,128)(2,1)}, bf16[384,1152]{1,0:T(8,128)(2,1)}, u32[]{:S(2)}, u32[]{:S(2)}) collective-permute-start(bf16[384,1152]{1,0:T(8,128)(2,1)} %get-tuple-element.50), channel_id=1, source_target_pairs={{0,4},{4,0},{8,12},{12,8},{1,5},{5,1},{9,13},{13,9},{2,6},{6,2},{1... | collective-permute-start | bytes 2654216 | tf_op jit(solution)/shard_map/ppermute | solution.py:314
  66.3 2.8 %collective-permute-start.9 = (bf16[384,1152]{1,0:T(8,128)(2,1)}, bf16[384,1152]{1,0:T(8,128)(2,1)S(1)}, u32[]{:S(2)}, u32[]{:S(2)}) collective-permute-start(bf16[384,1152]{1,0:T(8,128)(2,1)} %collective-permute-done.8), channel_id=1, source_target_pairs={{0,4},{4,0},{8,12},{12,8},{1,5},{5,1},{9,13},{13,9},{2,6},{6,2},{1... | collective-permute-start | bytes 2654216 | tf_op jit(solution)/shard_map/ppermute | solution.py:342
  99.4 35.3 %collective-permute-start.13 = (bf16[384,1152]{1,0:T(8,128)(2,1)}, bf16[384,1152]{1,0:T(8,128)(2,1)}, u32[]{:S(2)}, u32[]{:S(2)}) collective-permute-start(bf16[384,1152]{1,0:T(8,128)(2,1)} %get-tuple-element.59), channel_id=1, source_target_pairs={{0,16},{16,32},{32,48},{48,0},{64,80},{80,96},{96,112},{112,64},{1... | collective-permute-start | bytes 2654216 | tf_op jit(solution)/shard_map/ppermute | solution.py:355
  101.0 33.7 %collective-permute-start.12 = (bf16[384,1152]{1,0:T(8,128)(2,1)}, bf16[384,1152]{1,0:T(8,128)(2,1)}, u32[]{:S(2)}, u32[]{:S(2)}) collective-permute-start(bf16[384,1152]{1,0:T(8,128)(2,1)} %get-tuple-element.53), channel_id=1, source_target_pairs={{0,48},{16,0},{32,16},{48,32},{64,112},{80,64},{96,80},{112,96},{1... | collective-permute-start | bytes 2654216 | tf_op jit(solution)/shard_map/ppermute | solution.py:354
  102.6 21.6 %collective-permute-start.11 = (bf16[128,1536]{1,0:T(8,128)(2,1)}, bf16[128,1536]{1,0:T(8,128)(2,1)}, u32[]{:S(2)}, u32[]{:S(2)}) collective-permute-start(bf16[128,1536]{1,0:T(8,128)(2,1)} %get-tuple-element.57), channel_id=1, source_target_pairs={{0,1},{1,2},{2,3},{3,0},{4,5},{5,6},{6,7},{7,4},{8,9},{9,10},{10,1... | collective-permute-start | bytes 1179656 | tf_op jit(solution)/shard_map/ppermute | solution.py:339
  102.6 23.4 %collective-permute-start.10 = (bf16[128,1536]{1,0:T(8,128)(2,1)}, bf16[128,1536]{1,0:T(8,128)(2,1)}, u32[]{:S(2)}, u32[]{:S(2)}) collective-permute-start(bf16[128,1536]{1,0:T(8,128)(2,1)} %get-tuple-element.46), channel_id=1, source_target_pairs={{0,3},{1,0},{2,1},{3,2},{4,7},{5,4},{6,5},{7,6},{8,11},{9,8},{10,9... | collective-permute-start | bytes 1179656 | tf_op jit(solution)/shard_map/ppermute | solution.py:338
  115.2 32.7 %collective-permute-start.14 = (bf16[384,1152]{1,0:T(8,128)(2,1)}, bf16[384,1152]{1,0:T(8,128)(2,1)S(1)}, u32[]{:S(2)}, u32[]{:S(2)}) collective-permute-start(bf16[384,1152]{1,0:T(8,128)(2,1)} %get-tuple-element.55), channel_id=1, source_target_pairs={{0,16},{16,32},{32,48},{48,0},{64,80},{80,96},{96,112},{112,64},{1... | collective-permute-start | bytes 2654216 | tf_op jit(solution)/shard_map/ppermute | solution.py:358
  124.3 23.6 %collective-permute-start.16 = (bf16[384,1152]{1,0:T(8,128)(2,1)}, bf16[384,1152]{1,0:T(8,128)(2,1)}, u32[]{:S(2)}, u32[]{:S(2)}) collective-permute-start(bf16[384,1152]{1,0:T(8,128)(2,1)} %get-tuple-element.62), channel_id=1, source_target_pairs={{0,48},{16,0},{32,16},{48,32},{64,112},{80,64},{96,80},{112,96},{1... | collective-permute-start | bytes 2654216 | tf_op jit(solution)/shard_map/ppermute | solution.py:359
  144.6 22.0 %collective-permute-start.17 = (bf16[384,1152]{1,0:T(8,128)(2,1)}, bf16[384,1152]{1,0:T(8,128)(2,1)}, u32[]{:S(2)}, u32[]{:S(2)}) collective-permute-start(bf16[384,1152]{1,0:T(8,128)(2,1)} %get-tuple-element.63), channel_id=1, source_target_pairs={{0,16},{16,32},{32,48},{48,0},{64,80},{80,96},{96,112},{112,64},{1... | collective-permute-start | bytes 2654216 | tf_op jit(solution)/shard_map/ppermute | solution.py:367
  145.0 21.7 %collective-permute-start.15 = (bf16[384,1152]{1,0:T(8,128)(2,1)}, bf16[384,1152]{1,0:T(8,128)(2,1)}, u32[]{:S(2)}, u32[]{:S(2)}) collective-permute-start(bf16[384,1152]{1,0:T(8,128)(2,1)} %get-tuple-element.60), channel_id=1, source_target_pairs={{0,48},{16,0},{32,16},{48,32},{64,112},{80,64},{96,80},{112,96},{1... | collective-permute-start | bytes 2654216 | tf_op jit(solution)/shard_map/ppermute | solution.py:366
  147.9 18.8 %copy-start.1 = (bf16[384,1152]{1,0:T(8,128)(2,1)}, bf16[384,1152]{1,0:T(8,128)(2,1)S(1)}, u32[]{:S(2)}) copy-start(bf16[384,1152]{1,0:T(8,128)(2,1)S(1)} %collective-permute-done.14.refs_0_) | copy-start | bytes 2654212
  177.4 21.4 %collective-permute-start.18 = (bf16[384,1152]{1,0:T(8,128)(2,1)}, bf16[384,1152]{1,0:T(8,128)(2,1)S(1)}, u32[]{:S(2)}, u32[]{:S(2)}) collective-permute-start(bf16[384,1152]{1,0:T(8,128)(2,1)} %get-tuple-element.65), channel_id=1, source_target_pairs={{0,64},{16,80},{32,96},{48,112},{64,0},{80,16},{96,32},{112,48},{1... | collective-permute-start | bytes 2654216 | tf_op jit(solution)/shard_map/ppermute | solution.py:371
Sparse Core Ops, SparseCore 0:
  90.2 99.1 reduce-scatter.1

commit v3 on v0

v3 whole, which is shorter than its diff:
```python
import functools
import math

import jax
import jax.numpy as jnp
from jax import lax
from jax.experimental import pallas as pl
from jax.experimental.pallas import tpu as pltpu
from jax.sharding import PartitionSpec as P

root_half = 1.0 / math.sqrt(2.0)
slope_scale = 1.0 / math.sqrt(2.0 * math.pi)
bf16 = jnp.bfloat16
f32 = jnp.float32
HEAD = 128
TILE = 512
STEP = 256
Y_FIRST = 640
SHORT, LONG = 1 / 64, 512
VMEM = 63 * 1024 * 1024


def gelu(values):
    return 0.5 * values * (1.0 + lax.erf(values * root_half))


def unit_slope(values):
    return (
        0.5 * (1.0 + lax.erf(values * root_half))
        + values * jnp.exp(-0.5 * values * values) * slope_scale
    )


def gz_ring(step):
    return [(i, (i + step) % 4) for i in range(4)]


def gx_move(dh, dy):
    return [(h * 4 + y, (h + dh) % 2 * 4 + (y + dy) % 4) for h in range(2) for y in range(4)]


def gy_move(dl, dc):
    return [(l * 2 + c, (l + dl) % 2 * 2 + (c + dc) % 2) for l in range(2) for c in range(2)]


def after(value, *others):
    return lax.optimization_barrier((value,) + others)[0]


def call(body, name, grid, prefetch, in_specs, out_specs, out_shape, flops, moved, scratch=(), cost=1, aliases=None):
    return pl.pallas_call(
        body,
        name=name,
        out_shape=out_shape,
        grid_spec=pltpu.PrefetchScalarGridSpec(
            num_scalar_prefetch=prefetch, grid=grid, in_specs=in_specs, out_specs=out_specs,
            scratch_shapes=list(scratch),
        ),
        compiler_params=pltpu.CompilerParams(
            dimension_semantics=("arbitrary",) * len(grid), vmem_limit_bytes=VMEM
        ),
        input_output_aliases=aliases or {},
        cost_estimate=pl.CostEstimate(
            flops=int(flops * cost), bytes_accessed=int(moved * cost), transcendentals=0
        ),
    )


def rows_dot(rows, weights):
    return lax.dot_general(rows, weights, (((1,), (1,)), ((), ())), preferred_element_type=f32)


def cols_dot(left, right):
    return lax.dot_general(left, right, (((0,), (0,)), ((), ())), preferred_element_type=f32)


ORDER, FAR, UP, DOWN, OWN, GZ, H = 0, 4, 5, 6, 7, 8, 9


def first_body(table, rows, weights, out):
    part = rows_dot(rows[...], weights[...]).astype(bf16)
    count = out.shape[1]
    for j in range(4):
        out[table[ORDER + j]] = part[j * count : (j + 1) * count]


def first_parts(rows, weights, table):
    _, count, depth = rows.shape
    hidden = weights.shape[0]
    return call(
        first_body,
        "first_parts",
        (hidden // TILE,),
        1,
        [
            pl.BlockSpec((4 * count, depth), lambda t, o: (0, 0)),
            pl.BlockSpec((TILE, depth), lambda t, o: (t, 0)),
        ],
        pl.BlockSpec((4, count, TILE), lambda t, o: (0, 0, t)),
        jax.ShapeDtypeStruct((4, count, hidden), bf16),
        8 * count * depth * hidden,
        2 * (4 * count * depth + depth * hidden + 4 * count * hidden),
    )(table, rows.reshape(4 * count, depth), weights)


def pair_body(adds, table, rows_a, rows_b, weights_a, weights_b, *refs):
    out_a, out_b = refs[-2:]
    sum_a = rows_dot(rows_a[0], weights_a[...])
    sum_b = rows_dot(rows_b[0], weights_b[...])
    if adds:
        sum_a += refs[0][...].astype(f32)
        sum_b += refs[1][...].astype(f32)
    out_a[...] = sum_a.astype(bf16)
    out_b[...] = sum_b.astype(bf16)


def pair_parts(rows, weights, table, at_a, at_b, *arrived):
    _, count, depth = rows.shape
    hidden = weights.shape[0]
    tiles = hidden // 2 // STEP
    half = pl.BlockSpec((count, STEP), lambda t, p: (0, t))
    shape = jax.ShapeDtypeStruct((count, hidden // 2), bf16)
    return call(
        functools.partial(pair_body, bool(arrived)),
        "pair_parts",
        (tiles,),
        1,
        [
            pl.BlockSpec((1, count, depth), lambda t, p: (p[at_a], 0, 0)),
            pl.BlockSpec((1, count, depth), lambda t, p: (p[at_b], 0, 0)),
            pl.BlockSpec((STEP, depth), lambda t, p: (t, 0)),
            pl.BlockSpec((STEP, depth), lambda t, p: (tiles + t, 0)),
        ]
        + [half] * len(arrived),
        [half, half],
        [shape, shape],
        2 * count * depth * hidden,
        2 * (2 * count * depth + depth * hidden + count * hidden * (1 + len(arrived) // 2)),
        cost=SHORT,
    )(table, rows, rows, weights, weights, *arrived)


def own_body(table, rows, weights, pre, side_a, sum_a, side_b, sum_b, held, out):
    total = rows_dot(rows[0], weights[...])
    slope = unit_slope(pre[...].astype(f32))
    first = pl.program_id(0) < pl.num_programs(0) // 2
    head = out.shape[0] - total.shape[0]
    out[:head] = held[...]

    @pl.when(first)
    def _():
        whole = total + side_a[...].astype(f32) + sum_a[...].astype(f32)
        out[head:] = (whole * slope[head:]).astype(bf16)

    @pl.when(jnp.logical_not(first))
    def _():
        whole = total + side_b[...].astype(f32) + sum_b[...].astype(f32)
        out[head:] = (whole * slope[head:]).astype(bf16)


def own_rows(rows, weights, preact, table, side_a, sum_a, side_b, sum_b, held):
    share = preact.shape[0] // 4
    _, count, depth = rows.shape
    hidden = weights.shape[0]
    tiles = hidden // TILE
    half_a = pl.BlockSpec((count, TILE), lambda t, p: (0, jnp.minimum(t, tiles // 2 - 1)))
    half_b = pl.BlockSpec((count, TILE), lambda t, p: (0, jnp.maximum(t - tiles // 2, 0)))
    return call(
        own_body,
        "own_rows",
        (tiles,),
        1,
        [
            pl.BlockSpec((1, count, depth), lambda t, p: (p[OWN], 0, 0)),
            pl.BlockSpec((TILE, depth), lambda t, p: (t, 0)),
            pl.BlockSpec((share, TILE), lambda t, p: (p[GZ], t)),
            half_a,
            half_a,
            half_b,
            half_b,
            pl.BlockSpec((share - count, TILE), lambda t, p: (0, t)),
        ],
        pl.BlockSpec((share, TILE), lambda t, p: (0, t)),
        jax.ShapeDtypeStruct((share, hidden), bf16),
        2 * count * depth * hidden,
        2 * (count * depth + depth * hidden + 4 * count * hidden),
        cost=LONG,
    )(table, rows, weights, preact, side_a, sum_a, side_b, sum_b, held)


def sloped_body(table, summed, pre, out):
    out[...] = (summed[...].astype(f32) * unit_slope(pre[...].astype(f32))).astype(bf16)


def sloped(summed, preact, table):
    count, hidden = summed.shape
    share = preact.shape[0] // 4
    width = hidden // 2
    return call(
        sloped_body,
        "sloped",
        (2,),
        1,
        [
            pl.BlockSpec((count, width), lambda t, p: (0, t)),
            pl.BlockSpec((count, width), lambda t, p: (p[GZ] * (share // count), t)),
        ],
        pl.BlockSpec((count, width), lambda t, p: (0, t)),
        jax.ShapeDtypeStruct((count, hidden), bf16),
        count * hidden * 40,
        6 * count * hidden,
        cost=LONG,
    )(table, summed, preact)


def near_body(table, pre_own, pre_partner, own, partner, *refs):
    total = cols_dot(gelu(pre_own[...].astype(f32)).astype(bf16), own[...])
    total += cols_dot(gelu(pre_partner[...].astype(f32)).astype(bf16), partner[...])
    refs[-1][...] = total


def near_terms(preact, own, partner, table, *held):
    rows, hidden = preact.shape
    share, features = own.shape
    chunk = hidden // 8
    start = 4 if held else 0
    return call(
        near_body,
        "near_terms",
        (4,),
        1,
        [
            pl.BlockSpec((share, chunk), lambda t, p: (p[ORDER], start + t)),
            pl.BlockSpec((share, chunk), lambda t, p: (p[ORDER + 1], start + t)),
            pl.BlockSpec((share, features), lambda t, p: (0, 0)),
            pl.BlockSpec((share, features), lambda t, p: (0, 0)),
        ]
        + [pl.BlockSpec(memory_space=pl.ANY)] * len(held),
        pl.BlockSpec((chunk, features), lambda t, p: (start + t, 0)),
        jax.ShapeDtypeStruct((hidden, features), f32),
        2 * share * features * hidden,
        share * hidden + 2 * share * features + 2 * features * hidden,
        cost=LONG if held else SHORT,
        aliases={5: 0} if held else {},
    )(table, preact, preact, own, partner, *held)


def far_body(table, pre_a, pre_b, head, tail, held, y_first, give, keep, rows):
    share = pre_a.shape[0]
    count = head.shape[1]

    @pl.when(pl.program_id(0) == 0)
    def _():
        for j in range(2):
            rows[j * share : j * share + count] = head[j]
            rows[j * share + count : (j + 1) * share] = tail[j]

    total = held[...]
    total += cols_dot(gelu(pre_a[...].astype(f32)).astype(bf16), rows[:share])
    total += cols_dot(gelu(pre_b[...].astype(f32)).astype(bf16), rows[share:])
    total = total.astype(bf16)
    split = y_first.shape[1]
    y_first[...] = total[:, :split]

    @pl.when(pl.program_id(0) < 4)
    def _():
        give[...] = total[:, split:]

    @pl.when(pl.program_id(0) >= 4)
    def _():
        keep[...] = total[:, split:]


def far_terms(preact, head, tail, held, table):
    rows, hidden = preact.shape
    features = held.shape[1]
    share = rows // 4
    chunk = hidden // 8
    rest = features - Y_FIRST

    def half(t, p):
        return (p[H] + 1 + t // 4) % 2

    def source(t, p):
        return half(t, p) * 4 + t % 4

    return call(
        far_body,
        "far_terms",
        (8,),
        1,
        [
            pl.BlockSpec((share, chunk), lambda t, p: (p[ORDER + 2], source(t, p))),
            pl.BlockSpec((share, chunk), lambda t, p: (p[ORDER + 3], source(t, p))),
            pl.BlockSpec((2, head.shape[1], features), lambda t, p: (1, 0, 0)),
            pl.BlockSpec((2, tail.shape[1], features), lambda t, p: (1, 0, 0)),
            pl.BlockSpec((chunk, features), lambda t, p: (source(t, p), 0)),
        ],
        [
            pl.BlockSpec((chunk, Y_FIRST), lambda t, p: (t % 4 * 2 + half(t, p), 0)),
            pl.BlockSpec((chunk, rest), lambda t, p: (jnp.minimum(t, 3), 0)),
            pl.BlockSpec((chunk, rest), lambda t, p: (jnp.maximum(t - 4, 0), 0)),
        ],
        [
            jax.ShapeDtypeStruct((hidden, Y_FIRST), bf16),
            jax.ShapeDtypeStruct((hidden // 2, rest), bf16),
            jax.ShapeDtypeStruct((hidden // 2, rest), bf16),
        ],
        4 * share * features * hidden,
        2 * (2 * share * hidden + 2 * share * features + 3 * features * hidden),
        scratch=[pltpu.VMEM((2 * share, features), bf16)],
        cost=SHORT,
    )(table, preact, preact, head, tail, held)


def shards(preact, grad_output, down_weight):
    gy = lax.axis_index("gy")
    gz = lax.axis_index("gz")
    gx = lax.axis_index("gx")
    y, h = gx % 4, gx // 4
    entries = [gy ^ j for j in range(4)]
    entries += [(gz + 2) % 4 ^ gy, (gz + 1) % 4 ^ gy, (gz + 3) % 4 ^ gy, gz ^ gy, gz, h, 0, 0]
    table = jnp.stack([jnp.asarray(entry, jnp.int32) for entry in entries])

    other_chip, other_core = gy_move(1, 0), gy_move(0, 1)
    z_up, z_down = gz_ring(1), gz_ring(-1)
    along_y = [[0, 1, 2, 3], [4, 5, 6, 7]]

    own_head, own_tail = grad_output[:HEAD], grad_output[HEAD:]
    across = lax.ppermute(own_head, "gy", other_chip)
    partner = lax.ppermute(grad_output, "gy", other_core)
    corner = lax.ppermute(across, "gy", other_core)
    across_tail = lax.ppermute(after(own_tail, across), "gy", other_chip)

    head = jnp.stack((own_head, partner[:HEAD], across, corner))
    parts = first_parts(head, down_weight, table)
    table = after(table, parts)
    summed = lax.psum_scatter(
        parts.reshape(-1, parts.shape[2]), "gz", scatter_dimension=0, tiled=True
    )

    near = near_terms(preact, grad_output, partner, table)
    table = after(table, near)
    corner_tail = lax.ppermute(after(across_tail, table), "gy", other_core)
    near = near_terms(preact, grad_output, partner, table, near)
    table = after(table, near)

    tail = jnp.stack((own_tail, partner[HEAD:], across_tail, corner_tail))
    a_far, b_far = pair_parts(tail, down_weight, table, FAR, FAR)
    table = after(table, a_far)
    a_far = lax.ppermute(a_far, "gz", z_down)
    b_far = lax.ppermute(b_far, "gz", z_up)

    y_first, give, keep = far_terms(preact, head, tail, near, table)
    table = after(table, y_first)
    taken = lax.ppermute(give, "gx", gx_move(1, 0))
    y_first = lax.psum_scatter(
        y_first, "gx", scatter_dimension=0, axis_index_groups=along_y, tiled=True
    )

    a_side, b_side = pair_parts(tail, down_weight, table, UP, DOWN)
    table = after(table, a_side)
    a_side = lax.ppermute(after(a_side, a_far, b_far), "gz", z_up)
    b_side = lax.ppermute(after(b_side, a_far, b_far), "gz", z_down)

    a_sum, b_sum = pair_parts(tail, down_weight, table, DOWN, UP, a_far, b_far)
    table = after(table, a_sum)
    a_sum = lax.ppermute(a_sum, "gz", z_down)
    b_sum = lax.ppermute(b_sum, "gz", z_up)

    held = sloped(summed, preact, after(table, a_side, b_side))
    table = after(table, held)

    both = (keep.astype(f32) + after(taken, table).astype(f32)).astype(bf16)
    x_first = lax.psum_scatter(
        after(both, y_first), "gx", scatter_dimension=0, axis_index_groups=along_y, tiled=True
    )
    table = after(table, both)

    mine, other = jnp.split(after(y_first, table), 2)
    mine, other = jnp.where(h == 0, mine, other), jnp.where(h == 0, other, mine)
    crossed = lax.ppermute(other, "gx", gx_move(1, 0))

    grad_pre = own_rows(
        tail, down_weight, preact, table, a_side, a_sum, b_side, b_sum, held
    )
    y_first = (mine.astype(f32) + crossed.astype(f32)).astype(bf16)
    grad_down = jnp.concatenate((y_first, x_first), axis=1)
    return (grad_pre, grad_down)


def solution(mesh):
    return jax.shard_map(
        shards,
        mesh=mesh,
        in_specs=(P("gx", "gy"), P(("gx", "gy"), "gz"), P("gy", "gz")),
        out_specs=(P(("gx", "gz"), "gy"), P(("gy", "gx"), "gz")),
        check_vma=False,
    )
```

time: 431 us -> 193 us (0.45)
  waiting for transfers between devices: 321 us -> 49 us
  Pallas kernels: 0 us -> 91.1 us
  matrix products: 47.3 us -> 0 us
  other arithmetic: 47.6 us -> 12 us
  starting transfers between devices: 0.3 us -> 18.1 us
  local copies, waits for them, and re-layouts: 0 us -> 7.47 us
    psum x1 -> x0, waiting for transfers between devices: 167 us -> none  [shards(): grad_act = lax.psum(part.astype(jnp.bfloat16), 'gz').astype(jnp.float32)]
    reduce_scatter x1 -> x3, waiting for transfers between devices: 99.2 us -> 1.07 us  [the longest x1 1.06 us: shards(): lax.psum_scatter(after(both, y_first), 'gx', scatter_dimension=0, axis_in...]
    pallas_call x0 -> x9, Pallas kernels: none -> 91.1 us  [the longest x3 28.7 us: pair_parts(): call(functools.partial(pair_body, bool(arrived)), 'pair_parts', (tiles,),...]
    all_gather x1 -> x0, waiting for transfers between devices: 54.5 us -> none  [shards(): output_rows = lax.all_gather(grad_output, 'gy', axis=0, tiled=True)]
    ppermute x0 -> x13, waiting for transfers between devices: none -> 47.9 us  [the longest x1 17.2 us: shards(): b_far = lax.ppermute(b_far, 'gz', z_up)]
    dot_general x2 -> x0, matrix products: 47.3 us -> none  [the longest x1 25.2 us: shards(): lax.dot_general(activation, output_rows, contract_rows, preferred_element...]
    mul x1 -> x0, other arithmetic: 22.6 us -> none  [unit_slope(): -0.5 * values * values]
    convert_element_type x2, other arithmetic: 25 us -> 4.7 us  [the longest x1 3.48 us: shards(): both = (keep.astype(f32) + after(taken, table).astype(f32)).astype(bf16)]
  transfers between devices with their start and end apart: 3 -> 16, of which waited for: 3 -> 8; matrix products, arithmetic and copies ran while one was open for 17% -> 8% of each run, Pallas kernels for 0% -> 48%
where the time goes in v3:
time: 193 us; the launch traced here: 192 us
  Pallas kernels  91.1 us (47%)
  waiting for transfers between devices  49 us (25%)
  starting transfers between devices  18.1 us (9%)
  between operations  13.8 us (7%)
  other arithmetic  12 us (6%)
  local copies, waits for them, and re-layouts  7.47 us (4%)
    pallas_call x3, Pallas kernels, pair_parts(): call(functools.partial(pair_body, bool(arrived)), 'pair_parts', (tiles,),...  28.7 us
    pallas_call x2, Pallas kernels, near_terms(): call(near_body, 'near_terms', (4,), 1, [pl.BlockSpec((share, chunk), lamb...  19.2 us
    pallas_call x1, Pallas kernels, far_terms(): call(far_body, 'far_terms', (8,), 1, [pl.BlockSpec((share, chunk), lambda...  17.5 us
    ppermute x1, waiting for transfers between devices, shards(): b_far = lax.ppermute(b_far, 'gz', z_up)  17.2 us
    pallas_call x1, Pallas kernels, own_rows(): call(own_body, 'own_rows', (tiles,), 1, [pl.BlockSpec((1, count, depth),...  12.7 us
    ppermute x1, waiting for transfers between devices, shards(): a_side = lax.ppermute(after(a_side, a_far, b_far), 'gz', z_up)  12.5 us
    pallas_call x1, Pallas kernels, first_parts(): call(first_body, 'first_parts', (hidden // TILE,), 1, [pl.BlockSpec((4 *...  9.73 us
    ppermute x1, waiting for transfers between devices, shards(): taken = lax.ppermute(give, 'gx', gx_move(1, 0))  6.69 us
  transfers between devices with their start and end apart: 16, of which 8 were waited for; matrix products, arithmetic and copies ran while one was open for 8% of the time, Pallas kernels for 48%

profile of v3, /device:TPU:0, one launch (start us, length us, event | category | flops | bytes accessed | tf_op | source)
XLA Modules:
  0.0 191.6 jit_solution(3866616484183085249)
XLA Ops:
  7.2 0.0 reduce-scatter.4.cloned.1.call-start
  7.2 0.1 collective-permute-start
  7.3 1.0 slice_bitcast_fusion.2
  8.3 1.7 collective-permute-start.1
  10.0 0.6 stack.73.table
  10.5 2.2 %slice_bitcast_fusion.3 = (bf16[1,384,1152]{2,1,0:T(8,128)(2,1)}, bf16[384,1152]{1,0:T(8,128)(2,1)S(1)}) fusion(bf16[512,1152]{1,0:T(8,128)(2,1)} %own.3), kind=kLoop, calls=%fused_computation.9 | loop fusion | bytes 2654208 | tf_op jit(solution)/shard_map/stack | solution.py:348
  12.8 5.0 %collective-permute-done.1 = bf16[128,1152]{1,0:T(8,128)(2,1)S(1)} collective-permute-done((bf16[128,1152]{1,0:T(8,128)(2,1)S(1)}, bf16[128,1152]{1,0:T(8,128)(2,1)S(1)}, u32[]{:S(2)}, u32[]{:S(2)}) %collective-permute-start.1) | collective-permute-done | bytes 294944 | tf_op jit(solution)/shard_map/ppermute | solution.py:330
  17.8 1.6 collective-permute-start.3
  19.4 0.0 collective-permute-start.2
  19.4 0.0 collective-permute-done.partner
  19.4 0.0 copy-start
  19.4 1.0 copy-done
  20.4 0.5 collective-permute-done.2
  21.0 1.3 pad_maximum_fusion.1.head
  22.2 9.7 %first_parts.1 = bf16[4,128,3072]{2,1,0:T(8,128)(2,1)} custom-call(s32[12]{0:T(128)} %stack.73.table, bf16[512,1152]{1,0:T(8,128)(2,1)} %bitcast.24, bf16[3072,1152]{1,0:T(8,128)(2,1)} %weights.3), custom_call_target="tpu_custom_call" | custom-call | flops 3623878656 | bytes 11403264 | tf_op jit(solution)/shard_map/first_parts/pallas_call | solution.py:90
  32.0 0.0 reduce-scatter.4.cloned.1.call-update
  32.0 0.0 reduce-scatter.6.cloned.1.call-start
  32.0 9.3 %near_terms.2.refs_0_ = f32[3072,1152]{1,0:T(8,128)} custom-call(s32[12]{0:T(128)} %stack.73.table, bf16[2048,3072]{1,0:T(8,128)(2,1)} %pre.3, bf16[2048,3072]{1,0:T(8,128)(2,1)} %pre.3, bf16[512,1152]{1,0:T(8,128)(2,1)} %own.3, bf16[512,1152]{1,0:T(8,128)(2,1)} %copy-done), custom_call_target="tpu_custom_call" | custom-call | flops 56623104 | bytes 153600 | tf_op jit(solution)/shard_map/near_terms/pallas_call | solution.py:227
  41.4 0.0 collective-permute-done.3
  41.4 0.1 collective-permute-start.4
  41.5 9.8 %near_terms.3.held = f32[3072,1152]{1,0:T(8,128)} custom-call(s32[12]{0:T(128)} %stack.73.table, bf16[2048,3072]{1,0:T(8,128)(2,1)} %pre.3, bf16[2048,3072]{1,0:T(8,128)(2,1)} %pre.3, bf16[512,1152]{1,0:T(8,128)(2,1)} %own.3, bf16[512,1152]{1,0:T(8,128)(2,1)} %copy-done, f32[3072,1152]{1,0:T(8,128)} %near_terms.2.refs_0_), custom_call_target="tpu_custom_call", output_to_operand_aliasing={{}: (5, {})} | custom-call | flops 1855425871872 | bytes 5033164800 | tf_op jit(solution)/shard_map/near_terms/pallas_call | solution.py:227
  51.3 0.0 copy-start.3
  51.3 1.3 slice_bitcast_fusion
  52.7 0.0 collective-permute-done.4
  52.7 0.1 copy-done.3
  52.8 3.2 %pad_maximum_fusion.rows_a.rows_b.tail.rows = bf16[4,384,1152]{2,1,0:T(8,128)(2,1)} fusion(bf16[1,384,1152]{2,1,0:T(8,128)(2,1)} %bitcast.18, bf16[1,384,1152]{2,1,0:T(8,128)(2,1)} %bitcast.17, bf16[1,384,1152]{2,1,0:T(8,128)(2,1)S(1)} %slice_bitcast_fusion, bf16[1,384,1152]{2,1,0:T(8,128)(2,1)S(1)} %copy-done.3), kind=kLoop, calls=%fused_computation | loop fusion | flops 5308416 | bytes 7077888 | tf_op jit(solution)/shard_map/stack | solution.py:348
  56.1 9.4 %pair_parts.3 = (bf16[384,1536]{1,0:T(8,128)(2,1)}, bf16[384,1536]{1,0:T(8,128)(2,1)}) custom-call(s32[12]{0:T(128)} %stack.73.table, bf16[4,384,1152]{2,1,0:T(8,128)(2,1)} %pad_maximum_fusion.rows_a.rows_b.tail.rows, bf16[4,384,1152]{2,1,0:T(8,128)(2,1)} %pad_maximum_fusion.rows_a.rows_b.tail.rows, bf16[3072,1152]{1,0:T(8,128)(2,1)} %weights.3, ...), custom_call_target="tpu_custom_call" | custom-call | flops 42467328 | bytes 175104 | tf_op jit(solution)/shard_map/pair_parts/pallas_call | solution.py:123
  65.5 17.5 %far_terms.1 = (bf16[3072,640]{1,0:T(8,128)(2,1)}, bf16[1536,512]{1,0:T(8,128)(2,1)}, bf16[1536,512]{1,0:T(8,128)(2,1)}) custom-call(s32[12]{0:T(128)} %stack.73.table, bf16[2048,3072]{1,0:T(8,128)(2,1)} %pre.3, bf16[2048,3072]{1,0:T(8,128)(2,1)} %pre.3, bf16[4,128,1152]{2,1,0:T(8,128)(2,1)} %pad_maximum_fusion.1.head, ...), custom_call_target="tpu_custom_call" | custom-call | flops 113246208 | bytes 466944 | tf_op jit(solution)/shard_map/far_terms/pallas_call | solution.py:287
  83.0 0.0 reduce-scatter.6.cloned.1.call-update
  83.0 0.0 reduce-scatter.8.cloned.1.call-start
  83.1 1.8 collective-permute-start.6
  84.9 2.0 %collective-permute-start.5 = (bf16[384,1536]{1,0:T(8,128)(2,1)}, bf16[384,1536]{1,0:T(8,128)(2,1)}, u32[]{:S(2)}, u32[]{:S(2)}) collective-permute-start(bf16[384,1536]{1,0:T(8,128)(2,1)} %get-tuple-element.33), channel_id=1, source_target_pairs={{0,3},{1,0},{2,1},{3,2},{4,7},{5,4},{6,5},{7,6},{8,11},{9,8},{10,9... | collective-permute-start | bytes 3538952 | tf_op jit(solution)/shard_map/ppermute | solution.py:351
  86.9 9.4 %pair_parts.4 = (bf16[384,1536]{1,0:T(8,128)(2,1)}, bf16[384,1536]{1,0:T(8,128)(2,1)}) custom-call(s32[12]{0:T(128)} %stack.73.table, bf16[4,384,1152]{2,1,0:T(8,128)(2,1)} %pad_maximum_fusion.rows_a.rows_b.tail.rows, bf16[4,384,1152]{2,1,0:T(8,128)(2,1)} %pad_maximum_fusion.rows_a.rows_b.tail.rows, bf16[3072,1152]{1,0:T(8,128)(2,1)} %weights.3, ...), custom_call_target="tpu_custom_call" | custom-call | flops 42467328 | bytes 175104 | tf_op jit(solution)/shard_map/pair_parts/pallas_call | solution.py:123
  96.3 17.2 %collective-permute-done.6.refs_1_ = bf16[384,1536]{1,0:T(8,128)(2,1)} collective-permute-done((bf16[384,1536]{1,0:T(8,128)(2,1)}, bf16[384,1536]{1,0:T(8,128)(2,1)}, u32[]{:S(2)}, u32[]{:S(2)}) %collective-permute-start.6) | collective-permute-done | bytes 1179680 | tf_op jit(solution)/shard_map/ppermute | solution.py:352
  113.6 0.0 collective-permute-done.5.refs_0_
  113.6 1.4 collective-permute-start.7
  115.0 1.8 collective-permute-start.8
  116.8 2.8 %collective-permute-start.9 = (bf16[1536,512]{1,0:T(8,128)(2,1)}, bf16[1536,512]{1,0:T(8,128)(2,1)}, u32[]{:S(2)}, u32[]{:S(2)}) collective-permute-start(bf16[1536,512]{1,0:T(8,128)(2,1)} %get-tuple-element.48), channel_id=1, source_target_pairs={{0,64},{16,80},{32,96},{48,112},{64,0},{80,16},{96,32},{112,48},{1... | collective-permute-start | bytes 4718600 | tf_op jit(solution)/shard_map/ppermute | solution.py:356
  119.6 9.9 %pair_parts.5 = (bf16[384,1536]{1,0:T(8,128)(2,1)}, bf16[384,1536]{1,0:T(8,128)(2,1)}) custom-call(s32[12]{0:T(128)} %stack.73.table, bf16[4,384,1152]{2,1,0:T(8,128)(2,1)} %pad_maximum_fusion.rows_a.rows_b.tail.rows, bf16[4,384,1152]{2,1,0:T(8,128)(2,1)} %pad_maximum_fusion.rows_a.rows_b.tail.rows, bf16[3072,1152]{1,0:T(8,128)(2,1)} %weights.3, ...), custom_call_target="tpu_custom_call" | custom-call | flops 42467328 | bytes 211968 | tf_op jit(solution)/shard_map/pair_parts/pallas_call | solution.py:123
  129.4 1.7 collective-permute-start.10
  131.1 0.4 collective-permute-start.11
  131.5 12.5 %collective-permute-done.7.side_a = bf16[384,1536]{1,0:T(8,128)(2,1)} collective-permute-done((bf16[384,1536]{1,0:T(8,128)(2,1)}, bf16[384,1536]{1,0:T(8,128)(2,1)}, u32[]{:S(2)}, u32[]{:S(2)}) %collective-permute-start.7) | collective-permute-done | bytes 1179680 | tf_op jit(solution)/shard_map/ppermute | solution.py:363
  143.9 0.2 collective-permute-done.8.side_b
  144.2 0.0 reduce-scatter.4.cloned.1.call-done.summed
  144.2 3.3 %sloped.1.held = bf16[128,3072]{1,0:T(8,128)(2,1)} custom-call(s32[12]{0:T(128)} %stack.73.table, bf16[128,3072]{1,0:T(8,128)(2,1)} %reduce-scatter.4.cloned.1.call-done.summed, bf16[2048,3072]{1,0:T(8,128)(2,1)} %pre.3), custom_call_target="tpu_custom_call" | custom-call | flops 8053063680 | bytes 1207959552 | tf_op jit(solution)/shard_map/sloped/pallas_call | solution.py:199
  147.5 6.7 %collective-permute-done.9 = bf16[1536,512]{1,0:T(8,128)(2,1)} collective-permute-done((bf16[1536,512]{1,0:T(8,128)(2,1)}, bf16[1536,512]{1,0:T(8,128)(2,1)}, u32[]{:S(2)}, u32[]{:S(2)}) %collective-permute-start.9) | collective-permute-done | bytes 1572896 | tf_op jit(solution)/shard_map/ppermute | solution.py:356
  154.2 3.5 %add_convert_fusion = bf16[1536,512]{1,0:T(8,128)(2,1)} fusion(bf16[1536,512]{1,0:T(8,128)(2,1)} %collective-permute-done.9, bf16[1536,512]{1,0:T(8,128)(2,1)} %get-tuple-element.47), kind=kLoop, calls=%fused_computation.1 | loop fusion | flops 3145728 | bytes 4718592 | tf_op jit(solution)/shard_map/convert_element_type | solution.py:374
  157.7 0.0 reduce-scatter.6.cloned.1.call-done
  157.7 0.0 copy-start.1
  157.7 0.0 reduce-scatter.8.cloned.1.call-update
  157.7 1.2 copy-done.1
  158.9 0.8 broadcast_select_fusion
  159.7 2.7 %collective-permute-start.12 = (bf16[384,640]{1,0:T(8,128)(2,1)}, bf16[384,640]{1,0:T(8,128)(2,1)}, u32[]{:S(2)}, u32[]{:S(2)}) collective-permute-start(bf16[384,640]{1,0:T(8,128)(2,1)} %broadcast_select_fusion), channel_id=1, source_target_pairs={{0,64},{16,80},{32,96},{48,112},{64,0},{80,16},{96,32},{112,48},{1... | collective-permute-start | bytes 1474568 | tf_op jit(solution)/shard_map/ppermute | solution.py:382
  162.4 5.6 %collective-permute-done.11.sum_b = bf16[384,1536]{1,0:T(8,128)(2,1)} collective-permute-done((bf16[384,1536]{1,0:T(8,128)(2,1)}, bf16[384,1536]{1,0:T(8,128)(2,1)}, u32[]{:S(2)}, u32[]{:S(2)}) %collective-permute-start.11) | collective-permute-done | bytes 1179680 | tf_op jit(solution)/shard_map/ppermute | solution.py:369
  168.1 0.0 collective-permute-done.10.sum_a
  168.1 0.0 copy-start.2
  168.1 12.7 %own_rows.1 = bf16[512,3072]{1,0:T(8,128)(2,1)} custom-call(s32[12]{0:T(128)} %stack.73.table, bf16[4,384,1152]{2,1,0:T(8,128)(2,1)} %pad_maximum_fusion.rows_a.rows_b.tail.rows, bf16[3072,1152]{1,0:T(8,128)(2,1)} %weights.3, bf16[2048,3072]{1,0:T(8,128)(2,1)} %pre.3, bf16[384,1536]{1,0:T(8,128)(2,1)} %collective-permute-done.7.side_a, ...), custom_call_target="tpu_custom_call" | custom-call | flops 1391569403904 | bytes 8908701696 | tf_op jit(solution)/shard_map/own_rows/pallas_call | solution.py:168
  180.8 0.0 collective-permute-done.12
  180.8 0.0 copy-done.2
  180.8 1.2 add_convert_fusion.1
  182.0 1.1 reduce-scatter.8.cloned.1.call-done
  183.1 2.0 %pad_maximum_fusion.2 = bf16[384,1152]{1,0:T(8,128)(2,1)} fusion(bf16[384,512]{1,0:T(8,128)(2,1)} %reduce-scatter.8.cloned.1.call-done, bf16[384,640]{1,0:T(8,128)(2,1)S(1)} %add_convert_fusion.1), kind=kLoop, calls=%fused_computation.5 | loop fusion | flops 1769472 | bytes 1769472 | tf_op jit(solution)/shard_map/concatenate | solution.py:388
  (2 shorter events, 0.0 us)
Async XLA Ops:
  7.2 137.0 %reduce-scatter.4.cloned.1.call-start = ((), (), s32[]{:S(2)}) async-start(), calls=%async_computation.3 | async-start | bytes 3932160 | tf_op jit(solution)/shard_map/reduce_scatter | solution.py:338
  7.2 12.2 %collective-permute-start = (bf16[512,1152]{1,0:T(8,128)(2,1)}, bf16[512,1152]{1,0:T(8,128)(2,1)S(1)}, u32[]{:S(2)}, u32[]{:S(2)}) collective-permute-start(bf16[512,1152]{1,0:T(8,128)(2,1)} %own.3), channel_id=1, source_target_pairs={{0,4},{4,0},{8,12},{12,8},{1,5},{5,1},{9,13},{13,9},{2,6},{6,2},{1... | collective-permute-start | bytes 3538952 | tf_op jit(solution)/shard_map/ppermute | solution.py:331
  8.3 9.5 %collective-permute-start.1 = (bf16[128,1152]{1,0:T(8,128)(2,1)S(1)}, bf16[128,1152]{1,0:T(8,128)(2,1)S(1)}, u32[]{:S(2)}, u32[]{:S(2)}) collective-permute-start(bf16[128,1152]{1,0:T(8,128)(2,1)S(1)} %get-tuple-element.57), channel_id=1, source_target_pairs={{0,8},{4,12},{8,0},{12,4},{1,9},{5,13},{9,1},{13,5},{2,10},{6,14},... | collective-permute-start | bytes 884744 | tf_op jit(solution)/shard_map/ppermute | solution.py:330
  17.8 23.6 %collective-permute-start.3 = (bf16[384,1152]{1,0:T(8,128)(2,1)S(1)}, bf16[384,1152]{1,0:T(8,128)(2,1)}, u32[]{:S(2)}, u32[]{:S(2)}) collective-permute-start(bf16[384,1152]{1,0:T(8,128)(2,1)S(1)} %get-tuple-element.31), channel_id=1, source_target_pairs={{0,8},{4,12},{8,0},{12,4},{1,9},{5,13},{9,1},{13,5},{2,10},{6,14},... | collective-permute-start | bytes 2654216 | tf_op jit(solution)/shard_map/ppermute | solution.py:333
  19.4 1.6 collective-permute-start.2
  19.4 1.0 copy-start
  32.0 125.7 %reduce-scatter.6.cloned.1.call-start = ((), (), s32[]{:S(2)}) async-start(), calls=%async_computation.4 | async-start | bytes 4915200 | tf_op jit(solution)/shard_map/reduce_scatter | solution.py:357
  41.4 11.3 %collective-permute-start.4 = (bf16[384,1152]{1,0:T(8,128)(2,1)}, bf16[384,1152]{1,0:T(8,128)(2,1)}, u32[]{:S(2)}, u32[]{:S(2)}) collective-permute-start(bf16[384,1152]{1,0:T(8,128)(2,1)} %collective-permute-done.3), channel_id=1, source_target_pairs={{0,4},{4,0},{8,12},{12,8},{1,5},{5,1},{9,13},{13,9},{2,6},{6,2},{1... | collective-permute-start | bytes 2654216 | tf_op jit(solution)/shard_map/ppermute | solution.py:344
  51.3 1.5 copy-start.3
  83.0 100.0 %reduce-scatter.8.cloned.1.call-start = ((), (), s32[]{:S(2)}) async-start(), calls=%async_computation.5 | async-start | bytes 1966080 | tf_op jit(solution)/shard_map/reduce_scatter | solution.py:375
  83.1 30.5 %collective-permute-start.6 = (bf16[384,1536]{1,0:T(8,128)(2,1)}, bf16[384,1536]{1,0:T(8,128)(2,1)}, u32[]{:S(2)}, u32[]{:S(2)}) collective-permute-start(bf16[384,1536]{1,0:T(8,128)(2,1)} %get-tuple-element.39), channel_id=1, source_target_pairs={{0,1},{1,2},{2,3},{3,0},{4,5},{5,6},{6,7},{7,4},{8,9},{9,10},{10,1... | collective-permute-start | bytes 3538952 | tf_op jit(solution)/shard_map/ppermute | solution.py:352
  84.9 28.7 %collective-permute-start.5 = (bf16[384,1536]{1,0:T(8,128)(2,1)}, bf16[384,1536]{1,0:T(8,128)(2,1)}, u32[]{:S(2)}, u32[]{:S(2)}) collective-permute-start(bf16[384,1536]{1,0:T(8,128)(2,1)} %get-tuple-element.33), channel_id=1, source_target_pairs={{0,3},{1,0},{2,1},{3,2},{4,7},{5,4},{6,5},{7,6},{8,11},{9,8},{10,9... | collective-permute-start | bytes 3538952 | tf_op jit(solution)/shard_map/ppermute | solution.py:351
  113.6 30.4 %collective-permute-start.7 = (bf16[384,1536]{1,0:T(8,128)(2,1)}, bf16[384,1536]{1,0:T(8,128)(2,1)}, u32[]{:S(2)}, u32[]{:S(2)}) collective-permute-start(bf16[384,1536]{1,0:T(8,128)(2,1)} %get-tuple-element.42), channel_id=1, source_target_pairs={{0,1},{1,2},{2,3},{3,0},{4,5},{5,6},{6,7},{7,4},{8,9},{9,10},{10,1... | collective-permute-start | bytes 3538952 | tf_op jit(solution)/shard_map/ppermute | solution.py:363
  115.0 29.2 %collective-permute-start.8 = (bf16[384,1536]{1,0:T(8,128)(2,1)}, bf16[384,1536]{1,0:T(8,128)(2,1)}, u32[]{:S(2)}, u32[]{:S(2)}) collective-permute-start(bf16[384,1536]{1,0:T(8,128)(2,1)} %get-tuple-element.44), channel_id=1, source_target_pairs={{0,3},{1,0},{2,1},{3,2},{4,7},{5,4},{6,5},{7,6},{8,11},{9,8},{10,9... | collective-permute-start | bytes 3538952 | tf_op jit(solution)/shard_map/ppermute | solution.py:364
  116.8 37.4 %collective-permute-start.9 = (bf16[1536,512]{1,0:T(8,128)(2,1)}, bf16[1536,512]{1,0:T(8,128)(2,1)}, u32[]{:S(2)}, u32[]{:S(2)}) collective-permute-start(bf16[1536,512]{1,0:T(8,128)(2,1)} %get-tuple-element.48), channel_id=1, source_target_pairs={{0,64},{16,80},{32,96},{48,112},{64,0},{80,16},{96,32},{112,48},{1... | collective-permute-start | bytes 4718600 | tf_op jit(solution)/shard_map/ppermute | solution.py:356
  129.4 38.6 %collective-permute-start.10 = (bf16[384,1536]{1,0:T(8,128)(2,1)}, bf16[384,1536]{1,0:T(8,128)(2,1)}, u32[]{:S(2)}, u32[]{:S(2)}) collective-permute-start(bf16[384,1536]{1,0:T(8,128)(2,1)} %get-tuple-element.40), channel_id=1, source_target_pairs={{0,3},{1,0},{2,1},{3,2},{4,7},{5,4},{6,5},{7,6},{8,11},{9,8},{10,9... | collective-permute-start | bytes 3538952 | tf_op jit(solution)/shard_map/ppermute | solution.py:368
  131.1 37.0 %collective-permute-start.11 = (bf16[384,1536]{1,0:T(8,128)(2,1)}, bf16[384,1536]{1,0:T(8,128)(2,1)}, u32[]{:S(2)}, u32[]{:S(2)}) collective-permute-start(bf16[384,1536]{1,0:T(8,128)(2,1)} %get-tuple-element.51), channel_id=1, source_target_pairs={{0,1},{1,2},{2,3},{3,0},{4,5},{5,6},{6,7},{7,4},{8,9},{9,10},{10,1... | collective-permute-start | bytes 3538952 | tf_op jit(solution)/shard_map/ppermute | solution.py:369
  157.7 1.2 copy-start.1
  159.7 21.0 %collective-permute-start.12 = (bf16[384,640]{1,0:T(8,128)(2,1)}, bf16[384,640]{1,0:T(8,128)(2,1)}, u32[]{:S(2)}, u32[]{:S(2)}) collective-permute-start(bf16[384,640]{1,0:T(8,128)(2,1)} %broadcast_select_fusion), channel_id=1, source_target_pairs={{0,64},{16,80},{32,96},{48,112},{64,0},{80,16},{96,32},{112,48},{1... | collective-permute-start | bytes 1474568 | tf_op jit(solution)/shard_map/ppermute | solution.py:382
  168.1 12.7 %copy-start.2 = (bf16[768,640]{1,0:T(8,128)(2,1)S(1)}, bf16[768,640]{1,0:T(8,128)(2,1)}, u32[]{:S(2)}) copy-start(bf16[768,640]{1,0:T(8,128)(2,1)} %reduce-scatter.6.cloned.1.call-done) | copy-start | bytes 2949124
Sparse Core Ops, SparseCore 0:
  32.1 40.5 reduce-scatter.3
  83.2 46.3 reduce-scatter.5
  157.8 25.1 reduce-scatter.7

commit v4 on v0

v4 whole, which is shorter than its diff:
```python
import functools
import math

import jax
import jax.numpy as jnp
from jax import lax
from jax.experimental import pallas as pl
from jax.experimental.pallas import tpu as pltpu
from jax.sharding import PartitionSpec as P

root_half = 1.0 / math.sqrt(2.0)
slope_scale = 1.0 / math.sqrt(2.0 * math.pi)
bf16 = jnp.bfloat16
f32 = jnp.float32
HEAD = 128
TILE = 512
SHORT, SIDE, LAST, LONG = 1 / 64, 1 / 64, 2, 512
VMEM = 63 * 1024 * 1024


def gelu(values):
    return 0.5 * values * (1.0 + lax.erf(values * root_half))


def unit_slope(values):
    return (
        0.5 * (1.0 + lax.erf(values * root_half))
        + values * jnp.exp(-0.5 * values * values) * slope_scale
    )


def gz_ring(step):
    return [(i, (i + step) % 4) for i in range(4)]


def gx_move(dh, dy):
    return [(h * 4 + y, (h + dh) % 2 * 4 + (y + dy) % 4) for h in range(2) for y in range(4)]


def gy_move(dl, dc):
    return [(l * 2 + c, (l + dl) % 2 * 2 + (c + dc) % 2) for l in range(2) for c in range(2)]


def after(value, *others):
    return lax.optimization_barrier((value,) + others)[0]


def call(body, name, grid, prefetch, in_specs, out_specs, out_shape, flops, moved, scratch=(), cost=1, aliases=None):
    return pl.pallas_call(
        body,
        name=name,
        out_shape=out_shape,
        grid_spec=pltpu.PrefetchScalarGridSpec(
            num_scalar_prefetch=prefetch, grid=grid, in_specs=in_specs, out_specs=out_specs,
            scratch_shapes=list(scratch),
        ),
        compiler_params=pltpu.CompilerParams(
            dimension_semantics=("arbitrary",) * len(grid), vmem_limit_bytes=VMEM
        ),
        input_output_aliases=aliases or {},
        cost_estimate=pl.CostEstimate(
            flops=int(flops * cost), bytes_accessed=int(moved * cost), transcendentals=0
        ),
    )


def rows_dot(rows, weights):
    return lax.dot_general(rows, weights, (((1,), (1,)), ((), ())), preferred_element_type=f32)


def cols_dot(left, right):
    return lax.dot_general(left, right, (((0,), (0,)), ((), ())), preferred_element_type=f32)


ORDER, FAR, UP, DOWN, OWN, GZ = 0, 4, 5, 6, 7, 8
C_FAR, C_SIDE, C_SUM, C_OWN = 10, 12, 14, 16


def first_body(table, rows, weights, up, down, far, own, part):
    count = up.shape[0]
    total = rows_dot(rows[...], weights[...]).astype(bf16)
    for j in range(4):
        part[j] = total[j * count : (j + 1) * count]
    up[...] = part[table[UP]]
    down[...] = part[table[DOWN]]
    far[...] = part[table[FAR]]
    own[...] = part[table[OWN]]


def first_parts(rows, weights, table):
    _, count, depth = rows.shape
    hidden = weights.shape[0]
    block = pl.BlockSpec((count, TILE), lambda t, o: (0, t))
    return call(
        first_body,
        "first_parts",
        (hidden // TILE,),
        1,
        [
            pl.BlockSpec((4 * count, depth), lambda t, o: (0, 0)),
            pl.BlockSpec((TILE, depth), lambda t, o: (t, 0)),
        ],
        [block] * 4,
        [jax.ShapeDtypeStruct((count, hidden), bf16)] * 4,
        8 * count * depth * hidden,
        2 * (4 * count * depth + depth * hidden + 4 * count * hidden),
        scratch=[pltpu.VMEM((4, count, TILE), bf16)],
        cost=SHORT,
    )(table, rows.reshape(4 * count, depth), weights)


def tail_body(table, rows, weights, far_a, far_b, side_a, side_b, sum_a, sum_b, own, left, part):
    count = own.shape[0]
    first = pl.program_id(0) < pl.num_programs(0) // 2

    @pl.when(pl.program_id(0) == 0)
    def _():
        for j in range(4):
            left[j * count : (j + 1) * count] = rows[j, HEAD:]

    total = rows_dot(left[...], weights[...]).astype(bf16)
    for j in range(4):
        part[j] = total[j * count : (j + 1) * count]
    own[...] = part[table[OWN]]

    @pl.when(first)
    def _():
        far_a[...] = part[table[FAR]]
        side_a[...] = part[table[UP]]
        sum_a[...] = part[table[DOWN]]

    @pl.when(jnp.logical_not(first))
    def _():
        far_b[...] = part[table[FAR]]
        side_b[...] = part[table[DOWN]]
        sum_b[...] = part[table[UP]]


def tail_parts(rows, weights, table):
    _, share, depth = rows.shape
    count = share - HEAD
    hidden = weights.shape[0]
    tiles = hidden // TILE
    half_a = pl.BlockSpec((count, TILE), lambda t, p: (0, jnp.minimum(t, tiles // 2 - 1)))
    half_b = pl.BlockSpec((count, TILE), lambda t, p: (0, jnp.maximum(t - tiles // 2, 0)))
    half = jax.ShapeDtypeStruct((count, hidden // 2), bf16)
    return call(
        tail_body,
        "tail_parts",
        (tiles,),
        1,
        [
            pl.BlockSpec((4, share, depth), lambda t, o: (0, 0, 0)),
            pl.BlockSpec((TILE, depth), lambda t, o: (t, 0)),
        ],
        [half_a, half_b] * 3 + [pl.BlockSpec((count, TILE), lambda t, o: (0, t))],
        [half] * 6 + [jax.ShapeDtypeStruct((count, hidden), bf16)],
        8 * count * depth * hidden,
        2 * (4 * share * depth + depth * hidden + 4 * count * hidden),
        scratch=[pltpu.VMEM((4 * count, depth), bf16), pltpu.VMEM((4, count, TILE), bf16)],
        cost=SHORT,
    )(table, rows, weights)


def head_last_body(table, own, one, two, three, pre, out):
    total = own[...].astype(f32) + one[...].astype(f32)
    total += two[...].astype(f32) + three[...].astype(f32)
    out[...] = (total * unit_slope(pre[...].astype(f32))).astype(bf16)


def head_last(own, arrived, preact, table):
    count, hidden = own.shape
    share = preact.shape[0] // 4
    width = hidden // 2
    block = pl.BlockSpec((count, width), lambda t, p: (0, t))
    return call(
        head_last_body,
        "head_last",
        (2,),
        1,
        [block] * 4
        + [pl.BlockSpec((count, width), lambda t, p: (p[GZ] * (share // count), t))],
        block,
        jax.ShapeDtypeStruct((share, hidden), bf16),
        count * hidden * 40,
        12 * count * hidden,
        cost=LONG,
    )(table, own, *arrived, preact)


def tail_last_body(table, own, side_a, sum_a, side_b, sum_b, pre, held, out):
    width = side_a.shape[1]
    slope = unit_slope(pre[...].astype(f32))
    total = own[...].astype(f32)
    first = total[:, :width] + side_a[...].astype(f32) + sum_a[...].astype(f32)
    second = total[:, width:] + side_b[...].astype(f32) + sum_b[...].astype(f32)
    out[:, :width] = (first * slope[:, :width]).astype(bf16)
    out[:, width:] = (second * slope[:, width:]).astype(bf16)


def tail_last(own, side_a, sum_a, side_b, sum_b, preact, table, held):
    count, hidden = own.shape
    share = preact.shape[0] // 4
    step = 128
    start, blocks = HEAD // step, share // step
    half = pl.BlockSpec((step, hidden // 2), lambda t, p: (t, 0))
    return call(
        tail_last_body,
        "tail_last",
        (count // step,),
        1,
        [
            pl.BlockSpec((step, hidden), lambda t, p: (t, 0)),
            half,
            half,
            half,
            half,
            pl.BlockSpec((step, hidden), lambda t, p: (p[GZ] * blocks + start + t, 0)),
            pl.BlockSpec(memory_space=pl.ANY),
        ],
        pl.BlockSpec((step, hidden), lambda t, p: (start + t, 0)),
        jax.ShapeDtypeStruct((share, hidden), bf16),
        count * hidden * 40,
        10 * count * hidden,
        aliases={7: 0},
    )(table, own, side_a, sum_a, side_b, sum_b, preact, held)


def near_body(table, pre_own, pre_partner, own, partner, out):
    total = cols_dot(gelu(pre_own[...].astype(f32)).astype(bf16), own[...])
    total += cols_dot(gelu(pre_partner[...].astype(f32)).astype(bf16), partner[...])
    out[0] = total.astype(bf16)


def near_terms(preact, own, partner, table, at, cost=SHORT):
    rows, hidden = preact.shape
    share, features = own.shape
    chunk = hidden // 8
    return call(
        near_body,
        "near_terms",
        (2,),
        1,
        [
            pl.BlockSpec((share, chunk), lambda t, p: (p[ORDER], p[at + t])),
            pl.BlockSpec((share, chunk), lambda t, p: (p[ORDER + 1], p[at + t])),
            pl.BlockSpec((share, features), lambda t, p: (0, 0)),
            pl.BlockSpec((share, features), lambda t, p: (0, 0)),
        ],
        pl.BlockSpec((1, chunk, features), lambda t, p: (t, 0, 0)),
        jax.ShapeDtypeStruct((2, chunk, features), bf16),
        8 * share * features * chunk,
        2 * (4 * share * chunk + 2 * share * features + 2 * features * chunk),
        cost=cost,
    )(table, preact, preact, own, partner)


def terms_body(near, table, *refs):
    extra = refs[-4] if near else None
    rows, out_a, out_b = refs[-3:]
    total = None
    share = refs[0].shape[0]
    for j, pre in enumerate(refs[: 2 if near else 4]):
        act = gelu(pre[...].astype(f32)).astype(bf16)
        term = cols_dot(act, rows[j])
        total = term if total is None else total + term
    if near:
        total += extra[0].astype(f32)

    @pl.when(pl.program_id(0) == 0)
    def _():
        out_a[...] = total.astype(bf16)

    @pl.when(pl.program_id(0) == 1)
    def _():
        out_b[...] = total.astype(bf16)


def terms(preact, rows, table, at, held=None, cost=SHORT):
    hidden = preact.shape[1]
    _, share, features = rows.shape
    chunk = hidden // 8
    near = held is not None
    pieces = (2, 3) if near else (0, 1, 2, 3)

    def source(j):
        return pl.BlockSpec((share, chunk), lambda t, p: (p[ORDER + j], p[at + t]))

    out = pl.BlockSpec((chunk, features), lambda t, p: (0, 0))
    return call(
        functools.partial(terms_body, near),
        "terms",
        (2,),
        1,
        [source(j) for j in pieces]
        + [pl.BlockSpec((1, chunk, features), lambda t, p: (t, 0, 0))] * near
        + [pl.BlockSpec((len(pieces), share, features), lambda t, p: (int(near), 0, 0))],
        [out, out],
        [jax.ShapeDtypeStruct((chunk, features), bf16)] * 2,
        4 * len(pieces) * share * features * chunk,
        2 * (2 * len(pieces) * share * chunk + len(pieces) * share * features),
        cost=cost,
    )(table, *[preact] * len(pieces), *([held] if near else []), rows)


def shards(preact, grad_output, down_weight):
    gy = lax.axis_index("gy")
    gz = lax.axis_index("gz")
    gx = lax.axis_index("gx")
    y, h = gx % 4, gx // 4
    entries = [gy ^ j for j in range(4)]
    entries += [(gz + 2) % 4 ^ gy, (gz + 1) % 4 ^ gy, (gz + 3) % 4 ^ gy, gz ^ gy, gz, 0]
    up, down, far = (y + 1) % 4, (y + 3) % 4, (y + 2) % 4
    entries += [far, 4 + far, up, 4 + down, down, 4 + up, y, 4 + y]
    table = jnp.stack([jnp.asarray(entry, jnp.int32) for entry in entries])

    other_chip, other_core = gy_move(1, 0), gy_move(0, 1)
    z_up, z_down, z_far = gz_ring(1), gz_ring(-1), gz_ring(2)
    y_up, y_down = gx_move(0, 1), gx_move(0, -1)

    def add(*values):
        return sum(value.astype(f32) for value in values)

    own_head, own_tail = grad_output[:HEAD], grad_output[HEAD:]
    across = lax.ppermute(own_head, "gy", other_chip)
    partner = lax.ppermute(grad_output, "gy", other_core)
    near_far = near_terms(preact, grad_output, partner, table, C_FAR)
    table = after(table, near_far)
    corner = lax.ppermute(after(across, table), "gy", other_core)
    across_tail = lax.ppermute(after(own_tail, across, table), "gy", other_chip)

    head = jnp.stack((own_head, partner[:HEAD], across, corner))
    to_up, to_down, to_far, own = first_parts(head, down_weight, table)
    table = after(table, own)
    arrived = [
        lax.ppermute(to_up, "gz", z_up),
        lax.ppermute(to_down, "gz", z_down),
        lax.ppermute(to_far, "gz", z_far),
    ]

    near_side = near_terms(preact, grad_output, partner, table, C_SIDE)
    table = after(table, near_side)
    across_tail = after(across_tail, table)
    corner_tail = [
        lax.ppermute(across_tail[start : start + 96], "gy", other_core)
        for start in range(0, across_tail.shape[0], 96)
    ]
    rows = jnp.stack(
        (
            grad_output,
            partner,
            lax.optimization_barrier(jnp.concatenate((across, across_tail))),
            lax.optimization_barrier(jnp.concatenate((corner, *corner_tail))),
        )
    )

    c_far, d_far = terms(preact, rows, table, C_FAR, near_far)
    table = after(table, c_far)
    c_far = lax.ppermute(c_far, "gx", y_down)
    d_far = lax.ppermute(d_far, "gx", y_up)

    a_far, b_far, a_side, b_side, a_sum, b_sum, own_tail = tail_parts(rows, down_weight, table)
    table = after(table, own_tail)
    a_far = lax.ppermute(after(a_far, *arrived), "gz", z_down)
    b_far = lax.ppermute(after(b_far, *arrived), "gz", z_up)
    table = after(table, *arrived)

    c_side, d_side = terms(preact, rows, table, C_SIDE, near_side, cost=SIDE)
    table = after(table, c_side)
    c_side = lax.ppermute(after(c_side, c_far, d_far), "gx", y_up)
    d_side = lax.ppermute(after(d_side, c_far, d_far), "gx", y_down)

    c_sum, d_sum = terms(preact, rows, table, C_SUM)
    table = after(table, c_sum)
    c_own, d_own = terms(preact, rows, table, C_OWN, cost=LAST)
    table = after(table, c_own)

    a_side = lax.ppermute(after(a_side, table, a_far, b_far), "gz", z_up)
    b_side = lax.ppermute(after(b_side, table, a_far, b_far), "gz", z_down)
    c_sum = lax.ppermute(after(add(c_sum, c_far).astype(bf16), table, c_side, d_side, a_far, b_far), "gx", y_down)
    d_sum = lax.ppermute(after(add(d_sum, d_far).astype(bf16), table, c_side, d_side, a_far, b_far), "gx", y_up)

    held = head_last(own, arrived, preact, table)
    table = after(table, held)

    a_sum = lax.ppermute(after(add(a_sum, a_far).astype(bf16), a_side, b_side), "gz", z_down)
    b_sum = lax.ppermute(after(add(b_sum, b_far).astype(bf16), a_side, b_side), "gz", z_up)

    c_sum, d_sum = after(c_sum, a_side, b_side), after(d_sum, a_side, b_side)
    c_own = add(after(c_own, a_side, b_side), c_side, c_sum)
    d_own = add(d_own, d_side, d_sum)
    keep = jnp.where(h == 0, c_own, d_own)
    give = jnp.where(h == 0, d_own, c_own).astype(bf16)
    taken = lax.ppermute(give, "gx", gx_move(1, 0))

    grad_pre = tail_last(own_tail, a_side, a_sum, b_side, b_sum, preact, table, held)
    grad_down = add(keep, taken).astype(bf16)
    return (grad_pre, grad_down)


def solution(mesh):
    return jax.shard_map(
        shards,
        mesh=mesh,
        in_specs=(P("gx", "gy"), P(("gx", "gy"), "gz"), P("gy", "gz")),
        out_specs=(P(("gx", "gz"), "gy"), P(("gy", "gx"), "gz")),
        check_vma=False,
    )
```

time: 431 us -> 188 us (0.44)
  waiting for transfers between devices: 321 us -> 39.9 us
  Pallas kernels: 0 us -> 86.7 us
  matrix products: 47.3 us -> 0 us
  starting transfers between devices: 0.3 us -> 30.9 us
  other arithmetic: 47.6 us -> 22 us
  between operations: 13.7 us -> 0.79 us
  local copies, waits for them, and re-layouts: 0 us -> 7.52 us
    psum x1 -> x0, waiting for transfers between devices: 167 us -> none  [shards(): grad_act = lax.psum(part.astype(jnp.bfloat16), 'gz').astype(jnp.float32)]
    reduce_scatter x1 -> x0, waiting for transfers between devices: 99.2 us -> none  [shards(): lax.psum_scatter(lax.dot_general(activation, output_rows, contract_rows,...]
    pallas_call x0 -> x10, Pallas kernels: none -> 86.7 us  [the longest x4 33.3 us: terms(): call(functools.partial(terms_body, near), 'terms', (2,), 1, [source(j) fo...]
    all_gather x1 -> x0, waiting for transfers between devices: 54.5 us -> none  [shards(): output_rows = lax.all_gather(grad_output, 'gy', axis=0, tiled=True)]
    dot_general x2 -> x0, matrix products: 47.3 us -> none  [the longest x1 25.2 us: shards(): lax.dot_general(activation, output_rows, contract_rows, preferred_element...]
    ppermute x0 -> x24, waiting for transfers between devices: none -> 39.9 us  [the longest x1 15.6 us: shards(): a_side = lax.ppermute(after(a_side, table, a_far, b_far), 'gz', z_up)]
    ppermute x0 -> x24, starting transfers between devices: none -> 30.9 us  [the longest x1 3.22 us: shards(): b_side = lax.ppermute(after(b_side, table, a_far, b_far), 'gz', z_down)]
    mul x1 -> x0, other arithmetic: 22.6 us -> none  [unit_slope(): -0.5 * values * values]
  transfers between devices with their start and end apart: 3 -> 24, of which waited for: 3 -> 8; matrix products, arithmetic and copies ran while one was open for 17% -> 13% of each run, Pallas kernels for 0% -> 42%
where the time goes in v4:
time: 188 us
  Pallas kernels  86.7 us (46%)
  waiting for transfers between devices  39.9 us (21%)
  starting transfers between devices  30.9 us (16%)
  other arithmetic  22 us (12%)
  local copies, waits for them, and re-layouts  7.52 us (4%)
    pallas_call x4, Pallas kernels, terms(): call(functools.partial(terms_body, near), 'terms', (2,), 1, [source(j) fo...  33.3 us
    pallas_call x1, Pallas kernels, tail_parts(): call(tail_body, 'tail_parts', (tiles,), 1, [pl.BlockSpec((4, share, depth...  19.7 us
    ppermute x1, waiting for transfers between devices, shards(): a_side = lax.ppermute(after(a_side, table, a_far, b_far), 'gz', z_up)  15.6 us
    pallas_call x2, Pallas kernels, near_terms(): call(near_body, 'near_terms', (2,), 1, [pl.BlockSpec((share, chunk), lamb...  12.1 us
    pallas_call x1, Pallas kernels, first_parts(): call(first_body, 'first_parts', (hidden // TILE,), 1, [pl.BlockSpec((4 *...  9.85 us
    ppermute x1, waiting for transfers between devices, shards(): taken = lax.ppermute(give, 'gx', gx_move(1, 0))  8.16 us
    pallas_call x1, Pallas kernels, tail_last(): call(tail_last_body, 'tail_last', (count // step,), 1, [pl.BlockSpec((ste...  7.72 us
    ppermute x1, waiting for transfers between devices, shards(): lax.ppermute(after(add(a_sum, a_far).astype(bf16), a_side, b_side), 'gz',...  7.03 us
  transfers between devices with their start and end apart: 24, of which 8 were waited for; matrix products, arithmetic and copies ran while one was open for 13% of the time, Pallas kernels for 42%

profile of v4, /device:TPU:0, one launch (start us, length us, event | category | flops | bytes accessed | tf_op | source)
XLA Modules:
  0.0 187.8 jit_solution(3596813534276951297)
XLA Ops:
  0.6 0.1 collective-permute-start
  0.7 1.7 slice_bitcast_fusion.1
  2.4 1.6 collective-permute-start.1
  4.0 2.1 %slice.23 = bf16[384,1152]{1,0:T(8,128)(2,1)} slice(bf16[512,1152]{1,0:T(8,128)(2,1)} %own.3), slice={[128:512], [0:1152]} | slice | bytes 1769472 | tf_op jit(solution)/shard_map/slice | solution.py:324
  6.2 0.6 stack.101.table
  6.7 0.0 collective-permute-done.partner
  6.7 6.0 %near_terms.2.refs_2_ = bf16[2,384,1152]{2,1,0:T(8,128)(2,1)} custom-call(s32[18]{0:T(128)} %stack.101.table, bf16[2048,3072]{1,0:T(8,128)(2,1)} %pre.3, bf16[2048,3072]{1,0:T(8,128)(2,1)} %pre.3, bf16[512,1152]{1,0:T(8,128)(2,1)} %own.3, bf16[512,1152]{1,0:T(8,128)(2,1)} %collective-permute-done.partner), custom_call_target="tpu_custom_call" | custom-call | flops 28311552 | bytes 89088 | tf_op jit(solution)/shard_map/near_terms/pallas_call | solution.py:239
  12.7 0.0 collective-permute-done.1
  12.8 0.2 collective-permute-start.2
  13.0 0.6 collective-permute-start.3
  13.5 1.0 slice_bitcast_fusion
  14.5 0.0 collective-permute-done.2
  14.5 2.4 %pad_maximum_fusion.1 = bf16[4,128,1152]{2,1,0:T(8,128)(2,1)} fusion(bf16[1,128,1152]{2,1,0:T(8,128)(2,1)S(1)} %bitcast.32, bf16[1,128,1152]{2,1,0:T(8,128)(2,1)} %bitcast.19, bf16[1,128,1152]{2,1,0:T(8,128)(2,1)S(1)} %slice_bitcast_fusion, bf16[1,128,1152]{2,1,0:T(8,128)(2,1)} %get-tuple-element.92), kind=kLoop, calls=%fused_computation.9 | loop fusion | flops 1769472 | bytes 2359296 | tf_op jit(solution)/shard_map/stack | solution.py:332
  16.9 9.9 %first_parts.1 = (bf16[128,3072]{1,0:T(8,128)(2,1)}, bf16[128,3072]{1,0:T(8,128)(2,1)}, bf16[128,3072]{1,0:T(8,128)(2,1)}, bf16[128,3072]{1,0:T(8,128)(2,1)}) custom-call(s32[18]{0:T(128)} %stack.101.table, bf16[512,1152]{1,0:T(8,128)(2,1)} %bitcast.30, bf16[3072,1152]{1,0:T(8,128)(2,1)} %weights.3), custom_call_target="tpu_custom_call" | custom-call | flops 56623104 | bytes 178176 | tf_op jit(solution)/shard_map/first_parts/pallas_call | solution.py:94
  26.8 1.9 %collective-permute-start.8 = (bf16[128,3072]{1,0:T(8,128)(2,1)}, bf16[128,3072]{1,0:T(8,128)(2,1)}, u32[]{:S(2)}, u32[]{:S(2)}) collective-permute-start(bf16[128,3072]{1,0:T(8,128)(2,1)} %get-tuple-element.58), channel_id=1, source_target_pairs={{0,1},{1,2},{2,3},{3,0},{4,5},{5,6},{6,7},{7,4},{8,9},{9,10},{10,1... | collective-permute-start | bytes 2359304 | tf_op jit(solution)/shard_map/ppermute | solution.py:336
  28.7 2.2 %collective-permute-start.9 = (bf16[128,3072]{1,0:T(8,128)(2,1)}, bf16[128,3072]{1,0:T(8,128)(2,1)}, u32[]{:S(2)}, u32[]{:S(2)}) collective-permute-start(bf16[128,3072]{1,0:T(8,128)(2,1)} %get-tuple-element.59), channel_id=1, source_target_pairs={{0,3},{1,0},{2,1},{3,2},{4,7},{5,4},{6,5},{7,6},{8,11},{9,8},{10,9... | collective-permute-start | bytes 2359304 | tf_op jit(solution)/shard_map/ppermute | solution.py:337
  30.9 1.8 collective-permute-start.10
  32.7 6.1 %near_terms.3.refs_2_ = bf16[2,384,1152]{2,1,0:T(8,128)(2,1)} custom-call(s32[18]{0:T(128)} %stack.101.table, bf16[2048,3072]{1,0:T(8,128)(2,1)} %pre.3, bf16[2048,3072]{1,0:T(8,128)(2,1)} %pre.3, bf16[512,1152]{1,0:T(8,128)(2,1)} %own.3, bf16[512,1152]{1,0:T(8,128)(2,1)} %collective-permute-done.partner), custom_call_target="tpu_custom_call" | custom-call | flops 28311552 | bytes 89088 | tf_op jit(solution)/shard_map/near_terms/pallas_call | solution.py:239
  38.8 1.0 constant_dynamic-update-slice_fusion.4
  39.8 0.0 collective-permute-done.3
  39.8 0.1 fusion
  39.8 0.1 collective-permute-start.4
  39.9 1.1 pad_maximum_fusion.2
  41.0 0.0 copy-start
  41.0 0.6 collective-permute-start.7
  41.6 0.0 collective-permute-done.4
  41.6 0.1 collective-permute-start.5
  41.7 1.4 collective-permute-done.5
  43.1 0.3 collective-permute-start.6
  43.4 1.1 collective-permute-done.6
  44.6 0.0 collective-permute-done.7
  44.6 3.6 %pad_maximum_fusion.refs_3_.rows.refs_4_ = bf16[4,512,1152]{2,1,0:T(8,128)(2,1)} fusion(bf16[1,512,1152]{2,1,0:T(8,128)(2,1)S(1)} %bitcast.31, bf16[1,512,1152]{2,1,0:T(8,128)(2,1)S(1)} %bitcast.29, bf16[1,512,1152]{2,1,0:T(8,128)(2,1)} %bitcast.23, bf16[1,512,1152]{2,1,0:T(8,128)(2,1)S(1)} %bitcast.28), kind=kLoop, calls=%fused_computation | loop fusion | flops 7077888 | bytes 9437184 | tf_op jit(solution)/shard_map/stack | solution.py:348
  48.2 6.9 %terms.4 = (bf16[384,1152]{1,0:T(8,128)(2,1)}, bf16[384,1152]{1,0:T(8,128)(2,1)}) custom-call(s32[18]{0:T(128)} %stack.101.table, bf16[2048,3072]{1,0:T(8,128)(2,1)} %pre.3, bf16[2048,3072]{1,0:T(8,128)(2,1)} %pre.3, bf16[2,384,1152]{2,1,0:T(8,128)(2,1)} %near_terms.2.refs_2_, bf16[4,512,1152]{2,1,0:T(8,128)(2,1)} %pad_maximum_fusion.refs_3_.rows.refs_4_), custom_call_target="tpu_custom_call" | custom-call | flops 28311552 | bytes 61440 | tf_op jit(solution)/shard_map/terms/pallas_call | solution.py:290
  55.1 1.6 collective-permute-start.18
  56.7 1.7 collective-permute-start.17
  58.4 19.7 %tail_parts.1 = (bf16[384,1536]{1,0:T(8,128)(2,1)}, bf16[384,1536]{1,0:T(8,128)(2,1)}, bf16[384,1536]{1,0:T(8,128)(2,1)}, bf16[384,1536]{1,0:T(8,128)(2,1)}, bf1...) custom-call(s32[18]{0:T(128)} %stack.101.table, ...), custom_call_target="tpu_custom_call" | custom-call | flops 169869312 | bytes 331776 | tf_op jit(solution)/shard_map/tail_parts/pallas_call | solution.py:147
  78.1 0.0 collective-permute-done.8.one
  78.1 1.3 collective-permute-start.12
  79.4 2.2 %collective-permute-start.11 = (bf16[384,1536]{1,0:T(8,128)(2,1)}, bf16[384,1536]{1,0:T(8,128)(2,1)}, u32[]{:S(2)}, u32[]{:S(2)}) collective-permute-start(bf16[384,1536]{1,0:T(8,128)(2,1)} %get-tuple-element.71), channel_id=1, source_target_pairs={{0,3},{1,0},{2,1},{3,2},{4,7},{5,4},{6,5},{7,6},{8,11},{9,8},{10,9... | collective-permute-start | bytes 3538952 | tf_op jit(solution)/shard_map/ppermute | solution.py:364
  81.6 6.9 %terms.5 = (bf16[384,1152]{1,0:T(8,128)(2,1)}, bf16[384,1152]{1,0:T(8,128)(2,1)}) custom-call(s32[18]{0:T(128)} %stack.101.table, bf16[2048,3072]{1,0:T(8,128)(2,1)} %pre.3, bf16[2048,3072]{1,0:T(8,128)(2,1)} %pre.3, bf16[2,384,1152]{2,1,0:T(8,128)(2,1)} %near_terms.3.refs_2_, bf16[4,512,1152]{2,1,0:T(8,128)(2,1)} %pad_maximum_fusion.refs_3_.rows.refs_4_), custom_call_target="tpu_custom_call" | custom-call | flops 28311552 | bytes 61440 | tf_op jit(solution)/shard_map/terms/pallas_call | solution.py:290
  88.5 9.7 %terms.6 = (bf16[384,1152]{1,0:T(8,128)(2,1)}, bf16[384,1152]{1,0:T(8,128)(2,1)}) custom-call(s32[18]{0:T(128)} %stack.101.table, bf16[2048,3072]{1,0:T(8,128)(2,1)} %pre.3, bf16[2048,3072]{1,0:T(8,128)(2,1)} %pre.3, bf16[2048,3072]{1,0:T(8,128)(2,1)} %pre.3, bf16[2048,3072]{1,0:T(8,128)(2,1)} %pre.3, bf16[4,512,1152]{2,1,0:T(8,128)(2,1)} %pad_maximum_fusion.refs_3_.rows.refs_4_), custom_call_target="tpu_custom_call" | custom-call | flops 56623104 | bytes 122880 | tf_op jit(solution)/shard_map/terms/pallas_call | solution.py:290
  98.3 0.9 copy-done.6
  99.2 0.4 collective-permute-start.19
  99.5 2.9 %collective-permute-start.20 = (bf16[384,1152]{1,0:T(8,128)(2,1)}, bf16[384,1152]{1,0:T(8,128)(2,1)}, u32[]{:S(2)}, u32[]{:S(2)}) collective-permute-start(bf16[384,1152]{1,0:T(8,128)(2,1)} %get-tuple-element.85), channel_id=1, source_target_pairs={{0,48},{16,0},{32,16},{48,32},{64,112},{80,64},{96,80},{112,96},{1... | collective-permute-start | bytes 2654216 | tf_op jit(solution)/shard_map/ppermute | solution.py:371
  102.4 9.7 %terms.7 = (bf16[384,1152]{1,0:T(8,128)(2,1)}, bf16[384,1152]{1,0:T(8,128)(2,1)}) custom-call(s32[18]{0:T(128)} %stack.101.table, bf16[2048,3072]{1,0:T(8,128)(2,1)} %pre.3, bf16[2048,3072]{1,0:T(8,128)(2,1)} %pre.3, bf16[2048,3072]{1,0:T(8,128)(2,1)} %pre.3, bf16[2048,3072]{1,0:T(8,128)(2,1)} %pre.3, bf16[4,512,1152]{2,1,0:T(8,128)(2,1)} %pad_maximum_fusion.refs_3_.rows.refs_4_), custom_call_target="tpu_custom_call" | custom-call | flops 7247757312 | bytes 15728640 | tf_op jit(solution)/shard_map/terms/pallas_call | solution.py:290
  112.1 0.1 collective-permute-start.13
  112.2 3.2 %collective-permute-start.14 = (bf16[384,1536]{1,0:T(8,128)(2,1)}, bf16[384,1536]{1,0:T(8,128)(2,1)}, u32[]{:S(2)}, u32[]{:S(2)}) collective-permute-start(bf16[384,1536]{1,0:T(8,128)(2,1)} %get-tuple-element.77), channel_id=1, source_target_pairs={{0,3},{1,0},{2,1},{3,2},{4,7},{5,4},{6,5},{7,6},{8,11},{9,8},{10,9... | collective-permute-start | bytes 3538952 | tf_op jit(solution)/shard_map/ppermute | solution.py:379
  115.4 3.7 %add_convert_fusion.3 = (bf16[384,1152]{1,0:T(8,128)(2,1)}, bf16[384,1152]{1,0:T(8,128)(2,1)}) fusion(bf16[384,1152]{1,0:T(8,128)(2,1)} %copy-done.6, bf16[384,1152]{1,0:T(8,128)(2,1)} %get-tuple-element.89, bf16[384,1152]{1,0:T(8,128)(2,1)} %collective-permute-done.17, bf16[384,1152]{1,0:T(8,128)(2,1)} %get-tuple-element.64), kind=kLoop, calls=%fused_computation.6 | loop fusion | flops 3538944 | bytes 5308416 | tf_op jit(solution)/shard_map/convert_element_type | solution.py:381
  119.1 2.3 %collective-permute-done.19 = bf16[384,1152]{1,0:T(8,128)(2,1)S(1)} collective-permute-done((bf16[384,1152]{1,0:T(8,128)(2,1)}, bf16[384,1152]{1,0:T(8,128)(2,1)S(1)}, u32[]{:S(2)}, u32[]{:S(2)}) %collective-permute-start.19) | collective-permute-done | bytes 884768 | tf_op jit(solution)/shard_map/ppermute | solution.py:370
  121.4 0.5 collective-permute-start.22
  121.9 2.7 %collective-permute-start.21 = (bf16[384,1152]{1,0:T(8,128)(2,1)}, bf16[384,1152]{1,0:T(8,128)(2,1)}, u32[]{:S(2)}, u32[]{:S(2)}) collective-permute-start(bf16[384,1152]{1,0:T(8,128)(2,1)} %get-tuple-element.86), channel_id=1, source_target_pairs={{0,48},{16,0},{32,16},{48,32},{64,112},{80,64},{96,80},{112,96},{1... | collective-permute-start | bytes 2654216 | tf_op jit(solution)/shard_map/ppermute | solution.py:380
  124.7 15.6 %collective-permute-done.13.side_a = bf16[384,1536]{1,0:T(8,128)(2,1)} collective-permute-done((bf16[384,1536]{1,0:T(8,128)(2,1)}, bf16[384,1536]{1,0:T(8,128)(2,1)}, u32[]{:S(2)}, u32[]{:S(2)}) %collective-permute-start.13) | collective-permute-done | bytes 1179680 | tf_op jit(solution)/shard_map/ppermute | solution.py:378
  140.3 2.6 %collective-permute-done.22 = bf16[384,1152]{1,0:T(8,128)(2,1)} collective-permute-done((bf16[384,1152]{1,0:T(8,128)(2,1)}, bf16[384,1152]{1,0:T(8,128)(2,1)}, u32[]{:S(2)}, u32[]{:S(2)}) %collective-permute-start.22) | collective-permute-done | bytes 884768 | tf_op jit(solution)/shard_map/ppermute | solution.py:381
  143.0 3.4 %select_convert_fusion = bf16[384,1152]{1,0:T(8,128)(2,1)} fusion(bf16[384,1152]{1,0:T(8,128)(2,1)} %collective-permute-done.21, bf16[384,1152]{1,0:T(8,128)(2,1)S(1)} %collective-permute-done.19, bf16[384,1152]{1,0:T(8,128)(2,1)S(1)} %copy-done.1, bf16[384,1152]{1,0:T(8,128)(2,1)} %collective-permute-done.22, bf16[384,1152]{1,0:T(8,128)(2,1)} %collective-permute-done.20, ...), kind=kLoop, calls=%fused_computation.4 | loop fusion | flops 5308416 | bytes 6193153 | tf_op jit(solution)/shard_map/convert_element_type | solution.py:393
  146.4 3.0 %collective-permute-start.23 = (bf16[384,1152]{1,0:T(8,128)(2,1)}, bf16[384,1152]{1,0:T(8,128)(2,1)}, u32[]{:S(2)}, u32[]{:S(2)}) collective-permute-start(bf16[384,1152]{1,0:T(8,128)(2,1)} %select_convert_fusion), channel_id=1, source_target_pairs={{0,64},{16,80},{32,96},{48,112},{64,0},{80,16},{96,32},{112,48},{1... | collective-permute-start | bytes 2654216 | tf_op jit(solution)/shard_map/ppermute | solution.py:394
  149.4 3.7 %add_convert_fusion = (bf16[384,1536]{1,0:T(8,128)(2,1)}, bf16[384,1536]{1,0:T(8,128)(2,1)}) fusion(bf16[384,1536]{1,0:T(8,128)(2,1)} %collective-permute-done.12, bf16[384,1536]{1,0:T(8,128)(2,1)S(1)} %copy-done.5, bf16[384,1536]{1,0:T(8,128)(2,1)} %collective-permute-done.11, bf16[384,1536]{1,0:T(8,128)(2,1)S(1)} %copy-done.4), kind=kLoop, calls=%fused_computation.1 | loop fusion | flops 4718592 | bytes 7077888 | tf_op jit(solution)/shard_map/convert_element_type | solution.py:387
  153.1 0.5 collective-permute-start.15
  153.5 1.6 collective-permute-start.16
  155.1 4.0 %head_last.1.held = bf16[512,3072]{1,0:T(8,128)(2,1)} custom-call(s32[18]{0:T(128)} %stack.101.table, bf16[128,3072]{1,0:T(8,128)(2,1)} %get-tuple-element.49.own, bf16[128,3072]{1,0:T(8,128)(2,1)} %collective-permute-done.8.one, bf16[128,3072]{1,0:T(8,128)(2,1)} %collective-permute-done.9.two, bf16[128,3072]{1,0:T(8,128)(2,1)} %collective-permute-done.10.three, ...), custom_call_target="tpu_custom_call" | custom-call | flops 8053063680 | bytes 2415919104 | tf_op jit(solution)/shard_map/head_last/pallas_call | solution.py:176
  159.1 8.2 %collective-permute-done.23 = bf16[384,1152]{1,0:T(8,128)(2,1)} collective-permute-done((bf16[384,1152]{1,0:T(8,128)(2,1)}, bf16[384,1152]{1,0:T(8,128)(2,1)}, u32[]{:S(2)}, u32[]{:S(2)}) %collective-permute-start.23) | collective-permute-done | bytes 884768 | tf_op jit(solution)/shard_map/ppermute | solution.py:394
  167.3 4.2 %add_convert_fusion.2 = bf16[384,1152]{1,0:T(8,128)(2,1)} fusion(bf16[384,1152]{1,0:T(8,128)(2,1)} %collective-permute-done.23, bf16[384,1152]{1,0:T(8,128)(2,1)} %collective-permute-done.21, bf16[384,1152]{1,0:T(8,128)(2,1)S(1)} %collective-permute-done.19, bf16[384,1152]{1,0:T(8,128)(2,1)} %get-tuple-element.81, ...), kind=kLoop, calls=%fused_computation.3 | loop fusion | flops 6193152 | bytes 7077889 | tf_op jit(solution)/shard_map/convert_element_type | solution.py:397
  171.5 7.0 %collective-permute-done.15.sum_a = bf16[384,1536]{1,0:T(8,128)(2,1)} collective-permute-done((bf16[384,1536]{1,0:T(8,128)(2,1)}, bf16[384,1536]{1,0:T(8,128)(2,1)}, u32[]{:S(2)}, u32[]{:S(2)}) %collective-permute-start.15) | collective-permute-done | bytes 1179680 | tf_op jit(solution)/shard_map/ppermute | solution.py:386
  178.5 1.6 collective-permute-done.16.sum_b
  180.1 7.7 %tail_last.1 = bf16[512,3072]{1,0:T(8,128)(2,1)} custom-call(s32[18]{0:T(128)} %stack.101.table, bf16[384,3072]{1,0:T(8,128)(2,1)} %get-tuple-element.56.own, bf16[384,1536]{1,0:T(8,128)(2,1)} %collective-permute-done.13.side_a, bf16[384,1536]{1,0:T(8,128)(2,1)} %collective-permute-done.15.sum_a, ...), custom_call_target="tpu_custom_call", output_to_operand_aliasing={{}: (7, {})} | custom-call | flops 47185920 | bytes 11796480 | tf_op jit(solution)/shard_map/tail_last/pallas_call | solution.py:207
  (25 shorter events, 0.1 us)
Async XLA Ops:
  0.6 6.1 %collective-permute-start = (bf16[512,1152]{1,0:T(8,128)(2,1)}, bf16[512,1152]{1,0:T(8,128)(2,1)}, u32[]{:S(2)}, u32[]{:S(2)}) collective-permute-start(bf16[512,1152]{1,0:T(8,128)(2,1)} %own.3), channel_id=1, source_target_pairs={{0,4},{4,0},{8,12},{12,8},{1,5},{5,1},{9,13},{13,9},{2,6},{6,2},{1... | collective-permute-start | bytes 3538952 | tf_op jit(solution)/shard_map/ppermute | solution.py:326
  2.4 10.3 %collective-permute-start.1 = (bf16[128,1152]{1,0:T(8,128)(2,1)S(1)}, bf16[128,1152]{1,0:T(8,128)(2,1)}, u32[]{:S(2)}, u32[]{:S(2)}) collective-permute-start(bf16[128,1152]{1,0:T(8,128)(2,1)S(1)} %get-tuple-element.93), channel_id=1, source_target_pairs={{0,8},{4,12},{8,0},{12,4},{1,9},{5,13},{9,1},{13,5},{2,10},{6,14},... | collective-permute-start | bytes 884744 | tf_op jit(solution)/shard_map/ppermute | solution.py:325
  12.8 1.8 collective-permute-start.2
  13.0 26.8 %collective-permute-start.3 = (bf16[384,1152]{1,0:T(8,128)(2,1)}, bf16[384,1152]{1,0:T(8,128)(2,1)S(1)}, u32[]{:S(2)}, u32[]{:S(2)}) collective-permute-start(bf16[384,1152]{1,0:T(8,128)(2,1)} %slice.23), channel_id=1, source_target_pairs={{0,8},{4,12},{8,0},{12,4},{1,9},{5,13},{9,1},{13,5},{2,10},{6,14},... | collective-permute-start | bytes 2654216 | tf_op jit(solution)/shard_map/ppermute | solution.py:330
  14.5 2.4 %copy-start.3 = (bf16[128,1152]{1,0:T(8,128)(2,1)}, bf16[128,1152]{1,0:T(8,128)(2,1)S(1)}, u32[]{:S(2)}) copy-start(bf16[128,1152]{1,0:T(8,128)(2,1)S(1)} %collective-permute-done.2) | copy-start | bytes 884740
  26.8 51.3 %collective-permute-start.8 = (bf16[128,3072]{1,0:T(8,128)(2,1)}, bf16[128,3072]{1,0:T(8,128)(2,1)}, u32[]{:S(2)}, u32[]{:S(2)}) collective-permute-start(bf16[128,3072]{1,0:T(8,128)(2,1)} %get-tuple-element.58), channel_id=1, source_target_pairs={{0,1},{1,2},{2,3},{3,0},{4,5},{5,6},{6,7},{7,4},{8,9},{9,10},{10,1... | collective-permute-start | bytes 2359304 | tf_op jit(solution)/shard_map/ppermute | solution.py:336
  28.7 49.4 %collective-permute-start.9 = (bf16[128,3072]{1,0:T(8,128)(2,1)}, bf16[128,3072]{1,0:T(8,128)(2,1)}, u32[]{:S(2)}, u32[]{:S(2)}) collective-permute-start(bf16[128,3072]{1,0:T(8,128)(2,1)} %get-tuple-element.59), channel_id=1, source_target_pairs={{0,3},{1,0},{2,1},{3,2},{4,7},{5,4},{6,5},{7,6},{8,11},{9,8},{10,9... | collective-permute-start | bytes 2359304 | tf_op jit(solution)/shard_map/ppermute | solution.py:337
  30.9 47.2 %collective-permute-start.10 = (bf16[128,3072]{1,0:T(8,128)(2,1)}, bf16[128,3072]{1,0:T(8,128)(2,1)}, u32[]{:S(2)}, u32[]{:S(2)}) collective-permute-start(bf16[128,3072]{1,0:T(8,128)(2,1)} %get-tuple-element.60), channel_id=1, source_target_pairs={{0,2},{1,3},{2,0},{3,1},{4,6},{5,7},{6,4},{7,5},{8,10},{9,11},{10,... | collective-permute-start | bytes 2359304 | tf_op jit(solution)/shard_map/ppermute | solution.py:338
  39.8 1.7 collective-permute-start.4
  41.0 3.6 %copy-start = (bf16[512,1152]{1,0:T(8,128)(2,1)S(1)}, bf16[512,1152]{1,0:T(8,128)(2,1)}, u32[]{:S(2)}) copy-start(bf16[512,1152]{1,0:T(8,128)(2,1)} %own.3) | copy-start | bytes 3538948
  41.0 3.6 %collective-permute-start.7 = (bf16[96,1152]{1,0:T(8,128)(2,1)S(1)}, bf16[96,1152]{1,0:T(8,128)(2,1)S(1)}, u32[]{:S(2)}, u32[]{:S(2)}) collective-permute-start(bf16[96,1152]{1,0:T(8,128)(2,1)S(1)} %get-tuple-element.94), channel_id=1, source_target_pairs={{0,4},{4,0},{8,12},{12,8},{1,5},{5,1},{9,13},{13,9},{2,6},{6,2},{1... | collective-permute-start | bytes 663560 | tf_op jit(solution)/shard_map/ppermute | solution.py:345
  41.6 1.5 collective-permute-start.5
  43.1 1.5 collective-permute-start.6
  55.1 43.1 %collective-permute-start.18 = (bf16[384,1152]{1,0:T(8,128)(2,1)}, bf16[384,1152]{1,0:T(8,128)(2,1)S(1)}, u32[]{:S(2)}, u32[]{:S(2)}) collective-permute-start(bf16[384,1152]{1,0:T(8,128)(2,1)} %get-tuple-element.82), channel_id=1, source_target_pairs={{0,16},{16,32},{32,48},{48,0},{64,80},{80,96},{96,112},{112,64},{1... | collective-permute-start | bytes 2654216 | tf_op jit(solution)/shard_map/ppermute | solution.py:360
  56.7 41.6 %collective-permute-start.17 = (bf16[384,1152]{1,0:T(8,128)(2,1)}, bf16[384,1152]{1,0:T(8,128)(2,1)}, u32[]{:S(2)}, u32[]{:S(2)}) collective-permute-start(bf16[384,1152]{1,0:T(8,128)(2,1)} %get-tuple-element.54), channel_id=1, source_target_pairs={{0,48},{16,0},{32,16},{48,32},{64,112},{80,64},{96,80},{112,96},{1... | collective-permute-start | bytes 2654216 | tf_op jit(solution)/shard_map/ppermute | solution.py:359
  78.1 34.0 %collective-permute-start.12 = (bf16[384,1536]{1,0:T(8,128)(2,1)}, bf16[384,1536]{1,0:T(8,128)(2,1)}, u32[]{:S(2)}, u32[]{:S(2)}) collective-permute-start(bf16[384,1536]{1,0:T(8,128)(2,1)} %get-tuple-element.73), channel_id=1, source_target_pairs={{0,1},{1,2},{2,3},{3,0},{4,5},{5,6},{6,7},{7,4},{8,9},{9,10},{10,1... | collective-permute-start | bytes 3538952 | tf_op jit(solution)/shard_map/ppermute | solution.py:365
  79.4 32.7 %collective-permute-start.11 = (bf16[384,1536]{1,0:T(8,128)(2,1)}, bf16[384,1536]{1,0:T(8,128)(2,1)}, u32[]{:S(2)}, u32[]{:S(2)}) collective-permute-start(bf16[384,1536]{1,0:T(8,128)(2,1)} %get-tuple-element.71), channel_id=1, source_target_pairs={{0,3},{1,0},{2,1},{3,2},{4,7},{5,4},{6,5},{7,6},{8,11},{9,8},{10,9... | collective-permute-start | bytes 3538952 | tf_op jit(solution)/shard_map/ppermute | solution.py:364
  98.3 0.9 copy-start.6
  99.2 22.2 %collective-permute-start.19 = (bf16[384,1152]{1,0:T(8,128)(2,1)}, bf16[384,1152]{1,0:T(8,128)(2,1)S(1)}, u32[]{:S(2)}, u32[]{:S(2)}) collective-permute-start(bf16[384,1152]{1,0:T(8,128)(2,1)} %get-tuple-element.83), channel_id=1, source_target_pairs={{0,16},{16,32},{32,48},{48,0},{64,80},{80,96},{96,112},{112,64},{1... | collective-permute-start | bytes 2654216 | tf_op jit(solution)/shard_map/ppermute | solution.py:370
  99.5 21.9 %collective-permute-start.20 = (bf16[384,1152]{1,0:T(8,128)(2,1)}, bf16[384,1152]{1,0:T(8,128)(2,1)}, u32[]{:S(2)}, u32[]{:S(2)}) collective-permute-start(bf16[384,1152]{1,0:T(8,128)(2,1)} %get-tuple-element.85), channel_id=1, source_target_pairs={{0,48},{16,0},{32,16},{48,32},{64,112},{80,64},{96,80},{112,96},{1... | collective-permute-start | bytes 2654216 | tf_op jit(solution)/shard_map/ppermute | solution.py:371
  112.1 28.2 %collective-permute-start.13 = (bf16[384,1536]{1,0:T(8,128)(2,1)}, bf16[384,1536]{1,0:T(8,128)(2,1)}, u32[]{:S(2)}, u32[]{:S(2)}) collective-permute-start(bf16[384,1536]{1,0:T(8,128)(2,1)} %get-tuple-element.74), channel_id=1, source_target_pairs={{0,1},{1,2},{2,3},{3,0},{4,5},{5,6},{6,7},{7,4},{8,9},{9,10},{10,1... | collective-permute-start | bytes 3538952 | tf_op jit(solution)/shard_map/ppermute | solution.py:378
  112.2 28.1 %collective-permute-start.14 = (bf16[384,1536]{1,0:T(8,128)(2,1)}, bf16[384,1536]{1,0:T(8,128)(2,1)}, u32[]{:S(2)}, u32[]{:S(2)}) collective-permute-start(bf16[384,1536]{1,0:T(8,128)(2,1)} %get-tuple-element.77), channel_id=1, source_target_pairs={{0,3},{1,0},{2,1},{3,2},{4,7},{5,4},{6,5},{7,6},{8,11},{9,8},{10,9... | collective-permute-start | bytes 3538952 | tf_op jit(solution)/shard_map/ppermute | solution.py:379
  115.4 27.5 %copy-start.1 = (bf16[384,1152]{1,0:T(8,128)(2,1)S(1)}, bf16[384,1152]{1,0:T(8,128)(2,1)}, u32[]{:S(2)}) copy-start(bf16[384,1152]{1,0:T(8,128)(2,1)} %get-tuple-element.81) | copy-start | bytes 2654212
  115.4 27.5 %copy-start.2 = (bf16[384,1152]{1,0:T(8,128)(2,1)S(1)}, bf16[384,1152]{1,0:T(8,128)(2,1)}, u32[]{:S(2)}) copy-start(bf16[384,1152]{1,0:T(8,128)(2,1)} %get-tuple-element.88) | copy-start | bytes 2654212
  121.4 21.5 %collective-permute-start.22 = (bf16[384,1152]{1,0:T(8,128)(2,1)}, bf16[384,1152]{1,0:T(8,128)(2,1)}, u32[]{:S(2)}, u32[]{:S(2)}) collective-permute-start(bf16[384,1152]{1,0:T(8,128)(2,1)} %get-tuple-element.90), channel_id=1, source_target_pairs={{0,16},{16,32},{32,48},{48,0},{64,80},{80,96},{96,112},{112,64},{1... | collective-permute-start | bytes 2654216 | tf_op jit(solution)/shard_map/ppermute | solution.py:381
  121.9 21.0 %collective-permute-start.21 = (bf16[384,1152]{1,0:T(8,128)(2,1)}, bf16[384,1152]{1,0:T(8,128)(2,1)}, u32[]{:S(2)}, u32[]{:S(2)}) collective-permute-start(bf16[384,1152]{1,0:T(8,128)(2,1)} %get-tuple-element.86), channel_id=1, source_target_pairs={{0,48},{16,0},{32,16},{48,32},{64,112},{80,64},{96,80},{112,96},{1... | collective-permute-start | bytes 2654216 | tf_op jit(solution)/shard_map/ppermute | solution.py:380
  142.9 6.4 %copy-start.4 = (bf16[384,1536]{1,0:T(8,128)(2,1)S(1)}, bf16[384,1536]{1,0:T(8,128)(2,1)}, u32[]{:S(2)}) copy-start(bf16[384,1536]{1,0:T(8,128)(2,1)} %get-tuple-element.75) | copy-start | bytes 3538948
  143.0 6.4 %copy-start.5 = (bf16[384,1536]{1,0:T(8,128)(2,1)S(1)}, bf16[384,1536]{1,0:T(8,128)(2,1)}, u32[]{:S(2)}) copy-start(bf16[384,1536]{1,0:T(8,128)(2,1)} %get-tuple-element.79) | copy-start | bytes 3538948
  146.4 20.9 %collective-permute-start.23 = (bf16[384,1152]{1,0:T(8,128)(2,1)}, bf16[384,1152]{1,0:T(8,128)(2,1)}, u32[]{:S(2)}, u32[]{:S(2)}) collective-permute-start(bf16[384,1152]{1,0:T(8,128)(2,1)} %select_convert_fusion), channel_id=1, source_target_pairs={{0,64},{16,80},{32,96},{48,112},{64,0},{80,16},{96,32},{112,48},{1... | collective-permute-start | bytes 2654216 | tf_op jit(solution)/shard_map/ppermute | solution.py:394
  153.1 25.4 %collective-permute-start.15 = (bf16[384,1536]{1,0:T(8,128)(2,1)}, bf16[384,1536]{1,0:T(8,128)(2,1)}, u32[]{:S(2)}, u32[]{:S(2)}) collective-permute-start(bf16[384,1536]{1,0:T(8,128)(2,1)} %get-tuple-element.78), channel_id=1, source_target_pairs={{0,3},{1,0},{2,1},{3,2},{4,7},{5,4},{6,5},{7,6},{8,11},{9,8},{10,9... | collective-permute-start | bytes 3538952 | tf_op jit(solution)/shard_map/ppermute | solution.py:386
  153.5 26.5 %collective-permute-start.16 = (bf16[384,1536]{1,0:T(8,128)(2,1)}, bf16[384,1536]{1,0:T(8,128)(2,1)}, u32[]{:S(2)}, u32[]{:S(2)}) collective-permute-start(bf16[384,1536]{1,0:T(8,128)(2,1)} %get-tuple-element.80), channel_id=1, source_target_pairs={{0,1},{1,2},{2,3},{3,0},{4,5},{5,6},{6,7},{7,4},{8,9},{9,10},{10,1... | collective-permute-start | bytes 3538952 | tf_op jit(solution)/shard_map/ppermute | solution.py:387

commit v5 on v4

--- a/solution.py
+++ b/solution.py
@@ -12,9 +12,10 @@
 slope_scale = 1.0 / math.sqrt(2.0 * math.pi)
 bf16 = jnp.bfloat16
 f32 = jnp.float32
-HEAD = 128
+HEAD = 192
 TILE = 512
-SHORT, SIDE, LAST, LONG = 1 / 64, 1 / 64, 2, 512
+PIECE = 80
+SHORT, MID, LAST, LONG = 1 / 64, 1/64, 1/64, 1/64
 VMEM = 63 * 1024 * 1024
 
 
@@ -165,7 +166,7 @@
 def head_last_body(table, own, one, two, three, pre, out):
     total = own[...].astype(f32) + one[...].astype(f32)
     total += two[...].astype(f32) + three[...].astype(f32)
-    out[...] = (total * unit_slope(pre[...].astype(f32))).astype(bf16)
+    out[...] = (total * unit_slope(pre[: own.shape[0]].astype(f32))).astype(bf16)
 
 
 def head_last(own, arrived, preact, table):
@@ -179,7 +180,7 @@
         (2,),
         1,
         [block] * 4
-        + [pl.BlockSpec((count, width), lambda t, p: (p[GZ] * (share // count), t))],
+        + [pl.BlockSpec((share, width), lambda t, p: (p[GZ], t))],
         block,
         jax.ShapeDtypeStruct((share, hidden), bf16),
         count * hidden * 40,
@@ -201,7 +202,7 @@
 def tail_last(own, side_a, sum_a, side_b, sum_b, preact, table, held):
     count, hidden = own.shape
     share = preact.shape[0] // 4
-    step = 128
+    step = 64
     start, blocks = HEAD // step, share // step
     half = pl.BlockSpec((step, hidden // 2), lambda t, p: (t, 0))
     return call(
@@ -342,8 +343,8 @@
     table = after(table, near_side)
     across_tail = after(across_tail, table)
     corner_tail = [
-        lax.ppermute(across_tail[start : start + 96], "gy", other_core)
-        for start in range(0, across_tail.shape[0], 96)
+        lax.ppermute(across_tail[start : start + PIECE], "gy", other_core)
+        for start in range(0, across_tail.shape[0], PIECE)
     ]
     rows = jnp.stack(
         (
@@ -365,33 +366,41 @@
     b_far = lax.ppermute(after(b_far, *arrived), "gz", z_up)
     table = after(table, *arrived)
 
-    c_side, d_side = terms(preact, rows, table, C_SIDE, near_side, cost=SIDE)
+    c_side, d_side = terms(preact, rows, table, C_SIDE, near_side)
     table = after(table, c_side)
     c_side = lax.ppermute(after(c_side, c_far, d_far), "gx", y_up)
     d_side = lax.ppermute(after(d_side, c_far, d_far), "gx", y_down)
 
-    c_sum, d_sum = terms(preact, rows, table, C_SUM)
+    table = after(table, c_far, d_far)
+    c_sum, d_sum = terms(preact, rows, table, C_SUM, cost=MID)
     table = after(table, c_sum)
+    a_side = lax.ppermute(after(a_side, table, a_far, b_far), "gz", z_up)
+    b_side = lax.ppermute(after(b_side, table, a_far, b_far), "gz", z_down)
+    a_sum = add(a_sum, after(a_far, table)).astype(bf16)
+    b_sum = add(b_sum, after(b_far, table)).astype(bf16)
+    table = after(table, a_sum, b_sum)
+
     c_own, d_own = terms(preact, rows, table, C_OWN, cost=LAST)
     table = after(table, c_own)
 
-    a_side = lax.ppermute(after(a_side, table, a_far, b_far), "gz", z_up)
-    b_side = lax.ppermute(after(b_side, table, a_far, b_far), "gz", z_down)
-    c_sum = lax.ppermute(after(add(c_sum, c_far).astype(bf16), table, c_side, d_side, a_far, b_far), "gx", y_down)
-    d_sum = lax.ppermute(after(add(d_sum, d_far).astype(bf16), table, c_side, d_side, a_far, b_far), "gx", y_up)
+    c_sum = add(c_sum, c_far).astype(bf16)
+    d_sum = add(d_sum, d_far).astype(bf16)
+    c_sum = lax.ppermute(after(c_sum, table, c_side, d_side), "gx", y_down)
+    d_sum = lax.ppermute(after(d_sum, table, c_side, d_side), "gx", y_up)
 
     held = head_last(own, arrived, preact, table)
     table = after(table, held)
 
-    a_sum = lax.ppermute(after(add(a_sum, a_far).astype(bf16), a_side, b_side), "gz", z_down)
-    b_sum = lax.ppermute(after(add(b_sum, b_far).astype(bf16), a_side, b_side), "gz", z_up)
-
-    c_sum, d_sum = after(c_sum, a_side, b_side), after(d_sum, a_side, b_side)
-    c_own = add(after(c_own, a_side, b_side), c_side, c_sum)
+    a_sum = lax.ppermute(after(a_sum, table, a_side, b_side), "gz", z_down)
+    b_sum = lax.ppermute(after(b_sum, table, a_side, b_side), "gz", z_up)
+
+    c_sum, d_sum = after(c_sum, table, a_side, b_side), after(d_sum, table, a_side, b_side)
+    c_own = add(c_own, c_side, c_sum)
     d_own = add(d_own, d_side, d_sum)
     keep = jnp.where(h == 0, c_own, d_own)
     give = jnp.where(h == 0, d_own, c_own).astype(bf16)
     taken = lax.ppermute(give, "gx", gx_move(1, 0))
+    taken = after(taken, a_sum, b_sum)
 
     grad_pre = tail_last(own_tail, a_side, a_sum, b_side, b_sum, preact, table, held)
     grad_down = add(keep, taken).astype(bf16)

time: 188 us -> 192 us (1.021)
  waiting for transfers between devices: 39.9 us -> 43 us
    ppermute x1, waiting for transfers between devices: 15.6 us -> 0.01 us  [shards(): a_side = lax.ppermute(after(a_side, table, a_far, b_far), 'gz', z_up)]
    ppermute x1, waiting for transfers between devices: 8.16 us -> 16.7 us  [shards(): taken = lax.ppermute(give, 'gx', gx_move(1, 0))]
    ppermute x1, waiting for transfers between devices: 0.01 us -> 6.48 us  [shards(): lax.ppermute(to_down, 'gz', z_down)]
    ppermute x1, waiting for transfers between devices: 0.01 us -> 3.47 us  [shards(): across = lax.ppermute(own_head, 'gy', other_chip)]
    pallas_call x1, Pallas kernels: 19.7 us -> 17.4 us  [tail_parts(): call(tail_body, 'tail_parts', (tiles,), 1, [pl.BlockSpec((4, share, depth...]
    ppermute x1, waiting for transfers between devices: 2.27 us -> 0.01 us  [shards(): c_side = lax.ppermute(after(c_side, c_far, d_far), 'gx', y_up)]
  transfers between devices with their start and end apart: 24 -> 24, of which waited for: 8 -> 7; matrix products, arithmetic and copies ran while one was open for 13% -> 12% of each run, Pallas kernels for 42% -> 42%
where the time goes in v5:
time: 192 us; the launch traced here: 191 us
  Pallas kernels  87.6 us (46%)
  waiting for transfers between devices  43 us (22%)
  starting transfers between devices  31.3 us (16%)
  other arithmetic  21.7 us (11%)
  local copies, waits for them, and re-layouts  6.65 us (3%)
    pallas_call x4, Pallas kernels, terms(): call(functools.partial(terms_body, near), 'terms', (2,), 1, [source(j) fo...  33.2 us
    pallas_call x1, Pallas kernels, tail_parts(): call(tail_body, 'tail_parts', (tiles,), 1, [pl.BlockSpec((4, share, depth...  17.4 us
    ppermute x1, waiting for transfers between devices, shards(): taken = lax.ppermute(give, 'gx', gx_move(1, 0))  16.7 us
    ppermute x1, waiting for transfers between devices, shards(): d_sum = lax.ppermute(after(d_sum, table, c_side, d_side), 'gx', y_up)  12 us
    pallas_call x2, Pallas kernels, near_terms(): call(near_body, 'near_terms', (2,), 1, [pl.BlockSpec((share, chunk), lamb...  12 us
    pallas_call x1, Pallas kernels, first_parts(): call(first_body, 'first_parts', (hidden // TILE,), 1, [pl.BlockSpec((4 *...  11.7 us
    pallas_call x1, Pallas kernels, tail_last(): call(tail_last_body, 'tail_last', (count // step,), 1, [pl.BlockSpec((ste...  7.69 us
    ppermute x1, waiting for transfers between devices, shards(): lax.ppermute(to_down, 'gz', z_down)  6.48 us
  transfers between devices with their start and end apart: 24, of which 7 were waited for; matrix products, arithmetic and copies ran while one was open for 12% of the time, Pallas kernels for 42%

profile of v5, /device:TPU:0, one launch (start us, length us, event | category | flops | bytes accessed | tf_op | source)
XLA Modules:
  0.0 191.0 jit_solution(86790941710669708)
XLA Ops:
  0.6 0.0 copy-start
  0.6 0.1 collective-permute-start
  0.7 1.9 %slice_bitcast_fusion.1 = (bf16[1,192,1152]{2,1,0:T(8,128)(2,1)}, bf16[192,1152]{1,0:T(8,128)(2,1)S(1)}) fusion(bf16[512,1152]{1,0:T(8,128)(2,1)} %own.3), kind=kLoop, calls=%fused_computation.17 | loop fusion | bytes 1327104 | tf_op jit(solution)/shard_map/stack | solution.py:333
  2.7 1.6 collective-permute-start.1
  4.2 0.9 slice.23
  5.2 0.6 stack.101.table
  5.8 6.0 %near_terms.2.refs_2_ = bf16[2,384,1152]{2,1,0:T(8,128)(2,1)} custom-call(s32[18]{0:T(128)} %stack.101.table, bf16[2048,3072]{1,0:T(8,128)(2,1)} %pre.3, bf16[2048,3072]{1,0:T(8,128)(2,1)} %pre.3, bf16[512,1152]{1,0:T(8,128)(2,1)} %own.3, bf16[512,1152]{1,0:T(8,128)(2,1)} %collective-permute-done.partner), custom_call_target="tpu_custom_call" | custom-call | flops 28311552 | bytes 89088 | tf_op jit(solution)/shard_map/near_terms/pallas_call | solution.py:240
  11.8 3.5 %collective-permute-done.1 = bf16[192,1152]{1,0:T(8,128)(2,1)} collective-permute-done((bf16[192,1152]{1,0:T(8,128)(2,1)S(1)}, bf16[192,1152]{1,0:T(8,128)(2,1)}, u32[]{:S(2)}, u32[]{:S(2)}) %collective-permute-start.1) | collective-permute-done | bytes 442400 | tf_op jit(solution)/shard_map/ppermute | solution.py:326
  15.3 1.6 collective-permute-start.3
  16.9 1.0 slice_bitcast_fusion
  17.9 2.8 %pad_maximum_fusion.1 = bf16[4,192,1152]{2,1,0:T(8,128)(2,1)} fusion(bf16[1,192,1152]{2,1,0:T(8,128)(2,1)S(1)} %bitcast.32, bf16[1,192,1152]{2,1,0:T(8,128)(2,1)} %bitcast.19, bf16[1,192,1152]{2,1,0:T(8,128)(2,1)S(1)} %slice_bitcast_fusion, bf16[1,192,1152]{2,1,0:T(8,128)(2,1)} %get-tuple-element.100), kind=kLoop, calls=%fused_computation.3 | loop fusion | flops 2654208 | bytes 3538944 | tf_op jit(solution)/shard_map/stack | solution.py:333
  20.7 11.7 %first_parts.1 = (bf16[192,3072]{1,0:T(8,128)(2,1)}, bf16[192,3072]{1,0:T(8,128)(2,1)}, bf16[192,3072]{1,0:T(8,128)(2,1)}, bf16[192,3072]{1,0:T(8,128)(2,1)}) custom-call(s32[18]{0:T(128)} %stack.101.table, bf16[768,1152]{1,0:T(8,128)(2,1)} %bitcast.29, bf16[3072,1152]{1,0:T(8,128)(2,1)} %weights.3), custom_call_target="tpu_custom_call" | custom-call | flops 84934656 | bytes 211968 | tf_op jit(solution)/shard_map/first_parts/pallas_call | solution.py:95
  32.4 1.9 %collective-permute-start.8 = (bf16[192,3072]{1,0:T(8,128)(2,1)}, bf16[192,3072]{1,0:T(8,128)(2,1)}, u32[]{:S(2)}, u32[]{:S(2)}) collective-permute-start(bf16[192,3072]{1,0:T(8,128)(2,1)} %get-tuple-element.62), channel_id=1, source_target_pairs={{0,1},{1,2},{2,3},{3,0},{4,5},{5,6},{6,7},{7,4},{8,9},{9,10},{10,1... | collective-permute-start | bytes 3538952 | tf_op jit(solution)/shard_map/ppermute | solution.py:337
  34.3 2.2 %collective-permute-start.9 = (bf16[192,3072]{1,0:T(8,128)(2,1)}, bf16[192,3072]{1,0:T(8,128)(2,1)}, u32[]{:S(2)}, u32[]{:S(2)}) collective-permute-start(bf16[192,3072]{1,0:T(8,128)(2,1)} %get-tuple-element.63), channel_id=1, source_target_pairs={{0,3},{1,0},{2,1},{3,2},{4,7},{5,4},{6,5},{7,6},{8,11},{9,8},{10,9... | collective-permute-start | bytes 3538952 | tf_op jit(solution)/shard_map/ppermute | solution.py:338
  36.5 1.8 collective-permute-start.10
  38.3 6.0 %near_terms.3.refs_2_ = bf16[2,384,1152]{2,1,0:T(8,128)(2,1)} custom-call(s32[18]{0:T(128)} %stack.101.table, bf16[2048,3072]{1,0:T(8,128)(2,1)} %pre.3, bf16[2048,3072]{1,0:T(8,128)(2,1)} %pre.3, bf16[512,1152]{1,0:T(8,128)(2,1)} %own.3, bf16[512,1152]{1,0:T(8,128)(2,1)} %collective-permute-done.partner), custom_call_target="tpu_custom_call" | custom-call | flops 28311552 | bytes 89088 | tf_op jit(solution)/shard_map/near_terms/pallas_call | solution.py:240
  44.3 1.0 constant_dynamic-update-slice_fusion.4
  45.4 0.0 collective-permute-done.3
  45.4 0.1 fusion
  45.4 0.0 copy-start.1
  45.4 0.1 collective-permute-start.4
  45.5 1.2 pad_maximum_fusion.2
  46.7 0.5 collective-permute-start.7
  47.2 0.1 collective-permute-start.5
  47.3 1.3 collective-permute-done.5
  48.6 0.3 collective-permute-start.6
  48.9 1.1 collective-permute-done.6
  50.1 0.0 collective-permute-done.7
  50.1 3.6 %pad_maximum_fusion.refs_3_.rows.refs_4_ = bf16[4,512,1152]{2,1,0:T(8,128)(2,1)} fusion(bf16[1,512,1152]{2,1,0:T(8,128)(2,1)S(1)} %bitcast.31, bf16[1,512,1152]{2,1,0:T(8,128)(2,1)S(1)} %bitcast.30, bf16[1,512,1152]{2,1,0:T(8,128)(2,1)} %bitcast.23, bf16[1,512,1152]{2,1,0:T(8,128)(2,1)S(1)} %bitcast.28), kind=kLoop, calls=%fused_computation | loop fusion | flops 7077888 | bytes 9437184 | tf_op jit(solution)/shard_map/stack | solution.py:349
  53.7 6.9 %terms.4 = (bf16[384,1152]{1,0:T(8,128)(2,1)}, bf16[384,1152]{1,0:T(8,128)(2,1)}) custom-call(s32[18]{0:T(128)} %stack.101.table, bf16[2048,3072]{1,0:T(8,128)(2,1)} %pre.3, bf16[2048,3072]{1,0:T(8,128)(2,1)} %pre.3, bf16[2,384,1152]{2,1,0:T(8,128)(2,1)} %near_terms.2.refs_2_, bf16[4,512,1152]{2,1,0:T(8,128)(2,1)} %pad_maximum_fusion.refs_3_.rows.refs_4_), custom_call_target="tpu_custom_call" | custom-call | flops 28311552 | bytes 61440 | tf_op jit(solution)/shard_map/terms/pallas_call | solution.py:291
  60.6 1.6 collective-permute-start.12
  62.2 1.7 collective-permute-start.11
  63.9 17.4 %tail_parts.1 = (bf16[320,1536]{1,0:T(8,128)(2,1)}, bf16[320,1536]{1,0:T(8,128)(2,1)}, bf16[320,1536]{1,0:T(8,128)(2,1)}, bf16[320,1536]{1,0:T(8,128)(2,1)}, bf1...) custom-call(s32[18]{0:T(128)} %stack.101.table, ...), custom_call_target="tpu_custom_call" | custom-call | flops 141557760 | bytes 307200 | tf_op jit(solution)/shard_map/tail_parts/pallas_call | solution.py:148
  81.2 0.0 collective-permute-done.8.one
  81.2 6.5 %collective-permute-done.9.two = bf16[192,3072]{1,0:T(8,128)(2,1)} collective-permute-done((bf16[192,3072]{1,0:T(8,128)(2,1)}, bf16[192,3072]{1,0:T(8,128)(2,1)}, u32[]{:S(2)}, u32[]{:S(2)}) %collective-permute-start.9) | collective-permute-done | bytes 1179680 | tf_op jit(solution)/shard_map/ppermute | solution.py:338
  87.7 1.8 collective-permute-done.10.three
  89.6 1.1 collective-permute-start.14
  90.7 2.1 %collective-permute-start.13 = (bf16[320,1536]{1,0:T(8,128)(2,1)}, bf16[320,1536]{1,0:T(8,128)(2,1)}, u32[]{:S(2)}, u32[]{:S(2)}) collective-permute-start(bf16[320,1536]{1,0:T(8,128)(2,1)} %get-tuple-element.74), channel_id=1, source_target_pairs={{0,3},{1,0},{2,1},{3,2},{4,7},{5,4},{6,5},{7,6},{8,11},{9,8},{10,9... | collective-permute-start | bytes 2949128 | tf_op jit(solution)/shard_map/ppermute | solution.py:365
  92.8 7.0 %terms.5 = (bf16[384,1152]{1,0:T(8,128)(2,1)}, bf16[384,1152]{1,0:T(8,128)(2,1)}) custom-call(s32[18]{0:T(128)} %stack.101.table, bf16[2048,3072]{1,0:T(8,128)(2,1)} %pre.3, bf16[2048,3072]{1,0:T(8,128)(2,1)} %pre.3, bf16[2,384,1152]{2,1,0:T(8,128)(2,1)} %near_terms.3.refs_2_, bf16[4,512,1152]{2,1,0:T(8,128)(2,1)} %pad_maximum_fusion.refs_3_.rows.refs_4_), custom_call_target="tpu_custom_call" | custom-call | flops 28311552 | bytes 61440 | tf_op jit(solution)/shard_map/terms/pallas_call | solution.py:291
  99.8 0.0 collective-permute-done.11
  99.8 0.9 copy-done.5
  100.7 1.6 collective-permute-start.19
  102.3 1.7 collective-permute-start.20
  103.9 9.7 %terms.6 = (bf16[384,1152]{1,0:T(8,128)(2,1)}, bf16[384,1152]{1,0:T(8,128)(2,1)}) custom-call(s32[18]{0:T(128)} %stack.101.table, bf16[2048,3072]{1,0:T(8,128)(2,1)} %pre.3, bf16[2048,3072]{1,0:T(8,128)(2,1)} %pre.3, bf16[2048,3072]{1,0:T(8,128)(2,1)} %pre.3, bf16[2048,3072]{1,0:T(8,128)(2,1)} %pre.3, bf16[4,512,1152]{2,1,0:T(8,128)(2,1)} %pad_maximum_fusion.refs_3_.rows.refs_4_), custom_call_target="tpu_custom_call" | custom-call | flops 56623104 | bytes 122880 | tf_op jit(solution)/shard_map/terms/pallas_call | solution.py:291
  113.6 3.8 %add_convert_fusion.3 = (bf16[384,1152]{1,0:T(8,128)(2,1)}, bf16[384,1152]{1,0:T(8,128)(2,1)}) fusion(bf16[384,1152]{1,0:T(8,128)(2,1)} %copy-done.5, bf16[384,1152]{1,0:T(8,128)(2,1)} %get-tuple-element.96, bf16[384,1152]{1,0:T(8,128)(2,1)} %collective-permute-done.11, bf16[384,1152]{1,0:T(8,128)(2,1)} %get-tuple-element.70), kind=kLoop, calls=%fused_computation.7 | loop fusion | flops 3538944 | bytes 5308416 | tf_op jit(solution)/shard_map/convert_element_type | solution.py:387
  117.4 0.1 collective-permute-start.15
  117.5 3.2 %collective-permute-start.16 = (bf16[320,1536]{1,0:T(8,128)(2,1)}, bf16[320,1536]{1,0:T(8,128)(2,1)}, u32[]{:S(2)}, u32[]{:S(2)}) collective-permute-start(bf16[320,1536]{1,0:T(8,128)(2,1)} %get-tuple-element.87), channel_id=1, source_target_pairs={{0,3},{1,0},{2,1},{3,2},{4,7},{5,4},{6,5},{7,6},{8,11},{9,8},{10,9... | collective-permute-start | bytes 2949128 | tf_op jit(solution)/shard_map/ppermute | solution.py:378
  120.7 3.3 %add_convert_fusion = (bf16[320,1536]{1,0:T(8,128)(2,1)}, bf16[320,1536]{1,0:T(8,128)(2,1)}) fusion(bf16[320,1536]{1,0:T(8,128)(2,1)} %collective-permute-done.14, bf16[320,1536]{1,0:T(8,128)(2,1)S(1)} %copy-done.4, bf16[320,1536]{1,0:T(8,128)(2,1)} %collective-permute-done.13, bf16[320,1536]{1,0:T(8,128)(2,1)S(1)} %copy-done.3), kind=kLoop, calls=%fused_computation.1 | loop fusion | flops 3932160 | bytes 5898240 | tf_op jit(solution)/shard_map/convert_element_type | solution.py:380
  124.0 9.6 %terms.7 = (bf16[384,1152]{1,0:T(8,128)(2,1)}, bf16[384,1152]{1,0:T(8,128)(2,1)}) custom-call(s32[18]{0:T(128)} %stack.101.table, bf16[2048,3072]{1,0:T(8,128)(2,1)} %pre.3, bf16[2048,3072]{1,0:T(8,128)(2,1)} %pre.3, bf16[2048,3072]{1,0:T(8,128)(2,1)} %pre.3, bf16[2048,3072]{1,0:T(8,128)(2,1)} %pre.3, bf16[4,512,1152]{2,1,0:T(8,128)(2,1)} %pad_maximum_fusion.refs_3_.rows.refs_4_), custom_call_target="tpu_custom_call" | custom-call | flops 56623104 | bytes 122880 | tf_op jit(solution)/shard_map/terms/pallas_call | solution.py:291
  133.7 0.0 collective-permute-done.19
  133.7 0.0 collective-permute-done.20
  133.7 0.4 collective-permute-start.22
  134.1 2.9 %collective-permute-start.21 = (bf16[384,1152]{1,0:T(8,128)(2,1)}, bf16[384,1152]{1,0:T(8,128)(2,1)}, u32[]{:S(2)}, u32[]{:S(2)}) collective-permute-start(bf16[384,1152]{1,0:T(8,128)(2,1)} %get-tuple-element.93), channel_id=1, source_target_pairs={{0,48},{16,0},{32,16},{48,32},{64,112},{80,64},{96,80},{112,96},{1... | collective-permute-start | bytes 2654216 | tf_op jit(solution)/shard_map/ppermute | solution.py:388
  137.0 5.6 %head_last.1.held = bf16[512,3072]{1,0:T(8,128)(2,1)} custom-call(s32[18]{0:T(128)} %stack.101.table, bf16[192,3072]{1,0:T(8,128)(2,1)} %get-tuple-element.53.own, bf16[192,3072]{1,0:T(8,128)(2,1)} %collective-permute-done.8.one, bf16[192,3072]{1,0:T(8,128)(2,1)} %collective-permute-done.9.two, bf16[192,3072]{1,0:T(8,128)(2,1)} %collective-permute-done.10.three, ...), custom_call_target="tpu_custom_call" | custom-call | flops 368640 | bytes 110592 | tf_op jit(solution)/shard_map/head_last/pallas_call | solution.py:177
  142.6 12.0 %collective-permute-done.22 = bf16[384,1152]{1,0:T(8,128)(2,1)} collective-permute-done((bf16[384,1152]{1,0:T(8,128)(2,1)}, bf16[384,1152]{1,0:T(8,128)(2,1)}, u32[]{:S(2)}, u32[]{:S(2)}) %collective-permute-start.22) | collective-permute-done | bytes 884768 | tf_op jit(solution)/shard_map/ppermute | solution.py:389
  154.6 0.0 collective-permute-done.15.side_a
  154.6 0.4 collective-permute-start.17
  155.0 1.7 collective-permute-start.18
  156.7 2.9 %select_convert_fusion = bf16[384,1152]{1,0:T(8,128)(2,1)S(1)} fusion(bf16[384,1152]{1,0:T(8,128)(2,1)} %collective-permute-done.21, bf16[384,1152]{1,0:T(8,128)(2,1)S(1)} %collective-permute-done.19, bf16[384,1152]{1,0:T(8,128)(2,1)} %get-tuple-element.81, bf16[384,1152]{1,0:T(8,128)(2,1)} %collective-permute-done.22, ...), kind=kLoop, calls=%fused_computation.5 | loop fusion | flops 5308416 | bytes 6193153 | tf_op jit(solution)/shard_map/convert_element_type | solution.py:401
  159.6 2.8 %collective-permute-start.23 = (bf16[384,1152]{1,0:T(8,128)(2,1)S(1)}, bf16[384,1152]{1,0:T(8,128)(2,1)}, u32[]{:S(2)}, u32[]{:S(2)}) collective-permute-start(bf16[384,1152]{1,0:T(8,128)(2,1)S(1)} %select_convert_fusion), channel_id=1, source_target_pairs={{0,64},{16,80},{32,96},{48,112},{64,0},{80,16},{96,32},{112,48},{1... | collective-permute-start | bytes 2654216 | tf_op jit(solution)/shard_map/ppermute | solution.py:402
  162.4 16.7 %collective-permute-done.23 = bf16[384,1152]{1,0:T(8,128)(2,1)} collective-permute-done((bf16[384,1152]{1,0:T(8,128)(2,1)S(1)}, bf16[384,1152]{1,0:T(8,128)(2,1)}, u32[]{:S(2)}, u32[]{:S(2)}) %collective-permute-start.23) | collective-permute-done | bytes 884768 | tf_op jit(solution)/shard_map/ppermute | solution.py:402
  179.2 0.0 collective-permute-done.17.sum_a
  179.2 7.7 %tail_last.1 = bf16[512,3072]{1,0:T(8,128)(2,1)} custom-call(s32[18]{0:T(128)} %stack.101.table, bf16[320,3072]{1,0:T(8,128)(2,1)} %get-tuple-element.60.own, bf16[320,1536]{1,0:T(8,128)(2,1)} %collective-permute-done.15.side_a, bf16[320,1536]{1,0:T(8,128)(2,1)} %collective-permute-done.17.sum_a, ...), custom_call_target="tpu_custom_call", output_to_operand_aliasing={{}: (7, {})} | custom-call | flops 39321600 | bytes 9830400 | tf_op jit(solution)/shard_map/tail_last/pallas_call | solution.py:208
  186.9 4.2 %add_convert_fusion.2 = bf16[384,1152]{1,0:T(8,128)(2,1)} fusion(bf16[384,1152]{1,0:T(8,128)(2,1)} %collective-permute-done.23, bf16[384,1152]{1,0:T(8,128)(2,1)} %collective-permute-done.21, bf16[384,1152]{1,0:T(8,128)(2,1)S(1)} %collective-permute-done.19, bf16[384,1152]{1,0:T(8,128)(2,1)} %get-tuple-element.81, ...), kind=kLoop, calls=%fused_computation.4 | loop fusion | flops 6193152 | bytes 7077889 | tf_op jit(solution)/shard_map/convert_element_type | solution.py:406
  (23 shorter events, 0.1 us)
Async XLA Ops:
  0.6 3.6 %copy-start = (bf16[512,1152]{1,0:T(8,128)(2,1)S(1)}, bf16[512,1152]{1,0:T(8,128)(2,1)}, u32[]{:S(2)}) copy-start(bf16[512,1152]{1,0:T(8,128)(2,1)} %own.3) | copy-start | bytes 3538948
  0.6 5.2 %collective-permute-start = (bf16[512,1152]{1,0:T(8,128)(2,1)}, bf16[512,1152]{1,0:T(8,128)(2,1)}, u32[]{:S(2)}, u32[]{:S(2)}) collective-permute-start(bf16[512,1152]{1,0:T(8,128)(2,1)} %own.3), channel_id=1, source_target_pairs={{0,4},{4,0},{8,12},{12,8},{1,5},{5,1},{9,13},{13,9},{2,6},{6,2},{1... | collective-permute-start | bytes 3538952 | tf_op jit(solution)/shard_map/ppermute | solution.py:327
  2.7 12.6 %collective-permute-start.1 = (bf16[192,1152]{1,0:T(8,128)(2,1)S(1)}, bf16[192,1152]{1,0:T(8,128)(2,1)}, u32[]{:S(2)}, u32[]{:S(2)}) collective-permute-start(bf16[192,1152]{1,0:T(8,128)(2,1)S(1)} %get-tuple-element.101), channel_id=1, source_target_pairs={{0,8},{4,12},{8,0},{12,4},{1,9},{5,13},{9,1},{13,5},{2,10},{6,14},... | collective-permute-start | bytes 1327112 | tf_op jit(solution)/shard_map/ppermute | solution.py:326
  15.3 2.6 %collective-permute-start.2 = (bf16[192,1152]{1,0:T(8,128)(2,1)}, bf16[192,1152]{1,0:T(8,128)(2,1)S(1)}, u32[]{:S(2)}, u32[]{:S(2)}) collective-permute-start(bf16[192,1152]{1,0:T(8,128)(2,1)} %collective-permute-done.1), channel_id=1, source_target_pairs={{0,4},{4,0},{8,12},{12,8},{1,5},{5,1},{9,13},{13,9},{2,6},{6,2},{1... | collective-permute-start | bytes 1327112 | tf_op jit(solution)/shard_map/ppermute | solution.py:330
  15.3 30.1 %collective-permute-start.3 = (bf16[320,1152]{1,0:T(8,128)(2,1)}, bf16[320,1152]{1,0:T(8,128)(2,1)S(1)}, u32[]{:S(2)}, u32[]{:S(2)}) collective-permute-start(bf16[320,1152]{1,0:T(8,128)(2,1)} %slice.23), channel_id=1, source_target_pairs={{0,8},{4,12},{8,0},{12,4},{1,9},{5,13},{9,1},{13,5},{2,10},{6,14},... | collective-permute-start | bytes 2211848 | tf_op jit(solution)/shard_map/ppermute | solution.py:331
  17.9 2.8 %copy-start.2 = (bf16[192,1152]{1,0:T(8,128)(2,1)}, bf16[192,1152]{1,0:T(8,128)(2,1)S(1)}, u32[]{:S(2)}) copy-start(bf16[192,1152]{1,0:T(8,128)(2,1)S(1)} %collective-permute-done.2) | copy-start | bytes 1327108
  32.4 48.8 %collective-permute-start.8 = (bf16[192,3072]{1,0:T(8,128)(2,1)}, bf16[192,3072]{1,0:T(8,128)(2,1)}, u32[]{:S(2)}, u32[]{:S(2)}) collective-permute-start(bf16[192,3072]{1,0:T(8,128)(2,1)} %get-tuple-element.62), channel_id=1, source_target_pairs={{0,1},{1,2},{2,3},{3,0},{4,5},{5,6},{6,7},{7,4},{8,9},{9,10},{10,1... | collective-permute-start | bytes 3538952 | tf_op jit(solution)/shard_map/ppermute | solution.py:337
  34.3 53.4 %collective-permute-start.9 = (bf16[192,3072]{1,0:T(8,128)(2,1)}, bf16[192,3072]{1,0:T(8,128)(2,1)}, u32[]{:S(2)}, u32[]{:S(2)}) collective-permute-start(bf16[192,3072]{1,0:T(8,128)(2,1)} %get-tuple-element.63), channel_id=1, source_target_pairs={{0,3},{1,0},{2,1},{3,2},{4,7},{5,4},{6,5},{7,6},{8,11},{9,8},{10,9... | collective-permute-start | bytes 3538952 | tf_op jit(solution)/shard_map/ppermute | solution.py:338
  36.5 53.1 %collective-permute-start.10 = (bf16[192,3072]{1,0:T(8,128)(2,1)}, bf16[192,3072]{1,0:T(8,128)(2,1)}, u32[]{:S(2)}, u32[]{:S(2)}) collective-permute-start(bf16[192,3072]{1,0:T(8,128)(2,1)} %get-tuple-element.64), channel_id=1, source_target_pairs={{0,2},{1,3},{2,0},{3,1},{4,6},{5,7},{6,4},{7,5},{8,10},{9,11},{10,... | collective-permute-start | bytes 3538952 | tf_op jit(solution)/shard_map/ppermute | solution.py:339
  45.4 4.7 %copy-start.1 = (bf16[512,1152]{1,0:T(8,128)(2,1)S(1)}, bf16[512,1152]{1,0:T(8,128)(2,1)}, u32[]{:S(2)}) copy-start(bf16[512,1152]{1,0:T(8,128)(2,1)} %own.3) | copy-start | bytes 3538948
  45.4 1.8 collective-permute-start.4
  46.7 3.4 %collective-permute-start.7 = (bf16[80,1152]{1,0:T(8,128)(2,1)S(1)}, bf16[80,1152]{1,0:T(8,128)(2,1)S(1)}, u32[]{:S(2)}, u32[]{:S(2)}) collective-permute-start(bf16[80,1152]{1,0:T(8,128)(2,1)S(1)} %get-tuple-element.102), channel_id=1, source_target_pairs={{0,4},{4,0},{8,12},{12,8},{1,5},{5,1},{9,13},{13,9},{2,6},{6,2},{1... | collective-permute-start | bytes 552968 | tf_op jit(solution)/shard_map/ppermute | solution.py:346
  47.2 1.4 collective-permute-start.5
  48.6 1.4 collective-permute-start.6
  60.6 39.1 %collective-permute-start.12 = (bf16[384,1152]{1,0:T(8,128)(2,1)}, bf16[384,1152]{1,0:T(8,128)(2,1)S(1)}, u32[]{:S(2)}, u32[]{:S(2)}) collective-permute-start(bf16[384,1152]{1,0:T(8,128)(2,1)} %get-tuple-element.68), channel_id=1, source_target_pairs={{0,16},{16,32},{32,48},{48,0},{64,80},{80,96},{96,112},{112,64},{1... | collective-permute-start | bytes 2654216 | tf_op jit(solution)/shard_map/ppermute | solution.py:361
  62.2 37.6 %collective-permute-start.11 = (bf16[384,1152]{1,0:T(8,128)(2,1)}, bf16[384,1152]{1,0:T(8,128)(2,1)}, u32[]{:S(2)}, u32[]{:S(2)}) collective-permute-start(bf16[384,1152]{1,0:T(8,128)(2,1)} %get-tuple-element.58), channel_id=1, source_target_pairs={{0,48},{16,0},{32,16},{48,32},{64,112},{80,64},{96,80},{112,96},{1... | collective-permute-start | bytes 2654216 | tf_op jit(solution)/shard_map/ppermute | solution.py:360
  89.6 27.8 %collective-permute-start.14 = (bf16[320,1536]{1,0:T(8,128)(2,1)}, bf16[320,1536]{1,0:T(8,128)(2,1)}, u32[]{:S(2)}, u32[]{:S(2)}) collective-permute-start(bf16[320,1536]{1,0:T(8,128)(2,1)} %get-tuple-element.78), channel_id=1, source_target_pairs={{0,1},{1,2},{2,3},{3,0},{4,5},{5,6},{6,7},{7,4},{8,9},{9,10},{10,1... | collective-permute-start | bytes 2949128 | tf_op jit(solution)/shard_map/ppermute | solution.py:366
  90.7 26.7 %collective-permute-start.13 = (bf16[320,1536]{1,0:T(8,128)(2,1)}, bf16[320,1536]{1,0:T(8,128)(2,1)}, u32[]{:S(2)}, u32[]{:S(2)}) collective-permute-start(bf16[320,1536]{1,0:T(8,128)(2,1)} %get-tuple-element.74), channel_id=1, source_target_pairs={{0,3},{1,0},{2,1},{3,2},{4,7},{5,4},{6,5},{7,6},{8,11},{9,8},{10,9... | collective-permute-start | bytes 2949128 | tf_op jit(solution)/shard_map/ppermute | solution.py:365
  99.8 0.9 copy-start.5
  100.7 33.0 %collective-permute-start.19 = (bf16[384,1152]{1,0:T(8,128)(2,1)}, bf16[384,1152]{1,0:T(8,128)(2,1)S(1)}, u32[]{:S(2)}, u32[]{:S(2)}) collective-permute-start(bf16[384,1152]{1,0:T(8,128)(2,1)} %get-tuple-element.90), channel_id=1, source_target_pairs={{0,16},{16,32},{32,48},{48,0},{64,80},{80,96},{96,112},{112,64},{1... | collective-permute-start | bytes 2654216 | tf_op jit(solution)/shard_map/ppermute | solution.py:371
  102.3 31.4 %collective-permute-start.20 = (bf16[384,1152]{1,0:T(8,128)(2,1)}, bf16[384,1152]{1,0:T(8,128)(2,1)}, u32[]{:S(2)}, u32[]{:S(2)}) collective-permute-start(bf16[384,1152]{1,0:T(8,128)(2,1)} %get-tuple-element.92), channel_id=1, source_target_pairs={{0,48},{16,0},{32,16},{48,32},{64,112},{80,64},{96,80},{112,96},{1... | collective-permute-start | bytes 2654216 | tf_op jit(solution)/shard_map/ppermute | solution.py:372
  113.6 7.1 %copy-start.3 = (bf16[320,1536]{1,0:T(8,128)(2,1)S(1)}, bf16[320,1536]{1,0:T(8,128)(2,1)}, u32[]{:S(2)}) copy-start(bf16[320,1536]{1,0:T(8,128)(2,1)} %get-tuple-element.72) | copy-start | bytes 2949124
  113.6 7.1 %copy-start.4 = (bf16[320,1536]{1,0:T(8,128)(2,1)S(1)}, bf16[320,1536]{1,0:T(8,128)(2,1)}, u32[]{:S(2)}) copy-start(bf16[320,1536]{1,0:T(8,128)(2,1)} %get-tuple-element.76) | copy-start | bytes 2949124
  117.4 37.2 %collective-permute-start.15 = (bf16[320,1536]{1,0:T(8,128)(2,1)}, bf16[320,1536]{1,0:T(8,128)(2,1)}, u32[]{:S(2)}, u32[]{:S(2)}) collective-permute-start(bf16[320,1536]{1,0:T(8,128)(2,1)} %get-tuple-element.85), channel_id=1, source_target_pairs={{0,1},{1,2},{2,3},{3,0},{4,5},{5,6},{6,7},{7,4},{8,9},{9,10},{10,1... | collective-permute-start | bytes 2949128 | tf_op jit(solution)/shard_map/ppermute | solution.py:377
  117.5 37.1 %collective-permute-start.16 = (bf16[320,1536]{1,0:T(8,128)(2,1)}, bf16[320,1536]{1,0:T(8,128)(2,1)}, u32[]{:S(2)}, u32[]{:S(2)}) collective-permute-start(bf16[320,1536]{1,0:T(8,128)(2,1)} %get-tuple-element.87), channel_id=1, source_target_pairs={{0,3},{1,0},{2,1},{3,2},{4,7},{5,4},{6,5},{7,6},{8,11},{9,8},{10,9... | collective-permute-start | bytes 2949128 | tf_op jit(solution)/shard_map/ppermute | solution.py:378
  133.7 20.9 %collective-permute-start.22 = (bf16[384,1152]{1,0:T(8,128)(2,1)}, bf16[384,1152]{1,0:T(8,128)(2,1)}, u32[]{:S(2)}, u32[]{:S(2)}) collective-permute-start(bf16[384,1152]{1,0:T(8,128)(2,1)} %get-tuple-element.97), channel_id=1, source_target_pairs={{0,16},{16,32},{32,48},{48,0},{64,80},{80,96},{96,112},{112,64},{1... | collective-permute-start | bytes 2654216 | tf_op jit(solution)/shard_map/ppermute | solution.py:389
  134.1 20.5 %collective-permute-start.21 = (bf16[384,1152]{1,0:T(8,128)(2,1)}, bf16[384,1152]{1,0:T(8,128)(2,1)}, u32[]{:S(2)}, u32[]{:S(2)}) collective-permute-start(bf16[384,1152]{1,0:T(8,128)(2,1)} %get-tuple-element.93), channel_id=1, source_target_pairs={{0,48},{16,0},{32,16},{48,32},{64,112},{80,64},{96,80},{112,96},{1... | collective-permute-start | bytes 2654216 | tf_op jit(solution)/shard_map/ppermute | solution.py:388
  154.6 24.5 %collective-permute-start.17 = (bf16[320,1536]{1,0:T(8,128)(2,1)}, bf16[320,1536]{1,0:T(8,128)(2,1)}, u32[]{:S(2)}, u32[]{:S(2)}) collective-permute-start(bf16[320,1536]{1,0:T(8,128)(2,1)} %get-tuple-element.88), channel_id=1, source_target_pairs={{0,3},{1,0},{2,1},{3,2},{4,7},{5,4},{6,5},{7,6},{8,11},{9,8},{10,9... | collective-permute-start | bytes 2949128 | tf_op jit(solution)/shard_map/ppermute | solution.py:394
  155.0 24.2 %collective-permute-start.18 = (bf16[320,1536]{1,0:T(8,128)(2,1)}, bf16[320,1536]{1,0:T(8,128)(2,1)}, u32[]{:S(2)}, u32[]{:S(2)}) collective-permute-start(bf16[320,1536]{1,0:T(8,128)(2,1)} %get-tuple-element.89), channel_id=1, source_target_pairs={{0,1},{1,2},{2,3},{3,0},{4,5},{5,6},{6,7},{7,4},{8,9},{9,10},{10,1... | collective-permute-start | bytes 2949128 | tf_op jit(solution)/shard_map/ppermute | solution.py:395
  159.6 19.5 %collective-permute-start.23 = (bf16[384,1152]{1,0:T(8,128)(2,1)S(1)}, bf16[384,1152]{1,0:T(8,128)(2,1)}, u32[]{:S(2)}, u32[]{:S(2)}) collective-permute-start(bf16[384,1152]{1,0:T(8,128)(2,1)S(1)} %select_convert_fusion), channel_id=1, source_target_pairs={{0,64},{16,80},{32,96},{48,112},{64,0},{80,16},{96,32},{112,48},{1... | collective-permute-start | bytes 2654216 | tf_op jit(solution)/shard_map/ppermute | solution.py:402

commit v6 on v5

--- a/solution.py
+++ b/solution.py
@@ -12,9 +12,9 @@
 slope_scale = 1.0 / math.sqrt(2.0 * math.pi)
 bf16 = jnp.bfloat16
 f32 = jnp.float32
-HEAD = 192
+HEAD = 160
 TILE = 512
-PIECE = 80
+PIECE = 96
 SHORT, MID, LAST, LONG = 1 / 64, 1/64, 1/64, 1/64
 VMEM = 63 * 1024 * 1024
 
@@ -182,7 +182,7 @@
         [block] * 4
         + [pl.BlockSpec((share, width), lambda t, p: (p[GZ], t))],
         block,
-        jax.ShapeDtypeStruct((share, hidden), bf16),
+        jax.ShapeDtypeStruct((count, hidden), bf16),
         count * hidden * 40,
         12 * count * hidden,
         cost=LONG,
@@ -190,40 +190,47 @@
 
 
 def tail_last_body(table, own, side_a, sum_a, side_b, sum_b, pre, held, out):
-    width = side_a.shape[1]
-    slope = unit_slope(pre[...].astype(f32))
+    head = held.shape[0]
+    slope = unit_slope(pre[head:].astype(f32))
     total = own[...].astype(f32)
-    first = total[:, :width] + side_a[...].astype(f32) + sum_a[...].astype(f32)
-    second = total[:, width:] + side_b[...].astype(f32) + sum_b[...].astype(f32)
-    out[:, :width] = (first * slope[:, :width]).astype(bf16)
-    out[:, width:] = (second * slope[:, width:]).astype(bf16)
+    first = pl.program_id(0) < pl.num_programs(0) // 2
+    out[:head] = held[...]
+
+    @pl.when(first)
+    def _():
+        whole = total + side_a[...].astype(f32) + sum_a[...].astype(f32)
+        out[head:] = (whole * slope).astype(bf16)
+
+    @pl.when(jnp.logical_not(first))
+    def _():
+        whole = total + side_b[...].astype(f32) + sum_b[...].astype(f32)
+        out[head:] = (whole * slope).astype(bf16)
 
 
 def tail_last(own, side_a, sum_a, side_b, sum_b, preact, table, held):
     count, hidden = own.shape
     share = preact.shape[0] // 4
-    step = 64
-    start, blocks = HEAD // step, share // step
-    half = pl.BlockSpec((step, hidden // 2), lambda t, p: (t, 0))
+    tiles = hidden // TILE
+    half_a = pl.BlockSpec((count, TILE), lambda t, p: (0, jnp.minimum(t, tiles // 2 - 1)))
+    half_b = pl.BlockSpec((count, TILE), lambda t, p: (0, jnp.maximum(t - tiles // 2, 0)))
     return call(
         tail_last_body,
         "tail_last",
-        (count // step,),
+        (tiles,),
         1,
         [
-            pl.BlockSpec((step, hidden), lambda t, p: (t, 0)),
-            half,
-            half,
-            half,
-            half,
-            pl.BlockSpec((step, hidden), lambda t, p: (p[GZ] * blocks + start + t, 0)),
-            pl.BlockSpec(memory_space=pl.ANY),
+            pl.BlockSpec((count, TILE), lambda t, p: (0, t)),
+            half_a,
+            half_a,
+            half_b,
+            half_b,
+            pl.BlockSpec((share, TILE), lambda t, p: (p[GZ], t)),
+            pl.BlockSpec((share - count, TILE), lambda t, p: (0, t)),
         ],
-        pl.BlockSpec((step, hidden), lambda t, p: (start + t, 0)),
+        pl.BlockSpec((share, TILE), lambda t, p: (0, t)),
         jax.ShapeDtypeStruct((share, hidden), bf16),
         count * hidden * 40,
         10 * count * hidden,
-        aliases={7: 0},
     )(table, own, side_a, sum_a, side_b, sum_b, preact, held)
 
 
@@ -378,15 +385,16 @@
     b_side = lax.ppermute(after(b_side, table, a_far, b_far), "gz", z_down)
     a_sum = add(a_sum, after(a_far, table)).astype(bf16)
     b_sum = add(b_sum, after(b_far, table)).astype(bf16)
-    table = after(table, a_sum, b_sum)
+    c_sum = add(c_sum, c_far).astype(bf16)
+    d_sum = add(d_sum, d_far).astype(bf16)
+    table = after(table, a_sum, b_sum, c_sum)
+
+    c_sum = lax.ppermute(after(c_sum, c_side, d_side), "gx", y_down)
+    d_sum = lax.ppermute(after(d_sum, c_side, d_side), "gx", y_up)
+    table = after(table, c_side, d_side)
 
     c_own, d_own = terms(preact, rows, table, C_OWN, cost=LAST)
     table = after(table, c_own)
-
-    c_sum = add(c_sum, c_far).astype(bf16)
-    d_sum = add(d_sum, d_far).astype(bf16)
-    c_sum = lax.ppermute(after(c_sum, table, c_side, d_side), "gx", y_down)
-    d_sum = lax.ppermute(after(d_sum, table, c_side, d_side), "gx", y_up)
 
     held = head_last(own, arrived, preact, table)
     table = after(table, held)

time: 192 us -> 176 us (0.917)
  waiting for transfers between devices: 43 us -> 26.3 us
    ppermute x2, waiting for transfers between devices: 12 us -> 0.01 us  [the longest x1 0.01 us: shards(): d_sum = lax.ppermute(after(d_sum, c_side, d_side), 'gx', y_up)]
    ppermute x1, waiting for transfers between devices: 6.48 us -> 0.01 us  [shards(): lax.ppermute(to_down, 'gz', z_down)]
    ppermute x1, waiting for transfers between devices: 0.01 us -> 3.27 us  [shards(): b_far = lax.ppermute(after(b_far, *arrived), 'gz', z_up)]
  transfers between devices with their start and end apart: 24 -> 24, of which waited for: 7 -> 7; matrix products, arithmetic and copies ran while one was open for 12% -> 13% of each run, Pallas kernels for 42% -> 45%
where the time goes in v6:
time: 176 us
  Pallas kernels  89 us (51%)
  starting transfers between devices  31.5 us (18%)
  waiting for transfers between devices  26.3 us (15%)
  other arithmetic  21.6 us (12%)
  local copies, waits for them, and re-layouts  6.58 us (4%)
    pallas_call x4, Pallas kernels, terms(): call(functools.partial(terms_body, near), 'terms', (2,), 1, [source(j) fo...  33.2 us
    pallas_call x1, Pallas kernels, tail_parts(): call(tail_body, 'tail_parts', (tiles,), 1, [pl.BlockSpec((4, share, depth...  18.5 us
    ppermute x1, waiting for transfers between devices, shards(): taken = lax.ppermute(give, 'gx', gx_move(1, 0))  17.9 us
    pallas_call x2, Pallas kernels, near_terms(): call(near_body, 'near_terms', (2,), 1, [pl.BlockSpec((share, chunk), lamb...  12.1 us
    pallas_call x1, Pallas kernels, first_parts(): call(first_body, 'first_parts', (hidden // TILE,), 1, [pl.BlockSpec((4 *...  10.8 us
    pallas_call x1, Pallas kernels, tail_last(): call(tail_last_body, 'tail_last', (tiles,), 1, [pl.BlockSpec((count, TILE...  9.17 us
    pallas_call x1, Pallas kernels, head_last(): call(head_last_body, 'head_last', (2,), 1, [block] * 4 + [pl.BlockSpec((s...  5.24 us
    convert_element_type x1, other arithmetic, shards(): grad_down = add(keep, taken).astype(bf16)  4.19 us
  transfers between devices with their start and end apart: 24, of which 7 were waited for; matrix products, arithmetic and copies ran while one was open for 13% of the time, Pallas kernels for 45%

profile of v6, /device:TPU:0, one launch (start us, length us, event | category | flops | bytes accessed | tf_op | source)
XLA Modules:
  0.0 175.8 jit_solution(16729666439597393231)
XLA Ops:
  0.6 0.0 copy-start
  0.6 0.1 collective-permute-start
  0.7 1.9 %slice_bitcast_fusion.1 = (bf16[1,160,1152]{2,1,0:T(8,128)(2,1)}, bf16[160,1152]{1,0:T(8,128)(2,1)S(1)}) fusion(bf16[512,1152]{1,0:T(8,128)(2,1)} %own.3), kind=kLoop, calls=%fused_computation.17 | loop fusion | bytes 1105920 | tf_op jit(solution)/shard_map/stack | solution.py:340
  2.6 1.6 collective-permute-start.1
  4.2 0.9 slice.23
  5.1 0.6 stack.101.table
  5.8 6.0 %near_terms.2.refs_2_ = bf16[2,384,1152]{2,1,0:T(8,128)(2,1)} custom-call(s32[18]{0:T(128)} %stack.101.table, bf16[2048,3072]{1,0:T(8,128)(2,1)} %pre.3, bf16[2048,3072]{1,0:T(8,128)(2,1)} %pre.3, bf16[512,1152]{1,0:T(8,128)(2,1)} %own.3, bf16[512,1152]{1,0:T(8,128)(2,1)} %collective-permute-done.partner), custom_call_target="tpu_custom_call" | custom-call | flops 28311552 | bytes 89088 | tf_op jit(solution)/shard_map/near_terms/pallas_call | solution.py:247
  11.8 1.9 %collective-permute-done.1 = bf16[160,1152]{1,0:T(8,128)(2,1)} collective-permute-done((bf16[160,1152]{1,0:T(8,128)(2,1)S(1)}, bf16[160,1152]{1,0:T(8,128)(2,1)}, u32[]{:S(2)}, u32[]{:S(2)}) %collective-permute-start.1) | collective-permute-done | bytes 368672 | tf_op jit(solution)/shard_map/ppermute | solution.py:333
  13.6 1.6 collective-permute-start.3
  15.2 1.0 slice_bitcast_fusion
  16.3 2.6 %pad_maximum_fusion.1 = bf16[4,160,1152]{2,1,0:T(8,128)(2,1)} fusion(bf16[1,160,1152]{2,1,0:T(8,128)(2,1)S(1)} %bitcast.32, bf16[1,160,1152]{2,1,0:T(8,128)(2,1)} %bitcast.19, bf16[1,160,1152]{2,1,0:T(8,128)(2,1)S(1)} %slice_bitcast_fusion, bf16[1,160,1152]{2,1,0:T(8,128)(2,1)} %get-tuple-element.102), kind=kLoop, calls=%fused_computation.9 | loop fusion | flops 2211840 | bytes 2949120 | tf_op jit(solution)/shard_map/stack | solution.py:340
  18.9 10.8 %first_parts.1 = (bf16[160,3072]{1,0:T(8,128)(2,1)}, bf16[160,3072]{1,0:T(8,128)(2,1)}, bf16[160,3072]{1,0:T(8,128)(2,1)}, bf16[160,3072]{1,0:T(8,128)(2,1)}) custom-call(s32[18]{0:T(128)} %stack.101.table, bf16[640,1152]{1,0:T(8,128)(2,1)} %bitcast.29, bf16[3072,1152]{1,0:T(8,128)(2,1)} %weights.3), custom_call_target="tpu_custom_call" | custom-call | flops 70778880 | bytes 195072 | tf_op jit(solution)/shard_map/first_parts/pallas_call | solution.py:95
  29.7 1.9 %collective-permute-start.8 = (bf16[160,3072]{1,0:T(8,128)(2,1)}, bf16[160,3072]{1,0:T(8,128)(2,1)}, u32[]{:S(2)}, u32[]{:S(2)}) collective-permute-start(bf16[160,3072]{1,0:T(8,128)(2,1)} %get-tuple-element.63), channel_id=1, source_target_pairs={{0,1},{1,2},{2,3},{3,0},{4,5},{5,6},{6,7},{7,4},{8,9},{9,10},{10,1... | collective-permute-start | bytes 2949128 | tf_op jit(solution)/shard_map/ppermute | solution.py:344
  31.6 2.2 %collective-permute-start.9 = (bf16[160,3072]{1,0:T(8,128)(2,1)}, bf16[160,3072]{1,0:T(8,128)(2,1)}, u32[]{:S(2)}, u32[]{:S(2)}) collective-permute-start(bf16[160,3072]{1,0:T(8,128)(2,1)} %get-tuple-element.64), channel_id=1, source_target_pairs={{0,3},{1,0},{2,1},{3,2},{4,7},{5,4},{6,5},{7,6},{8,11},{9,8},{10,9... | collective-permute-start | bytes 2949128 | tf_op jit(solution)/shard_map/ppermute | solution.py:345
  33.7 1.8 %collective-permute-start.10 = (bf16[160,3072]{1,0:T(8,128)(2,1)}, bf16[160,3072]{1,0:T(8,128)(2,1)}, u32[]{:S(2)}, u32[]{:S(2)}) collective-permute-start(bf16[160,3072]{1,0:T(8,128)(2,1)} %get-tuple-element.65), channel_id=1, source_target_pairs={{0,2},{1,3},{2,0},{3,1},{4,6},{5,7},{6,4},{7,5},{8,10},{9,11},{10,... | collective-permute-start | bytes 2949128 | tf_op jit(solution)/shard_map/ppermute | solution.py:346
  35.6 6.1 %near_terms.3.refs_2_ = bf16[2,384,1152]{2,1,0:T(8,128)(2,1)} custom-call(s32[18]{0:T(128)} %stack.101.table, bf16[2048,3072]{1,0:T(8,128)(2,1)} %pre.3, bf16[2048,3072]{1,0:T(8,128)(2,1)} %pre.3, bf16[512,1152]{1,0:T(8,128)(2,1)} %own.3, bf16[512,1152]{1,0:T(8,128)(2,1)} %collective-permute-done.partner), custom_call_target="tpu_custom_call" | custom-call | flops 28311552 | bytes 89088 | tf_op jit(solution)/shard_map/near_terms/pallas_call | solution.py:247
  41.6 1.0 constant_dynamic-update-slice_fusion.4
  42.6 0.0 collective-permute-done.3
  42.7 0.1 fusion
  42.7 0.1 collective-permute-start.7
  42.8 0.0 copy-start.1
  42.8 0.5 collective-permute-start.4
  43.3 1.1 pad_maximum_fusion.2
  44.4 0.1 collective-permute-done.4
  44.5 0.3 collective-permute-start.5
  44.8 1.1 collective-permute-done.5
  46.0 0.3 collective-permute-start.6
  46.3 1.1 collective-permute-done.6
  47.5 3.6 %pad_maximum_fusion.refs_3_.rows.refs_4_ = bf16[4,512,1152]{2,1,0:T(8,128)(2,1)} fusion(bf16[1,512,1152]{2,1,0:T(8,128)(2,1)S(1)} %bitcast.31, bf16[1,512,1152]{2,1,0:T(8,128)(2,1)S(1)} %bitcast.30, bf16[1,512,1152]{2,1,0:T(8,128)(2,1)} %bitcast.23, bf16[1,512,1152]{2,1,0:T(8,128)(2,1)S(1)} %bitcast.28), kind=kLoop, calls=%fused_computation | loop fusion | flops 7077888 | bytes 9437184 | tf_op jit(solution)/shard_map/stack | solution.py:356
  51.1 6.9 %terms.4 = (bf16[384,1152]{1,0:T(8,128)(2,1)}, bf16[384,1152]{1,0:T(8,128)(2,1)}) custom-call(s32[18]{0:T(128)} %stack.101.table, bf16[2048,3072]{1,0:T(8,128)(2,1)} %pre.3, bf16[2048,3072]{1,0:T(8,128)(2,1)} %pre.3, bf16[2,384,1152]{2,1,0:T(8,128)(2,1)} %near_terms.2.refs_2_, bf16[4,512,1152]{2,1,0:T(8,128)(2,1)} %pad_maximum_fusion.refs_3_.rows.refs_4_), custom_call_target="tpu_custom_call" | custom-call | flops 28311552 | bytes 61440 | tf_op jit(solution)/shard_map/terms/pallas_call | solution.py:298
  58.0 3.0 %collective-permute-start.11 = (bf16[384,1152]{1,0:T(8,128)(2,1)}, bf16[384,1152]{1,0:T(8,128)(2,1)S(1)}, u32[]{:S(2)}, u32[]{:S(2)}) collective-permute-start(bf16[384,1152]{1,0:T(8,128)(2,1)} %get-tuple-element.59), channel_id=1, source_target_pairs={{0,48},{16,0},{32,16},{48,32},{64,112},{80,64},{96,80},{112,96},{1... | collective-permute-start | bytes 2654216 | tf_op jit(solution)/shard_map/ppermute | solution.py:367
  61.0 18.5 %tail_parts.1 = (bf16[352,1536]{1,0:T(8,128)(2,1)}, bf16[352,1536]{1,0:T(8,128)(2,1)}, bf16[352,1536]{1,0:T(8,128)(2,1)}, bf16[352,1536]{1,0:T(8,128)(2,1)}, bf1...) custom-call(s32[18]{0:T(128)} %stack.101.table, ...), custom_call_target="tpu_custom_call" | custom-call | flops 155713536 | bytes 319488 | tf_op jit(solution)/shard_map/tail_parts/pallas_call | solution.py:148
  79.5 0.0 collective-permute-done.8.one
  79.5 0.0 collective-permute-done.10.three
  79.5 1.3 collective-permute-start.14
  80.8 2.2 %collective-permute-start.13 = (bf16[352,1536]{1,0:T(8,128)(2,1)}, bf16[352,1536]{1,0:T(8,128)(2,1)}, u32[]{:S(2)}, u32[]{:S(2)}) collective-permute-start(bf16[352,1536]{1,0:T(8,128)(2,1)} %get-tuple-element.75), channel_id=1, source_target_pairs={{0,3},{1,0},{2,1},{3,2},{4,7},{5,4},{6,5},{7,6},{8,11},{9,8},{10,9... | collective-permute-start | bytes 3244040 | tf_op jit(solution)/shard_map/ppermute | solution.py:372
  83.0 7.0 %terms.5 = (bf16[384,1152]{1,0:T(8,128)(2,1)}, bf16[384,1152]{1,0:T(8,128)(2,1)}) custom-call(s32[18]{0:T(128)} %stack.101.table, bf16[2048,3072]{1,0:T(8,128)(2,1)} %pre.3, bf16[2048,3072]{1,0:T(8,128)(2,1)} %pre.3, bf16[2,384,1152]{2,1,0:T(8,128)(2,1)} %near_terms.3.refs_2_, bf16[4,512,1152]{2,1,0:T(8,128)(2,1)} %pad_maximum_fusion.refs_3_.rows.refs_4_), custom_call_target="tpu_custom_call" | custom-call | flops 28311552 | bytes 61440 | tf_op jit(solution)/shard_map/terms/pallas_call | solution.py:298
  90.0 0.0 collective-permute-done.12
  90.0 0.0 collective-permute-done.11
  90.0 0.9 copy-done.5
  90.9 0.6 collective-permute-start.15
  91.5 2.7 %collective-permute-start.16 = (bf16[384,1152]{1,0:T(8,128)(2,1)}, bf16[384,1152]{1,0:T(8,128)(2,1)}, u32[]{:S(2)}, u32[]{:S(2)}) collective-permute-start(bf16[384,1152]{1,0:T(8,128)(2,1)} %get-tuple-element.84), channel_id=1, source_target_pairs={{0,48},{16,0},{32,16},{48,32},{64,112},{80,64},{96,80},{112,96},{1... | collective-permute-start | bytes 2654216 | tf_op jit(solution)/shard_map/ppermute | solution.py:379
  94.2 9.7 %terms.6 = (bf16[384,1152]{1,0:T(8,128)(2,1)}, bf16[384,1152]{1,0:T(8,128)(2,1)}) custom-call(s32[18]{0:T(128)} %stack.101.table, bf16[2048,3072]{1,0:T(8,128)(2,1)} %pre.3, bf16[2048,3072]{1,0:T(8,128)(2,1)} %pre.3, bf16[2048,3072]{1,0:T(8,128)(2,1)} %pre.3, bf16[2048,3072]{1,0:T(8,128)(2,1)} %pre.3, bf16[4,512,1152]{2,1,0:T(8,128)(2,1)} %pad_maximum_fusion.refs_3_.rows.refs_4_), custom_call_target="tpu_custom_call" | custom-call | flops 56623104 | bytes 122880 | tf_op jit(solution)/shard_map/terms/pallas_call | solution.py:298
  103.8 3.3 %collective-permute-done.14 = bf16[352,1536]{1,0:T(8,128)(2,1)} collective-permute-done((bf16[352,1536]{1,0:T(8,128)(2,1)}, bf16[352,1536]{1,0:T(8,128)(2,1)}, u32[]{:S(2)}, u32[]{:S(2)}) %collective-permute-start.14) | collective-permute-done | bytes 1081376 | tf_op jit(solution)/shard_map/ppermute | solution.py:373
  107.1 0.0 collective-permute-done.13
  107.1 0.2 collective-permute-start.17
  107.3 3.1 %collective-permute-start.18 = (bf16[352,1536]{1,0:T(8,128)(2,1)}, bf16[352,1536]{1,0:T(8,128)(2,1)}, u32[]{:S(2)}, u32[]{:S(2)}) collective-permute-start(bf16[352,1536]{1,0:T(8,128)(2,1)} %get-tuple-element.92), channel_id=1, source_target_pairs={{0,3},{1,0},{2,1},{3,2},{4,7},{5,4},{6,5},{7,6},{8,11},{9,8},{10,9... | collective-permute-start | bytes 3244040 | tf_op jit(solution)/shard_map/ppermute | solution.py:385
  110.4 3.7 %add_convert_fusion.3 = (bf16[384,1152]{1,0:T(8,128)(2,1)}, bf16[384,1152]{1,0:T(8,128)(2,1)}) fusion(bf16[384,1152]{1,0:T(8,128)(2,1)} %collective-permute-done.12, bf16[384,1152]{1,0:T(8,128)(2,1)} %get-tuple-element.98, bf16[384,1152]{1,0:T(8,128)(2,1)} %copy-done.5, bf16[384,1152]{1,0:T(8,128)(2,1)} %get-tuple-element.71), kind=kLoop, calls=%fused_computation.6 | loop fusion | flops 3538944 | bytes 5308416 | tf_op jit(solution)/shard_map/convert_element_type | solution.py:389
  114.1 0.0 collective-permute-done.15
  114.1 0.0 collective-permute-done.16
  114.1 0.5 collective-permute-start.22
  114.6 2.8 %collective-permute-start.21 = (bf16[384,1152]{1,0:T(8,128)(2,1)}, bf16[384,1152]{1,0:T(8,128)(2,1)}, u32[]{:S(2)}, u32[]{:S(2)}) collective-permute-start(bf16[384,1152]{1,0:T(8,128)(2,1)} %get-tuple-element.95), channel_id=1, source_target_pairs={{0,48},{16,0},{32,16},{48,32},{64,112},{80,64},{96,80},{112,96},{1... | collective-permute-start | bytes 2654216 | tf_op jit(solution)/shard_map/ppermute | solution.py:392
  117.4 3.5 %add_convert_fusion = (bf16[352,1536]{1,0:T(8,128)(2,1)}, bf16[352,1536]{1,0:T(8,128)(2,1)}) fusion(bf16[352,1536]{1,0:T(8,128)(2,1)} %collective-permute-done.14, bf16[352,1536]{1,0:T(8,128)(2,1)S(1)} %copy-done.4, bf16[352,1536]{1,0:T(8,128)(2,1)} %collective-permute-done.13, bf16[352,1536]{1,0:T(8,128)(2,1)S(1)} %copy-done.3), kind=kLoop, calls=%fused_computation.1 | loop fusion | flops 4325376 | bytes 6488064 | tf_op jit(solution)/shard_map/convert_element_type | solution.py:387
  121.0 9.7 %terms.7 = (bf16[384,1152]{1,0:T(8,128)(2,1)}, bf16[384,1152]{1,0:T(8,128)(2,1)}) custom-call(s32[18]{0:T(128)} %stack.101.table, bf16[2048,3072]{1,0:T(8,128)(2,1)} %pre.3, bf16[2048,3072]{1,0:T(8,128)(2,1)} %pre.3, bf16[2048,3072]{1,0:T(8,128)(2,1)} %pre.3, bf16[2048,3072]{1,0:T(8,128)(2,1)} %pre.3, bf16[4,512,1152]{2,1,0:T(8,128)(2,1)} %pad_maximum_fusion.refs_3_.rows.refs_4_), custom_call_target="tpu_custom_call" | custom-call | flops 56623104 | bytes 122880 | tf_op jit(solution)/shard_map/terms/pallas_call | solution.py:298
  130.6 5.2 %head_last.1.held = bf16[160,3072]{1,0:T(8,128)(2,1)} custom-call(s32[18]{0:T(128)} %stack.101.table, bf16[160,3072]{1,0:T(8,128)(2,1)} %get-tuple-element.54.own, bf16[160,3072]{1,0:T(8,128)(2,1)} %collective-permute-done.8.one, bf16[160,3072]{1,0:T(8,128)(2,1)} %collective-permute-done.9.two, bf16[160,3072]{1,0:T(8,128)(2,1)} %collective-permute-done.10.three, ...), custom_call_target="tpu_custom_call" | custom-call | flops 307200 | bytes 92160 | tf_op jit(solution)/shard_map/head_last/pallas_call | solution.py:177
  135.8 1.8 %collective-permute-start.19 = (bf16[352,1536]{1,0:T(8,128)(2,1)}, bf16[352,1536]{1,0:T(8,128)(2,1)}, u32[]{:S(2)}, u32[]{:S(2)}) collective-permute-start(bf16[352,1536]{1,0:T(8,128)(2,1)} %get-tuple-element.93), channel_id=1, source_target_pairs={{0,3},{1,0},{2,1},{3,2},{4,7},{5,4},{6,5},{7,6},{8,11},{9,8},{10,9... | collective-permute-start | bytes 3244040 | tf_op jit(solution)/shard_map/ppermute | solution.py:402
  137.7 0.3 collective-permute-start.20
  138.0 2.9 %select_convert_fusion = bf16[384,1152]{1,0:T(8,128)(2,1)S(1)} fusion(bf16[384,1152]{1,0:T(8,128)(2,1)} %collective-permute-done.21, bf16[384,1152]{1,0:T(8,128)(2,1)S(1)} %collective-permute-done.15, bf16[384,1152]{1,0:T(8,128)(2,1)} %get-tuple-element.86, bf16[384,1152]{1,0:T(8,128)(2,1)} %collective-permute-done.22, ...), kind=kLoop, calls=%fused_computation.4 | loop fusion | flops 5308416 | bytes 6193153 | tf_op jit(solution)/shard_map/convert_element_type | solution.py:409
  140.9 2.8 %collective-permute-start.23 = (bf16[384,1152]{1,0:T(8,128)(2,1)S(1)}, bf16[384,1152]{1,0:T(8,128)(2,1)}, u32[]{:S(2)}, u32[]{:S(2)}) collective-permute-start(bf16[384,1152]{1,0:T(8,128)(2,1)S(1)} %select_convert_fusion), channel_id=1, source_target_pairs={{0,64},{16,80},{32,96},{48,112},{64,0},{80,16},{96,32},{112,48},{1... | collective-permute-start | bytes 2654216 | tf_op jit(solution)/shard_map/ppermute | solution.py:410
  143.7 17.9 %collective-permute-done.23 = bf16[384,1152]{1,0:T(8,128)(2,1)} collective-permute-done((bf16[384,1152]{1,0:T(8,128)(2,1)S(1)}, bf16[384,1152]{1,0:T(8,128)(2,1)}, u32[]{:S(2)}, u32[]{:S(2)}) %collective-permute-start.23) | collective-permute-done | bytes 884768 | tf_op jit(solution)/shard_map/ppermute | solution.py:410
  161.6 0.0 collective-permute-done.19.sum_a
  161.6 0.8 collective-permute-done.20.sum_b
  162.4 9.2 %tail_last.1 = bf16[512,3072]{1,0:T(8,128)(2,1)} custom-call(s32[18]{0:T(128)} %stack.101.table, bf16[352,3072]{1,0:T(8,128)(2,1)} %get-tuple-element.61.own, bf16[352,1536]{1,0:T(8,128)(2,1)} %collective-permute-done.17.side_a, bf16[352,1536]{1,0:T(8,128)(2,1)} %collective-permute-done.19.sum_a, bf16[352,1536]{1,0:T(8,128)(2,1)} %collective-permute-done.18.side_b, ...), custom_call_target="tpu_custom_call" | custom-call | flops 43253760 | bytes 10813440 | tf_op jit(solution)/shard_map/tail_last/pallas_call | solution.py:216
  171.6 4.2 %add_convert_fusion.2 = bf16[384,1152]{1,0:T(8,128)(2,1)} fusion(bf16[384,1152]{1,0:T(8,128)(2,1)} %collective-permute-done.23, bf16[384,1152]{1,0:T(8,128)(2,1)} %collective-permute-done.21, bf16[384,1152]{1,0:T(8,128)(2,1)S(1)} %collective-permute-done.15, bf16[384,1152]{1,0:T(8,128)(2,1)} %get-tuple-element.86, ...), kind=kLoop, calls=%fused_computation.3 | loop fusion | flops 6193152 | bytes 7077889 | tf_op jit(solution)/shard_map/convert_element_type | solution.py:414
  (24 shorter events, 0.2 us)
Async XLA Ops:
  0.6 3.6 %copy-start = (bf16[512,1152]{1,0:T(8,128)(2,1)S(1)}, bf16[512,1152]{1,0:T(8,128)(2,1)}, u32[]{:S(2)}) copy-start(bf16[512,1152]{1,0:T(8,128)(2,1)} %own.3) | copy-start | bytes 3538948
  0.6 5.1 %collective-permute-start = (bf16[512,1152]{1,0:T(8,128)(2,1)}, bf16[512,1152]{1,0:T(8,128)(2,1)}, u32[]{:S(2)}, u32[]{:S(2)}) collective-permute-start(bf16[512,1152]{1,0:T(8,128)(2,1)} %own.3), channel_id=1, source_target_pairs={{0,4},{4,0},{8,12},{12,8},{1,5},{5,1},{9,13},{13,9},{2,6},{6,2},{1... | collective-permute-start | bytes 3538952 | tf_op jit(solution)/shard_map/ppermute | solution.py:334
  2.6 11.0 %collective-permute-start.1 = (bf16[160,1152]{1,0:T(8,128)(2,1)S(1)}, bf16[160,1152]{1,0:T(8,128)(2,1)}, u32[]{:S(2)}, u32[]{:S(2)}) collective-permute-start(bf16[160,1152]{1,0:T(8,128)(2,1)S(1)} %get-tuple-element.103), channel_id=1, source_target_pairs={{0,8},{4,12},{8,0},{12,4},{1,9},{5,13},{9,1},{13,5},{2,10},{6,14},... | collective-permute-start | bytes 1105928 | tf_op jit(solution)/shard_map/ppermute | solution.py:333
  13.6 2.6 %collective-permute-start.2 = (bf16[160,1152]{1,0:T(8,128)(2,1)}, bf16[160,1152]{1,0:T(8,128)(2,1)S(1)}, u32[]{:S(2)}, u32[]{:S(2)}) collective-permute-start(bf16[160,1152]{1,0:T(8,128)(2,1)} %collective-permute-done.1), channel_id=1, source_target_pairs={{0,4},{4,0},{8,12},{12,8},{1,5},{5,1},{9,13},{13,9},{2,6},{6,2},{1... | collective-permute-start | bytes 1105928 | tf_op jit(solution)/shard_map/ppermute | solution.py:337
  13.6 29.0 %collective-permute-start.3 = (bf16[352,1152]{1,0:T(8,128)(2,1)}, bf16[352,1152]{1,0:T(8,128)(2,1)S(1)}, u32[]{:S(2)}, u32[]{:S(2)}) collective-permute-start(bf16[352,1152]{1,0:T(8,128)(2,1)} %slice.23), channel_id=1, source_target_pairs={{0,8},{4,12},{8,0},{12,4},{1,9},{5,13},{9,1},{13,5},{2,10},{6,14},... | collective-permute-start | bytes 2433032 | tf_op jit(solution)/shard_map/ppermute | solution.py:338
  16.2 2.6 %copy-start.2 = (bf16[160,1152]{1,0:T(8,128)(2,1)}, bf16[160,1152]{1,0:T(8,128)(2,1)S(1)}, u32[]{:S(2)}) copy-start(bf16[160,1152]{1,0:T(8,128)(2,1)S(1)} %collective-permute-done.2) | copy-start | bytes 1105924
  29.7 49.9 %collective-permute-start.8 = (bf16[160,3072]{1,0:T(8,128)(2,1)}, bf16[160,3072]{1,0:T(8,128)(2,1)}, u32[]{:S(2)}, u32[]{:S(2)}) collective-permute-start(bf16[160,3072]{1,0:T(8,128)(2,1)} %get-tuple-element.63), channel_id=1, source_target_pairs={{0,1},{1,2},{2,3},{3,0},{4,5},{5,6},{6,7},{7,4},{8,9},{9,10},{10,1... | collective-permute-start | bytes 2949128 | tf_op jit(solution)/shard_map/ppermute | solution.py:344
  31.6 48.0 %collective-permute-start.9 = (bf16[160,3072]{1,0:T(8,128)(2,1)}, bf16[160,3072]{1,0:T(8,128)(2,1)}, u32[]{:S(2)}, u32[]{:S(2)}) collective-permute-start(bf16[160,3072]{1,0:T(8,128)(2,1)} %get-tuple-element.64), channel_id=1, source_target_pairs={{0,3},{1,0},{2,1},{3,2},{4,7},{5,4},{6,5},{7,6},{8,11},{9,8},{10,9... | collective-permute-start | bytes 2949128 | tf_op jit(solution)/shard_map/ppermute | solution.py:345
  33.7 45.8 %collective-permute-start.10 = (bf16[160,3072]{1,0:T(8,128)(2,1)}, bf16[160,3072]{1,0:T(8,128)(2,1)}, u32[]{:S(2)}, u32[]{:S(2)}) collective-permute-start(bf16[160,3072]{1,0:T(8,128)(2,1)} %get-tuple-element.65), channel_id=1, source_target_pairs={{0,2},{1,3},{2,0},{3,1},{4,6},{5,7},{6,4},{7,5},{8,10},{9,11},{10,... | collective-permute-start | bytes 2949128 | tf_op jit(solution)/shard_map/ppermute | solution.py:346
  42.7 4.8 %collective-permute-start.7 = (bf16[64,1152]{1,0:T(8,128)(2,1)S(1)}, bf16[64,1152]{1,0:T(8,128)(2,1)S(1)}, u32[]{:S(2)}, u32[]{:S(2)}) collective-permute-start(bf16[64,1152]{1,0:T(8,128)(2,1)S(1)} %slice.27), channel_id=1, source_target_pairs={{0,4},{4,0},{8,12},{12,8},{1,5},{5,1},{9,13},{13,9},{2,6},{6,2},{1... | collective-permute-start | bytes 442376 | tf_op jit(solution)/shard_map/ppermute | solution.py:353
  42.8 4.7 %copy-start.1 = (bf16[512,1152]{1,0:T(8,128)(2,1)S(1)}, bf16[512,1152]{1,0:T(8,128)(2,1)}, u32[]{:S(2)}) copy-start(bf16[512,1152]{1,0:T(8,128)(2,1)} %own.3) | copy-start | bytes 3538948
  42.8 1.7 collective-permute-start.4
  44.5 1.5 collective-permute-start.5
  46.0 1.5 collective-permute-start.6
  58.0 32.0 %collective-permute-start.11 = (bf16[384,1152]{1,0:T(8,128)(2,1)}, bf16[384,1152]{1,0:T(8,128)(2,1)S(1)}, u32[]{:S(2)}, u32[]{:S(2)}) collective-permute-start(bf16[384,1152]{1,0:T(8,128)(2,1)} %get-tuple-element.59), channel_id=1, source_target_pairs={{0,48},{16,0},{32,16},{48,32},{64,112},{80,64},{96,80},{112,96},{1... | collective-permute-start | bytes 2654216 | tf_op jit(solution)/shard_map/ppermute | solution.py:367
  61.0 29.0 %collective-permute-start.12 = (bf16[384,1152]{1,0:T(8,128)(2,1)}, bf16[384,1152]{1,0:T(8,128)(2,1)}, u32[]{:S(2)}, u32[]{:S(2)}) collective-permute-start(bf16[384,1152]{1,0:T(8,128)(2,1)} %get-tuple-element.69), channel_id=1, source_target_pairs={{0,16},{16,32},{32,48},{48,0},{64,80},{80,96},{96,112},{112,64},{1... | collective-permute-start | bytes 2654216 | tf_op jit(solution)/shard_map/ppermute | solution.py:368
  79.5 27.6 %collective-permute-start.14 = (bf16[352,1536]{1,0:T(8,128)(2,1)}, bf16[352,1536]{1,0:T(8,128)(2,1)}, u32[]{:S(2)}, u32[]{:S(2)}) collective-permute-start(bf16[352,1536]{1,0:T(8,128)(2,1)} %get-tuple-element.79), channel_id=1, source_target_pairs={{0,1},{1,2},{2,3},{3,0},{4,5},{5,6},{6,7},{7,4},{8,9},{9,10},{10,1... | collective-permute-start | bytes 3244040 | tf_op jit(solution)/shard_map/ppermute | solution.py:373
  80.8 26.3 %collective-permute-start.13 = (bf16[352,1536]{1,0:T(8,128)(2,1)}, bf16[352,1536]{1,0:T(8,128)(2,1)}, u32[]{:S(2)}, u32[]{:S(2)}) collective-permute-start(bf16[352,1536]{1,0:T(8,128)(2,1)} %get-tuple-element.75), channel_id=1, source_target_pairs={{0,3},{1,0},{2,1},{3,2},{4,7},{5,4},{6,5},{7,6},{8,11},{9,8},{10,9... | collective-permute-start | bytes 3244040 | tf_op jit(solution)/shard_map/ppermute | solution.py:372
  90.0 0.9 copy-start.5
  90.9 23.2 %collective-permute-start.15 = (bf16[384,1152]{1,0:T(8,128)(2,1)}, bf16[384,1152]{1,0:T(8,128)(2,1)S(1)}, u32[]{:S(2)}, u32[]{:S(2)}) collective-permute-start(bf16[384,1152]{1,0:T(8,128)(2,1)} %get-tuple-element.82), channel_id=1, source_target_pairs={{0,16},{16,32},{32,48},{48,0},{64,80},{80,96},{96,112},{112,64},{1... | collective-permute-start | bytes 2654216 | tf_op jit(solution)/shard_map/ppermute | solution.py:378
  91.5 22.6 %collective-permute-start.16 = (bf16[384,1152]{1,0:T(8,128)(2,1)}, bf16[384,1152]{1,0:T(8,128)(2,1)}, u32[]{:S(2)}, u32[]{:S(2)}) collective-permute-start(bf16[384,1152]{1,0:T(8,128)(2,1)} %get-tuple-element.84), channel_id=1, source_target_pairs={{0,48},{16,0},{32,16},{48,32},{64,112},{80,64},{96,80},{112,96},{1... | collective-permute-start | bytes 2654216 | tf_op jit(solution)/shard_map/ppermute | solution.py:379
  107.1 28.7 %collective-permute-start.17 = (bf16[352,1536]{1,0:T(8,128)(2,1)}, bf16[352,1536]{1,0:T(8,128)(2,1)}, u32[]{:S(2)}, u32[]{:S(2)}) collective-permute-start(bf16[352,1536]{1,0:T(8,128)(2,1)} %get-tuple-element.90), channel_id=1, source_target_pairs={{0,1},{1,2},{2,3},{3,0},{4,5},{5,6},{6,7},{7,4},{8,9},{9,10},{10,1... | collective-permute-start | bytes 3244040 | tf_op jit(solution)/shard_map/ppermute | solution.py:384
  107.3 28.6 %collective-permute-start.18 = (bf16[352,1536]{1,0:T(8,128)(2,1)}, bf16[352,1536]{1,0:T(8,128)(2,1)}, u32[]{:S(2)}, u32[]{:S(2)}) collective-permute-start(bf16[352,1536]{1,0:T(8,128)(2,1)} %get-tuple-element.92), channel_id=1, source_target_pairs={{0,3},{1,0},{2,1},{3,2},{4,7},{5,4},{6,5},{7,6},{8,11},{9,8},{10,9... | collective-permute-start | bytes 3244040 | tf_op jit(solution)/shard_map/ppermute | solution.py:385
  110.4 7.1 %copy-start.3 = (bf16[352,1536]{1,0:T(8,128)(2,1)S(1)}, bf16[352,1536]{1,0:T(8,128)(2,1)}, u32[]{:S(2)}) copy-start(bf16[352,1536]{1,0:T(8,128)(2,1)} %get-tuple-element.73) | copy-start | bytes 3244036
  110.4 7.1 %copy-start.4 = (bf16[352,1536]{1,0:T(8,128)(2,1)S(1)}, bf16[352,1536]{1,0:T(8,128)(2,1)}, u32[]{:S(2)}) copy-start(bf16[352,1536]{1,0:T(8,128)(2,1)} %get-tuple-element.77) | copy-start | bytes 3244036
  114.1 23.8 %collective-permute-start.22 = (bf16[384,1152]{1,0:T(8,128)(2,1)}, bf16[384,1152]{1,0:T(8,128)(2,1)}, u32[]{:S(2)}, u32[]{:S(2)}) collective-permute-start(bf16[384,1152]{1,0:T(8,128)(2,1)} %get-tuple-element.99), channel_id=1, source_target_pairs={{0,16},{16,32},{32,48},{48,0},{64,80},{80,96},{96,112},{112,64},{1... | collective-permute-start | bytes 2654216 | tf_op jit(solution)/shard_map/ppermute | solution.py:393
  114.6 23.3 %collective-permute-start.21 = (bf16[384,1152]{1,0:T(8,128)(2,1)}, bf16[384,1152]{1,0:T(8,128)(2,1)}, u32[]{:S(2)}, u32[]{:S(2)}) collective-permute-start(bf16[384,1152]{1,0:T(8,128)(2,1)} %get-tuple-element.95), channel_id=1, source_target_pairs={{0,48},{16,0},{32,16},{48,32},{64,112},{80,64},{96,80},{112,96},{1... | collective-permute-start | bytes 2654216 | tf_op jit(solution)/shard_map/ppermute | solution.py:392
  135.8 25.7 %collective-permute-start.19 = (bf16[352,1536]{1,0:T(8,128)(2,1)}, bf16[352,1536]{1,0:T(8,128)(2,1)}, u32[]{:S(2)}, u32[]{:S(2)}) collective-permute-start(bf16[352,1536]{1,0:T(8,128)(2,1)} %get-tuple-element.93), channel_id=1, source_target_pairs={{0,3},{1,0},{2,1},{3,2},{4,7},{5,4},{6,5},{7,6},{8,11},{9,8},{10,9... | collective-permute-start | bytes 3244040 | tf_op jit(solution)/shard_map/ppermute | solution.py:402
  137.7 24.8 %collective-permute-start.20 = (bf16[352,1536]{1,0:T(8,128)(2,1)}, bf16[352,1536]{1,0:T(8,128)(2,1)}, u32[]{:S(2)}, u32[]{:S(2)}) collective-permute-start(bf16[352,1536]{1,0:T(8,128)(2,1)} %get-tuple-element.94), channel_id=1, source_target_pairs={{0,1},{1,2},{2,3},{3,0},{4,5},{5,6},{6,7},{7,4},{8,9},{9,10},{10,1... | collective-permute-start | bytes 3244040 | tf_op jit(solution)/shard_map/ppermute | solution.py:403
  140.9 20.7 %collective-permute-start.23 = (bf16[384,1152]{1,0:T(8,128)(2,1)S(1)}, bf16[384,1152]{1,0:T(8,128)(2,1)}, u32[]{:S(2)}, u32[]{:S(2)}) collective-permute-start(bf16[384,1152]{1,0:T(8,128)(2,1)S(1)} %select_convert_fusion), channel_id=1, source_target_pairs={{0,64},{16,80},{32,96},{48,112},{64,0},{80,16},{96,32},{112,48},{1... | collective-permute-start | bytes 2654216 | tf_op jit(solution)/shard_map/ppermute | solution.py:410

commit v7 on v6

--- a/solution.py
+++ b/solution.py
@@ -189,49 +189,92 @@
     )(table, own, *arrived, preact)
 
 
-def tail_last_body(table, own, side_a, sum_a, side_b, sum_b, pre, held, out):
+def ready_body(table, own, side_a, side_b, pre, held, partial, slope):
     head = held.shape[0]
-    slope = unit_slope(pre[head:].astype(f32))
+    slope[...] = unit_slope(pre[head:].astype(f32)).astype(bf16)
     total = own[...].astype(f32)
     first = pl.program_id(0) < pl.num_programs(0) // 2
-    out[:head] = held[...]
+    partial[:head] = held[...]
 
     @pl.when(first)
     def _():
-        whole = total + side_a[...].astype(f32) + sum_a[...].astype(f32)
-        out[head:] = (whole * slope).astype(bf16)
+        partial[head:] = (total + side_a[...].astype(f32)).astype(bf16)
 
     @pl.when(jnp.logical_not(first))
     def _():
-        whole = total + side_b[...].astype(f32) + sum_b[...].astype(f32)
-        out[head:] = (whole * slope).astype(bf16)
-
-
-def tail_last(own, side_a, sum_a, side_b, sum_b, preact, table, held):
+        partial[head:] = (total + side_b[...].astype(f32)).astype(bf16)
+
+
+def halves(count, hidden):
+    tiles = hidden // TILE
+    return [
+        pl.BlockSpec((count, TILE), lambda t, p: (0, jnp.minimum(t, tiles // 2 - 1))),
+        pl.BlockSpec((count, TILE), lambda t, p: (0, jnp.maximum(t - tiles // 2, 0))),
+    ]
+
+
+def tail_ready(own, side_a, side_b, preact, table, held):
     count, hidden = own.shape
     share = preact.shape[0] // 4
+    block = pl.BlockSpec((count, TILE), lambda t, p: (0, t))
+    return call(
+        ready_body,
+        "tail_ready",
+        (hidden // TILE,),
+        1,
+        [block]
+        + halves(count, hidden)
+        + [
+            pl.BlockSpec((share, TILE), lambda t, p: (p[GZ], t)),
+            pl.BlockSpec((share - count, TILE), lambda t, p: (0, t)),
+        ],
+        [pl.BlockSpec((share, TILE), lambda t, p: (0, t)), block],
+        [jax.ShapeDtypeStruct((share, hidden), bf16), jax.ShapeDtypeStruct((count, hidden), bf16)],
+        count * hidden * 40,
+        10 * count * hidden,
+        cost=SHORT,
+    )(table, own, side_a, side_b, preact, held)
+
+
+def tail_last_body(table, partial, slope, sum_a, sum_b, keep, taken, out, down):
+    head = out.shape[0] - slope.shape[0]
+    out[:head] = partial[:head]
+    down[...] = (keep[...] + taken[...].astype(f32)).astype(bf16)
+    total = partial[head:].astype(f32)
+    first = pl.program_id(0) < pl.num_programs(0) // 2
+
+    @pl.when(first)
+    def _():
+        out[head:] = ((total + sum_a[...].astype(f32)) * slope[...].astype(f32)).astype(bf16)
+
+    @pl.when(jnp.logical_not(first))
+    def _():
+        out[head:] = ((total + sum_b[...].astype(f32)) * slope[...].astype(f32)).astype(bf16)
+
+
+def tail_last(partial, slope, sum_a, sum_b, keep, taken, table):
+    count, hidden = slope.shape
+    share = partial.shape[0]
+    chunk, features = keep.shape
     tiles = hidden // TILE
-    half_a = pl.BlockSpec((count, TILE), lambda t, p: (0, jnp.minimum(t, tiles // 2 - 1)))
-    half_b = pl.BlockSpec((count, TILE), lambda t, p: (0, jnp.maximum(t - tiles // 2, 0)))
+    whole = pl.BlockSpec((share, TILE), lambda t, p: (0, t))
+    down = pl.BlockSpec((chunk // tiles, features), lambda t, p: (t, 0))
     return call(
         tail_last_body,
         "tail_last",
         (tiles,),
         1,
+        [whole, pl.BlockSpec((count, TILE), lambda t, p: (0, t))]
+        + halves(count, hidden)
+        + [down, down],
+        [whole, down],
         [
-            pl.BlockSpec((count, TILE), lambda t, p: (0, t)),
-            half_a,
-            half_a,
-            half_b,
-            half_b,
-            pl.BlockSpec((share, TILE), lambda t, p: (p[GZ], t)),
-            pl.BlockSpec((share - count, TILE), lambda t, p: (0, t)),
+            jax.ShapeDtypeStruct((share, hidden), bf16),
+            jax.ShapeDtypeStruct((chunk, features), bf16),
         ],
-        pl.BlockSpec((share, TILE), lambda t, p: (0, t)),
-        jax.ShapeDtypeStruct((share, hidden), bf16),
-        count * hidden * 40,
+        count * hidden * 4,
         10 * count * hidden,
-    )(table, own, side_a, sum_a, side_b, sum_b, preact, held)
+    )(table, partial, slope, sum_a, sum_b, keep, taken)
 
 
 def near_body(table, pre_own, pre_partner, own, partner, out):
@@ -408,10 +451,9 @@
     keep = jnp.where(h == 0, c_own, d_own)
     give = jnp.where(h == 0, d_own, c_own).astype(bf16)
     taken = lax.ppermute(give, "gx", gx_move(1, 0))
-    taken = after(taken, a_sum, b_sum)
-
-    grad_pre = tail_last(own_tail, a_side, a_sum, b_side, b_sum, preact, table, held)
-    grad_down = add(keep, taken).astype(bf16)
+    own_tail = after(own_tail, give)
+    partial, slope = tail_ready(own_tail, a_side, b_side, preact, table, held)
+    grad_pre, grad_down = tail_last(partial, slope, a_sum, b_sum, keep, taken, table)
     return (grad_pre, grad_down)
 
 

time: 176 us -> 173 us (0.983)
  waiting for transfers between devices: 26.3 us -> 17 us
  Pallas kernels: 89 us -> 96.5 us
  other arithmetic: 21.6 us -> 19 us
    ppermute x1, waiting for transfers between devices: 17.9 us -> 8.96 us  [shards(): taken = lax.ppermute(give, 'gx', gx_move(1, 0))]
    pallas_call x1 -> x2, Pallas kernels: 9.17 us -> 16.7 us  [the longest x1 8.67 us: tail_ready(): call(ready_body, 'tail_ready', (hidden // TILE,), 1, [block] + halves(cou...]
    convert_element_type x2 -> x0, other arithmetic: 7.08 us -> none  [the longest x1 4.19 us: shards(): grad_down = add(keep, taken).astype(bf16)]
    select_n x0 -> x1, other arithmetic: none -> 4.44 us  [shards(): keep = jnp.where(h == 0, c_own, d_own)]
  transfers between devices with their start and end apart: 24 -> 24, of which waited for: 7 -> 7; matrix products, arithmetic and copies ran while one was open for 13% -> 14% of each run, Pallas kernels for 45% -> 51%
where the time goes in v7:
time: 173 us; the launch traced here: 172 us
  Pallas kernels  96.5 us (56%)
  starting transfers between devices  31.1 us (18%)
  other arithmetic  19 us (11%)
  waiting for transfers between devices  17 us (10%)
  local copies, waits for them, and re-layouts  7.62 us (4%)
    pallas_call x4, Pallas kernels, terms(): call(functools.partial(terms_body, near), 'terms', (2,), 1, [source(j) fo...  33.3 us
    pallas_call x1, Pallas kernels, tail_parts(): call(tail_body, 'tail_parts', (tiles,), 1, [pl.BlockSpec((4, share, depth...  18.5 us
    pallas_call x2, Pallas kernels, near_terms(): call(near_body, 'near_terms', (2,), 1, [pl.BlockSpec((share, chunk), lamb...  12 us
    pallas_call x1, Pallas kernels, first_parts(): call(first_body, 'first_parts', (hidden // TILE,), 1, [pl.BlockSpec((4 *...  10.8 us
    ppermute x1, waiting for transfers between devices, shards(): taken = lax.ppermute(give, 'gx', gx_move(1, 0))  8.96 us
    pallas_call x1, Pallas kernels, tail_ready(): call(ready_body, 'tail_ready', (hidden // TILE,), 1, [block] + halves(cou...  8.67 us
    pallas_call x1, Pallas kernels, tail_last(): call(tail_last_body, 'tail_last', (tiles,), 1, [whole, pl.BlockSpec((coun...  8.01 us
    pallas_call x1, Pallas kernels, head_last(): call(head_last_body, 'head_last', (2,), 1, [block] * 4 + [pl.BlockSpec((s...  5.24 us
  transfers between devices with their start and end apart: 24, of which 7 were waited for; matrix products, arithmetic and copies ran while one was open for 14% of the time, Pallas kernels for 51%

profile of v7, /device:TPU:0, one launch (start us, length us, event | category | flops | bytes accessed | tf_op | source)
XLA Modules:
  0.0 172.0 jit_solution(15400985775239531751)
XLA Ops:
  0.6 0.0 copy-start
  0.6 0.1 collective-permute-start
  0.7 1.9 %slice_bitcast_fusion.1 = (bf16[1,160,1152]{2,1,0:T(8,128)(2,1)}, bf16[160,1152]{1,0:T(8,128)(2,1)S(1)}) fusion(bf16[512,1152]{1,0:T(8,128)(2,1)} %own.3), kind=kLoop, calls=%fused_computation.17 | loop fusion | bytes 1105920 | tf_op jit(solution)/shard_map/stack | solution.py:383
  2.6 1.6 collective-permute-start.1
  4.2 0.9 slice.23
  5.1 0.7 stack.101.table
  5.8 0.0 collective-permute-done.partner
  5.8 6.0 %near_terms.2.refs_2_ = bf16[2,384,1152]{2,1,0:T(8,128)(2,1)} custom-call(s32[18]{0:T(128)} %stack.101.table, bf16[2048,3072]{1,0:T(8,128)(2,1)} %pre.3, bf16[2048,3072]{1,0:T(8,128)(2,1)} %pre.3, bf16[512,1152]{1,0:T(8,128)(2,1)} %own.3, bf16[512,1152]{1,0:T(8,128)(2,1)} %collective-permute-done.partner), custom_call_target="tpu_custom_call" | custom-call | flops 28311552 | bytes 89088 | tf_op jit(solution)/shard_map/near_terms/pallas_call | solution.py:290
  11.8 1.8 %collective-permute-done.1 = bf16[160,1152]{1,0:T(8,128)(2,1)} collective-permute-done((bf16[160,1152]{1,0:T(8,128)(2,1)S(1)}, bf16[160,1152]{1,0:T(8,128)(2,1)}, u32[]{:S(2)}, u32[]{:S(2)}) %collective-permute-start.1) | collective-permute-done | bytes 368672 | tf_op jit(solution)/shard_map/ppermute | solution.py:376
  13.6 0.0 collective-permute-start.2
  13.6 1.6 collective-permute-start.3
  15.2 1.0 slice_bitcast_fusion
  16.2 2.6 %pad_maximum_fusion.1 = bf16[4,160,1152]{2,1,0:T(8,128)(2,1)} fusion(bf16[1,160,1152]{2,1,0:T(8,128)(2,1)S(1)} %bitcast.32, bf16[1,160,1152]{2,1,0:T(8,128)(2,1)} %bitcast.19, bf16[1,160,1152]{2,1,0:T(8,128)(2,1)S(1)} %slice_bitcast_fusion, bf16[1,160,1152]{2,1,0:T(8,128)(2,1)} %get-tuple-element.108), kind=kLoop, calls=%fused_computation.8 | loop fusion | flops 2211840 | bytes 2949120 | tf_op jit(solution)/shard_map/stack | solution.py:383
  18.8 10.8 %first_parts.1 = (bf16[160,3072]{1,0:T(8,128)(2,1)}, bf16[160,3072]{1,0:T(8,128)(2,1)}, bf16[160,3072]{1,0:T(8,128)(2,1)}, bf16[160,3072]{1,0:T(8,128)(2,1)}) custom-call(s32[18]{0:T(128)} %stack.101.table, bf16[640,1152]{1,0:T(8,128)(2,1)} %bitcast.29, bf16[3072,1152]{1,0:T(8,128)(2,1)} %weights.3), custom_call_target="tpu_custom_call" | custom-call | flops 70778880 | bytes 195072 | tf_op jit(solution)/shard_map/first_parts/pallas_call | solution.py:95
  29.6 1.9 %collective-permute-start.8 = (bf16[160,3072]{1,0:T(8,128)(2,1)}, bf16[160,3072]{1,0:T(8,128)(2,1)}, u32[]{:S(2)}, u32[]{:S(2)}) collective-permute-start(bf16[160,3072]{1,0:T(8,128)(2,1)} %get-tuple-element.65), channel_id=1, source_target_pairs={{0,1},{1,2},{2,3},{3,0},{4,5},{5,6},{6,7},{7,4},{8,9},{9,10},{10,1... | collective-permute-start | bytes 2949128 | tf_op jit(solution)/shard_map/ppermute | solution.py:387
  31.5 2.2 %collective-permute-start.9 = (bf16[160,3072]{1,0:T(8,128)(2,1)}, bf16[160,3072]{1,0:T(8,128)(2,1)}, u32[]{:S(2)}, u32[]{:S(2)}) collective-permute-start(bf16[160,3072]{1,0:T(8,128)(2,1)} %get-tuple-element.66), channel_id=1, source_target_pairs={{0,3},{1,0},{2,1},{3,2},{4,7},{5,4},{6,5},{7,6},{8,11},{9,8},{10,9... | collective-permute-start | bytes 2949128 | tf_op jit(solution)/shard_map/ppermute | solution.py:388
  33.7 1.8 %collective-permute-start.10 = (bf16[160,3072]{1,0:T(8,128)(2,1)}, bf16[160,3072]{1,0:T(8,128)(2,1)}, u32[]{:S(2)}, u32[]{:S(2)}) collective-permute-start(bf16[160,3072]{1,0:T(8,128)(2,1)} %get-tuple-element.67), channel_id=1, source_target_pairs={{0,2},{1,3},{2,0},{3,1},{4,6},{5,7},{6,4},{7,5},{8,10},{9,11},{10,... | collective-permute-start | bytes 2949128 | tf_op jit(solution)/shard_map/ppermute | solution.py:389
  35.5 6.0 %near_terms.3.refs_2_ = bf16[2,384,1152]{2,1,0:T(8,128)(2,1)} custom-call(s32[18]{0:T(128)} %stack.101.table, bf16[2048,3072]{1,0:T(8,128)(2,1)} %pre.3, bf16[2048,3072]{1,0:T(8,128)(2,1)} %pre.3, bf16[512,1152]{1,0:T(8,128)(2,1)} %own.3, bf16[512,1152]{1,0:T(8,128)(2,1)} %collective-permute-done.partner), custom_call_target="tpu_custom_call" | custom-call | flops 28311552 | bytes 89088 | tf_op jit(solution)/shard_map/near_terms/pallas_call | solution.py:290
  41.5 1.0 constant_dynamic-update-slice_fusion.4
  42.6 0.1 fusion.1
  42.7 0.1 collective-permute-start.7
  42.7 0.0 copy-start.1
  42.8 0.5 collective-permute-start.4
  43.2 1.1 pad_maximum_fusion.2
  44.3 0.1 collective-permute-done.4
  44.4 0.3 collective-permute-start.5
  44.7 1.1 collective-permute-done.5
  45.9 0.3 collective-permute-start.6
  46.2 1.1 collective-permute-done.6
  47.4 0.0 collective-permute-done.7
  47.4 3.6 %pad_maximum_fusion.refs_3_.rows.refs_4_ = bf16[4,512,1152]{2,1,0:T(8,128)(2,1)} fusion(bf16[1,512,1152]{2,1,0:T(8,128)(2,1)S(1)} %bitcast.31, bf16[1,512,1152]{2,1,0:T(8,128)(2,1)S(1)} %bitcast.30, bf16[1,512,1152]{2,1,0:T(8,128)(2,1)} %bitcast.23, bf16[1,512,1152]{2,1,0:T(8,128)(2,1)S(1)} %bitcast.28), kind=kLoop, calls=%fused_computation | loop fusion | flops 7077888 | bytes 9437184 | tf_op jit(solution)/shard_map/stack | solution.py:399
  51.0 7.0 %terms.4 = (bf16[384,1152]{1,0:T(8,128)(2,1)}, bf16[384,1152]{1,0:T(8,128)(2,1)}) custom-call(s32[18]{0:T(128)} %stack.101.table, bf16[2048,3072]{1,0:T(8,128)(2,1)} %pre.3, bf16[2048,3072]{1,0:T(8,128)(2,1)} %pre.3, bf16[2,384,1152]{2,1,0:T(8,128)(2,1)} %near_terms.2.refs_2_, bf16[4,512,1152]{2,1,0:T(8,128)(2,1)} %pad_maximum_fusion.refs_3_.rows.refs_4_), custom_call_target="tpu_custom_call" | custom-call | flops 28311552 | bytes 61440 | tf_op jit(solution)/shard_map/terms/pallas_call | solution.py:341
  58.0 3.0 %collective-permute-start.11 = (bf16[384,1152]{1,0:T(8,128)(2,1)}, bf16[384,1152]{1,0:T(8,128)(2,1)S(1)}, u32[]{:S(2)}, u32[]{:S(2)}) collective-permute-start(bf16[384,1152]{1,0:T(8,128)(2,1)} %get-tuple-element.61), channel_id=1, source_target_pairs={{0,48},{16,0},{32,16},{48,32},{64,112},{80,64},{96,80},{112,96},{1... | collective-permute-start | bytes 2654216 | tf_op jit(solution)/shard_map/ppermute | solution.py:410
  61.0 0.0 collective-permute-start.12
  61.0 18.5 %tail_parts.1 = (bf16[352,1536]{1,0:T(8,128)(2,1)}, bf16[352,1536]{1,0:T(8,128)(2,1)}, bf16[352,1536]{1,0:T(8,128)(2,1)}, bf16[352,1536]{1,0:T(8,128)(2,1)}, bf1...) custom-call(s32[18]{0:T(128)} %stack.101.table, ...), custom_call_target="tpu_custom_call" | custom-call | flops 155713536 | bytes 319488 | tf_op jit(solution)/shard_map/tail_parts/pallas_call | solution.py:148
  79.5 0.0 collective-permute-done.8.one
  79.5 0.0 collective-permute-done.9.two
  79.5 1.3 collective-permute-start.14
  80.8 2.2 %collective-permute-start.13 = (bf16[352,1536]{1,0:T(8,128)(2,1)}, bf16[352,1536]{1,0:T(8,128)(2,1)}, u32[]{:S(2)}, u32[]{:S(2)}) collective-permute-start(bf16[352,1536]{1,0:T(8,128)(2,1)} %get-tuple-element.77), channel_id=1, source_target_pairs={{0,3},{1,0},{2,1},{3,2},{4,7},{5,4},{6,5},{7,6},{8,11},{9,8},{10,9... | collective-permute-start | bytes 3244040 | tf_op jit(solution)/shard_map/ppermute | solution.py:415
  83.0 6.9 %terms.5 = (bf16[384,1152]{1,0:T(8,128)(2,1)}, bf16[384,1152]{1,0:T(8,128)(2,1)}) custom-call(s32[18]{0:T(128)} %stack.101.table, bf16[2048,3072]{1,0:T(8,128)(2,1)} %pre.3, bf16[2048,3072]{1,0:T(8,128)(2,1)} %pre.3, bf16[2,384,1152]{2,1,0:T(8,128)(2,1)} %near_terms.3.refs_2_, bf16[4,512,1152]{2,1,0:T(8,128)(2,1)} %pad_maximum_fusion.refs_3_.rows.refs_4_), custom_call_target="tpu_custom_call" | custom-call | flops 28311552 | bytes 61440 | tf_op jit(solution)/shard_map/terms/pallas_call | solution.py:341
  89.9 0.9 copy-done.6
  90.8 0.6 collective-permute-start.15
  91.4 2.6 %collective-permute-start.16 = (bf16[384,1152]{1,0:T(8,128)(2,1)}, bf16[384,1152]{1,0:T(8,128)(2,1)}, u32[]{:S(2)}, u32[]{:S(2)}) collective-permute-start(bf16[384,1152]{1,0:T(8,128)(2,1)} %get-tuple-element.86), channel_id=1, source_target_pairs={{0,48},{16,0},{32,16},{48,32},{64,112},{80,64},{96,80},{112,96},{1... | collective-permute-start | bytes 2654216 | tf_op jit(solution)/shard_map/ppermute | solution.py:422
  94.1 9.7 %terms.6 = (bf16[384,1152]{1,0:T(8,128)(2,1)}, bf16[384,1152]{1,0:T(8,128)(2,1)}) custom-call(s32[18]{0:T(128)} %stack.101.table, bf16[2048,3072]{1,0:T(8,128)(2,1)} %pre.3, bf16[2048,3072]{1,0:T(8,128)(2,1)} %pre.3, bf16[2048,3072]{1,0:T(8,128)(2,1)} %pre.3, bf16[2048,3072]{1,0:T(8,128)(2,1)} %pre.3, bf16[4,512,1152]{2,1,0:T(8,128)(2,1)} %pad_maximum_fusion.refs_3_.rows.refs_4_), custom_call_target="tpu_custom_call" | custom-call | flops 56623104 | bytes 122880 | tf_op jit(solution)/shard_map/terms/pallas_call | solution.py:341
  103.8 3.3 %collective-permute-done.14 = bf16[352,1536]{1,0:T(8,128)(2,1)} collective-permute-done((bf16[352,1536]{1,0:T(8,128)(2,1)}, bf16[352,1536]{1,0:T(8,128)(2,1)}, u32[]{:S(2)}, u32[]{:S(2)}) %collective-permute-start.14) | collective-permute-done | bytes 1081376 | tf_op jit(solution)/shard_map/ppermute | solution.py:416
  107.1 0.2 collective-permute-start.18
  107.2 3.1 %collective-permute-start.19 = (bf16[352,1536]{1,0:T(8,128)(2,1)}, bf16[352,1536]{1,0:T(8,128)(2,1)}, u32[]{:S(2)}, u32[]{:S(2)}) collective-permute-start(bf16[352,1536]{1,0:T(8,128)(2,1)} %get-tuple-element.97), channel_id=1, source_target_pairs={{0,3},{1,0},{2,1},{3,2},{4,7},{5,4},{6,5},{7,6},{8,11},{9,8},{10,9... | collective-permute-start | bytes 3244040 | tf_op jit(solution)/shard_map/ppermute | solution.py:428
  110.3 3.8 %add_convert_fusion.2 = (bf16[384,1152]{1,0:T(8,128)(2,1)}, bf16[384,1152]{1,0:T(8,128)(2,1)}) fusion(bf16[384,1152]{1,0:T(8,128)(2,1)} %collective-permute-done.12, bf16[384,1152]{1,0:T(8,128)(2,1)} %get-tuple-element.92, bf16[384,1152]{1,0:T(8,128)(2,1)} %copy-done.6, bf16[384,1152]{1,0:T(8,128)(2,1)} %get-tuple-element.73), kind=kLoop, calls=%fused_computation.6 | loop fusion | flops 3538944 | bytes 5308416 | tf_op jit(solution)/shard_map/convert_element_type | solution.py:432
  114.1 3.0 %collective-permute-start.20 = (bf16[384,1152]{1,0:T(8,128)(2,1)}, bf16[384,1152]{1,0:T(8,128)(2,1)}, u32[]{:S(2)}, u32[]{:S(2)}) collective-permute-start(bf16[384,1152]{1,0:T(8,128)(2,1)} %get-tuple-element.99), channel_id=1, source_target_pairs={{0,48},{16,0},{32,16},{48,32},{64,112},{80,64},{96,80},{112,96},{1... | collective-permute-start | bytes 2654216 | tf_op jit(solution)/shard_map/ppermute | solution.py:435
  117.1 3.6 %add_convert_fusion = (bf16[352,1536]{1,0:T(8,128)(2,1)}, bf16[352,1536]{1,0:T(8,128)(2,1)}) fusion(bf16[352,1536]{1,0:T(8,128)(2,1)} %collective-permute-done.14, bf16[352,1536]{1,0:T(8,128)(2,1)S(1)} %copy-done.4, bf16[352,1536]{1,0:T(8,128)(2,1)} %collective-permute-done.13, bf16[352,1536]{1,0:T(8,128)(2,1)S(1)} %copy-done.3), kind=kLoop, calls=%fused_computation.1 | loop fusion | flops 4325376 | bytes 6488064 | tf_op jit(solution)/shard_map/convert_element_type | solution.py:430
  120.7 9.7 %terms.7 = (bf16[384,1152]{1,0:T(8,128)(2,1)}, bf16[384,1152]{1,0:T(8,128)(2,1)}) custom-call(s32[18]{0:T(128)} %stack.101.table, bf16[2048,3072]{1,0:T(8,128)(2,1)} %pre.3, bf16[2048,3072]{1,0:T(8,128)(2,1)} %pre.3, bf16[2048,3072]{1,0:T(8,128)(2,1)} %pre.3, bf16[2048,3072]{1,0:T(8,128)(2,1)} %pre.3, bf16[4,512,1152]{2,1,0:T(8,128)(2,1)} %pad_maximum_fusion.refs_3_.rows.refs_4_), custom_call_target="tpu_custom_call" | custom-call | flops 56623104 | bytes 122880 | tf_op jit(solution)/shard_map/terms/pallas_call | solution.py:341
  130.4 5.2 %head_last.1.held = bf16[160,3072]{1,0:T(8,128)(2,1)} custom-call(s32[18]{0:T(128)} %stack.101.table, bf16[160,3072]{1,0:T(8,128)(2,1)} %get-tuple-element.56.own, bf16[160,3072]{1,0:T(8,128)(2,1)} %collective-permute-done.8.one, bf16[160,3072]{1,0:T(8,128)(2,1)} %collective-permute-done.9.two, bf16[160,3072]{1,0:T(8,128)(2,1)} %collective-permute-done.10.three, ...), custom_call_target="tpu_custom_call" | custom-call | flops 307200 | bytes 92160 | tf_op jit(solution)/shard_map/head_last/pallas_call | solution.py:177
  135.6 0.0 collective-permute-done.18.side_a
  135.6 1.8 %collective-permute-start.21 = (bf16[352,1536]{1,0:T(8,128)(2,1)}, bf16[352,1536]{1,0:T(8,128)(2,1)}, u32[]{:S(2)}, u32[]{:S(2)}) collective-permute-start(bf16[352,1536]{1,0:T(8,128)(2,1)} %get-tuple-element.104), channel_id=1, source_target_pairs={{0,3},{1,0},{2,1},{3,2},{4,7},{5,4},{6,5},{7,6},{8,11},{9,8},{10,9... | collective-permute-start | bytes 3244040 | tf_op jit(solution)/shard_map/ppermute | solution.py:445
  137.4 0.3 collective-permute-start.22
  137.7 0.0 collective-permute-done.20
  137.7 0.5 collective-permute-done.17
  138.2 4.4 %fusion = (f32[384,1152]{1,0:T(8,128)}, bf16[384,1152]{1,0:T(8,128)(2,1)}) fusion(bf16[384,1152]{1,0:T(8,128)(2,1)} %collective-permute-done.17, bf16[384,1152]{1,0:T(8,128)(2,1)} %collective-permute-done.16, bf16[384,1152]{1,0:T(8,128)(2,1)} %get-tuple-element.91, bf16[384,1152]{1,0:T(8,128)(2,1)} %collective-permute-done.20, ...), kind=kLoop, calls=%fused_computation.10 | loop fusion | flops 5750784 | bytes 7962625 | tf_op jit(solution)/shard_map/jit(_where)/select_n | solution.py:451
  142.7 2.7 %collective-permute-start.23 = (bf16[384,1152]{1,0:T(8,128)(2,1)}, bf16[384,1152]{1,0:T(8,128)(2,1)S(1)}, u32[]{:S(2)}, u32[]{:S(2)}) collective-permute-start(bf16[384,1152]{1,0:T(8,128)(2,1)} %get-tuple-element.107), channel_id=1, source_target_pairs={{0,64},{16,80},{32,96},{48,112},{64,0},{80,16},{96,32},{112,48},{1... | collective-permute-start | bytes 2654216 | tf_op jit(solution)/shard_map/ppermute | solution.py:453
  145.4 8.7 %tail_ready.1 = (bf16[512,3072]{1,0:T(8,128)(2,1)}, bf16[352,3072]{1,0:T(8,128)(2,1)}) custom-call(s32[18]{0:T(128)} %stack.101.table, bf16[352,3072]{1,0:T(8,128)(2,1)} %get-tuple-element.101.own, bf16[352,1536]{1,0:T(8,128)(2,1)} %collective-permute-done.18.side_a, bf16[352,1536]{1,0:T(8,128)(2,1)} %collective-permute-done.19.side_b, ...), custom_call_target="tpu_custom_call" | custom-call | flops 675840 | bytes 168960 | tf_op jit(solution)/shard_map/tail_ready/pallas_call | solution.py:220
  154.1 9.0 %collective-permute-done.23.taken = bf16[384,1152]{1,0:T(8,128)(2,1)S(1)} collective-permute-done((bf16[384,1152]{1,0:T(8,128)(2,1)}, bf16[384,1152]{1,0:T(8,128)(2,1)S(1)}, u32[]{:S(2)}, u32[]{:S(2)}) %collective-permute-start.23) | collective-permute-done | bytes 884768 | tf_op jit(solution)/shard_map/ppermute | solution.py:453
  163.0 0.0 collective-permute-done.21.sum_a
  163.0 1.0 copy-done.5
  164.0 8.0 %tail_last.1 = (bf16[512,3072]{1,0:T(8,128)(2,1)}, bf16[384,1152]{1,0:T(8,128)(2,1)}) custom-call(s32[18]{0:T(128)} %stack.101.table, bf16[512,3072]{1,0:T(8,128)(2,1)} %get-tuple-element.102.partial, bf16[352,3072]{1,0:T(8,128)(2,1)} %get-tuple-element.103.slope, bf16[352,1536]{1,0:T(8,128)(2,1)} %collective-permute-done.21.sum_a, ...), custom_call_target="tpu_custom_call" | custom-call | flops 4325376 | bytes 10813440 | tf_op jit(solution)/shard_map/tail_last/pallas_call | solution.py:262
  (26 shorter events, 0.2 us)
Async XLA Ops:
  0.6 3.5 %copy-start = (bf16[512,1152]{1,0:T(8,128)(2,1)S(1)}, bf16[512,1152]{1,0:T(8,128)(2,1)}, u32[]{:S(2)}) copy-start(bf16[512,1152]{1,0:T(8,128)(2,1)} %own.3) | copy-start | bytes 3538948
  0.6 5.2 %collective-permute-start = (bf16[512,1152]{1,0:T(8,128)(2,1)}, bf16[512,1152]{1,0:T(8,128)(2,1)}, u32[]{:S(2)}, u32[]{:S(2)}) collective-permute-start(bf16[512,1152]{1,0:T(8,128)(2,1)} %own.3), channel_id=1, source_target_pairs={{0,4},{4,0},{8,12},{12,8},{1,5},{5,1},{9,13},{13,9},{2,6},{6,2},{1... | collective-permute-start | bytes 3538952 | tf_op jit(solution)/shard_map/ppermute | solution.py:377
  2.6 11.0 %collective-permute-start.1 = (bf16[160,1152]{1,0:T(8,128)(2,1)S(1)}, bf16[160,1152]{1,0:T(8,128)(2,1)}, u32[]{:S(2)}, u32[]{:S(2)}) collective-permute-start(bf16[160,1152]{1,0:T(8,128)(2,1)S(1)} %get-tuple-element.109), channel_id=1, source_target_pairs={{0,8},{4,12},{8,0},{12,4},{1,9},{5,13},{9,1},{13,5},{2,10},{6,14},... | collective-permute-start | bytes 1105928 | tf_op jit(solution)/shard_map/ppermute | solution.py:376
  13.6 2.6 %collective-permute-start.2 = (bf16[160,1152]{1,0:T(8,128)(2,1)}, bf16[160,1152]{1,0:T(8,128)(2,1)S(1)}, u32[]{:S(2)}, u32[]{:S(2)}) collective-permute-start(bf16[160,1152]{1,0:T(8,128)(2,1)} %collective-permute-done.1), channel_id=1, source_target_pairs={{0,4},{4,0},{8,12},{12,8},{1,5},{5,1},{9,13},{13,9},{2,6},{6,2},{1... | collective-permute-start | bytes 1105928 | tf_op jit(solution)/shard_map/ppermute | solution.py:380
  13.6 28.9 %collective-permute-start.3 = (bf16[352,1152]{1,0:T(8,128)(2,1)}, bf16[352,1152]{1,0:T(8,128)(2,1)S(1)}, u32[]{:S(2)}, u32[]{:S(2)}) collective-permute-start(bf16[352,1152]{1,0:T(8,128)(2,1)} %slice.23), channel_id=1, source_target_pairs={{0,8},{4,12},{8,0},{12,4},{1,9},{5,13},{9,1},{13,5},{2,10},{6,14},... | collective-permute-start | bytes 2433032 | tf_op jit(solution)/shard_map/ppermute | solution.py:381
  16.2 2.6 %copy-start.2 = (bf16[160,1152]{1,0:T(8,128)(2,1)}, bf16[160,1152]{1,0:T(8,128)(2,1)S(1)}, u32[]{:S(2)}) copy-start(bf16[160,1152]{1,0:T(8,128)(2,1)S(1)} %collective-permute-done.2) | copy-start | bytes 1105924
  29.6 49.8 %collective-permute-start.8 = (bf16[160,3072]{1,0:T(8,128)(2,1)}, bf16[160,3072]{1,0:T(8,128)(2,1)}, u32[]{:S(2)}, u32[]{:S(2)}) collective-permute-start(bf16[160,3072]{1,0:T(8,128)(2,1)} %get-tuple-element.65), channel_id=1, source_target_pairs={{0,1},{1,2},{2,3},{3,0},{4,5},{5,6},{6,7},{7,4},{8,9},{9,10},{10,1... | collective-permute-start | bytes 2949128 | tf_op jit(solution)/shard_map/ppermute | solution.py:387
  31.5 47.9 %collective-permute-start.9 = (bf16[160,3072]{1,0:T(8,128)(2,1)}, bf16[160,3072]{1,0:T(8,128)(2,1)}, u32[]{:S(2)}, u32[]{:S(2)}) collective-permute-start(bf16[160,3072]{1,0:T(8,128)(2,1)} %get-tuple-element.66), channel_id=1, source_target_pairs={{0,3},{1,0},{2,1},{3,2},{4,7},{5,4},{6,5},{7,6},{8,11},{9,8},{10,9... | collective-permute-start | bytes 2949128 | tf_op jit(solution)/shard_map/ppermute | solution.py:388
  33.7 45.8 %collective-permute-start.10 = (bf16[160,3072]{1,0:T(8,128)(2,1)}, bf16[160,3072]{1,0:T(8,128)(2,1)}, u32[]{:S(2)}, u32[]{:S(2)}) collective-permute-start(bf16[160,3072]{1,0:T(8,128)(2,1)} %get-tuple-element.67), channel_id=1, source_target_pairs={{0,2},{1,3},{2,0},{3,1},{4,6},{5,7},{6,4},{7,5},{8,10},{9,11},{10,... | collective-permute-start | bytes 2949128 | tf_op jit(solution)/shard_map/ppermute | solution.py:389
  42.7 4.8 %collective-permute-start.7 = (bf16[64,1152]{1,0:T(8,128)(2,1)S(1)}, bf16[64,1152]{1,0:T(8,128)(2,1)S(1)}, u32[]{:S(2)}, u32[]{:S(2)}) collective-permute-start(bf16[64,1152]{1,0:T(8,128)(2,1)S(1)} %slice.27), channel_id=1, source_target_pairs={{0,4},{4,0},{8,12},{12,8},{1,5},{5,1},{9,13},{13,9},{2,6},{6,2},{1... | collective-permute-start | bytes 442376 | tf_op jit(solution)/shard_map/ppermute | solution.py:396
  42.7 4.7 %copy-start.1 = (bf16[512,1152]{1,0:T(8,128)(2,1)S(1)}, bf16[512,1152]{1,0:T(8,128)(2,1)}, u32[]{:S(2)}) copy-start(bf16[512,1152]{1,0:T(8,128)(2,1)} %own.3) | copy-start | bytes 3538948
  42.8 1.7 collective-permute-start.4
  44.4 1.5 collective-permute-start.5
  45.9 1.5 collective-permute-start.6
  58.0 31.9 %collective-permute-start.11 = (bf16[384,1152]{1,0:T(8,128)(2,1)}, bf16[384,1152]{1,0:T(8,128)(2,1)S(1)}, u32[]{:S(2)}, u32[]{:S(2)}) collective-permute-start(bf16[384,1152]{1,0:T(8,128)(2,1)} %get-tuple-element.61), channel_id=1, source_target_pairs={{0,48},{16,0},{32,16},{48,32},{64,112},{80,64},{96,80},{112,96},{1... | collective-permute-start | bytes 2654216 | tf_op jit(solution)/shard_map/ppermute | solution.py:410
  61.0 28.9 %collective-permute-start.12 = (bf16[384,1152]{1,0:T(8,128)(2,1)}, bf16[384,1152]{1,0:T(8,128)(2,1)}, u32[]{:S(2)}, u32[]{:S(2)}) collective-permute-start(bf16[384,1152]{1,0:T(8,128)(2,1)} %get-tuple-element.71), channel_id=1, source_target_pairs={{0,16},{16,32},{32,48},{48,0},{64,80},{80,96},{96,112},{112,64},{1... | collective-permute-start | bytes 2654216 | tf_op jit(solution)/shard_map/ppermute | solution.py:411
  79.5 27.6 %collective-permute-start.14 = (bf16[352,1536]{1,0:T(8,128)(2,1)}, bf16[352,1536]{1,0:T(8,128)(2,1)}, u32[]{:S(2)}, u32[]{:S(2)}) collective-permute-start(bf16[352,1536]{1,0:T(8,128)(2,1)} %get-tuple-element.81), channel_id=1, source_target_pairs={{0,1},{1,2},{2,3},{3,0},{4,5},{5,6},{6,7},{7,4},{8,9},{9,10},{10,1... | collective-permute-start | bytes 3244040 | tf_op jit(solution)/shard_map/ppermute | solution.py:416
  80.8 26.3 %collective-permute-start.13 = (bf16[352,1536]{1,0:T(8,128)(2,1)}, bf16[352,1536]{1,0:T(8,128)(2,1)}, u32[]{:S(2)}, u32[]{:S(2)}) collective-permute-start(bf16[352,1536]{1,0:T(8,128)(2,1)} %get-tuple-element.77), channel_id=1, source_target_pairs={{0,3},{1,0},{2,1},{3,2},{4,7},{5,4},{6,5},{7,6},{8,11},{9,8},{10,9... | collective-permute-start | bytes 3244040 | tf_op jit(solution)/shard_map/ppermute | solution.py:415
  89.9 0.9 copy-start.6
  90.8 23.2 %collective-permute-start.15 = (bf16[384,1152]{1,0:T(8,128)(2,1)}, bf16[384,1152]{1,0:T(8,128)(2,1)S(1)}, u32[]{:S(2)}, u32[]{:S(2)}) collective-permute-start(bf16[384,1152]{1,0:T(8,128)(2,1)} %get-tuple-element.84), channel_id=1, source_target_pairs={{0,16},{16,32},{32,48},{48,0},{64,80},{80,96},{96,112},{112,64},{1... | collective-permute-start | bytes 2654216 | tf_op jit(solution)/shard_map/ppermute | solution.py:421
  91.4 22.7 %collective-permute-start.16 = (bf16[384,1152]{1,0:T(8,128)(2,1)}, bf16[384,1152]{1,0:T(8,128)(2,1)}, u32[]{:S(2)}, u32[]{:S(2)}) collective-permute-start(bf16[384,1152]{1,0:T(8,128)(2,1)} %get-tuple-element.86), channel_id=1, source_target_pairs={{0,48},{16,0},{32,16},{48,32},{64,112},{80,64},{96,80},{112,96},{1... | collective-permute-start | bytes 2654216 | tf_op jit(solution)/shard_map/ppermute | solution.py:422
  107.1 28.5 %collective-permute-start.18 = (bf16[352,1536]{1,0:T(8,128)(2,1)}, bf16[352,1536]{1,0:T(8,128)(2,1)}, u32[]{:S(2)}, u32[]{:S(2)}) collective-permute-start(bf16[352,1536]{1,0:T(8,128)(2,1)} %get-tuple-element.95), channel_id=1, source_target_pairs={{0,1},{1,2},{2,3},{3,0},{4,5},{5,6},{6,7},{7,4},{8,9},{9,10},{10,1... | collective-permute-start | bytes 3244040 | tf_op jit(solution)/shard_map/ppermute | solution.py:427
  107.2 28.4 %collective-permute-start.19 = (bf16[352,1536]{1,0:T(8,128)(2,1)}, bf16[352,1536]{1,0:T(8,128)(2,1)}, u32[]{:S(2)}, u32[]{:S(2)}) collective-permute-start(bf16[352,1536]{1,0:T(8,128)(2,1)} %get-tuple-element.97), channel_id=1, source_target_pairs={{0,3},{1,0},{2,1},{3,2},{4,7},{5,4},{6,5},{7,6},{8,11},{9,8},{10,9... | collective-permute-start | bytes 3244040 | tf_op jit(solution)/shard_map/ppermute | solution.py:428
  110.3 6.8 %copy-start.3 = (bf16[352,1536]{1,0:T(8,128)(2,1)S(1)}, bf16[352,1536]{1,0:T(8,128)(2,1)}, u32[]{:S(2)}) copy-start(bf16[352,1536]{1,0:T(8,128)(2,1)} %get-tuple-element.75) | copy-start | bytes 3244036
  110.3 6.8 %copy-start.4 = (bf16[352,1536]{1,0:T(8,128)(2,1)S(1)}, bf16[352,1536]{1,0:T(8,128)(2,1)}, u32[]{:S(2)}) copy-start(bf16[352,1536]{1,0:T(8,128)(2,1)} %get-tuple-element.79) | copy-start | bytes 3244036
  114.1 23.6 %collective-permute-start.20 = (bf16[384,1152]{1,0:T(8,128)(2,1)}, bf16[384,1152]{1,0:T(8,128)(2,1)}, u32[]{:S(2)}, u32[]{:S(2)}) collective-permute-start(bf16[384,1152]{1,0:T(8,128)(2,1)} %get-tuple-element.99), channel_id=1, source_target_pairs={{0,48},{16,0},{32,16},{48,32},{64,112},{80,64},{96,80},{112,96},{1... | collective-permute-start | bytes 2654216 | tf_op jit(solution)/shard_map/ppermute | solution.py:435
  117.1 21.1 %collective-permute-start.17 = (bf16[384,1152]{1,0:T(8,128)(2,1)}, bf16[384,1152]{1,0:T(8,128)(2,1)}, u32[]{:S(2)}, u32[]{:S(2)}) collective-permute-start(bf16[384,1152]{1,0:T(8,128)(2,1)} %get-tuple-element.93), channel_id=1, source_target_pairs={{0,16},{16,32},{32,48},{48,0},{64,80},{80,96},{96,112},{112,64},{1... | collective-permute-start | bytes 2654216 | tf_op jit(solution)/shard_map/ppermute | solution.py:436
  135.6 27.4 %collective-permute-start.21 = (bf16[352,1536]{1,0:T(8,128)(2,1)}, bf16[352,1536]{1,0:T(8,128)(2,1)}, u32[]{:S(2)}, u32[]{:S(2)}) collective-permute-start(bf16[352,1536]{1,0:T(8,128)(2,1)} %get-tuple-element.104), channel_id=1, source_target_pairs={{0,3},{1,0},{2,1},{3,2},{4,7},{5,4},{6,5},{7,6},{8,11},{9,8},{10,9... | collective-permute-start | bytes 3244040 | tf_op jit(solution)/shard_map/ppermute | solution.py:445
  137.4 25.6 %collective-permute-start.22 = (bf16[352,1536]{1,0:T(8,128)(2,1)}, bf16[352,1536]{1,0:T(8,128)(2,1)}, u32[]{:S(2)}, u32[]{:S(2)}) collective-permute-start(bf16[352,1536]{1,0:T(8,128)(2,1)} %get-tuple-element.105), channel_id=1, source_target_pairs={{0,1},{1,2},{2,3},{3,0},{4,5},{5,6},{6,7},{7,4},{8,9},{9,10},{10,1... | collective-permute-start | bytes 3244040 | tf_op jit(solution)/shard_map/ppermute | solution.py:446
  142.7 20.4 %collective-permute-start.23 = (bf16[384,1152]{1,0:T(8,128)(2,1)}, bf16[384,1152]{1,0:T(8,128)(2,1)S(1)}, u32[]{:S(2)}, u32[]{:S(2)}) collective-permute-start(bf16[384,1152]{1,0:T(8,128)(2,1)} %get-tuple-element.107), channel_id=1, source_target_pairs={{0,64},{16,80},{32,96},{48,112},{64,0},{80,16},{96,32},{112,48},{1... | collective-permute-start | bytes 2654216 | tf_op jit(solution)/shard_map/ppermute | solution.py:453
  163.0 1.0 copy-start.5

commit v8 on v7

--- a/solution.py
+++ b/solution.py
@@ -237,36 +237,36 @@
 
 
 def tail_last_body(table, partial, slope, sum_a, sum_b, keep, taken, out, down):
-    head = out.shape[0] - slope.shape[0]
-    out[:head] = partial[:head]
+    width = sum_a.shape[1]
     down[...] = (keep[...] + taken[...].astype(f32)).astype(bf16)
-    total = partial[head:].astype(f32)
-    first = pl.program_id(0) < pl.num_programs(0) // 2
-
-    @pl.when(first)
-    def _():
-        out[head:] = ((total + sum_a[...].astype(f32)) * slope[...].astype(f32)).astype(bf16)
-
-    @pl.when(jnp.logical_not(first))
-    def _():
-        out[head:] = ((total + sum_b[...].astype(f32)) * slope[...].astype(f32)).astype(bf16)
+    for start, arrived in ((0, sum_a), (width, sum_b)):
+        cols = slice(start, start + width)
+        total = partial[:, cols].astype(f32) + arrived[...].astype(f32)
+        out[:, cols] = (total * slope[:, cols].astype(f32)).astype(bf16)
 
 
 def tail_last(partial, slope, sum_a, sum_b, keep, taken, table):
     count, hidden = slope.shape
     share = partial.shape[0]
     chunk, features = keep.shape
-    tiles = hidden // TILE
-    whole = pl.BlockSpec((share, TILE), lambda t, p: (0, t))
-    down = pl.BlockSpec((chunk // tiles, features), lambda t, p: (t, 0))
+    step = 32
+    start, last = (share - count) // step, count // step - 1
+    half = pl.BlockSpec((step, hidden // 2), lambda t, p: (jnp.minimum(t, last), 0))
+    whole = pl.BlockSpec((step, hidden), lambda t, p: (start + jnp.minimum(t, last), 0))
+    down = pl.BlockSpec((step, features), lambda t, p: (t, 0))
     return call(
         tail_last_body,
         "tail_last",
-        (tiles,),
-        1,
-        [whole, pl.BlockSpec((count, TILE), lambda t, p: (0, t))]
-        + halves(count, hidden)
-        + [down, down],
+        (chunk // step,),
+        1,
+        [
+            whole,
+            pl.BlockSpec((step, hidden), lambda t, p: (jnp.minimum(t, last), 0)),
+            half,
+            half,
+            down,
+            down,
+        ],
         [whole, down],
         [
             jax.ShapeDtypeStruct((share, hidden), bf16),
@@ -274,6 +274,7 @@
         ],
         count * hidden * 4,
         10 * count * hidden,
+        aliases={1: 0},
     )(table, partial, slope, sum_a, sum_b, keep, taken)
 
 
@@ -389,8 +390,6 @@
         lax.ppermute(to_far, "gz", z_far),
     ]
 
-    near_side = near_terms(preact, grad_output, partner, table, C_SIDE)
-    table = after(table, near_side)
     across_tail = after(across_tail, table)
     corner_tail = [
         lax.ppermute(across_tail[start : start + PIECE], "gy", other_core)
@@ -416,7 +415,7 @@
     b_far = lax.ppermute(after(b_far, *arrived), "gz", z_up)
     table = after(table, *arrived)
 
-    c_side, d_side = terms(preact, rows, table, C_SIDE, near_side)
+    c_side, d_side = terms(preact, rows, table, C_SIDE)
     table = after(table, c_side)
     c_side = lax.ppermute(after(c_side, c_far, d_far), "gx", y_up)
     d_side = lax.ppermute(after(d_side, c_far, d_far), "gx", y_down)

time: 173 us -> 174 us (level)
  waiting for transfers between devices: 17 us -> 20 us
    pallas_call x2 -> x1, Pallas kernels: 12 us -> 6.01 us  [near_terms(): call(near_body, 'near_terms', (2,), 1, [pl.BlockSpec((share, chunk), lamb...]
    ppermute x1, waiting for transfers between devices: 3.27 us -> 0.01 us  [shards(): b_far = lax.ppermute(after(b_far, *arrived), 'gz', z_up)]
    ppermute x1, waiting for transfers between devices: 0.01 us -> 3.1 us  [shards(): lax.ppermute(to_down, 'gz', z_down)]
    pallas_call x4, Pallas kernels: 33.3 us -> 36 us  [terms(): call(functools.partial(terms_body, near), 'terms', (2,), 1, [source(j) fo...]
    ppermute x1, waiting for transfers between devices: 0.01 us -> 1.88 us  [shards(): c_side = lax.ppermute(after(c_side, c_far, d_far), 'gx', y_up)]
    pallas_call x1, Pallas kernels: 8.01 us -> 9.89 us  [tail_last(): call(tail_last_body, 'tail_last', (chunk // step,), 1, [whole, pl.BlockSp...]
    ppermute x1, waiting for transfers between devices: 0.01 us -> 1.83 us  [shards(): lax.ppermute(to_far, 'gz', z_far)]
  transfers between devices with their start and end apart: 24 -> 24, of which waited for: 7 -> 9; matrix products, arithmetic and copies ran while one was open for 14% -> 14% of each run, Pallas kernels for 51% -> 49%
where the time goes in v8:
time: 174 us; the launch traced here: 173 us
  Pallas kernels  95.1 us (55%)
  starting transfers between devices  30.9 us (18%)
  waiting for transfers between devices  20 us (11%)
  other arithmetic  19 us (11%)
  local copies, waits for them, and re-layouts  7.45 us (4%)
    pallas_call x4, Pallas kernels, terms(): call(functools.partial(terms_body, near), 'terms', (2,), 1, [source(j) fo...  36 us
    pallas_call x1, Pallas kernels, tail_parts(): call(tail_body, 'tail_parts', (tiles,), 1, [pl.BlockSpec((4, share, depth...  18.5 us
    pallas_call x1, Pallas kernels, first_parts(): call(first_body, 'first_parts', (hidden // TILE,), 1, [pl.BlockSpec((4 *...  10.8 us
    pallas_call x1, Pallas kernels, tail_last(): call(tail_last_body, 'tail_last', (chunk // step,), 1, [whole, pl.BlockSp...  9.89 us
    ppermute x1, waiting for transfers between devices, shards(): taken = lax.ppermute(give, 'gx', gx_move(1, 0))  8.71 us
    pallas_call x1, Pallas kernels, tail_ready(): call(ready_body, 'tail_ready', (hidden // TILE,), 1, [block] + halves(cou...  8.68 us
    pallas_call x1, Pallas kernels, near_terms(): call(near_body, 'near_terms', (2,), 1, [pl.BlockSpec((share, chunk), lamb...  6.01 us
    pallas_call x1, Pallas kernels, head_last(): call(head_last_body, 'head_last', (2,), 1, [block] * 4 + [pl.BlockSpec((s...  5.23 us
  transfers between devices with their start and end apart: 24, of which 9 were waited for; matrix products, arithmetic and copies ran while one was open for 14% of the time, Pallas kernels for 49%

profile of v8, /device:TPU:0, one launch (start us, length us, event | category | flops | bytes accessed | tf_op | source)
XLA Modules:
  0.0 173.2 jit_solution(3768692050530481240)
XLA Ops:
  0.6 0.0 copy-start
  0.6 0.1 collective-permute-start
  0.7 1.9 %slice_bitcast_fusion.1 = (bf16[1,160,1152]{2,1,0:T(8,128)(2,1)}, bf16[160,1152]{1,0:T(8,128)(2,1)S(1)}) fusion(bf16[512,1152]{1,0:T(8,128)(2,1)} %own.1), kind=kLoop, calls=%fused_computation.17 | loop fusion | bytes 1105920 | tf_op jit(solution)/shard_map/stack | solution.py:384
  2.6 1.6 collective-permute-start.1
  4.2 0.9 slice.23
  5.1 0.6 stack.101.table
  5.7 0.0 collective-permute-done.partner
  5.7 6.0 %near_terms.1.refs_2_ = bf16[2,384,1152]{2,1,0:T(8,128)(2,1)} custom-call(s32[18]{0:T(128)} %stack.101.table, bf16[2048,3072]{1,0:T(8,128)(2,1)} %pre.3, bf16[2048,3072]{1,0:T(8,128)(2,1)} %pre.3, bf16[512,1152]{1,0:T(8,128)(2,1)} %own.1, bf16[512,1152]{1,0:T(8,128)(2,1)} %collective-permute-done.partner), custom_call_target="tpu_custom_call" | custom-call | flops 28311552 | bytes 89088 | tf_op jit(solution)/shard_map/near_terms/pallas_call | solution.py:291
  11.8 1.9 %collective-permute-done.1 = bf16[160,1152]{1,0:T(8,128)(2,1)} collective-permute-done((bf16[160,1152]{1,0:T(8,128)(2,1)S(1)}, bf16[160,1152]{1,0:T(8,128)(2,1)}, u32[]{:S(2)}, u32[]{:S(2)}) %collective-permute-start.1) | collective-permute-done | bytes 368672 | tf_op jit(solution)/shard_map/ppermute | solution.py:377
  13.6 0.0 collective-permute-start.2
  13.6 1.6 collective-permute-start.3
  15.2 1.0 slice_bitcast_fusion
  16.2 2.6 %pad_maximum_fusion.1 = bf16[4,160,1152]{2,1,0:T(8,128)(2,1)} fusion(bf16[1,160,1152]{2,1,0:T(8,128)(2,1)S(1)} %bitcast.32, bf16[1,160,1152]{2,1,0:T(8,128)(2,1)} %bitcast.19, bf16[1,160,1152]{2,1,0:T(8,128)(2,1)S(1)} %slice_bitcast_fusion, bf16[1,160,1152]{2,1,0:T(8,128)(2,1)} %get-tuple-element.106), kind=kLoop, calls=%fused_computation.8 | loop fusion | flops 2211840 | bytes 2949120 | tf_op jit(solution)/shard_map/stack | solution.py:384
  18.8 10.8 %first_parts.1 = (bf16[160,3072]{1,0:T(8,128)(2,1)}, bf16[160,3072]{1,0:T(8,128)(2,1)}, bf16[160,3072]{1,0:T(8,128)(2,1)}, bf16[160,3072]{1,0:T(8,128)(2,1)}) custom-call(s32[18]{0:T(128)} %stack.101.table, bf16[640,1152]{1,0:T(8,128)(2,1)} %bitcast.29, bf16[3072,1152]{1,0:T(8,128)(2,1)} %weights.3), custom_call_target="tpu_custom_call" | custom-call | flops 70778880 | bytes 195072 | tf_op jit(solution)/shard_map/first_parts/pallas_call | solution.py:95
  29.6 1.9 %collective-permute-start.8 = (bf16[160,3072]{1,0:T(8,128)(2,1)}, bf16[160,3072]{1,0:T(8,128)(2,1)}, u32[]{:S(2)}, u32[]{:S(2)}) collective-permute-start(bf16[160,3072]{1,0:T(8,128)(2,1)} %get-tuple-element.63), channel_id=1, source_target_pairs={{0,1},{1,2},{2,3},{3,0},{4,5},{5,6},{6,7},{7,4},{8,9},{9,10},{10,1... | collective-permute-start | bytes 2949128 | tf_op jit(solution)/shard_map/ppermute | solution.py:388
  31.5 2.2 %collective-permute-start.9 = (bf16[160,3072]{1,0:T(8,128)(2,1)}, bf16[160,3072]{1,0:T(8,128)(2,1)}, u32[]{:S(2)}, u32[]{:S(2)}) collective-permute-start(bf16[160,3072]{1,0:T(8,128)(2,1)} %get-tuple-element.64), channel_id=1, source_target_pairs={{0,3},{1,0},{2,1},{3,2},{4,7},{5,4},{6,5},{7,6},{8,11},{9,8},{10,9... | collective-permute-start | bytes 2949128 | tf_op jit(solution)/shard_map/ppermute | solution.py:389
  33.7 1.8 %collective-permute-start.10 = (bf16[160,3072]{1,0:T(8,128)(2,1)}, bf16[160,3072]{1,0:T(8,128)(2,1)}, u32[]{:S(2)}, u32[]{:S(2)}) collective-permute-start(bf16[160,3072]{1,0:T(8,128)(2,1)} %get-tuple-element.65), channel_id=1, source_target_pairs={{0,2},{1,3},{2,0},{3,1},{4,6},{5,7},{6,4},{7,5},{8,10},{9,11},{10,... | collective-permute-start | bytes 2949128 | tf_op jit(solution)/shard_map/ppermute | solution.py:390
  35.5 1.0 constant_dynamic-update-slice_fusion.4
  36.6 0.1 fusion.1
  36.6 0.1 collective-permute-start.7
  36.7 0.0 copy-start.1
  36.7 0.5 collective-permute-start.4
  37.2 1.1 pad_maximum_fusion.2
  38.3 0.1 collective-permute-done.4
  38.4 0.3 collective-permute-start.5
  38.7 1.1 collective-permute-done.5
  39.9 0.3 collective-permute-start.6
  40.2 1.1 collective-permute-done.6
  41.4 3.6 %pad_maximum_fusion.refs_3_.rows.refs_4_ = bf16[4,512,1152]{2,1,0:T(8,128)(2,1)} fusion(bf16[1,512,1152]{2,1,0:T(8,128)(2,1)S(1)} %bitcast.31, bf16[1,512,1152]{2,1,0:T(8,128)(2,1)S(1)} %bitcast.30, bf16[1,512,1152]{2,1,0:T(8,128)(2,1)} %bitcast.23, bf16[1,512,1152]{2,1,0:T(8,128)(2,1)S(1)} %bitcast.28), kind=kLoop, calls=%fused_computation | loop fusion | flops 7077888 | bytes 9437184 | tf_op jit(solution)/shard_map/stack | solution.py:398
  45.0 6.9 %terms.4 = (bf16[384,1152]{1,0:T(8,128)(2,1)}, bf16[384,1152]{1,0:T(8,128)(2,1)}) custom-call(s32[18]{0:T(128)} %stack.101.table, bf16[2048,3072]{1,0:T(8,128)(2,1)} %pre.3, bf16[2048,3072]{1,0:T(8,128)(2,1)} %pre.3, bf16[2,384,1152]{2,1,0:T(8,128)(2,1)} %near_terms.1.refs_2_, bf16[4,512,1152]{2,1,0:T(8,128)(2,1)} %pad_maximum_fusion.refs_3_.rows.refs_4_), custom_call_target="tpu_custom_call" | custom-call | flops 28311552 | bytes 61440 | tf_op jit(solution)/shard_map/terms/pallas_call | solution.py:342
  51.9 3.0 %collective-permute-start.11 = (bf16[384,1152]{1,0:T(8,128)(2,1)}, bf16[384,1152]{1,0:T(8,128)(2,1)S(1)}, u32[]{:S(2)}, u32[]{:S(2)}) collective-permute-start(bf16[384,1152]{1,0:T(8,128)(2,1)} %get-tuple-element.59), channel_id=1, source_target_pairs={{0,48},{16,0},{32,16},{48,32},{64,112},{80,64},{96,80},{112,96},{1... | collective-permute-start | bytes 2654216 | tf_op jit(solution)/shard_map/ppermute | solution.py:409
  55.0 18.5 %tail_parts.1 = (bf16[352,1536]{1,0:T(8,128)(2,1)}, bf16[352,1536]{1,0:T(8,128)(2,1)}, bf16[352,1536]{1,0:T(8,128)(2,1)}, bf16[352,1536]{1,0:T(8,128)(2,1)}, bf1...) custom-call(s32[18]{0:T(128)} %stack.101.table, ...), custom_call_target="tpu_custom_call" | custom-call | flops 155713536 | bytes 319488 | tf_op jit(solution)/shard_map/tail_parts/pallas_call | solution.py:148
  73.4 0.0 collective-permute-done.8.one
  73.4 3.1 %collective-permute-done.9.two = bf16[160,3072]{1,0:T(8,128)(2,1)} collective-permute-done((bf16[160,3072]{1,0:T(8,128)(2,1)}, bf16[160,3072]{1,0:T(8,128)(2,1)}, u32[]{:S(2)}, u32[]{:S(2)}) %collective-permute-start.9) | collective-permute-done | bytes 983072 | tf_op jit(solution)/shard_map/ppermute | solution.py:389
  76.5 1.8 %collective-permute-done.10.three = bf16[160,3072]{1,0:T(8,128)(2,1)} collective-permute-done((bf16[160,3072]{1,0:T(8,128)(2,1)}, bf16[160,3072]{1,0:T(8,128)(2,1)}, u32[]{:S(2)}, u32[]{:S(2)}) %collective-permute-start.10) | collective-permute-done | bytes 983072 | tf_op jit(solution)/shard_map/ppermute | solution.py:390
  78.4 1.1 collective-permute-start.14
  79.5 2.1 %collective-permute-start.13 = (bf16[352,1536]{1,0:T(8,128)(2,1)}, bf16[352,1536]{1,0:T(8,128)(2,1)}, u32[]{:S(2)}, u32[]{:S(2)}) collective-permute-start(bf16[352,1536]{1,0:T(8,128)(2,1)} %get-tuple-element.75), channel_id=1, source_target_pairs={{0,3},{1,0},{2,1},{3,2},{4,7},{5,4},{6,5},{7,6},{8,11},{9,8},{10,9... | collective-permute-start | bytes 3244040 | tf_op jit(solution)/shard_map/ppermute | solution.py:414
  81.6 9.7 %terms.5 = (bf16[384,1152]{1,0:T(8,128)(2,1)}, bf16[384,1152]{1,0:T(8,128)(2,1)}) custom-call(s32[18]{0:T(128)} %stack.101.table, bf16[2048,3072]{1,0:T(8,128)(2,1)} %pre.3, bf16[2048,3072]{1,0:T(8,128)(2,1)} %pre.3, bf16[2048,3072]{1,0:T(8,128)(2,1)} %pre.3, bf16[2048,3072]{1,0:T(8,128)(2,1)} %pre.3, bf16[4,512,1152]{2,1,0:T(8,128)(2,1)} %pad_maximum_fusion.refs_3_.rows.refs_4_), custom_call_target="tpu_custom_call" | custom-call | flops 56623104 | bytes 122880 | tf_op jit(solution)/shard_map/terms/pallas_call | solution.py:342
  91.3 0.9 copy-done.6
  92.2 1.6 collective-permute-start.15
  93.8 1.7 collective-permute-start.16
  95.5 9.7 %terms.6 = (bf16[384,1152]{1,0:T(8,128)(2,1)}, bf16[384,1152]{1,0:T(8,128)(2,1)}) custom-call(s32[18]{0:T(128)} %stack.101.table, bf16[2048,3072]{1,0:T(8,128)(2,1)} %pre.3, bf16[2048,3072]{1,0:T(8,128)(2,1)} %pre.3, bf16[2048,3072]{1,0:T(8,128)(2,1)} %pre.3, bf16[2048,3072]{1,0:T(8,128)(2,1)} %pre.3, bf16[4,512,1152]{2,1,0:T(8,128)(2,1)} %pad_maximum_fusion.refs_3_.rows.refs_4_), custom_call_target="tpu_custom_call" | custom-call | flops 56623104 | bytes 122880 | tf_op jit(solution)/shard_map/terms/pallas_call | solution.py:342
  105.2 0.0 collective-permute-done.14
  105.2 0.0 collective-permute-done.13
  105.2 0.1 collective-permute-start.18
  105.3 3.2 %collective-permute-start.19 = (bf16[352,1536]{1,0:T(8,128)(2,1)}, bf16[352,1536]{1,0:T(8,128)(2,1)}, u32[]{:S(2)}, u32[]{:S(2)}) collective-permute-start(bf16[352,1536]{1,0:T(8,128)(2,1)} %get-tuple-element.95), channel_id=1, source_target_pairs={{0,3},{1,0},{2,1},{3,2},{4,7},{5,4},{6,5},{7,6},{8,11},{9,8},{10,9... | collective-permute-start | bytes 3244040 | tf_op jit(solution)/shard_map/ppermute | solution.py:427
  108.5 3.7 %add_convert_fusion.2 = (bf16[384,1152]{1,0:T(8,128)(2,1)}, bf16[384,1152]{1,0:T(8,128)(2,1)}) fusion(bf16[384,1152]{1,0:T(8,128)(2,1)} %collective-permute-done.12, bf16[384,1152]{1,0:T(8,128)(2,1)} %get-tuple-element.90, bf16[384,1152]{1,0:T(8,128)(2,1)} %copy-done.6, bf16[384,1152]{1,0:T(8,128)(2,1)} %get-tuple-element.71), kind=kLoop, calls=%fused_computation.6 | loop fusion | flops 3538944 | bytes 5308416 | tf_op jit(solution)/shard_map/convert_element_type | solution.py:431
  112.2 1.9 %collective-permute-done.15 = bf16[384,1152]{1,0:T(8,128)(2,1)S(1)} collective-permute-done((bf16[384,1152]{1,0:T(8,128)(2,1)}, bf16[384,1152]{1,0:T(8,128)(2,1)S(1)}, u32[]{:S(2)}, u32[]{:S(2)}) %collective-permute-start.15) | collective-permute-done | bytes 884768 | tf_op jit(solution)/shard_map/ppermute | solution.py:420
  114.1 0.1 collective-permute-done.16
  114.3 2.9 %collective-permute-start.20 = (bf16[384,1152]{1,0:T(8,128)(2,1)}, bf16[384,1152]{1,0:T(8,128)(2,1)}, u32[]{:S(2)}, u32[]{:S(2)}) collective-permute-start(bf16[384,1152]{1,0:T(8,128)(2,1)} %get-tuple-element.97), channel_id=1, source_target_pairs={{0,48},{16,0},{32,16},{48,32},{64,112},{80,64},{96,80},{112,96},{1... | collective-permute-start | bytes 2654216 | tf_op jit(solution)/shard_map/ppermute | solution.py:434
  117.2 3.6 %add_convert_fusion = (bf16[352,1536]{1,0:T(8,128)(2,1)}, bf16[352,1536]{1,0:T(8,128)(2,1)}) fusion(bf16[352,1536]{1,0:T(8,128)(2,1)} %collective-permute-done.14, bf16[352,1536]{1,0:T(8,128)(2,1)S(1)} %copy-done.4, bf16[352,1536]{1,0:T(8,128)(2,1)} %collective-permute-done.13, bf16[352,1536]{1,0:T(8,128)(2,1)S(1)} %copy-done.3), kind=kLoop, calls=%fused_computation.1 | loop fusion | flops 4325376 | bytes 6488064 | tf_op jit(solution)/shard_map/convert_element_type | solution.py:429
  120.8 9.7 %terms.7 = (bf16[384,1152]{1,0:T(8,128)(2,1)}, bf16[384,1152]{1,0:T(8,128)(2,1)}) custom-call(s32[18]{0:T(128)} %stack.101.table, bf16[2048,3072]{1,0:T(8,128)(2,1)} %pre.3, bf16[2048,3072]{1,0:T(8,128)(2,1)} %pre.3, bf16[2048,3072]{1,0:T(8,128)(2,1)} %pre.3, bf16[2048,3072]{1,0:T(8,128)(2,1)} %pre.3, bf16[4,512,1152]{2,1,0:T(8,128)(2,1)} %pad_maximum_fusion.refs_3_.rows.refs_4_), custom_call_target="tpu_custom_call" | custom-call | flops 56623104 | bytes 122880 | tf_op jit(solution)/shard_map/terms/pallas_call | solution.py:342
  130.4 5.2 %head_last.1.held = bf16[160,3072]{1,0:T(8,128)(2,1)} custom-call(s32[18]{0:T(128)} %stack.101.table, bf16[160,3072]{1,0:T(8,128)(2,1)} %get-tuple-element.55.own, bf16[160,3072]{1,0:T(8,128)(2,1)} %collective-permute-done.8.one, bf16[160,3072]{1,0:T(8,128)(2,1)} %collective-permute-done.9.two, bf16[160,3072]{1,0:T(8,128)(2,1)} %collective-permute-done.10.three, ...), custom_call_target="tpu_custom_call" | custom-call | flops 307200 | bytes 92160 | tf_op jit(solution)/shard_map/head_last/pallas_call | solution.py:177
  135.7 0.0 collective-permute-done.18.side_a
  135.7 0.0 collective-permute-done.19.side_b
  135.7 0.6 collective-permute-start.21
  136.3 1.5 collective-permute-start.22
  137.8 0.0 collective-permute-done.20
  137.8 4.4 %fusion = (f32[384,1152]{1,0:T(8,128)}, bf16[384,1152]{1,0:T(8,128)(2,1)}) fusion(bf16[384,1152]{1,0:T(8,128)(2,1)} %collective-permute-done.17, bf16[384,1152]{1,0:T(8,128)(2,1)} %collective-permute-done.16, bf16[384,1152]{1,0:T(8,128)(2,1)} %get-tuple-element.89, bf16[384,1152]{1,0:T(8,128)(2,1)} %collective-permute-done.20, ...), kind=kLoop, calls=%fused_computation.10 | loop fusion | flops 5750784 | bytes 7962625 | tf_op jit(solution)/shard_map/jit(_where)/select_n | solution.py:450
  142.2 2.7 %collective-permute-start.23 = (bf16[384,1152]{1,0:T(8,128)(2,1)}, bf16[384,1152]{1,0:T(8,128)(2,1)S(1)}, u32[]{:S(2)}, u32[]{:S(2)}) collective-permute-start(bf16[384,1152]{1,0:T(8,128)(2,1)} %get-tuple-element.105), channel_id=1, source_target_pairs={{0,64},{16,80},{32,96},{48,112},{64,0},{80,16},{96,32},{112,48},{1... | collective-permute-start | bytes 2654216 | tf_op jit(solution)/shard_map/ppermute | solution.py:452
  145.0 8.7 %tail_ready.1 = (bf16[512,3072]{1,0:T(8,128)(2,1)}, bf16[352,3072]{1,0:T(8,128)(2,1)}) custom-call(s32[18]{0:T(128)} %stack.101.table, bf16[352,3072]{1,0:T(8,128)(2,1)} %get-tuple-element.99.own, bf16[352,1536]{1,0:T(8,128)(2,1)} %collective-permute-done.18.side_a, bf16[352,1536]{1,0:T(8,128)(2,1)} %collective-permute-done.19.side_b, ...), custom_call_target="tpu_custom_call" | custom-call | flops 675840 | bytes 168960 | tf_op jit(solution)/shard_map/tail_ready/pallas_call | solution.py:220
  153.7 8.7 %collective-permute-done.23.taken = bf16[384,1152]{1,0:T(8,128)(2,1)S(1)} collective-permute-done((bf16[384,1152]{1,0:T(8,128)(2,1)}, bf16[384,1152]{1,0:T(8,128)(2,1)S(1)}, u32[]{:S(2)}, u32[]{:S(2)}) %collective-permute-start.23) | collective-permute-done | bytes 884768 | tf_op jit(solution)/shard_map/ppermute | solution.py:452
  162.4 0.9 copy-done.5
  163.3 9.9 %tail_last.1 = (bf16[512,3072]{1,0:T(8,128)(2,1)}, bf16[384,1152]{1,0:T(8,128)(2,1)}) custom-call(s32[18]{0:T(128)} %stack.101.table, bf16[512,3072]{1,0:T(8,128)(2,1)} %get-tuple-element.100.partial, bf16[352,3072]{1,0:T(8,128)(2,1)} %get-tuple-element.101.slope, bf16[352,1536]{1,0:T(8,128)(2,1)} %collective-permute-done.21.sum_a, ...), custom_call_target="tpu_custom_call", output_to_operand_aliasing={{0}: (1, {})} | custom-call | flops 4325376 | bytes 10813440 | tf_op jit(solution)/shard_map/tail_last/pallas_call | solution.py:257
  (25 shorter events, 0.2 us)
Async XLA Ops:
  0.6 3.5 %copy-start = (bf16[512,1152]{1,0:T(8,128)(2,1)S(1)}, bf16[512,1152]{1,0:T(8,128)(2,1)}, u32[]{:S(2)}) copy-start(bf16[512,1152]{1,0:T(8,128)(2,1)} %own.1) | copy-start | bytes 3538948
  0.6 5.1 %collective-permute-start = (bf16[512,1152]{1,0:T(8,128)(2,1)}, bf16[512,1152]{1,0:T(8,128)(2,1)}, u32[]{:S(2)}, u32[]{:S(2)}) collective-permute-start(bf16[512,1152]{1,0:T(8,128)(2,1)} %own.1), channel_id=1, source_target_pairs={{0,4},{4,0},{8,12},{12,8},{1,5},{5,1},{9,13},{13,9},{2,6},{6,2},{1... | collective-permute-start | bytes 3538952 | tf_op jit(solution)/shard_map/ppermute | solution.py:378
  2.6 11.0 %collective-permute-start.1 = (bf16[160,1152]{1,0:T(8,128)(2,1)S(1)}, bf16[160,1152]{1,0:T(8,128)(2,1)}, u32[]{:S(2)}, u32[]{:S(2)}) collective-permute-start(bf16[160,1152]{1,0:T(8,128)(2,1)S(1)} %get-tuple-element.107), channel_id=1, source_target_pairs={{0,8},{4,12},{8,0},{12,4},{1,9},{5,13},{9,1},{13,5},{2,10},{6,14},... | collective-permute-start | bytes 1105928 | tf_op jit(solution)/shard_map/ppermute | solution.py:377
  13.6 2.6 %collective-permute-start.2 = (bf16[160,1152]{1,0:T(8,128)(2,1)}, bf16[160,1152]{1,0:T(8,128)(2,1)S(1)}, u32[]{:S(2)}, u32[]{:S(2)}) collective-permute-start(bf16[160,1152]{1,0:T(8,128)(2,1)} %collective-permute-done.1), channel_id=1, source_target_pairs={{0,4},{4,0},{8,12},{12,8},{1,5},{5,1},{9,13},{13,9},{2,6},{6,2},{1... | collective-permute-start | bytes 1105928 | tf_op jit(solution)/shard_map/ppermute | solution.py:381
  13.6 22.9 %collective-permute-start.3 = (bf16[352,1152]{1,0:T(8,128)(2,1)}, bf16[352,1152]{1,0:T(8,128)(2,1)S(1)}, u32[]{:S(2)}, u32[]{:S(2)}) collective-permute-start(bf16[352,1152]{1,0:T(8,128)(2,1)} %slice.23), channel_id=1, source_target_pairs={{0,8},{4,12},{8,0},{12,4},{1,9},{5,13},{9,1},{13,5},{2,10},{6,14},... | collective-permute-start | bytes 2433032 | tf_op jit(solution)/shard_map/ppermute | solution.py:382
  16.2 2.6 %copy-start.2 = (bf16[160,1152]{1,0:T(8,128)(2,1)}, bf16[160,1152]{1,0:T(8,128)(2,1)S(1)}, u32[]{:S(2)}) copy-start(bf16[160,1152]{1,0:T(8,128)(2,1)S(1)} %collective-permute-done.2) | copy-start | bytes 1105924
  29.6 43.8 %collective-permute-start.8 = (bf16[160,3072]{1,0:T(8,128)(2,1)}, bf16[160,3072]{1,0:T(8,128)(2,1)}, u32[]{:S(2)}, u32[]{:S(2)}) collective-permute-start(bf16[160,3072]{1,0:T(8,128)(2,1)} %get-tuple-element.63), channel_id=1, source_target_pairs={{0,1},{1,2},{2,3},{3,0},{4,5},{5,6},{6,7},{7,4},{8,9},{9,10},{10,1... | collective-permute-start | bytes 2949128 | tf_op jit(solution)/shard_map/ppermute | solution.py:388
  31.5 45.0 %collective-permute-start.9 = (bf16[160,3072]{1,0:T(8,128)(2,1)}, bf16[160,3072]{1,0:T(8,128)(2,1)}, u32[]{:S(2)}, u32[]{:S(2)}) collective-permute-start(bf16[160,3072]{1,0:T(8,128)(2,1)} %get-tuple-element.64), channel_id=1, source_target_pairs={{0,3},{1,0},{2,1},{3,2},{4,7},{5,4},{6,5},{7,6},{8,11},{9,8},{10,9... | collective-permute-start | bytes 2949128 | tf_op jit(solution)/shard_map/ppermute | solution.py:389
  33.7 44.7 %collective-permute-start.10 = (bf16[160,3072]{1,0:T(8,128)(2,1)}, bf16[160,3072]{1,0:T(8,128)(2,1)}, u32[]{:S(2)}, u32[]{:S(2)}) collective-permute-start(bf16[160,3072]{1,0:T(8,128)(2,1)} %get-tuple-element.65), channel_id=1, source_target_pairs={{0,2},{1,3},{2,0},{3,1},{4,6},{5,7},{6,4},{7,5},{8,10},{9,11},{10,... | collective-permute-start | bytes 2949128 | tf_op jit(solution)/shard_map/ppermute | solution.py:390
  36.6 4.8 %collective-permute-start.7 = (bf16[64,1152]{1,0:T(8,128)(2,1)S(1)}, bf16[64,1152]{1,0:T(8,128)(2,1)S(1)}, u32[]{:S(2)}, u32[]{:S(2)}) collective-permute-start(bf16[64,1152]{1,0:T(8,128)(2,1)S(1)} %slice.27), channel_id=1, source_target_pairs={{0,4},{4,0},{8,12},{12,8},{1,5},{5,1},{9,13},{13,9},{2,6},{6,2},{1... | collective-permute-start | bytes 442376 | tf_op jit(solution)/shard_map/ppermute | solution.py:395
  36.7 4.7 %copy-start.1 = (bf16[512,1152]{1,0:T(8,128)(2,1)S(1)}, bf16[512,1152]{1,0:T(8,128)(2,1)}, u32[]{:S(2)}) copy-start(bf16[512,1152]{1,0:T(8,128)(2,1)} %own.1) | copy-start | bytes 3538948
  36.7 1.7 collective-permute-start.4
  38.4 1.5 collective-permute-start.5
  39.9 1.5 collective-permute-start.6
  51.9 39.4 %collective-permute-start.11 = (bf16[384,1152]{1,0:T(8,128)(2,1)}, bf16[384,1152]{1,0:T(8,128)(2,1)S(1)}, u32[]{:S(2)}, u32[]{:S(2)}) collective-permute-start(bf16[384,1152]{1,0:T(8,128)(2,1)} %get-tuple-element.59), channel_id=1, source_target_pairs={{0,48},{16,0},{32,16},{48,32},{64,112},{80,64},{96,80},{112,96},{1... | collective-permute-start | bytes 2654216 | tf_op jit(solution)/shard_map/ppermute | solution.py:409
  55.0 36.4 %collective-permute-start.12 = (bf16[384,1152]{1,0:T(8,128)(2,1)}, bf16[384,1152]{1,0:T(8,128)(2,1)}, u32[]{:S(2)}, u32[]{:S(2)}) collective-permute-start(bf16[384,1152]{1,0:T(8,128)(2,1)} %get-tuple-element.69), channel_id=1, source_target_pairs={{0,16},{16,32},{32,48},{48,0},{64,80},{80,96},{96,112},{112,64},{1... | collective-permute-start | bytes 2654216 | tf_op jit(solution)/shard_map/ppermute | solution.py:410
  78.4 26.8 %collective-permute-start.14 = (bf16[352,1536]{1,0:T(8,128)(2,1)}, bf16[352,1536]{1,0:T(8,128)(2,1)}, u32[]{:S(2)}, u32[]{:S(2)}) collective-permute-start(bf16[352,1536]{1,0:T(8,128)(2,1)} %get-tuple-element.79), channel_id=1, source_target_pairs={{0,1},{1,2},{2,3},{3,0},{4,5},{5,6},{6,7},{7,4},{8,9},{9,10},{10,1... | collective-permute-start | bytes 3244040 | tf_op jit(solution)/shard_map/ppermute | solution.py:415
  79.5 25.7 %collective-permute-start.13 = (bf16[352,1536]{1,0:T(8,128)(2,1)}, bf16[352,1536]{1,0:T(8,128)(2,1)}, u32[]{:S(2)}, u32[]{:S(2)}) collective-permute-start(bf16[352,1536]{1,0:T(8,128)(2,1)} %get-tuple-element.75), channel_id=1, source_target_pairs={{0,3},{1,0},{2,1},{3,2},{4,7},{5,4},{6,5},{7,6},{8,11},{9,8},{10,9... | collective-permute-start | bytes 3244040 | tf_op jit(solution)/shard_map/ppermute | solution.py:414
  91.3 0.9 copy-start.6
  92.2 21.9 %collective-permute-start.15 = (bf16[384,1152]{1,0:T(8,128)(2,1)}, bf16[384,1152]{1,0:T(8,128)(2,1)S(1)}, u32[]{:S(2)}, u32[]{:S(2)}) collective-permute-start(bf16[384,1152]{1,0:T(8,128)(2,1)} %get-tuple-element.82), channel_id=1, source_target_pairs={{0,16},{16,32},{32,48},{48,0},{64,80},{80,96},{96,112},{112,64},{1... | collective-permute-start | bytes 2654216 | tf_op jit(solution)/shard_map/ppermute | solution.py:420
  93.8 20.4 %collective-permute-start.16 = (bf16[384,1152]{1,0:T(8,128)(2,1)}, bf16[384,1152]{1,0:T(8,128)(2,1)}, u32[]{:S(2)}, u32[]{:S(2)}) collective-permute-start(bf16[384,1152]{1,0:T(8,128)(2,1)} %get-tuple-element.84), channel_id=1, source_target_pairs={{0,48},{16,0},{32,16},{48,32},{64,112},{80,64},{96,80},{112,96},{1... | collective-permute-start | bytes 2654216 | tf_op jit(solution)/shard_map/ppermute | solution.py:421
  105.2 30.5 %collective-permute-start.18 = (bf16[352,1536]{1,0:T(8,128)(2,1)}, bf16[352,1536]{1,0:T(8,128)(2,1)}, u32[]{:S(2)}, u32[]{:S(2)}) collective-permute-start(bf16[352,1536]{1,0:T(8,128)(2,1)} %get-tuple-element.93), channel_id=1, source_target_pairs={{0,1},{1,2},{2,3},{3,0},{4,5},{5,6},{6,7},{7,4},{8,9},{9,10},{10,1... | collective-permute-start | bytes 3244040 | tf_op jit(solution)/shard_map/ppermute | solution.py:426
  105.3 30.4 %collective-permute-start.19 = (bf16[352,1536]{1,0:T(8,128)(2,1)}, bf16[352,1536]{1,0:T(8,128)(2,1)}, u32[]{:S(2)}, u32[]{:S(2)}) collective-permute-start(bf16[352,1536]{1,0:T(8,128)(2,1)} %get-tuple-element.95), channel_id=1, source_target_pairs={{0,3},{1,0},{2,1},{3,2},{4,7},{5,4},{6,5},{7,6},{8,11},{9,8},{10,9... | collective-permute-start | bytes 3244040 | tf_op jit(solution)/shard_map/ppermute | solution.py:427
  108.5 8.7 %copy-start.3 = (bf16[352,1536]{1,0:T(8,128)(2,1)S(1)}, bf16[352,1536]{1,0:T(8,128)(2,1)}, u32[]{:S(2)}) copy-start(bf16[352,1536]{1,0:T(8,128)(2,1)} %get-tuple-element.73) | copy-start | bytes 3244036
  108.5 8.7 %copy-start.4 = (bf16[352,1536]{1,0:T(8,128)(2,1)S(1)}, bf16[352,1536]{1,0:T(8,128)(2,1)}, u32[]{:S(2)}) copy-start(bf16[352,1536]{1,0:T(8,128)(2,1)} %get-tuple-element.77) | copy-start | bytes 3244036
  114.3 23.5 %collective-permute-start.20 = (bf16[384,1152]{1,0:T(8,128)(2,1)}, bf16[384,1152]{1,0:T(8,128)(2,1)}, u32[]{:S(2)}, u32[]{:S(2)}) collective-permute-start(bf16[384,1152]{1,0:T(8,128)(2,1)} %get-tuple-element.97), channel_id=1, source_target_pairs={{0,48},{16,0},{32,16},{48,32},{64,112},{80,64},{96,80},{112,96},{1... | collective-permute-start | bytes 2654216 | tf_op jit(solution)/shard_map/ppermute | solution.py:434
  117.2 20.6 %collective-permute-start.17 = (bf16[384,1152]{1,0:T(8,128)(2,1)}, bf16[384,1152]{1,0:T(8,128)(2,1)}, u32[]{:S(2)}, u32[]{:S(2)}) collective-permute-start(bf16[384,1152]{1,0:T(8,128)(2,1)} %get-tuple-element.91), channel_id=1, source_target_pairs={{0,16},{16,32},{32,48},{48,0},{64,80},{80,96},{96,112},{112,64},{1... | collective-permute-start | bytes 2654216 | tf_op jit(solution)/shard_map/ppermute | solution.py:435
  135.7 26.7 %collective-permute-start.21 = (bf16[352,1536]{1,0:T(8,128)(2,1)}, bf16[352,1536]{1,0:T(8,128)(2,1)}, u32[]{:S(2)}, u32[]{:S(2)}) collective-permute-start(bf16[352,1536]{1,0:T(8,128)(2,1)} %get-tuple-element.102), channel_id=1, source_target_pairs={{0,3},{1,0},{2,1},{3,2},{4,7},{5,4},{6,5},{7,6},{8,11},{9,8},{10,9... | collective-permute-start | bytes 3244040 | tf_op jit(solution)/shard_map/ppermute | solution.py:444
  136.3 26.1 %collective-permute-start.22 = (bf16[352,1536]{1,0:T(8,128)(2,1)}, bf16[352,1536]{1,0:T(8,128)(2,1)}, u32[]{:S(2)}, u32[]{:S(2)}) collective-permute-start(bf16[352,1536]{1,0:T(8,128)(2,1)} %get-tuple-element.103), channel_id=1, source_target_pairs={{0,1},{1,2},{2,3},{3,0},{4,5},{5,6},{6,7},{7,4},{8,9},{9,10},{10,1... | collective-permute-start | bytes 3244040 | tf_op jit(solution)/shard_map/ppermute | solution.py:445
  142.2 20.1 %collective-permute-start.23 = (bf16[384,1152]{1,0:T(8,128)(2,1)}, bf16[384,1152]{1,0:T(8,128)(2,1)S(1)}, u32[]{:S(2)}, u32[]{:S(2)}) collective-permute-start(bf16[384,1152]{1,0:T(8,128)(2,1)} %get-tuple-element.105), channel_id=1, source_target_pairs={{0,64},{16,80},{32,96},{48,112},{64,0},{80,16},{96,32},{112,48},{1... | collective-permute-start | bytes 2654216 | tf_op jit(solution)/shard_map/ppermute | solution.py:452
  162.4 0.9 copy-start.5

commit v9 on v7

--- a/solution.py
+++ b/solution.py
@@ -12,10 +12,10 @@
 slope_scale = 1.0 / math.sqrt(2.0 * math.pi)
 bf16 = jnp.bfloat16
 f32 = jnp.float32
-HEAD = 160
+HEAD = 144
 TILE = 512
 PIECE = 96
-SHORT, MID, LAST, LONG = 1 / 64, 1/64, 1/64, 1/64
+SHORT, MID, LAST, LONG = 1 / 64, 2, 1 / 64, 1 / 64
 VMEM = 63 * 1024 * 1024
 
 
@@ -239,7 +239,7 @@
 def tail_last_body(table, partial, slope, sum_a, sum_b, keep, taken, out, down):
     head = out.shape[0] - slope.shape[0]
     out[:head] = partial[:head]
-    down[...] = (keep[...] + taken[...].astype(f32)).astype(bf16)
+    down[...] = (keep[...].astype(f32) + taken[...].astype(f32)).astype(bf16)
     total = partial[head:].astype(f32)
     first = pl.program_id(0) < pl.num_programs(0) // 2
 
@@ -389,8 +389,6 @@
         lax.ppermute(to_far, "gz", z_far),
     ]
 
-    near_side = near_terms(preact, grad_output, partner, table, C_SIDE)
-    table = after(table, near_side)
     across_tail = after(across_tail, table)
     corner_tail = [
         lax.ppermute(across_tail[start : start + PIECE], "gy", other_core)
@@ -416,7 +414,7 @@
     b_far = lax.ppermute(after(b_far, *arrived), "gz", z_up)
     table = after(table, *arrived)
 
-    c_side, d_side = terms(preact, rows, table, C_SIDE, near_side)
+    c_side, d_side = terms(preact, rows, table, C_SIDE)
     table = after(table, c_side)
     c_side = lax.ppermute(after(c_side, c_far, d_far), "gx", y_up)
     d_side = lax.ppermute(after(d_side, c_far, d_far), "gx", y_down)
@@ -448,7 +446,7 @@
     c_sum, d_sum = after(c_sum, table, a_side, b_side), after(d_sum, table, a_side, b_side)
     c_own = add(c_own, c_side, c_sum)
     d_own = add(d_own, d_side, d_sum)
-    keep = jnp.where(h == 0, c_own, d_own)
+    keep = jnp.where(h == 0, c_own, d_own).astype(bf16)
     give = jnp.where(h == 0, d_own, c_own).astype(bf16)
     taken = lax.ppermute(give, "gx", gx_move(1, 0))
     own_tail = after(own_tail, give)

time: 173 us -> 168 us (0.971)
  Pallas kernels: 96.5 us -> 93.1 us
  waiting for transfers between devices: 17 us -> 14.3 us
    pallas_call x2 -> x1, Pallas kernels: 12 us -> 6.01 us  [near_terms(): call(near_body, 'near_terms', (2,), 1, [pl.BlockSpec((share, chunk), lamb...]
    select_n x1 -> x0, other arithmetic: 4.44 us -> none  [shards(): keep = jnp.where(h == 0, c_own, d_own)]
    convert_element_type x0 -> x1, other arithmetic: none -> 4.22 us  [shards(): keep = jnp.where(h == 0, c_own, d_own).astype(bf16)]
    pallas_call x4, Pallas kernels: 33.3 us -> 35.9 us  [terms(): call(functools.partial(terms_body, near), 'terms', (2,), 1, [source(j) fo...]
    ppermute x1, waiting for transfers between devices: 3.27 us -> 1.4 us  [shards(): b_far = lax.ppermute(after(b_far, *arrived), 'gz', z_up)]
    ppermute x1, waiting for transfers between devices: 1.79 us -> 0.01 us  [shards(): across = lax.ppermute(own_head, 'gy', other_chip)]
  transfers between devices with their start and end apart: 24 -> 24, of which waited for: 7 -> 7; matrix products, arithmetic and copies ran while one was open for 14% -> 15% of each run, Pallas kernels for 51% -> 51%
where the time goes in v9:
time: 168 us; the launch traced here: 167 us
  Pallas kernels  93.1 us (55%)
  starting transfers between devices  31.6 us (19%)
  other arithmetic  18.7 us (11%)
  waiting for transfers between devices  14.3 us (9%)
  local copies, waits for them, and re-layouts  8.51 us (5%)
    pallas_call x4, Pallas kernels, terms(): call(functools.partial(terms_body, near), 'terms', (2,), 1, [source(j) fo...  35.9 us
    pallas_call x1, Pallas kernels, tail_parts(): call(tail_body, 'tail_parts', (tiles,), 1, [pl.BlockSpec((4, share, depth...  19.1 us
    pallas_call x1, Pallas kernels, first_parts(): call(first_body, 'first_parts', (hidden // TILE,), 1, [pl.BlockSpec((4 *...  10.3 us
    pallas_call x1, Pallas kernels, tail_ready(): call(ready_body, 'tail_ready', (hidden // TILE,), 1, [block] + halves(cou...  8.87 us
    ppermute x1, waiting for transfers between devices, shards(): taken = lax.ppermute(give, 'gx', gx_move(1, 0))  8.44 us
    pallas_call x1, Pallas kernels, tail_last(): call(tail_last_body, 'tail_last', (tiles,), 1, [whole, pl.BlockSpec((coun...  7.92 us
    pallas_call x1, Pallas kernels, near_terms(): call(near_body, 'near_terms', (2,), 1, [pl.BlockSpec((share, chunk), lamb...  6.01 us
    pallas_call x1, Pallas kernels, head_last(): call(head_last_body, 'head_last', (2,), 1, [block] * 4 + [pl.BlockSpec((s...  5 us
  transfers between devices with their start and end apart: 24, of which 7 were waited for; matrix products, arithmetic and copies ran while one was open for 15% of the time, Pallas kernels for 51%

profile of v9, /device:TPU:0, one launch (start us, length us, event | category | flops | bytes accessed | tf_op | source)
XLA Modules:
  0.0 167.0 jit_solution(13948544910071141002)
XLA Ops:
  0.6 0.1 collective-permute-start
  0.7 1.7 %slice_bitcast_fusion.1 = (bf16[1,144,1152]{2,1,0:T(8,128)(2,1)}, bf16[144,1152]{1,0:T(8,128)(2,1)S(1)}) fusion(bf16[512,1152]{1,0:T(8,128)(2,1)} %own.1), kind=kLoop, calls=%fused_computation.17 | loop fusion | bytes 995328 | tf_op jit(solution)/shard_map/stack | solution.py:383
  2.5 1.6 collective-permute-start.1
  4.0 2.1 %slice.23 = bf16[368,1152]{1,0:T(8,128)(2,1)} slice(bf16[512,1152]{1,0:T(8,128)(2,1)} %own.1), slice={[144:512], [0:1152]} | slice | bytes 1695744 | tf_op jit(solution)/shard_map/slice | solution.py:375
  6.2 0.6 stack.101.table
  6.8 0.0 collective-permute-done.partner
  6.8 6.0 %near_terms.1.refs_2_ = bf16[2,384,1152]{2,1,0:T(8,128)(2,1)} custom-call(s32[18]{0:T(128)} %stack.101.table, bf16[2048,3072]{1,0:T(8,128)(2,1)} %pre.3, bf16[2048,3072]{1,0:T(8,128)(2,1)} %pre.3, bf16[512,1152]{1,0:T(8,128)(2,1)} %own.1, bf16[512,1152]{1,0:T(8,128)(2,1)} %collective-permute-done.partner), custom_call_target="tpu_custom_call" | custom-call | flops 28311552 | bytes 89088 | tf_op jit(solution)/shard_map/near_terms/pallas_call | solution.py:290
  12.8 0.0 collective-permute-done.1
  12.8 0.2 collective-permute-start.2
  13.0 1.3 collective-permute-start.3
  14.4 1.0 slice_bitcast_fusion
  15.4 0.0 collective-permute-done.2
  15.4 2.5 %pad_maximum_fusion.1 = bf16[4,144,1152]{2,1,0:T(8,128)(2,1)} fusion(bf16[1,144,1152]{2,1,0:T(8,128)(2,1)S(1)} %bitcast.32, bf16[1,144,1152]{2,1,0:T(8,128)(2,1)} %bitcast.19, bf16[1,144,1152]{2,1,0:T(8,128)(2,1)S(1)} %slice_bitcast_fusion, bf16[1,144,1152]{2,1,0:T(8,128)(2,1)} %get-tuple-element.106), kind=kLoop, calls=%fused_computation.9 | loop fusion | flops 1990656 | bytes 2654208 | tf_op jit(solution)/shard_map/stack | solution.py:383
  17.9 10.3 %first_parts.1 = (bf16[144,3072]{1,0:T(8,128)(2,1)}, bf16[144,3072]{1,0:T(8,128)(2,1)}, bf16[144,3072]{1,0:T(8,128)(2,1)}, bf16[144,3072]{1,0:T(8,128)(2,1)}) custom-call(s32[18]{0:T(128)} %stack.101.table, bf16[576,1152]{1,0:T(8,128)(2,1)} %bitcast.29, bf16[3072,1152]{1,0:T(8,128)(2,1)} %weights.3), custom_call_target="tpu_custom_call" | custom-call | flops 63700992 | bytes 186624 | tf_op jit(solution)/shard_map/first_parts/pallas_call | solution.py:95
  28.2 1.9 %collective-permute-start.8 = (bf16[144,3072]{1,0:T(8,128)(2,1)}, bf16[144,3072]{1,0:T(8,128)(2,1)}, u32[]{:S(2)}, u32[]{:S(2)}) collective-permute-start(bf16[144,3072]{1,0:T(8,128)(2,1)} %get-tuple-element.63), channel_id=1, source_target_pairs={{0,1},{1,2},{2,3},{3,0},{4,5},{5,6},{6,7},{7,4},{8,9},{9,10},{10,1... | collective-permute-start | bytes 2654216 | tf_op jit(solution)/shard_map/ppermute | solution.py:387
  30.1 2.2 %collective-permute-start.9 = (bf16[144,3072]{1,0:T(8,128)(2,1)}, bf16[144,3072]{1,0:T(8,128)(2,1)}, u32[]{:S(2)}, u32[]{:S(2)}) collective-permute-start(bf16[144,3072]{1,0:T(8,128)(2,1)} %get-tuple-element.64), channel_id=1, source_target_pairs={{0,3},{1,0},{2,1},{3,2},{4,7},{5,4},{6,5},{7,6},{8,11},{9,8},{10,9... | collective-permute-start | bytes 2654216 | tf_op jit(solution)/shard_map/ppermute | solution.py:388
  32.3 1.8 %collective-permute-start.10 = (bf16[144,3072]{1,0:T(8,128)(2,1)}, bf16[144,3072]{1,0:T(8,128)(2,1)}, u32[]{:S(2)}, u32[]{:S(2)}) collective-permute-start(bf16[144,3072]{1,0:T(8,128)(2,1)} %get-tuple-element.65), channel_id=1, source_target_pairs={{0,2},{1,3},{2,0},{3,1},{4,6},{5,7},{6,4},{7,5},{8,10},{9,11},{10,... | collective-permute-start | bytes 2654216 | tf_op jit(solution)/shard_map/ppermute | solution.py:389
  34.1 1.0 constant_dynamic-update-slice_fusion.4
  35.1 0.0 collective-permute-done.3
  35.1 0.1 fusion
  35.2 0.1 collective-permute-start.7
  35.3 0.5 collective-permute-start.4
  35.8 1.1 pad_maximum_fusion.2
  36.9 0.0 copy-start
  36.9 0.1 collective-permute-done.4
  37.0 0.2 collective-permute-start.5
  37.3 1.2 collective-permute-done.5
  38.5 0.2 collective-permute-start.6
  38.8 1.2 collective-permute-done.6
  40.0 3.6 %pad_maximum_fusion.refs_3_.rows.refs_4_ = bf16[4,512,1152]{2,1,0:T(8,128)(2,1)} fusion(bf16[1,512,1152]{2,1,0:T(8,128)(2,1)S(1)} %bitcast.31, bf16[1,512,1152]{2,1,0:T(8,128)(2,1)S(1)} %bitcast.30, bf16[1,512,1152]{2,1,0:T(8,128)(2,1)} %bitcast.23, bf16[1,512,1152]{2,1,0:T(8,128)(2,1)S(1)} %bitcast.28), kind=kLoop, calls=%fused_computation | loop fusion | flops 7077888 | bytes 9437184 | tf_op jit(solution)/shard_map/stack | solution.py:397
  43.6 6.9 %terms.4 = (bf16[384,1152]{1,0:T(8,128)(2,1)}, bf16[384,1152]{1,0:T(8,128)(2,1)}) custom-call(s32[18]{0:T(128)} %stack.101.table, bf16[2048,3072]{1,0:T(8,128)(2,1)} %pre.3, bf16[2048,3072]{1,0:T(8,128)(2,1)} %pre.3, bf16[2,384,1152]{2,1,0:T(8,128)(2,1)} %near_terms.1.refs_2_, bf16[4,512,1152]{2,1,0:T(8,128)(2,1)} %pad_maximum_fusion.refs_3_.rows.refs_4_), custom_call_target="tpu_custom_call" | custom-call | flops 28311552 | bytes 61440 | tf_op jit(solution)/shard_map/terms/pallas_call | solution.py:341
  50.6 1.6 collective-permute-start.12
  52.1 1.7 collective-permute-start.11
  53.8 19.1 %tail_parts.1 = (bf16[368,1536]{1,0:T(8,128)(2,1)}, bf16[368,1536]{1,0:T(8,128)(2,1)}, bf16[368,1536]{1,0:T(8,128)(2,1)}, bf16[368,1536]{1,0:T(8,128)(2,1)}, bf1...) custom-call(s32[18]{0:T(128)} %stack.101.table, ...), custom_call_target="tpu_custom_call" | custom-call | flops 162791424 | bytes 325632 | tf_op jit(solution)/shard_map/tail_parts/pallas_call | solution.py:148
  72.9 0.0 collective-permute-done.8.one
  72.9 0.0 collective-permute-done.10.three
  72.9 1.2 collective-permute-start.14
  74.1 2.4 %collective-permute-start.13 = (bf16[368,1536]{1,0:T(8,128)(2,1)}, bf16[368,1536]{1,0:T(8,128)(2,1)}, u32[]{:S(2)}, u32[]{:S(2)}) collective-permute-start(bf16[368,1536]{1,0:T(8,128)(2,1)} %get-tuple-element.75), channel_id=1, source_target_pairs={{0,3},{1,0},{2,1},{3,2},{4,7},{5,4},{6,5},{7,6},{8,11},{9,8},{10,9... | collective-permute-start | bytes 3391496 | tf_op jit(solution)/shard_map/ppermute | solution.py:413
  76.5 9.7 %terms.5 = (bf16[384,1152]{1,0:T(8,128)(2,1)}, bf16[384,1152]{1,0:T(8,128)(2,1)}) custom-call(s32[18]{0:T(128)} %stack.101.table, bf16[2048,3072]{1,0:T(8,128)(2,1)} %pre.3, bf16[2048,3072]{1,0:T(8,128)(2,1)} %pre.3, bf16[2048,3072]{1,0:T(8,128)(2,1)} %pre.3, bf16[2048,3072]{1,0:T(8,128)(2,1)} %pre.3, bf16[4,512,1152]{2,1,0:T(8,128)(2,1)} %pad_maximum_fusion.refs_3_.rows.refs_4_), custom_call_target="tpu_custom_call" | custom-call | flops 56623104 | bytes 122880 | tf_op jit(solution)/shard_map/terms/pallas_call | solution.py:341
  86.2 0.0 collective-permute-done.11
  86.2 0.9 copy-done.5
  87.1 1.1 collective-permute-start.15
  88.1 2.2 %collective-permute-start.16 = (bf16[384,1152]{1,0:T(8,128)(2,1)}, bf16[384,1152]{1,0:T(8,128)(2,1)}, u32[]{:S(2)}, u32[]{:S(2)}) collective-permute-start(bf16[384,1152]{1,0:T(8,128)(2,1)} %get-tuple-element.84), channel_id=1, source_target_pairs={{0,48},{16,0},{32,16},{48,32},{64,112},{80,64},{96,80},{112,96},{1... | collective-permute-start | bytes 2654216 | tf_op jit(solution)/shard_map/ppermute | solution.py:420
  90.3 9.7 %terms.6 = (bf16[384,1152]{1,0:T(8,128)(2,1)}, bf16[384,1152]{1,0:T(8,128)(2,1)}) custom-call(s32[18]{0:T(128)} %stack.101.table, bf16[2048,3072]{1,0:T(8,128)(2,1)} %pre.3, bf16[2048,3072]{1,0:T(8,128)(2,1)} %pre.3, bf16[2048,3072]{1,0:T(8,128)(2,1)} %pre.3, bf16[2048,3072]{1,0:T(8,128)(2,1)} %pre.3, bf16[4,512,1152]{2,1,0:T(8,128)(2,1)} %pad_maximum_fusion.refs_3_.rows.refs_4_), custom_call_target="tpu_custom_call" | custom-call | flops 7247757312 | bytes 15728640 | tf_op jit(solution)/shard_map/terms/pallas_call | solution.py:341
  100.0 1.4 collective-permute-done.14
  101.4 0.0 collective-permute-done.13
  101.4 1.3 collective-permute-start.18
  102.6 2.0 %collective-permute-start.19 = (bf16[368,1536]{1,0:T(8,128)(2,1)}, bf16[368,1536]{1,0:T(8,128)(2,1)}, u32[]{:S(2)}, u32[]{:S(2)}) collective-permute-start(bf16[368,1536]{1,0:T(8,128)(2,1)} %get-tuple-element.95), channel_id=1, source_target_pairs={{0,3},{1,0},{2,1},{3,2},{4,7},{5,4},{6,5},{7,6},{8,11},{9,8},{10,9... | collective-permute-start | bytes 3391496 | tf_op jit(solution)/shard_map/ppermute | solution.py:426
  104.6 3.8 %add_convert_fusion.2 = (bf16[384,1152]{1,0:T(8,128)(2,1)}, bf16[384,1152]{1,0:T(8,128)(2,1)}) fusion(bf16[384,1152]{1,0:T(8,128)(2,1)} %copy-done.5, bf16[384,1152]{1,0:T(8,128)(2,1)} %get-tuple-element.90, bf16[384,1152]{1,0:T(8,128)(2,1)} %collective-permute-done.11, bf16[384,1152]{1,0:T(8,128)(2,1)} %get-tuple-element.71), kind=kLoop, calls=%fused_computation.7 | loop fusion | flops 3538944 | bytes 5308416 | tf_op jit(solution)/shard_map/convert_element_type | solution.py:430
  108.4 1.1 collective-permute-done.15
  109.5 3.1 %collective-permute-start.20 = (bf16[384,1152]{1,0:T(8,128)(2,1)}, bf16[384,1152]{1,0:T(8,128)(2,1)}, u32[]{:S(2)}, u32[]{:S(2)}) collective-permute-start(bf16[384,1152]{1,0:T(8,128)(2,1)} %get-tuple-element.97), channel_id=1, source_target_pairs={{0,48},{16,0},{32,16},{48,32},{64,112},{80,64},{96,80},{112,96},{1... | collective-permute-start | bytes 2654216 | tf_op jit(solution)/shard_map/ppermute | solution.py:433
  112.6 0.0 collective-permute-start.17
  112.6 3.5 %add_convert_fusion = (bf16[368,1536]{1,0:T(8,128)(2,1)}, bf16[368,1536]{1,0:T(8,128)(2,1)}) fusion(bf16[368,1536]{1,0:T(8,128)(2,1)} %collective-permute-done.14, bf16[368,1536]{1,0:T(8,128)(2,1)S(1)} %copy-done.3, bf16[368,1536]{1,0:T(8,128)(2,1)} %collective-permute-done.13, bf16[368,1536]{1,0:T(8,128)(2,1)S(1)} %copy-done.2), kind=kLoop, calls=%fused_computation.1 | loop fusion | flops 4521984 | bytes 6782976 | tf_op jit(solution)/shard_map/convert_element_type | solution.py:428
  116.1 9.7 %terms.7 = (bf16[384,1152]{1,0:T(8,128)(2,1)}, bf16[384,1152]{1,0:T(8,128)(2,1)}) custom-call(s32[18]{0:T(128)} %stack.101.table, bf16[2048,3072]{1,0:T(8,128)(2,1)} %pre.3, bf16[2048,3072]{1,0:T(8,128)(2,1)} %pre.3, bf16[2048,3072]{1,0:T(8,128)(2,1)} %pre.3, bf16[2048,3072]{1,0:T(8,128)(2,1)} %pre.3, bf16[4,512,1152]{2,1,0:T(8,128)(2,1)} %pad_maximum_fusion.refs_3_.rows.refs_4_), custom_call_target="tpu_custom_call" | custom-call | flops 56623104 | bytes 122880 | tf_op jit(solution)/shard_map/terms/pallas_call | solution.py:341
  125.8 5.0 %head_last.1.held = bf16[144,3072]{1,0:T(8,128)(2,1)} custom-call(s32[18]{0:T(128)} %stack.101.table, bf16[144,3072]{1,0:T(8,128)(2,1)} %get-tuple-element.55.own, bf16[144,3072]{1,0:T(8,128)(2,1)} %collective-permute-done.8.one, bf16[144,3072]{1,0:T(8,128)(2,1)} %collective-permute-done.9.two, bf16[144,3072]{1,0:T(8,128)(2,1)} %collective-permute-done.10.three, ...), custom_call_target="tpu_custom_call" | custom-call | flops 276480 | bytes 82944 | tf_op jit(solution)/shard_map/head_last/pallas_call | solution.py:177
  130.8 1.6 collective-permute-start.21
  132.3 0.5 collective-permute-start.22
  132.9 0.8 collective-permute-done.17
  133.6 4.2 %select_convert_fusion = (bf16[384,1152]{1,0:T(8,128)(2,1)}, bf16[384,1152]{1,0:T(8,128)(2,1)}) fusion(bf16[384,1152]{1,0:T(8,128)(2,1)} %collective-permute-done.17, bf16[384,1152]{1,0:T(8,128)(2,1)} %collective-permute-done.16, bf16[384,1152]{1,0:T(8,128)(2,1)} %get-tuple-element.89, bf16[384,1152]{1,0:T(8,128)(2,1)} %collective-permute-done.20, ...), kind=kLoop, calls=%fused_computation.3 | loop fusion | flops 6193152 | bytes 7077889 | tf_op jit(solution)/shard_map/convert_element_type | solution.py:449
  137.9 3.0 %collective-permute-start.23 = (bf16[384,1152]{1,0:T(8,128)(2,1)}, bf16[384,1152]{1,0:T(8,128)(2,1)S(1)}, u32[]{:S(2)}, u32[]{:S(2)}) collective-permute-start(bf16[384,1152]{1,0:T(8,128)(2,1)} %get-tuple-element.105), channel_id=1, source_target_pairs={{0,64},{16,80},{32,96},{48,112},{64,0},{80,16},{96,32},{112,48},{1... | collective-permute-start | bytes 2654216 | tf_op jit(solution)/shard_map/ppermute | solution.py:451
  140.9 8.9 %tail_ready.1 = (bf16[512,3072]{1,0:T(8,128)(2,1)}, bf16[368,3072]{1,0:T(8,128)(2,1)}) custom-call(s32[18]{0:T(128)} %stack.101.table, bf16[368,3072]{1,0:T(8,128)(2,1)} %get-tuple-element.99.own, bf16[368,1536]{1,0:T(8,128)(2,1)} %collective-permute-done.18.side_a, bf16[368,1536]{1,0:T(8,128)(2,1)} %collective-permute-done.19.side_b, ...), custom_call_target="tpu_custom_call" | custom-call | flops 706560 | bytes 176640 | tf_op jit(solution)/shard_map/tail_ready/pallas_call | solution.py:220
  149.8 8.4 %collective-permute-done.23.taken = bf16[384,1152]{1,0:T(8,128)(2,1)S(1)} collective-permute-done((bf16[384,1152]{1,0:T(8,128)(2,1)}, bf16[384,1152]{1,0:T(8,128)(2,1)S(1)}, u32[]{:S(2)}, u32[]{:S(2)}) %collective-permute-start.23) | collective-permute-done | bytes 884768 | tf_op jit(solution)/shard_map/ppermute | solution.py:451
  158.2 0.9 copy-done.4
  159.1 7.9 %tail_last.1 = (bf16[512,3072]{1,0:T(8,128)(2,1)}, bf16[384,1152]{1,0:T(8,128)(2,1)}) custom-call(s32[18]{0:T(128)} %stack.101.table, bf16[512,3072]{1,0:T(8,128)(2,1)} %get-tuple-element.100.partial, bf16[368,3072]{1,0:T(8,128)(2,1)} %get-tuple-element.101.slope, bf16[368,1536]{1,0:T(8,128)(2,1)} %collective-permute-done.21.sum_a, ...), custom_call_target="tpu_custom_call" | custom-call | flops 4521984 | bytes 11304960 | tf_op jit(solution)/shard_map/tail_last/pallas_call | solution.py:262
  (23 shorter events, 0.2 us)
Async XLA Ops:
  0.6 6.2 %collective-permute-start = (bf16[512,1152]{1,0:T(8,128)(2,1)}, bf16[512,1152]{1,0:T(8,128)(2,1)}, u32[]{:S(2)}, u32[]{:S(2)}) collective-permute-start(bf16[512,1152]{1,0:T(8,128)(2,1)} %own.1), channel_id=1, source_target_pairs={{0,4},{4,0},{8,12},{12,8},{1,5},{5,1},{9,13},{13,9},{2,6},{6,2},{1... | collective-permute-start | bytes 3538952 | tf_op jit(solution)/shard_map/ppermute | solution.py:377
  2.5 10.4 %collective-permute-start.1 = (bf16[144,1152]{1,0:T(8,128)(2,1)S(1)}, bf16[144,1152]{1,0:T(8,128)(2,1)}, u32[]{:S(2)}, u32[]{:S(2)}) collective-permute-start(bf16[144,1152]{1,0:T(8,128)(2,1)S(1)} %get-tuple-element.107), channel_id=1, source_target_pairs={{0,8},{4,12},{8,0},{12,4},{1,9},{5,13},{9,1},{13,5},{2,10},{6,14},... | collective-permute-start | bytes 995336 | tf_op jit(solution)/shard_map/ppermute | solution.py:376
  12.8 2.5 %collective-permute-start.2 = (bf16[144,1152]{1,0:T(8,128)(2,1)}, bf16[144,1152]{1,0:T(8,128)(2,1)S(1)}, u32[]{:S(2)}, u32[]{:S(2)}) collective-permute-start(bf16[144,1152]{1,0:T(8,128)(2,1)} %collective-permute-done.1), channel_id=1, source_target_pairs={{0,4},{4,0},{8,12},{12,8},{1,5},{5,1},{9,13},{13,9},{2,6},{6,2},{1... | collective-permute-start | bytes 995336 | tf_op jit(solution)/shard_map/ppermute | solution.py:380
  13.0 22.1 %collective-permute-start.3 = (bf16[368,1152]{1,0:T(8,128)(2,1)}, bf16[368,1152]{1,0:T(8,128)(2,1)S(1)}, u32[]{:S(2)}, u32[]{:S(2)}) collective-permute-start(bf16[368,1152]{1,0:T(8,128)(2,1)} %slice.23), channel_id=1, source_target_pairs={{0,8},{4,12},{8,0},{12,4},{1,9},{5,13},{9,1},{13,5},{2,10},{6,14},... | collective-permute-start | bytes 2543624 | tf_op jit(solution)/shard_map/ppermute | solution.py:381
  15.4 2.5 %copy-start.1 = (bf16[144,1152]{1,0:T(8,128)(2,1)}, bf16[144,1152]{1,0:T(8,128)(2,1)S(1)}, u32[]{:S(2)}) copy-start(bf16[144,1152]{1,0:T(8,128)(2,1)S(1)} %collective-permute-done.2) | copy-start | bytes 995332
  28.2 44.7 %collective-permute-start.8 = (bf16[144,3072]{1,0:T(8,128)(2,1)}, bf16[144,3072]{1,0:T(8,128)(2,1)}, u32[]{:S(2)}, u32[]{:S(2)}) collective-permute-start(bf16[144,3072]{1,0:T(8,128)(2,1)} %get-tuple-element.63), channel_id=1, source_target_pairs={{0,1},{1,2},{2,3},{3,0},{4,5},{5,6},{6,7},{7,4},{8,9},{9,10},{10,1... | collective-permute-start | bytes 2654216 | tf_op jit(solution)/shard_map/ppermute | solution.py:387
  30.1 42.8 %collective-permute-start.9 = (bf16[144,3072]{1,0:T(8,128)(2,1)}, bf16[144,3072]{1,0:T(8,128)(2,1)}, u32[]{:S(2)}, u32[]{:S(2)}) collective-permute-start(bf16[144,3072]{1,0:T(8,128)(2,1)} %get-tuple-element.64), channel_id=1, source_target_pairs={{0,3},{1,0},{2,1},{3,2},{4,7},{5,4},{6,5},{7,6},{8,11},{9,8},{10,9... | collective-permute-start | bytes 2654216 | tf_op jit(solution)/shard_map/ppermute | solution.py:388
  32.3 40.6 %collective-permute-start.10 = (bf16[144,3072]{1,0:T(8,128)(2,1)}, bf16[144,3072]{1,0:T(8,128)(2,1)}, u32[]{:S(2)}, u32[]{:S(2)}) collective-permute-start(bf16[144,3072]{1,0:T(8,128)(2,1)} %get-tuple-element.65), channel_id=1, source_target_pairs={{0,2},{1,3},{2,0},{3,1},{4,6},{5,7},{6,4},{7,5},{8,10},{9,11},{10,... | collective-permute-start | bytes 2654216 | tf_op jit(solution)/shard_map/ppermute | solution.py:389
  35.2 4.8 %collective-permute-start.7 = (bf16[80,1152]{1,0:T(8,128)(2,1)S(1)}, bf16[80,1152]{1,0:T(8,128)(2,1)S(1)}, u32[]{:S(2)}, u32[]{:S(2)}) collective-permute-start(bf16[80,1152]{1,0:T(8,128)(2,1)S(1)} %slice.27), channel_id=1, source_target_pairs={{0,4},{4,0},{8,12},{12,8},{1,5},{5,1},{9,13},{13,9},{2,6},{6,2},{1... | collective-permute-start | bytes 552968 | tf_op jit(solution)/shard_map/ppermute | solution.py:394
  35.3 1.7 %collective-permute-start.4 = (bf16[96,1152]{1,0:T(8,128)(2,1)S(1)}, bf16[96,1152]{1,0:T(8,128)(2,1)S(1)}, u32[]{:S(2)}, u32[]{:S(2)}) collective-permute-start(bf16[96,1152]{1,0:T(8,128)(2,1)S(1)} %get-tuple-element.110), channel_id=1, source_target_pairs={{0,4},{4,0},{8,12},{12,8},{1,5},{5,1},{9,13},{13,9},{2,6},{6,2},{1... | collective-permute-start | bytes 663560 | tf_op jit(solution)/shard_map/ppermute | solution.py:394
  36.9 3.2 %copy-start = (bf16[512,1152]{1,0:T(8,128)(2,1)S(1)}, bf16[512,1152]{1,0:T(8,128)(2,1)}, u32[]{:S(2)}) copy-start(bf16[512,1152]{1,0:T(8,128)(2,1)} %own.1) | copy-start | bytes 3538948
  37.0 1.5 collective-permute-start.5
  38.5 1.5 collective-permute-start.6
  50.6 35.6 %collective-permute-start.12 = (bf16[384,1152]{1,0:T(8,128)(2,1)}, bf16[384,1152]{1,0:T(8,128)(2,1)S(1)}, u32[]{:S(2)}, u32[]{:S(2)}) collective-permute-start(bf16[384,1152]{1,0:T(8,128)(2,1)} %get-tuple-element.69), channel_id=1, source_target_pairs={{0,16},{16,32},{32,48},{48,0},{64,80},{80,96},{96,112},{112,64},{1... | collective-permute-start | bytes 2654216 | tf_op jit(solution)/shard_map/ppermute | solution.py:409
  52.1 34.0 %collective-permute-start.11 = (bf16[384,1152]{1,0:T(8,128)(2,1)}, bf16[384,1152]{1,0:T(8,128)(2,1)}, u32[]{:S(2)}, u32[]{:S(2)}) collective-permute-start(bf16[384,1152]{1,0:T(8,128)(2,1)} %get-tuple-element.59), channel_id=1, source_target_pairs={{0,48},{16,0},{32,16},{48,32},{64,112},{80,64},{96,80},{112,96},{1... | collective-permute-start | bytes 2654216 | tf_op jit(solution)/shard_map/ppermute | solution.py:408
  72.9 28.5 %collective-permute-start.14 = (bf16[368,1536]{1,0:T(8,128)(2,1)}, bf16[368,1536]{1,0:T(8,128)(2,1)}, u32[]{:S(2)}, u32[]{:S(2)}) collective-permute-start(bf16[368,1536]{1,0:T(8,128)(2,1)} %get-tuple-element.79), channel_id=1, source_target_pairs={{0,1},{1,2},{2,3},{3,0},{4,5},{5,6},{6,7},{7,4},{8,9},{9,10},{10,1... | collective-permute-start | bytes 3391496 | tf_op jit(solution)/shard_map/ppermute | solution.py:414
  74.1 27.3 %collective-permute-start.13 = (bf16[368,1536]{1,0:T(8,128)(2,1)}, bf16[368,1536]{1,0:T(8,128)(2,1)}, u32[]{:S(2)}, u32[]{:S(2)}) collective-permute-start(bf16[368,1536]{1,0:T(8,128)(2,1)} %get-tuple-element.75), channel_id=1, source_target_pairs={{0,3},{1,0},{2,1},{3,2},{4,7},{5,4},{6,5},{7,6},{8,11},{9,8},{10,9... | collective-permute-start | bytes 3391496 | tf_op jit(solution)/shard_map/ppermute | solution.py:413
  86.2 0.9 copy-start.5
  87.1 22.4 %collective-permute-start.15 = (bf16[384,1152]{1,0:T(8,128)(2,1)}, bf16[384,1152]{1,0:T(8,128)(2,1)S(1)}, u32[]{:S(2)}, u32[]{:S(2)}) collective-permute-start(bf16[384,1152]{1,0:T(8,128)(2,1)} %get-tuple-element.82), channel_id=1, source_target_pairs={{0,16},{16,32},{32,48},{48,0},{64,80},{80,96},{96,112},{112,64},{1... | collective-permute-start | bytes 2654216 | tf_op jit(solution)/shard_map/ppermute | solution.py:419
  88.1 21.4 %collective-permute-start.16 = (bf16[384,1152]{1,0:T(8,128)(2,1)}, bf16[384,1152]{1,0:T(8,128)(2,1)}, u32[]{:S(2)}, u32[]{:S(2)}) collective-permute-start(bf16[384,1152]{1,0:T(8,128)(2,1)} %get-tuple-element.84), channel_id=1, source_target_pairs={{0,48},{16,0},{32,16},{48,32},{64,112},{80,64},{96,80},{112,96},{1... | collective-permute-start | bytes 2654216 | tf_op jit(solution)/shard_map/ppermute | solution.py:420
  101.4 29.4 %collective-permute-start.18 = (bf16[368,1536]{1,0:T(8,128)(2,1)}, bf16[368,1536]{1,0:T(8,128)(2,1)}, u32[]{:S(2)}, u32[]{:S(2)}) collective-permute-start(bf16[368,1536]{1,0:T(8,128)(2,1)} %get-tuple-element.93), channel_id=1, source_target_pairs={{0,1},{1,2},{2,3},{3,0},{4,5},{5,6},{6,7},{7,4},{8,9},{9,10},{10,1... | collective-permute-start | bytes 3391496 | tf_op jit(solution)/shard_map/ppermute | solution.py:425
  102.6 28.2 %collective-permute-start.19 = (bf16[368,1536]{1,0:T(8,128)(2,1)}, bf16[368,1536]{1,0:T(8,128)(2,1)}, u32[]{:S(2)}, u32[]{:S(2)}) collective-permute-start(bf16[368,1536]{1,0:T(8,128)(2,1)} %get-tuple-element.95), channel_id=1, source_target_pairs={{0,3},{1,0},{2,1},{3,2},{4,7},{5,4},{6,5},{7,6},{8,11},{9,8},{10,9... | collective-permute-start | bytes 3391496 | tf_op jit(solution)/shard_map/ppermute | solution.py:426
  104.6 8.0 %copy-start.2 = (bf16[368,1536]{1,0:T(8,128)(2,1)S(1)}, bf16[368,1536]{1,0:T(8,128)(2,1)}, u32[]{:S(2)}) copy-start(bf16[368,1536]{1,0:T(8,128)(2,1)} %get-tuple-element.73) | copy-start | bytes 3391492
  104.6 8.0 %copy-start.3 = (bf16[368,1536]{1,0:T(8,128)(2,1)S(1)}, bf16[368,1536]{1,0:T(8,128)(2,1)}, u32[]{:S(2)}) copy-start(bf16[368,1536]{1,0:T(8,128)(2,1)} %get-tuple-element.77) | copy-start | bytes 3391492
  109.5 23.4 %collective-permute-start.20 = (bf16[384,1152]{1,0:T(8,128)(2,1)}, bf16[384,1152]{1,0:T(8,128)(2,1)}, u32[]{:S(2)}, u32[]{:S(2)}) collective-permute-start(bf16[384,1152]{1,0:T(8,128)(2,1)} %get-tuple-element.97), channel_id=1, source_target_pairs={{0,48},{16,0},{32,16},{48,32},{64,112},{80,64},{96,80},{112,96},{1... | collective-permute-start | bytes 2654216 | tf_op jit(solution)/shard_map/ppermute | solution.py:433
  112.6 21.1 %collective-permute-start.17 = (bf16[384,1152]{1,0:T(8,128)(2,1)}, bf16[384,1152]{1,0:T(8,128)(2,1)}, u32[]{:S(2)}, u32[]{:S(2)}) collective-permute-start(bf16[384,1152]{1,0:T(8,128)(2,1)} %get-tuple-element.91), channel_id=1, source_target_pairs={{0,16},{16,32},{32,48},{48,0},{64,80},{80,96},{96,112},{112,64},{1... | collective-permute-start | bytes 2654216 | tf_op jit(solution)/shard_map/ppermute | solution.py:434
  130.8 27.4 %collective-permute-start.21 = (bf16[368,1536]{1,0:T(8,128)(2,1)}, bf16[368,1536]{1,0:T(8,128)(2,1)}, u32[]{:S(2)}, u32[]{:S(2)}) collective-permute-start(bf16[368,1536]{1,0:T(8,128)(2,1)} %get-tuple-element.102), channel_id=1, source_target_pairs={{0,3},{1,0},{2,1},{3,2},{4,7},{5,4},{6,5},{7,6},{8,11},{9,8},{10,9... | collective-permute-start | bytes 3391496 | tf_op jit(solution)/shard_map/ppermute | solution.py:443
  132.3 25.9 %collective-permute-start.22 = (bf16[368,1536]{1,0:T(8,128)(2,1)}, bf16[368,1536]{1,0:T(8,128)(2,1)}, u32[]{:S(2)}, u32[]{:S(2)}) collective-permute-start(bf16[368,1536]{1,0:T(8,128)(2,1)} %get-tuple-element.103), channel_id=1, source_target_pairs={{0,1},{1,2},{2,3},{3,0},{4,5},{5,6},{6,7},{7,4},{8,9},{9,10},{10,1... | collective-permute-start | bytes 3391496 | tf_op jit(solution)/shard_map/ppermute | solution.py:444
  137.9 20.3 %collective-permute-start.23 = (bf16[384,1152]{1,0:T(8,128)(2,1)}, bf16[384,1152]{1,0:T(8,128)(2,1)S(1)}, u32[]{:S(2)}, u32[]{:S(2)}) collective-permute-start(bf16[384,1152]{1,0:T(8,128)(2,1)} %get-tuple-element.105), channel_id=1, source_target_pairs={{0,64},{16,80},{32,96},{48,112},{64,0},{80,16},{96,32},{112,48},{1... | collective-permute-start | bytes 2654216 | tf_op jit(solution)/shard_map/ppermute | solution.py:451
  158.2 0.9 copy-start.4
